TPU v7x, 256 devices: a whole 4x4x8 slice. The times are simulated.
256 devices in a mesh: ctx: 64 (over z, x_hi, y), tp: 4 (over x_lo, core).
Axes of the slice: x: 4 (x_hi: 2, x_lo: 2; x = x_hi * 2 + x_lo), y: 4, z: 8, core: 2. Of those that a mesh axis runs over, the one named last changes fastest.
Arguments:
- queries: bfloat16 [9216, 3072], P('ctx', 'tp'), may hold values from -8 to 8
- keys: bfloat16 [9216, 3072], P('ctx', 'tp'), may hold values from -8 to 8
- values: bfloat16 [9216, 3072], P('ctx', 'tp'), may hold values from -6 to 6
- positions: int32 [9216], P('ctx'), may hold values from 0 to 9215, as said below
- lambda_vecs: float32 [4, 12, 128], P(None, 'tp'), may hold values from -0.6 to 0.6
- head_gain: float32 [3072], P('tp'), may hold values from 0.5 to 1.5
- out_weight: bfloat16 [3072, 5120], P('tp'), may hold values from -0.109375 to 0.109375
- residual: bfloat16 [9216, 5120], P('ctx', 'tp'), may hold values from -3 to 3
Outputs:
- mixed: bfloat16 [9216, 5120], P('ctx', 'tp')
Inputs may be any that keep to these rules, and one draw needn't show every extreme that they name: Each aligned run of 72 rows holds 72 consecutive positions in increasing order; the runs' first positions are the multiples of 72, each once.
All inputs are finite; a program needn't handle non-finite values.
Results may differ from a plain program's by a relative error of at most 0.012.
Values may be sent and summed in bfloat16 or wider, within the bound.
No kernel may reach another device: no remote copies, remote signals or barrier semaphores. Data moves between devices by JAX's collectives and lax.ppermute only.
A program may use at most 192 MiB of HBM per device.

v0:
```python
import math

import jax
import jax.numpy as jnp
from jax import lax
from jax.sharding import PartitionSpec as P

lambda_init = 0.2
out_factor = 0.8
norm_eps = 1e-05


def per_device(queries, keys, values, positions, lambda_vecs, head_gain, out_weight, residual):
    row_count = queries.shape[0]
    head_count = lambda_vecs.shape[1]
    head_depth = lambda_vecs.shape[2]
    score_scale = 1.0 / math.sqrt(head_depth)
    query_heads = queries.reshape(row_count, head_count, 2, head_depth)
    all_positions = lax.all_gather(positions, "ctx", axis=0, tiled=True)
    key_piece = lax.all_gather(keys, "ctx", axis=0, tiled=True)
    value_piece = lax.all_gather(values, "ctx", axis=0, tiled=True)
    piece_rows = key_piece.shape[0]
    allowed = all_positions[None, :] <= positions[:, None]
    highest = jnp.full((2, head_count, row_count), -1e30, jnp.float32)
    scores = (
        jnp.einsum(
            "ihad,jhad->ahij",
            query_heads,
            key_piece.reshape(piece_rows, head_count, 2, head_depth),
            preferred_element_type=jnp.float32,
        )
        * score_scale
    )
    scores = jnp.where(allowed, scores, -jnp.inf)
    fresh = jnp.maximum(highest, jnp.max(scores, -1))
    expo = jnp.where(allowed, jnp.exp(scores - fresh[..., None]), 0.0)
    total = jnp.sum(expo, -1)
    numerator = jnp.einsum(
        "ahij,jhe->ahie",
        expo.astype(jnp.bfloat16),
        value_piece.reshape(piece_rows, head_count, 2 * head_depth),
        preferred_element_type=jnp.float32,
    )
    highest, total, numerator = (fresh, total, numerator)
    attn = numerator / total[..., None]
    lambda_head = (
        jnp.exp(jnp.sum(lambda_vecs[0] * lambda_vecs[1], -1))
        - jnp.exp(jnp.sum(lambda_vecs[2] * lambda_vecs[3], -1))
        + lambda_init
    )
    diff = attn[0] - lambda_head[:, None, None] * attn[1]
    mean_square = jnp.mean(diff * diff, -1, keepdims=True)
    normed = (
        out_factor
        * diff
        / jnp.sqrt(mean_square + norm_eps)
        * head_gain.reshape(head_count, 1, 2 * head_depth)
    )
    normed = (
        jnp.transpose(normed, (1, 0, 2))
        .reshape(row_count, head_count * 2 * head_depth)
        .astype(jnp.bfloat16)
    )
    shares = lax.psum_scatter(
        lax.dot_general(
            out_weight, normed, (((0,), (1,)), ((), ())), preferred_element_type=jnp.float32
        ).astype(jnp.bfloat16),
        "tp",
        scatter_dimension=0,
        tiled=True,
    ).astype(jnp.float32)
    projected = jnp.transpose(shares)
    return (projected + residual.astype(jnp.float32)).astype(jnp.bfloat16)


def solution(mesh):
    placed = (
        P("ctx", "tp"),
        P("ctx", "tp"),
        P("ctx", "tp"),
        P("ctx"),
        P(None, "tp", None),
        P("tp"),
        P("tp", None),
        P("ctx", "tp"),
    )
    return jax.shard_map(
        per_device, mesh=mesh, in_specs=placed, out_specs=P("ctx", "tp"), check_vma=False
    )
```

profile of v0, /device:TPU:1, one launch (start us, length us, event | category | flops | bytes accessed | tf_op | source)
XLA Modules:
  0.0 507.1 jit_solution(6777662970282332329)
XLA Ops:
  6.5 0.7 all-gather.3.cloned.1.call-update
  7.3 0.0 all-gather.5.cloned.1.call-start
  7.3 0.7 all-gather.5.cloned.1.call-update
  8.0 0.0 reduce-scatter.2.cloned.1.call-start
  8.1 1.0 reshape.37
  9.1 0.7 mul.50
  9.8 1.3 dynamic-slice
  11.7 0.9 dynamic-update-slice
  12.6 310.0 %all-reduce = s32[9216]{0:T(1024)S(1)} all-reduce(s32[9216]{0:T(1024)S(1)} %dynamic-update-slice), channel_id=1, replica_groups=mesh['ctx'=64,'tp'=4] {'ctx'}, use_global_device_ids=true, to_apply=%add | all-reduce | flops 9216 | bytes 73728
  322.6 0.9 multiply_reduce_fusion.2
  323.6 1.4 broadcast_compare_fusion
  325.0 0.0 all-gather.3.cloned.1.call-done
  325.0 18.7 %copy.20 = bf16[9216,768]{0,1:T(8,128)(2,1)} copy(bf16[9216,768]{1,0:T(8,128)(2,1)} %all-gather.3.cloned.1.call-done) | data formatting | bytes 28311552 | tf_op jit(solution)/shard_map/all_gather | solution.py:20
  343.7 16.2 %fusion = (f32[2,3,144]{2,1,0:T(4,128)S(1)}, f32[2,3,144,9216]{3,2,1,0:T(8,128)}) fusion(pred[144,9216]{1,0:T(8,128)(4,1)S(1)} %broadcast_compare_fusion, bf16[9216,3,2,128]{0,3,2,1:T(8,128)(2,1)} %bitcast.44, bf16[144,3,2,128]{3,2,1,0:T(2,128)(2,1)S(1)} %reshape.37), kind=kOutput, calls=%fused_computation.2 | convolution fusion | flops 2062318720 | bytes 47558016 | tf_op jit(solution)/shard_map/ihad,jhad->ahij/dot_general | solution.py:26
  359.9 20.7 %fusion.1 = (f32[2,3,144]{2,1,0:T(4,128)S(1)}, bf16[2,3,144,9216]{3,2,1,0:T(8,128)(2,1)}) fusion(f32[2,3,144,9216]{3,2,1,0:T(8,128)} %get-tuple-element.10, f32[2,3,144]{2,1,0:T(4,128)S(1)} %broadcast_maximum_fusion, pred[144,9216]{1,0:T(8,128)(4,1)S(1)} %broadcast_compare_fusion), kind=kLoop, calls=%fused_computation.3 | loop fusion | flops 47774880 | bytes 49109760 | tf_op jit(solution)/shard_map/reduce_sum | solution.py:37
  380.6 16.6 %all-gather.5.cloned.1.call-done = bf16[9216,768]{1,0:T(8,128)(2,1)} async-done(((bf16[144,768]{1,0:T(8,128)(2,1)}), bf16[9216,768]{1,0:T(8,128)(2,1)}) %all-gather.5.cloned.1.call-update) | async-done | bytes 14155792 | tf_op jit(solution)/shard_map/all_gather | solution.py:21
  397.2 17.8 %copy.23 = bf16[9216,768]{0,1:T(8,128)(2,1)} copy(bf16[9216,768]{1,0:T(8,128)(2,1)} %all-gather.5.cloned.1.call-done) | data formatting | bytes 28311552 | tf_op jit(solution)/shard_map/all_gather | solution.py:21
  415.0 20.3 %fusion.11 = f32[2,3,144,256]{3,2,0,1:T(8,128)S(1)} fusion(bf16[9216,3,256,1]{0,2,3,1:T(8,128)(2,1)} %bitcast.45, bf16[2,3,144,9216]{3,2,1,0:T(8,128)(2,1)} %get-tuple-element.8, f32[2,3,144]{2,0,1:T(2,128)S(1)} %copy.26), kind=kOutput, calls=%fused_computation.13 | convolution fusion | flops 4077084672 | bytes 30969216 | tf_op jit(solution)/shard_map/ahij,jhe->ahie/dot_general | solution.py:38
  435.3 0.3 multiply_reduce_fusion
  435.5 0.2 fusion.18
  435.7 5.7 %fusion.7 = bf16[5120,144]{0,1:T(8,128)(2,1)} fusion(bf16[144,768]{1,0:T(8,128)(2,1)S(1)} %bitcast.46, bf16[768,5120]{1,0:T(8,128)(2,1)} %param.14), kind=kOutput, calls=%fused_computation.10 | convolution fusion | flops 1133199360 | bytes 9560064 | tf_op jit(solution)/shard_map/dot_general | solution.py:65
  441.5 0.0 reduce-scatter.2.cloned.1.call-update
  441.5 57.3 %reduce-scatter.2.cloned.1.call-done = bf16[1280,144]{0,1:T(8,128)(2,1)} async-done(((bf16[5120,144]{0,1:T(8,128)(2,1)}), bf16[1280,144]{0,1:T(8,128)(2,1)}) %reduce-scatter.2.cloned.1.call-update) | async-done | bytes 368656 | tf_op jit(solution)/shard_map/reduce_scatter | solution.py:64
  498.8 1.8 fusion.14
  (9 shorter events, 0.1 us)
Async XLA Ops:
  6.5 318.5 %all-gather.3.cloned.1.call-start = ((), (), s32[]{:S(2)}) async-start(), calls=%async_computation.1 | async-start | bytes 14376960 | tf_op jit(solution)/shard_map/all_gather | solution.py:20
  7.3 390.0 %all-gather.5.cloned.1.call-start = ((), (), s32[]{:S(2)}) async-start(), calls=%async_computation.2 | async-start | bytes 14376960 | tf_op jit(solution)/shard_map/all_gather | solution.py:21
  8.0 490.8 %reduce-scatter.2.cloned.1.call-start = ((), (), s32[]{:S(2)}) async-start(), calls=%async_computation.3 | async-start | bytes 1843200 | tf_op jit(solution)/shard_map/reduce_scatter | solution.py:64
  435.2 63.5 %copy-start = (bf16[144,1280]{1,0:T(8,128)(2,1)S(1)}, bf16[144,1280]{1,0:T(8,128)(2,1)}, u32[]{:S(2)}) copy-start(bf16[144,1280]{1,0:T(8,128)(2,1)} %param.15) | copy-start | bytes 1105924
Sparse Core Ops, SparseCore 0:
  11.0 194.6 all-gather.2
  209.4 187.7 all-gather.4
  441.6 57.1 reduce-scatter.1
where the time goes:
time: 508 us; the launch traced here: 507 us
  blocking collectives  310 us (61%)
  waiting for transfers between devices  75.3 us (15%)
  matrix products  42.2 us (8%)
  local copies, waits for them, and re-layouts  40.3 us (8%)
  other arithmetic  25.4 us (5%)
  between operations  13.8 us (3%)
    unnamed x1, blocking collectives  310 us
    reduce_scatter x1, waiting for transfers between devices, per_device(): lax.psum_scatter(lax.dot_general(out_weight, normed, (((0,), (1,)), ((),...  57.3 us
    reduce_sum x1, other arithmetic, per_device(): total = jnp.sum(expo, -1)  20.7 us
    dot_general x1, matrix products, per_device(): jnp.einsum('ahij,jhe->ahie', expo.astype(jnp.bfloat16), value_piece.resha...  20.3 us
    all_gather x1, local copies, waits for them, and re-layouts, per_device(): key_piece = lax.all_gather(keys, 'ctx', axis=0, tiled=True)  18.7 us
    all_gather x1, local copies, waits for them, and re-layouts, per_device(): value_piece = lax.all_gather(values, 'ctx', axis=0, tiled=True)  17.8 us
    all_gather x1, waiting for transfers between devices, per_device(): value_piece = lax.all_gather(values, 'ctx', axis=0, tiled=True)  16.6 us
    dot_general x1, matrix products, per_device(): jnp.einsum('ihad,jhad->ahij', query_heads, key_piece.reshape(piece_rows,...  16.2 us
  transfers between devices with their start and end apart: 3, of which 2 were waited for; matrix products, arithmetic and copies ran while one was open for 12% of the time, Pallas kernels for 0%

commit v1 on v0

v1 whole, which is shorter than its diff:
```python
import math

import jax
import jax.numpy as jnp
from jax import lax
from jax.experimental import pallas as pl
from jax.experimental.pallas import tpu as pltpu
from jax.sharding import Mesh, PartitionSpec as P

lambda_init = 0.2
out_factor = 0.8
norm_eps = 1e-05

HD = 128
RUN = 72
NEG = -1e30
FLOOR = -1e29
f32 = jnp.float32
bf16 = jnp.bfloat16


def shift(x, axis, size, step):
    return lax.ppermute(x, axis, [(i, (i + step) % size) for i in range(size)])


def attend_kernel(rows, slots, qb, kb, *refs):
    nq = slots // 2
    q_refs = refs[:nq]
    kv_ref = refs[nq]
    o_refs = refs[nq + 1 : 2 * nq + 1]
    lse_ref = refs[2 * nq + 1]
    q_s, k_s, v_s, lse_s = refs[2 * nq + 2 :]
    head = pl.program_id(0)
    keys = kv_ref.shape[0] * rows
    tile = 2 * rows
    for z in range(kv_ref.shape[0]):
        k_s[z * rows : (z + 1) * rows, :] = kv_ref[z, :rows, :]
        v_s[z * rows : (z + 1) * rows, :] = kv_ref[z, rows : 2 * rows, :]
    for i in range(nq):
        for d in range(2):
            q_s[(2 * i + d) * rows : (2 * i + d + 1) * rows, :] = q_refs[i][d, :rows, :]
    col = lax.broadcasted_iota(jnp.int32, (1, keys), 1)
    kpos = lax.rem(col, RUN)
    for b in range(keys // RUN):
        kpos = kpos + jnp.where(lax.div(col, RUN) == b, kb[b] * RUN, 0)
    row = lax.broadcasted_iota(jnp.int32, (tile, 1), 0)
    lane = lax.broadcasted_iota(jnp.int32, (tile, HD), 1)
    scale = math.log2(math.e) / math.sqrt(HD)

    @pl.when(head == 0)
    def _():
        lse_s[...] = jnp.zeros_like(lse_s)

    for t in range(nq):
        qpos = lax.rem(row, RUN)
        for b in range(tile // RUN):
            qpos = qpos + jnp.where(lax.div(row, RUN) == b, qb[t * (tile // RUN) + b] * RUN, 0)
        allowed = kpos <= qpos
        stats = lse_s[t * tile : (t + 1) * tile, :]
        for a in range(2):
            s = lax.dot_general(
                q_s[t * tile : (t + 1) * tile, a * HD : (a + 1) * HD],
                k_s[:, a * HD : (a + 1) * HD],
                (((1,), (1,)), ((), ())),
                preferred_element_type=f32,
            )
            s = jnp.where(allowed, s, NEG)
            m = jnp.maximum(jnp.max(s, -1, keepdims=True), FLOOR) * scale
            p = jnp.exp2(s * scale - m)
            total = jnp.sum(p, -1, keepdims=True)
            num = jnp.dot(p.astype(bf16), v_s[...], preferred_element_type=f32)
            some = total > 0.0
            safe = jnp.where(some, total, 1.0)
            o_refs[t][:, a * 2 * HD : (a + 1) * 2 * HD] = num * (1.0 / safe)
            lse = jnp.where(some, m + jnp.log2(safe), NEG)
            stats = jnp.where(lane == head * 2 + a, lse, stats)
        lse_s[t * tile : (t + 1) * tile, :] = stats

    @pl.when(head == pl.num_programs(0) - 1)
    def _():
        lse_ref[...] = jnp.transpose(lse_s[...])[: lse_ref.shape[0], :]


def attend(q_parts, kv, qb, kb, rows, heads):
    nq = len(q_parts)
    slots = 2 * nq
    zs = kv.shape[0]
    pad = q_parts[0].shape[1]
    return pl.pallas_call(
        lambda *r: attend_kernel(rows, slots, *r),
        out_shape=[jax.ShapeDtypeStruct((2 * rows, heads * 4 * HD), f32)] * nq
        + [jax.ShapeDtypeStruct((8, slots * rows), f32)],
        grid_spec=pltpu.PrefetchScalarGridSpec(
            num_scalar_prefetch=2,
            grid=(heads,),
            in_specs=[pl.BlockSpec((2, pad, 2 * HD), lambda h, *_: (0, 0, h))] * nq
            + [pl.BlockSpec((zs, kv.shape[1], 2 * HD), lambda h, *_: (0, 0, h))],
            out_specs=[pl.BlockSpec((2 * rows, 4 * HD), lambda h, *_: (0, h))] * nq
            + [pl.BlockSpec((8, slots * rows), lambda h, *_: (0, 0))],
            scratch_shapes=[
                pltpu.VMEM((slots * rows, 2 * HD), bf16),
                pltpu.VMEM((zs * rows, 2 * HD), bf16),
                pltpu.VMEM((zs * rows, 2 * HD), bf16),
                pltpu.VMEM((slots * rows, HD), f32),
            ],
        ),
        compiler_params=pltpu.CompilerParams(vmem_limit_bytes=56 << 20),
        name="attend",
    )(qb, kb, *q_parts, kv)


def weigh_kernel(heads, lam_ref, lse_ref, all_ref, *refs):
    nq = len(refs) // 2
    tile = refs[0].shape[0]
    w = jnp.exp2(lse_ref[...] - all_ref[...])
    w = jnp.concatenate([w, jnp.zeros((HD - w.shape[0], w.shape[1]), f32)], 0)
    w = jnp.transpose(w)
    for i in range(nq):
        for h in range(heads):
            w1 = w[i * tile : (i + 1) * tile, 2 * h : 2 * h + 1]
            w2 = w[i * tile : (i + 1) * tile, 2 * h + 1 : 2 * h + 2] * lam_ref[h]
            o1 = refs[i][:, h * 4 * HD : h * 4 * HD + 2 * HD]
            o2 = refs[i][:, h * 4 * HD + 2 * HD : (h + 1) * 4 * HD]
            refs[nq + i][:, h * 2 * HD : (h + 1) * 2 * HD] = (w1 * o1 - w2 * o2).astype(bf16)


def weigh(lam, lse, lse_all, outs, heads):
    nq = len(outs)
    vm = pl.BlockSpec(memory_space=pltpu.VMEM)
    return pl.pallas_call(
        lambda *r: weigh_kernel(heads, *r),
        out_shape=[jax.ShapeDtypeStruct((outs[0].shape[0], heads * 2 * HD), bf16)] * nq,
        in_specs=[pl.BlockSpec(memory_space=pltpu.SMEM), vm, vm] + [vm] * nq,
        out_specs=[vm] * nq,
        compiler_params=pltpu.CompilerParams(vmem_limit_bytes=48 << 20),
        name="weigh",
    )(lam, lse, lse_all, *outs)


def logsum(parts):
    top = parts[0]
    for p in parts[1:]:
        top = jnp.maximum(top, p)
    top = jnp.maximum(top, FLOOR)
    total = 0.0
    for p in parts:
        total = total + jnp.exp2(p - top)
    return jnp.where(total > 0.0, top + jnp.log2(jnp.maximum(total, 1e-37)), NEG)


def per_device(sizes, queries, keys, values, positions, lambda_vecs, head_gain, out_weight, residual):
    nz, nh, ny, nl, nc = sizes
    rows, width = queries.shape
    heads = lambda_vecs.shape[1]
    block = (positions[::RUN] // RUN).astype(bf16)
    ids = jnp.broadcast_to(jnp.pad(block, (0, width - block.shape[0]))[None, :], (16, width))

    kv = lax.all_gather(jnp.concatenate([keys, values, ids], 0), "z", axis=0, tiled=False)
    kb = kv[:, 2 * rows, : rows // RUN].astype(jnp.int32).reshape(-1)

    q_mine = jnp.concatenate([queries, ids], 0)
    q_pair = jnp.stack([q_mine, shift(q_mine, "h", nh, 1)], 0)
    q_parts = [q_pair] + [shift(q_pair, "y", ny, d) for d in range(1, ny)]
    qb = jnp.stack([q[:, rows, : rows // RUN] for q in q_parts], 0).astype(jnp.int32).reshape(-1)

    *outs, lse = attend(q_parts, kv, qb, kb, rows, heads)

    tile = 2 * rows
    own = [lse[:, i * tile : (i + 1) * tile] for i in range(ny)]
    back = [own[0]] + [shift(own[i], "y", ny, -i) for i in range(1, ny)]
    mine = logsum(back)
    swapped = jnp.concatenate([mine[:, rows:], mine[:, :rows]], 1)
    other = shift(swapped, "h", nh, 1)
    mine = logsum([mine, other])
    everyone = jnp.concatenate([mine] + [shift(mine, "y", ny, i) for i in range(1, ny)], 1)

    lam = (
        jnp.exp(jnp.sum(lambda_vecs[0] * lambda_vecs[1], -1))
        - jnp.exp(jnp.sum(lambda_vecs[2] * lambda_vecs[3], -1))
        + lambda_init
    )
    parts = weigh(lam, lse, everyone, outs, heads)

    got = [shift(parts[i], "y", ny, -i) for i in range(1, ny)]
    total = parts[0].astype(f32)
    for g in got:
        total = total + g.astype(f32)
    away = shift(total[rows:].astype(bf16), "h", nh, 1)
    diff = (total[:rows] + away.astype(f32)).reshape(rows, heads, 2 * HD)
    mean_square = jnp.mean(diff * diff, -1, keepdims=True)
    normed = out_factor * diff / jnp.sqrt(mean_square + norm_eps) * head_gain.reshape(1, heads, 2 * HD)
    normed = normed.reshape(rows, width).astype(bf16)

    share = jnp.dot(normed, out_weight, preferred_element_type=f32).astype(bf16)
    share = share.reshape(rows, nl, nc, -1)
    l, c = lax.axis_index("l"), lax.axis_index("c")
    keep = lax.dynamic_index_in_dim(share, c, 2, False)
    send = lax.dynamic_index_in_dim(share, 1 - c, 2, False)
    both = keep.astype(f32) + shift(send, "c", nc, 1).astype(f32)
    keep = lax.dynamic_index_in_dim(both, l, 1, False)
    send = lax.dynamic_index_in_dim(both, 1 - l, 1, False).astype(bf16)
    projected = keep + shift(send, "l", nl, 1).astype(f32)
    return (projected + residual.astype(f32)).astype(bf16)


def solution(mesh):
    sizes = (8, 2, 4, 2, 2)
    fine = Mesh(mesh.devices.reshape(sizes), ("z", "h", "y", "l", "c"))
    ctx, tp = ("z", "h", "y"), ("l", "c")
    placed = (
        P(ctx, tp),
        P(ctx, tp),
        P(ctx, tp),
        P(ctx),
        P(None, tp, None),
        P(tp),
        P(tp, None),
        P(ctx, tp),
    )
    return jax.shard_map(
        lambda *a: per_device(sizes, *a), mesh=fine, in_specs=placed, out_specs=P(ctx, tp), check_vma=False
    )
```

time: 508 us -> 180 us (0.35)
  blocking collectives: 310 us -> 0 us
  matrix products: 42.2 us -> 5.73 us
  starting transfers between devices: 0.08 us -> 27.1 us
  local copies, waits for them, and re-layouts: 40.3 us -> 15.5 us
  Pallas kernels: 0 us -> 23.3 us
  other arithmetic: 25.4 us -> 6.32 us
  waiting for transfers between devices: 75.3 us -> 88 us
    unnamed x1 -> x0, blocking collectives: 310 us -> none
    ppermute x0 -> x17, waiting for transfers between devices: none -> 71.7 us  [shift(): return lax.ppermute(x, axis, [(i, (i + step) % size) for i in range(size)])]
    reduce_scatter x1 -> x0, waiting for transfers between devices: 57.3 us -> none  [per_device(): lax.psum_scatter(lax.dot_general(out_weight, normed, (((0,), (1,)), ((),...]
    dot_general x3 -> x1, matrix products: 42.2 us -> 5.73 us  [per_device(): share = jnp.dot(normed, out_weight, preferred_element_type=f32).astype(bf16)]
    all_gather x2 -> x0, local copies, waits for them, and re-layouts: 36.4 us -> none  [the longest x1 18.7 us: per_device(): key_piece = lax.all_gather(keys, 'ctx', axis=0, tiled=True)]
    ppermute x0 -> x17, starting transfers between devices: none -> 27.1 us  [shift(): return lax.ppermute(x, axis, [(i, (i + step) % size) for i in range(size)])]
    pallas_call x0 -> x2, Pallas kernels: none -> 23.3 us  [the longest x1 20.1 us: attend(): pl.pallas_call(lambda *r: attend_kernel(rows, slots, *r), out_shape=[jax....]
    reduce_sum x1 -> x0, other arithmetic: 20.7 us -> none  [per_device(): total = jnp.sum(expo, -1)]
  transfers between devices with their start and end apart: 3 -> 18, of which waited for: 2 -> 17; matrix products, arithmetic and copies ran while one was open for 12% -> 1% of each run, Pallas kernels for 0% -> 0%
where the time goes in v1:
time: 180 us
  waiting for transfers between devices  88 us (49%)
  starting transfers between devices  27.1 us (15%)
  Pallas kernels  23.3 us (13%)
  local copies, waits for them, and re-layouts  15.5 us (9%)
  between operations  13.6 us (8%)
  other arithmetic  6.32 us (4%)
  matrix products  5.73 us (3%)
    ppermute x17, waiting for transfers between devices, shift(): return lax.ppermute(x, axis, [(i, (i + step) % size) for i in range(size)])  71.7 us
    ppermute x17, starting transfers between devices, shift(): return lax.ppermute(x, axis, [(i, (i + step) % size) for i in range(size)])  27.1 us
    pallas_call x1, Pallas kernels, attend(): pl.pallas_call(lambda *r: attend_kernel(rows, slots, *r), out_shape=[jax....  20.1 us
    all_gather x1, waiting for transfers between devices, per_device(): lax.all_gather(jnp.concatenate([keys, values, ids], 0), 'z', axis=0, tile...  16.3 us
    dot_general x1, matrix products, per_device(): share = jnp.dot(normed, out_weight, preferred_element_type=f32).astype(bf16)  5.73 us
    unnamed x29, local copies, waits for them, and re-layouts  4.82 us
    reshape x1, local copies, waits for them, and re-layouts, per_device(): share = share.reshape(rows, nl, nc, -1)  3.87 us
  transfers between devices with their start and end apart: 18, of which 17 were waited for; matrix products, arithmetic and copies ran while one was open for 1% of the time, Pallas kernels for 0%

profile of v1, /device:TPU:1, one launch (start us, length us, event | category | flops | bytes accessed | tf_op | source)
XLA Modules:
  0.0 179.6 jit_solution(15402441536983373057)
XLA Ops:
  7.4 1.8 %pad_maximum_fusion.1 = bf16[304,768]{1,0:T(8,128)(2,1)} fusion(bf16[16,768]{1,0:T(8,128)(2,1)S(1)} %broadcast_in_dim.12, bf16[144,768]{1,0:T(8,128)(2,1)} %param.10, bf16[144,768]{1,0:T(8,128)(2,1)} %param.9), kind=kLoop, calls=%fused_computation.12 | loop fusion | flops 1400832 | bytes 933888 | tf_op jit(solution)/shard_map/concatenate | solution.py:158
  9.3 3.7 %collective-permute-start = (bf16[160,768]{1,0:T(8,128)(2,1)S(1)}, bf16[160,768]{1,0:T(8,128)(2,1)S(1)}, u32[]{:S(2)}, u32[]{:S(2)}) collective-permute-start(bf16[160,768]{1,0:T(8,128)(2,1)S(1)} %get-tuple-element.28), channel_id=1, source_target_pairs={{0,16},{16,0},{1,17},{17,1},{2,18},{18,2},{3,19},{19,3},{4,20},{20... | collective-permute-start | bytes 737288 | tf_op jit(solution)/shard_map/ppermute | solution.py:23
  13.0 4.6 %collective-permute-done = bf16[160,768]{1,0:T(8,128)(2,1)S(1)} collective-permute-done((bf16[160,768]{1,0:T(8,128)(2,1)S(1)}, bf16[160,768]{1,0:T(8,128)(2,1)S(1)}, u32[]{:S(2)}, u32[]{:S(2)}) %collective-permute-start) | collective-permute-done | bytes 245792 | tf_op jit(solution)/shard_map/ppermute | solution.py:23
  17.6 3.8 %collective-permute-start.3 = (bf16[2,160,768]{2,1,0:T(8,128)(2,1)S(1)}, bf16[2,160,768]{2,1,0:T(8,128)(2,1)S(1)}, u32[]{:S(2)}, u32[]{:S(2)}) collective-permute-start(bf16[2,160,768]{2,1,0:T(8,128)(2,1)S(1)} %pad_maximum_fusion.r_2_), channel_id=1, source_target_pairs={{0,12},{4,0},{8,4},{12,8},{1,13},{5,1},{9,5},{13,9},{2,14},{6,2},{... | collective-permute-start | bytes 1474568 | tf_op jit(solution)/shard_map/ppermute | solution.py:23
  22.5 9.5 %collective-permute-done.3.r_5_ = bf16[2,160,768]{2,1,0:T(8,128)(2,1)S(1)} collective-permute-done((bf16[2,160,768]{2,1,0:T(8,128)(2,1)S(1)}, bf16[2,160,768]{2,1,0:T(8,128)(2,1)S(1)}, u32[]{:S(2)}, u32[]{:S(2)}) %collective-permute-start.3) | collective-permute-done | bytes 491552 | tf_op jit(solution)/shard_map/ppermute | solution.py:23
  32.0 1.9 %collective-permute-done.2.r_4_ = bf16[2,160,768]{2,1,0:T(8,128)(2,1)S(1)} collective-permute-done((bf16[2,160,768]{2,1,0:T(8,128)(2,1)S(1)}, bf16[2,160,768]{2,1,0:T(8,128)(2,1)S(1)}, u32[]{:S(2)}, u32[]{:S(2)}) %collective-permute-start.2) | collective-permute-done | bytes 491552 | tf_op jit(solution)/shard_map/ppermute | solution.py:23
  33.9 12.8 %collective-permute-done.1.r_3_ = bf16[2,160,768]{2,1,0:T(8,128)(2,1)S(1)} collective-permute-done((bf16[2,160,768]{2,1,0:T(8,128)(2,1)S(1)}, bf16[2,160,768]{2,1,0:T(8,128)(2,1)S(1)}, u32[]{:S(2)}, u32[]{:S(2)}) %collective-permute-start.1) | collective-permute-done | bytes 491552 | tf_op jit(solution)/shard_map/ppermute | solution.py:23
  47.4 16.3 %all-gather.3.cloned.1.call-done = bf16[2432,768]{1,0:T(8,128)(2,1)} async-done(((bf16[304,768]{1,0:T(8,128)(2,1)}), bf16[2432,768]{1,0:T(8,128)(2,1)}) %all-gather.3.cloned.1.call-update) | async-done | bytes 3735568 | tf_op jit(solution)/shard_map/all_gather | solution.py:158
  65.1 20.1 %attend.1 = (f32[288,1536]{1,0:T(8,128)}, f32[288,1536]{1,0:T(8,128)}, f32[288,1536]{1,0:T(8,128)}, f32[288,1536]{1,0:T(8,128)}, f32[8,1152]{1,0:T(8,128)}) custom-call(s32[16]{0:T(128)} %reshape.34.r_0_, s32[16]{0:T(128)} %reshape.35.r_1_, bf16[2,160,768]{2,1,0:T(8,128)(2,1)} %copy-done.3, bf16[2,160,768]{2,1,0:T(8,128)(2,1)} %copy-done.7, ...), custom_call_target="tpu_custom_call" | custom-call | tf_op jit(solution)/shard_map/attend/pallas_call | solution.py:89
  86.0 2.5 %collective-permute-start.4 = (f32[8,288]{1,0:T(8,128)S(1)}, f32[8,288]{1,0:T(8,128)S(1)}, u32[]{:S(2)}, u32[]{:S(2)}) collective-permute-start(f32[8,288]{1,0:T(8,128)S(1)} %get-tuple-element.29), channel_id=1, source_target_pairs={{0,12},{4,0},{8,4},{12,8},{1,13},{5,1},{9,5},{13,9},{2,14},{6,2},{... | collective-permute-start | bytes 27656 | tf_op jit(solution)/shard_map/ppermute | solution.py:23
  89.7 2.9 %collective-permute-done.5 = f32[8,288]{1,0:T(8,128)S(1)} collective-permute-done((f32[8,288]{1,0:T(8,128)S(1)}, f32[8,288]{1,0:T(8,128)S(1)}, u32[]{:S(2)}, u32[]{:S(2)}) %collective-permute-start.5) | collective-permute-done | bytes 9248 | tf_op jit(solution)/shard_map/ppermute | solution.py:23
  93.7 2.7 %collective-permute-start.7 = (f32[8,288]{1,0:T(8,128)S(1)}, f32[8,288]{1,0:T(8,128)S(1)}, u32[]{:S(2)}, u32[]{:S(2)}) collective-permute-start(f32[8,288]{1,0:T(8,128)S(1)} %pad_maximum_fusion.3), channel_id=1, source_target_pairs={{0,16},{16,0},{1,17},{17,1},{2,18},{18,2},{3,19},{19,3},{4,20},{20... | collective-permute-start | bytes 27656 | tf_op jit(solution)/shard_map/ppermute | solution.py:23
  107.4 3.3 %weigh.1 = (bf16[288,768]{1,0:T(8,128)(2,1)S(1)}, bf16[288,768]{1,0:T(8,128)(2,1)S(1)}, bf16[288,768]{1,0:T(8,128)(2,1)S(1)}, bf16[288,768]{1,0:T(8,128)(2,1)S(1)}) custom-call(f32[3]{0:T(128)S(1)} %subtract_add_fusion.r_0_, f32[8,1152]{1,0:T(8,128)S(1)} %copy-done.2, f32[8,1152]{1,0:T(8,128)S(1)} %concatenate.15.r_2_, f32[288,1536]{1,0:T(8,128)S(1)} %copy-done, ...), custom_call_target="tpu_custom_call" | custom-call | tf_op jit(solution)/shard_map/weigh/pallas_call | solution.py:130
  113.1 6.2 %collective-permute-done.11 = bf16[288,768]{1,0:T(8,128)(2,1)S(1)} collective-permute-done((bf16[288,768]{1,0:T(8,128)(2,1)S(1)}, bf16[288,768]{1,0:T(8,128)(2,1)S(1)}, u32[]{:S(2)}, u32[]{:S(2)}) %collective-permute-start.11) | collective-permute-done | bytes 442400 | tf_op jit(solution)/shard_map/ppermute | solution.py:23
  119.3 1.9 %collective-permute-done.12 = bf16[288,768]{1,0:T(8,128)(2,1)S(1)} collective-permute-done((bf16[288,768]{1,0:T(8,128)(2,1)S(1)}, bf16[288,768]{1,0:T(8,128)(2,1)S(1)}, u32[]{:S(2)}, u32[]{:S(2)}) %collective-permute-start.12) | collective-permute-done | bytes 442400 | tf_op jit(solution)/shard_map/ppermute | solution.py:23
  121.2 13.0 %collective-permute-done.13 = bf16[288,768]{1,0:T(8,128)(2,1)S(1)} collective-permute-done((bf16[288,768]{1,0:T(8,128)(2,1)S(1)}, bf16[288,768]{1,0:T(8,128)(2,1)S(1)}, u32[]{:S(2)}, u32[]{:S(2)}) %collective-permute-start.13) | collective-permute-done | bytes 442400 | tf_op jit(solution)/shard_map/ppermute | solution.py:23
  134.4 3.0 %collective-permute-start.14 = (bf16[144,768]{1,0:T(8,128)(2,1)S(1)}, bf16[144,768]{1,0:T(8,128)(2,1)S(1)}, u32[]{:S(2)}, u32[]{:S(2)}) collective-permute-start(bf16[144,768]{1,0:T(8,128)(2,1)S(1)} %slice.104), channel_id=1, source_target_pairs={{0,16},{16,0},{1,17},{17,1},{2,18},{18,2},{3,19},{19,3},{4,20},{20... | collective-permute-start | bytes 663560 | tf_op jit(solution)/shard_map/ppermute | solution.py:23
  137.4 4.1 %collective-permute-done.14 = bf16[144,768]{1,0:T(8,128)(2,1)S(1)} collective-permute-done((bf16[144,768]{1,0:T(8,128)(2,1)S(1)}, bf16[144,768]{1,0:T(8,128)(2,1)S(1)}, u32[]{:S(2)}, u32[]{:S(2)}) %collective-permute-start.14) | collective-permute-done | bytes 221216 | tf_op jit(solution)/shard_map/ppermute | solution.py:23
  142.5 5.7 %convolution_convert_fusion = bf16[144,5120]{1,0:T(8,128)(2,1)} fusion(bf16[768,5120]{1,0:T(8,128)(2,1)} %param.14, f32[144,768]{1,0:T(8,128)S(1)} %bitcast.41, bf16[144,768]{1,0:T(8,128)(2,1)S(1)} %collective-permute-done.14, f32[288,768]{1,0:T(8,128)S(1)} %convert_add_fusion.1, f32[768]{0:T(1024)S(1)} %copy-done.11), kind=kOutput, calls=%fused_computation | convolution fusion | flops 1133862912 | bytes 10448896 | tf_op jit(solution)/shard_map/dot_general | solution.py:194
  148.3 3.9 %reshape.33 = bf16[144,2,2,1280]{3,2,1,0:T(2,128)(2,1)S(1)} reshape(bf16[144,5120]{1,0:T(8,128)(2,1)} %convolution_convert_fusion) | data formatting | bytes 2949120 | tf_op jit(solution)/shard_map/reshape | solution.py:195
  152.2 3.0 %constant_dynamic-slice_fusion.1 = (bf16[144,2,1,1280]{3,2,1,0:T(2,128)(2,1)S(1)}, bf16[144,2,1,1280]{3,2,1,0:T(2,128)(2,1)S(1)}) fusion(bf16[144,2,2,1280]{3,2,1,0:T(2,128)(2,1)S(1)} %reshape.33, s32[]{:T(128)S(6)} %select_n.29, s32[]{:T(128)S(6)} %select_n.30), kind=kLoop, calls=%fused_computation.37 | loop fusion | bytes 2949128 | tf_op jit(solution)/shard_map/jit(dynamic_index_in_dim)/dynamic_slice | solution.py:197
  155.3 2.6 %collective-permute-start.15 = (bf16[144,2,1280]{2,0,1:T(8,128)(2,1)S(1)}, bf16[144,2,1280]{2,0,1:T(8,128)(2,1)S(1)}, u32[]{:S(2)}, u32[]{:S(2)}) collective-permute-start(bf16[144,2,1280]{2,0,1:T(8,128)(2,1)S(1)} %bitcast.40), channel_id=1, source_target_pairs={{0,1},{1,0},{2,3},{3,2},{4,5},{5,4},{6,7},{7,6},{8,9},{9,8},{10,11... | collective-permute-start | bytes 2211848 | tf_op jit(solution)/shard_map/ppermute | solution.py:23
  157.9 1.8 %collective-permute-done.15 = bf16[144,2,1280]{2,0,1:T(8,128)(2,1)S(1)} collective-permute-done((bf16[144,2,1280]{2,0,1:T(8,128)(2,1)S(1)}, bf16[144,2,1280]{2,0,1:T(8,128)(2,1)S(1)}, u32[]{:S(2)}, u32[]{:S(2)}) %collective-permute-start.15) | collective-permute-done | bytes 737312 | tf_op jit(solution)/shard_map/ppermute | solution.py:23
  163.2 8.6 %collective-permute-done.16 = bf16[144,1280]{1,0:T(8,128)(2,1)S(1)} collective-permute-done((bf16[144,1280]{1,0:T(8,128)(2,1)S(1)}, bf16[144,1280]{1,0:T(8,128)(2,1)S(1)}, u32[]{:S(2)}, u32[]{:S(2)}) %collective-permute-start.16) | collective-permute-done | bytes 368672 | tf_op jit(solution)/shard_map/ppermute | solution.py:23
  (81 shorter events, 26.2 us)
Async XLA Ops:
  6.5 57.2 %all-gather.3.cloned.1.call-start = ((), (), s32[]{:S(2)}) async-start(), calls=%async_computation | async-start | bytes 4202496 | tf_op jit(solution)/shard_map/all_gather | solution.py:158
  9.3 8.3 %collective-permute-start = (bf16[160,768]{1,0:T(8,128)(2,1)S(1)}, bf16[160,768]{1,0:T(8,128)(2,1)S(1)}, u32[]{:S(2)}, u32[]{:S(2)}) collective-permute-start(bf16[160,768]{1,0:T(8,128)(2,1)S(1)} %get-tuple-element.28), channel_id=1, source_target_pairs={{0,16},{16,0},{1,17},{17,1},{2,18},{18,2},{3,19},{19,3},{4,20},{20... | collective-permute-start | bytes 737288 | tf_op jit(solution)/shard_map/ppermute | solution.py:23
  17.6 47.4 %copy-start.3 = (bf16[2,160,768]{2,1,0:T(8,128)(2,1)}, bf16[2,160,768]{2,1,0:T(8,128)(2,1)S(1)}, u32[]{:S(2)}) copy-start(bf16[2,160,768]{2,1,0:T(8,128)(2,1)S(1)} %pad_maximum_fusion.r_2_) | copy-start | bytes 1474564
  17.6 14.4 %collective-permute-start.3 = (bf16[2,160,768]{2,1,0:T(8,128)(2,1)S(1)}, bf16[2,160,768]{2,1,0:T(8,128)(2,1)S(1)}, u32[]{:S(2)}, u32[]{:S(2)}) collective-permute-start(bf16[2,160,768]{2,1,0:T(8,128)(2,1)S(1)} %pad_maximum_fusion.r_2_), channel_id=1, source_target_pairs={{0,12},{4,0},{8,4},{12,8},{1,13},{5,1},{9,5},{13,9},{2,14},{6,2},{... | collective-permute-start | bytes 1474568 | tf_op jit(solution)/shard_map/ppermute | solution.py:23
  21.4 12.5 %collective-permute-start.2 = (bf16[2,160,768]{2,1,0:T(8,128)(2,1)S(1)}, bf16[2,160,768]{2,1,0:T(8,128)(2,1)S(1)}, u32[]{:S(2)}, u32[]{:S(2)}) collective-permute-start(bf16[2,160,768]{2,1,0:T(8,128)(2,1)S(1)} %pad_maximum_fusion.r_2_), channel_id=1, source_target_pairs={{0,8},{4,12},{8,0},{12,4},{1,9},{5,13},{9,1},{13,5},{2,10},{6,14},... | collective-permute-start | bytes 1474568 | tf_op jit(solution)/shard_map/ppermute | solution.py:23
  21.8 24.9 %collective-permute-start.1 = (bf16[2,160,768]{2,1,0:T(8,128)(2,1)S(1)}, bf16[2,160,768]{2,1,0:T(8,128)(2,1)S(1)}, u32[]{:S(2)}, u32[]{:S(2)}) collective-permute-start(bf16[2,160,768]{2,1,0:T(8,128)(2,1)S(1)} %pad_maximum_fusion.r_2_), channel_id=1, source_target_pairs={{0,4},{4,8},{8,12},{12,0},{1,5},{5,9},{9,13},{13,1},{2,6},{6,10},{... | collective-permute-start | bytes 1474568 | tf_op jit(solution)/shard_map/ppermute | solution.py:23
  32.0 33.1 %copy-start.5 = (bf16[2,160,768]{2,1,0:T(8,128)(2,1)}, bf16[2,160,768]{2,1,0:T(8,128)(2,1)S(1)}, u32[]{:S(2)}) copy-start(bf16[2,160,768]{2,1,0:T(8,128)(2,1)S(1)} %collective-permute-done.3.r_5_) | copy-start | bytes 1474564
  33.9 31.2 %copy-start.6 = (bf16[2,160,768]{2,1,0:T(8,128)(2,1)}, bf16[2,160,768]{2,1,0:T(8,128)(2,1)S(1)}, u32[]{:S(2)}) copy-start(bf16[2,160,768]{2,1,0:T(8,128)(2,1)S(1)} %collective-permute-done.2.r_4_) | copy-start | bytes 1474564
  46.7 18.4 %copy-start.7 = (bf16[2,160,768]{2,1,0:T(8,128)(2,1)}, bf16[2,160,768]{2,1,0:T(8,128)(2,1)S(1)}, u32[]{:S(2)}) copy-start(bf16[2,160,768]{2,1,0:T(8,128)(2,1)S(1)} %collective-permute-done.1.r_3_) | copy-start | bytes 1474564
  65.1 31.3 %copy-start.10 = (f32[4,3,128]{2,0,1:T(4,128)S(1)}, f32[4,3,128]{2,0,1:T(4,128)}, u32[]{:S(2)}) copy-start(f32[4,3,128]{2,0,1:T(4,128)} %param.12) | copy-start | bytes 18436
  86.0 3.6 %collective-permute-start.4 = (f32[8,288]{1,0:T(8,128)S(1)}, f32[8,288]{1,0:T(8,128)S(1)}, u32[]{:S(2)}, u32[]{:S(2)}) collective-permute-start(f32[8,288]{1,0:T(8,128)S(1)} %get-tuple-element.29), channel_id=1, source_target_pairs={{0,12},{4,0},{8,4},{12,8},{1,13},{5,1},{9,5},{13,9},{2,14},{6,2},{... | collective-permute-start | bytes 27656 | tf_op jit(solution)/shard_map/ppermute | solution.py:23
  88.5 4.0 %collective-permute-start.5 = (f32[8,288]{1,0:T(8,128)S(1)}, f32[8,288]{1,0:T(8,128)S(1)}, u32[]{:S(2)}, u32[]{:S(2)}) collective-permute-start(f32[8,288]{1,0:T(8,128)S(1)} %get-tuple-element.31), channel_id=1, source_target_pairs={{0,8},{4,12},{8,0},{12,4},{1,9},{5,13},{9,1},{13,5},{2,10},{6,14},... | collective-permute-start | bytes 27656 | tf_op jit(solution)/shard_map/ppermute | solution.py:23
  89.1 3.8 %collective-permute-start.6 = (f32[8,288]{1,0:T(8,128)S(1)}, f32[8,288]{1,0:T(8,128)S(1)}, u32[]{:S(2)}, u32[]{:S(2)}) collective-permute-start(f32[8,288]{1,0:T(8,128)S(1)} %get-tuple-element.30), channel_id=1, source_target_pairs={{0,4},{4,8},{8,12},{12,0},{1,5},{5,9},{9,13},{13,1},{2,6},{6,10},{... | collective-permute-start | bytes 27656 | tf_op jit(solution)/shard_map/ppermute | solution.py:23
  93.7 4.1 %collective-permute-start.7 = (f32[8,288]{1,0:T(8,128)S(1)}, f32[8,288]{1,0:T(8,128)S(1)}, u32[]{:S(2)}, u32[]{:S(2)}) collective-permute-start(f32[8,288]{1,0:T(8,128)S(1)} %pad_maximum_fusion.3), channel_id=1, source_target_pairs={{0,16},{16,0},{1,17},{17,1},{2,18},{18,2},{3,19},{19,3},{4,20},{20... | collective-permute-start | bytes 27656 | tf_op jit(solution)/shard_map/ppermute | solution.py:23
  97.8 3.1 %collective-permute-start.10 = (f32[8,288]{1,0:T(8,128)S(1)}, f32[8,288]{1,0:T(8,128)S(1)}, u32[]{:S(2)}, u32[]{:S(2)}) collective-permute-start(f32[8,288]{1,0:T(8,128)S(1)} %add_select_fusion), channel_id=1, source_target_pairs={{0,12},{4,0},{8,4},{12,8},{1,13},{5,1},{9,5},{13,9},{2,14},{6,2},{... | collective-permute-start | bytes 27656 | tf_op jit(solution)/shard_map/ppermute | solution.py:23
  98.5 3.8 %collective-permute-start.8 = (f32[8,288]{1,0:T(8,128)S(1)}, f32[8,288]{1,0:T(8,128)S(1)}, u32[]{:S(2)}, u32[]{:S(2)}) collective-permute-start(f32[8,288]{1,0:T(8,128)S(1)} %add_select_fusion), channel_id=1, source_target_pairs={{0,4},{4,8},{8,12},{12,0},{1,5},{5,9},{9,13},{13,1},{2,6},{6,10},{... | collective-permute-start | bytes 27656 | tf_op jit(solution)/shard_map/ppermute | solution.py:23
  99.5 4.0 %collective-permute-start.9 = (f32[8,288]{1,0:T(8,128)S(1)}, f32[8,288]{1,0:T(8,128)S(1)}, u32[]{:S(2)}, u32[]{:S(2)}) collective-permute-start(f32[8,288]{1,0:T(8,128)S(1)} %add_select_fusion), channel_id=1, source_target_pairs={{0,8},{4,12},{8,0},{12,4},{1,9},{5,13},{9,1},{13,5},{2,10},{6,14},... | collective-permute-start | bytes 27656 | tf_op jit(solution)/shard_map/ppermute | solution.py:23
  110.7 8.6 %collective-permute-start.11 = (bf16[288,768]{1,0:T(8,128)(2,1)S(1)}, bf16[288,768]{1,0:T(8,128)(2,1)S(1)}, u32[]{:S(2)}, u32[]{:S(2)}) collective-permute-start(bf16[288,768]{1,0:T(8,128)(2,1)S(1)} %get-tuple-element.20), channel_id=1, source_target_pairs={{0,12},{4,0},{8,4},{12,8},{1,13},{5,1},{9,5},{13,9},{2,14},{6,2},{... | collective-permute-start | bytes 1327112 | tf_op jit(solution)/shard_map/ppermute | solution.py:23
  112.4 8.8 %collective-permute-start.12 = (bf16[288,768]{1,0:T(8,128)(2,1)S(1)}, bf16[288,768]{1,0:T(8,128)(2,1)S(1)}, u32[]{:S(2)}, u32[]{:S(2)}) collective-permute-start(bf16[288,768]{1,0:T(8,128)(2,1)S(1)} %get-tuple-element.21), channel_id=1, source_target_pairs={{0,8},{4,12},{8,0},{12,4},{1,9},{5,13},{9,1},{13,5},{2,10},{6,14},... | collective-permute-start | bytes 1327112 | tf_op jit(solution)/shard_map/ppermute | solution.py:23
  112.5 21.7 %collective-permute-start.13 = (bf16[288,768]{1,0:T(8,128)(2,1)S(1)}, bf16[288,768]{1,0:T(8,128)(2,1)S(1)}, u32[]{:S(2)}, u32[]{:S(2)}) collective-permute-start(bf16[288,768]{1,0:T(8,128)(2,1)S(1)} %get-tuple-element.22), channel_id=1, source_target_pairs={{0,4},{4,8},{8,12},{12,0},{1,5},{5,9},{9,13},{13,1},{2,6},{6,10},{... | collective-permute-start | bytes 1327112 | tf_op jit(solution)/shard_map/ppermute | solution.py:23
  134.4 7.1 %collective-permute-start.14 = (bf16[144,768]{1,0:T(8,128)(2,1)S(1)}, bf16[144,768]{1,0:T(8,128)(2,1)S(1)}, u32[]{:S(2)}, u32[]{:S(2)}) collective-permute-start(bf16[144,768]{1,0:T(8,128)(2,1)S(1)} %slice.104), channel_id=1, source_target_pairs={{0,16},{16,0},{1,17},{17,1},{2,18},{18,2},{3,19},{19,3},{4,20},{20... | collective-permute-start | bytes 663560 | tf_op jit(solution)/shard_map/ppermute | solution.py:23
  155.3 4.5 %collective-permute-start.15 = (bf16[144,2,1280]{2,0,1:T(8,128)(2,1)S(1)}, bf16[144,2,1280]{2,0,1:T(8,128)(2,1)S(1)}, u32[]{:S(2)}, u32[]{:S(2)}) collective-permute-start(bf16[144,2,1280]{2,0,1:T(8,128)(2,1)S(1)} %bitcast.40), channel_id=1, source_target_pairs={{0,1},{1,0},{2,3},{3,2},{4,5},{5,4},{6,7},{7,6},{8,9},{9,8},{10,11... | collective-permute-start | bytes 2211848 | tf_op jit(solution)/shard_map/ppermute | solution.py:23
  160.6 11.2 %copy-start.8 = (bf16[144,1280]{1,0:T(8,128)(2,1)S(1)}, bf16[144,1280]{1,0:T(8,128)(2,1)}, u32[]{:S(2)}) copy-start(bf16[144,1280]{1,0:T(8,128)(2,1)} %param.15) | copy-start | bytes 1105924
  162.0 9.9 %collective-permute-start.16 = (bf16[144,1280]{1,0:T(8,128)(2,1)S(1)}, bf16[144,1280]{1,0:T(8,128)(2,1)S(1)}, u32[]{:S(2)}, u32[]{:S(2)}) collective-permute-start(bf16[144,1280]{1,0:T(8,128)(2,1)S(1)} %fusion.2), channel_id=1, source_target_pairs={{0,2},{2,0},{1,3},{3,1},{4,6},{6,4},{5,7},{7,5},{8,10},{10,8},{9,1... | collective-permute-start | bytes 1105928 | tf_op jit(solution)/shard_map/ppermute | solution.py:23
  (6 other events, 8.0 us)
Sparse Core Ops, SparseCore 0:
  9.4 54.3 all-gather.2

commit v2 on v1

v2 whole, which is shorter than its diff:
```python
import math

import jax
import jax.numpy as jnp
from jax import lax
from jax.experimental import pallas as pl
from jax.experimental.pallas import tpu as pltpu
from jax.sharding import Mesh, PartitionSpec as P

lambda_init = 0.2
out_factor = 0.8
norm_eps = 1e-05

HD = 128
RUN = 72
TILE = 4
NEG = -1e30
FLOOR = -1e29
f32 = jnp.float32
bf16 = jnp.bfloat16


def attend_kernel(rows, qb, kb, *refs):
    q_refs, (kv_ref, o_ref, lse_ref) = refs[:-11], refs[-11:-8]
    q3, k3, v3, q_s, k_s, v_s, lse_s, order = refs[-8:]
    head = pl.program_id(0)
    blocks = q3.shape[0]
    per = rows // RUN
    tile = TILE * RUN
    tiles = blocks // TILE
    scale = math.log2(math.e) / math.sqrt(HD)

    @pl.when(head == 0)
    def _():
        lse_s[...] = jnp.zeros_like(lse_s)
        for i in range(blocks):
            rk = jnp.int32(0)
            rq = jnp.int32(0)
            for j in range(blocks):
                rk = rk + (kb[j] < kb[i]).astype(jnp.int32)
                rq = rq + (qb[j] < qb[i]).astype(jnp.int32)
            order[0, i] = rk
            order[1, rk] = kb[i]
            order[2, i] = rq
            order[3, rq] = i
            order[4, rq] = qb[i]
        for t in range(tiles):
            last = order[4, t * TILE + TILE - 1]
            need = jnp.int32(0)
            for j in range(blocks):
                need = need + (kb[j] <= last).astype(jnp.int32)
            order[5, t] = lax.div(need + (TILE - 1), TILE)

    for i in range(blocks):
        z, d = i // per, i % per
        r = order[0, i]
        k3[r] = kv_ref[z, d * RUN : (d + 1) * RUN, :]
        v3[r] = kv_ref[z, rows + d * RUN : rows + (d + 1) * RUN, :]
        p, e = z // 2, z % 2
        q3[order[2, i]] = q_refs[p][e, d * RUN : (d + 1) * RUN, :]
    for i in range(blocks):
        q_s[i * RUN : (i + 1) * RUN, :] = q3[i]
        k_s[i * RUN : (i + 1) * RUN, :] = k3[i]
        v_s[i * RUN : (i + 1) * RUN, :] = v3[i]

    col = lax.broadcasted_iota(jnp.int32, (1, blocks * RUN), 1)
    kpos = lax.rem(col, RUN)
    for i in range(blocks):
        kpos = kpos + jnp.where(lax.div(col, RUN) == i, order[1, i] * RUN, 0)
    row = lax.broadcasted_iota(jnp.int32, (tile, 1), 0)
    lane = lax.broadcasted_iota(jnp.int32, (RUN, HD), 1)

    def one_tile(t, carry):
        need = order[5, t]
        start = pl.multiple_of(t * tile, tile)
        qpos = lax.rem(row, RUN)
        for i in range(TILE):
            qpos = qpos + jnp.where(lax.div(row, RUN) == i, order[4, t * TILE + i] * RUN, 0)

        def put(a, num, lse):
            for i in range(TILE):
                g = order[3, t * TILE + i]
                o_ref[g, :, a * 2 * HD : (a + 1) * 2 * HD] = num[i * RUN : (i + 1) * RUN]
                lse_s[g] = jnp.where(lane == head * 2 + a, lse[i * RUN : (i + 1) * RUN], lse_s[g])

        for n in range(1, tiles + 1):

            @pl.when(need == n)
            def _(n=n):
                allowed = kpos[:, : n * tile] <= qpos
                for a in range(2):
                    s = lax.dot_general(
                        q_s[pl.ds(start, tile), a * HD : (a + 1) * HD],
                        k_s[: n * tile, a * HD : (a + 1) * HD],
                        (((1,), (1,)), ((), ())),
                        preferred_element_type=f32,
                    )
                    s = jnp.where(allowed, s, NEG)
                    m = jnp.maximum(jnp.max(s, -1, keepdims=True), FLOOR) * scale
                    p = jnp.exp2(s * scale - m)
                    total = jnp.sum(p, -1, keepdims=True)
                    num = jnp.dot(p.astype(bf16), v_s[: n * tile, :], preferred_element_type=f32)
                    some = total > 0.0
                    safe = jnp.where(some, total, 1.0)
                    put(a, num * (1.0 / safe), jnp.where(some, m + jnp.log2(safe), NEG))

        @pl.when(need == 0)
        def _():
            for a in range(2):
                put(a, jnp.zeros((tile, 2 * HD), f32), jnp.full((tile, 1), NEG, f32))

        return carry

    lax.fori_loop(0, tiles, one_tile, 0)

    @pl.when(head == pl.num_programs(0) - 1)
    def _():
        lse_ref[...] = jnp.transpose(lse_s[...].reshape(blocks * RUN, HD))[: lse_ref.shape[0], :]


def attend(q_parts, kv, qb, kb, rows, heads):
    nq = len(q_parts)
    blocks = 2 * nq * rows // RUN
    zs = kv.shape[0]
    pad = q_parts[0].shape[1]
    return pl.pallas_call(
        lambda *r: attend_kernel(rows, *r),
        out_shape=[
            jax.ShapeDtypeStruct((blocks, RUN, heads * 4 * HD), f32),
            jax.ShapeDtypeStruct((8, blocks * RUN), f32),
        ],
        grid_spec=pltpu.PrefetchScalarGridSpec(
            num_scalar_prefetch=2,
            grid=(heads,),
            in_specs=[pl.BlockSpec((2, pad, 2 * HD), lambda h, *_: (0, 0, h))] * nq
            + [pl.BlockSpec((zs, kv.shape[1], 2 * HD), lambda h, *_: (0, 0, h))],
            out_specs=[
                pl.BlockSpec((blocks, RUN, 4 * HD), lambda h, *_: (0, 0, h)),
                pl.BlockSpec((8, blocks * RUN), lambda h, *_: (0, 0)),
            ],
            scratch_shapes=[pltpu.VMEM((blocks, RUN, 2 * HD), bf16)] * 3
            + [pltpu.VMEM((blocks * RUN, 2 * HD), bf16)] * 3
            + [pltpu.VMEM((blocks, RUN, HD), f32), pltpu.SMEM((6, 128), jnp.int32)],
        ),
        compiler_params=pltpu.CompilerParams(vmem_limit_bytes=40 << 20),
        name="attend",
    )(qb, kb, *q_parts, kv)


def weigh_kernel(heads, place, lam, lse_ref, all_ref, o_ref, out_ref, w_s):
    s = pl.program_id(0)
    rows = out_ref.shape[1]

    @pl.when(s == 0)
    def _():
        w = jnp.exp2(lse_ref[...] - all_ref[...])
        w = jnp.concatenate([w, jnp.zeros((HD - w.shape[0], w.shape[1]), f32)], 0)
        w_s[...] = jnp.transpose(w)

    w = w_s[pl.ds(pl.multiple_of(s * rows, rows), rows), :]
    for h in range(heads):
        w1 = w[:, 2 * h : 2 * h + 1]
        w2 = w[:, 2 * h + 1 : 2 * h + 2] * lam[h]
        o1 = o_ref[:, :, h * 4 * HD : h * 4 * HD + 2 * HD].reshape(rows, 2 * HD)
        o2 = o_ref[:, :, h * 4 * HD + 2 * HD : (h + 1) * 4 * HD].reshape(rows, 2 * HD)
        out_ref[0, :, h * 2 * HD : (h + 1) * 2 * HD] = (w1 * o1 - w2 * o2).astype(bf16)


def weigh(place, lam, lse, lse_all, o, rows, heads):
    slots = lse.shape[1] // rows
    return pl.pallas_call(
        lambda *r: weigh_kernel(heads, *r),
        out_shape=jax.ShapeDtypeStruct((slots, rows, heads * 2 * HD), bf16),
        grid_spec=pltpu.PrefetchScalarGridSpec(
            num_scalar_prefetch=2,
            grid=(slots,),
            in_specs=[pl.BlockSpec(lse.shape, lambda s, *_: (0, 0))] * 2
            + [pl.BlockSpec((rows // RUN, RUN, heads * 4 * HD), lambda s, *_: (s, 0, 0))],
            out_specs=pl.BlockSpec((1, rows, heads * 2 * HD), lambda s, place, lam: (place[s], 0, 0)),
            scratch_shapes=[pltpu.VMEM((slots * rows, HD), f32)],
        ),
        compiler_params=pltpu.CompilerParams(vmem_limit_bytes=16 << 20),
        name="weigh",
    )(place, lam, lse, lse_all, o)


def logsum(a, b):
    top = jnp.maximum(a, b)
    return top + jnp.log2(jnp.exp2(a - top) + jnp.exp2(b - top))


def reorder(x, rows, mask):
    slots = x.shape[1] // rows
    return jnp.concatenate([x[:, (s ^ mask) * rows : ((s ^ mask) + 1) * rows] for s in range(slots)], 1)


def swap(x, axis, size, mask):
    return lax.ppermute(x, axis, [(i, i ^ mask) for i in range(size)])


def per_device(sizes, queries, keys, values, positions, lambda_vecs, head_gain, out_weight, residual):
    nz, nh, ny, nl, nc = sizes
    rows, width = queries.shape
    heads = lambda_vecs.shape[1]
    lane = lax.broadcasted_iota(jnp.int32, (16, width), 1)
    ids = jnp.where(lane == 0, positions[0] // RUN, positions[RUN] // RUN).astype(bf16)

    kv = lax.all_gather(jnp.concatenate([keys, values, ids], 0), "z", axis=0, tiled=False)
    kb = kv[:, 2 * rows, : rows // RUN].astype(jnp.int32).reshape(-1)

    q_mine = jnp.concatenate([queries, ids], 0)
    q_pair = jnp.stack([q_mine, swap(q_mine, "h", nh, 1)], 0)
    q_parts = [q_pair] + [swap(q_pair, "y", ny, d) for d in range(1, ny)]
    qb = jnp.stack([q[:, rows, : rows // RUN] for q in q_parts], 0).astype(jnp.int32).reshape(-1)

    l, c = lax.axis_index("l"), lax.axis_index("c")
    w4 = out_weight.reshape(width, nl, nc, -1)
    w_keep = lax.dynamic_index_in_dim(w4, c, 2, False)
    w_away = swap(lax.dynamic_index_in_dim(w4, 1 - c, 2, False), "c", nc, 1)
    w_both = jnp.concatenate([w_keep, w_away], 0)
    w_mine = lax.dynamic_index_in_dim(w_both, l, 1, False)
    w_other = lax.dynamic_index_in_dim(w_both, 1 - l, 1, False)

    o, lse = attend(q_parts, kv, qb, kb, rows, heads)

    whole = lse
    for axis, size, mask, slot in (("h", nh, 1, 1), ("y", ny, 1, 2), ("y", ny, 3, 6)):
        whole = logsum(whole, reorder(swap(whole, axis, size, mask), rows, slot))

    lam = (
        jnp.exp(jnp.sum(lambda_vecs[0] * lambda_vecs[1], -1))
        - jnp.exp(jnp.sum(lambda_vecs[2] * lambda_vecs[3], -1))
        + lambda_init
    )
    slot = jnp.arange(nh * ny, dtype=jnp.int32)
    place = (lax.axis_index("h") ^ (slot & 1)) * ny + (lax.axis_index("y") ^ (slot >> 1))
    parts = weigh(place, lam, lse, whole, o, rows, heads)

    got = lax.all_to_all(parts, ("h", "y"), 0, 0, tiled=False)
    diff = jnp.sum(got.astype(f32), 0).reshape(rows, heads, 2 * HD)
    mean_square = jnp.mean(diff * diff, -1, keepdims=True)
    normed = out_factor * diff / jnp.sqrt(mean_square + norm_eps) * head_gain.reshape(1, heads, 2 * HD)
    normed = normed.reshape(rows, width).astype(bf16)

    normed = jnp.concatenate([normed, swap(normed, "c", nc, 1)], 1)
    send = jnp.dot(normed, w_other, preferred_element_type=f32).astype(bf16)
    away = swap(send, "l", nl, 1)
    keep = jnp.dot(normed, w_mine, preferred_element_type=f32)
    return (keep + away.astype(f32) + residual.astype(f32)).astype(bf16)


def solution(mesh):
    sizes = (8, 2, 4, 2, 2)
    fine = Mesh(mesh.devices.reshape(sizes), ("z", "h", "y", "l", "c"))
    ctx, tp = ("z", "h", "y"), ("l", "c")
    placed = (
        P(ctx, tp),
        P(ctx, tp),
        P(ctx, tp),
        P(ctx),
        P(None, tp, None),
        P(tp),
        P(tp, None),
        P(ctx, tp),
    )
    return jax.shard_map(
        lambda *a: per_device(sizes, *a), mesh=fine, in_specs=placed, out_specs=P(ctx, tp), check_vma=False
    )
```

time: 180 us -> 175 us (0.972)
  waiting for transfers between devices: 88 us -> 36.8 us
  blocking collectives: 0 us -> 25.5 us
  local copies, waits for them, and re-layouts: 15.5 us -> 40.9 us
  starting transfers between devices: 27.1 us -> 20.4 us
  between operations: 13.6 us -> 17.5 us
  other arithmetic: 6.32 us -> 4.51 us
    ppermute x17 -> x10, waiting for transfers between devices: 71.7 us -> 22.2 us  [swap(): return lax.ppermute(x, axis, [(i, i ^ mask) for i in range(size)])]
    all_to_all x0 -> x1, blocking collectives: none -> 25.5 us  [per_device(): got = lax.all_to_all(parts, ('h', 'y'), 0, 0, tiled=False)]
    dynamic_slice x2 -> x3, local copies, waits for them, and re-layouts: 3.12 us -> 19.7 us  [the longest x2 13.3 us: per_device(): w_away = swap(lax.dynamic_index_in_dim(w4, 1 - c, 2, False), 'c', nc, 1)]
    unnamed x29 -> x18, local copies, waits for them, and re-layouts: 4.82 us -> 18.7 us
    ppermute x17 -> x10, starting transfers between devices: 27.1 us -> 20.4 us  [swap(): return lax.ppermute(x, axis, [(i, i ^ mask) for i in range(size)])]
    reshape x1 -> x0, local copies, waits for them, and re-layouts: 3.87 us -> none  [per_device(): share = share.reshape(rows, nl, nc, -1)]
    dot_general x1 -> x2, matrix products: 5.73 us -> 6.6 us  [the longest x1 3.65 us: per_device(): keep = jnp.dot(normed, w_mine, preferred_element_type=f32)]
  transfers between devices with their start and end apart: 18 -> 11, of which waited for: 17 -> 7; matrix products, arithmetic and copies ran while one was open for 1% -> 20% of each run, Pallas kernels for 0% -> 13%
where the time goes in v2:
time: 175 us; the launch traced here: 174 us
  local copies, waits for them, and re-layouts  40.9 us (23%)
  waiting for transfers between devices  36.8 us (21%)
  blocking collectives  25.5 us (15%)
  Pallas kernels  22.3 us (13%)
  starting transfers between devices  20.4 us (12%)
  between operations  17.5 us (10%)
  matrix products  6.6 us (4%)
  other arithmetic  4.51 us (3%)
    all_to_all x1, blocking collectives, per_device(): got = lax.all_to_all(parts, ('h', 'y'), 0, 0, tiled=False)  25.5 us
    ppermute x10, waiting for transfers between devices, swap(): return lax.ppermute(x, axis, [(i, i ^ mask) for i in range(size)])  22.2 us
    ppermute x10, starting transfers between devices, swap(): return lax.ppermute(x, axis, [(i, i ^ mask) for i in range(size)])  20.4 us
    pallas_call x1, Pallas kernels, attend(): pl.pallas_call(lambda *r: attend_kernel(rows, *r), out_shape=[jax.ShapeDt...  19.8 us
    unnamed x18, local copies, waits for them, and re-layouts  18.7 us
    all_gather x1, waiting for transfers between devices, per_device(): lax.all_gather(jnp.concatenate([keys, values, ids], 0), 'z', axis=0, tile...  14.6 us
    dynamic_slice x2, local copies, waits for them, and re-layouts, per_device(): w_away = swap(lax.dynamic_index_in_dim(w4, 1 - c, 2, False), 'c', nc, 1)  13.3 us
    dynamic_slice x1, local copies, waits for them, and re-layouts, per_device(): w_keep = lax.dynamic_index_in_dim(w4, c, 2, False)  6.37 us
  transfers between devices with their start and end apart: 11, of which 7 were waited for; matrix products, arithmetic and copies ran while one was open for 20% of the time, Pallas kernels for 13%

profile of v2, /device:TPU:1, one launch (start us, length us, event | category | flops | bytes accessed | tf_op | source)
XLA Modules:
  0.0 174.5 jit_solution(9597186697310183499)
XLA Ops:
  11.8 1.9 %pad_maximum_fusion.1 = bf16[304,768]{1,0:T(8,128)(2,1)} fusion(bf16[16,768]{1,0:T(8,128)(2,1)S(1)} %iota.14, bf16[144,768]{1,0:T(8,128)(2,1)} %param.10, bf16[144,768]{1,0:T(8,128)(2,1)} %param.9), kind=kLoop, calls=%fused_computation.18 | loop fusion | flops 1400832 | bytes 933888 | tf_op jit(solution)/shard_map/concatenate | solution.py:208
  14.7 3.7 %collective-permute-start = (bf16[160,768]{1,0:T(8,128)(2,1)S(1)}, bf16[160,768]{1,0:T(8,128)(2,1)S(1)}, u32[]{:S(2)}, u32[]{:S(2)}) collective-permute-start(bf16[160,768]{1,0:T(8,128)(2,1)S(1)} %get-tuple-element.14), channel_id=1, source_target_pairs={{0,16},{16,0},{1,17},{17,1},{2,18},{18,2},{3,19},{19,3},{4,20},{20... | collective-permute-start | bytes 737288 | tf_op jit(solution)/shard_map/ppermute | solution.py:198
  18.3 10.7 %copy.18 = bf16[768,5120]{0,1:T(8,128)(2,1)} copy(bf16[768,5120]{1,0:T(8,128)(2,1)} %param.14) | data formatting | bytes 15728640 | tf_op args[6]
  29.1 2.8 %collective-permute-start.3 = (bf16[2,160,768]{2,1,0:T(8,128)(2,1)S(1)}, bf16[2,160,768]{2,1,0:T(8,128)(2,1)S(1)}, u32[]{:S(2)}, u32[]{:S(2)}) collective-permute-start(bf16[2,160,768]{2,1,0:T(8,128)(2,1)S(1)} %pad_maximum_fusion.r_2_), channel_id=1, source_target_pairs={{0,12},{4,8},{8,4},{12,0},{1,13},{5,9},{9,5},{13,1},{2,14},{6,10},... | collective-permute-start | bytes 1474568 | tf_op jit(solution)/shard_map/ppermute | solution.py:198
  32.6 7.1 %constant_dynamic-slice_fusion = (bf16[768,2,1,1280]{0,3,2,1:T(8,128)(2,1)}, bf16[768,2,1,1280]{0,3,2,1:T(8,128)(2,1)}) fusion(bf16[768,2,2,1280]{0,3,2,1:T(8,128)(2,1)} %bitcast.41, s32[]{:T(128)S(6)} %select_n.31, s32[]{:T(128)S(6)} %select_n.30), kind=kLoop, calls=%fused_computation.42 | loop fusion | bytes 15728648 | tf_op jit(solution)/shard_map/jit(dynamic_index_in_dim)/dynamic_slice | solution.py:219
  39.6 6.2 %copy.20 = bf16[768,2,1,1280]{3,0,2,1:T(8,128)(2,1)} copy(bf16[768,2,1,1280]{0,3,2,1:T(8,128)(2,1)} %get-tuple-element.11) | data formatting | bytes 7864320 | tf_op jit(solution)/shard_map/jit(dynamic_index_in_dim)/dynamic_slice | solution.py:219
  45.8 1.7 collective-permute-start.8
  47.5 5.4 %collective-permute-done.3.r_5_ = bf16[2,160,768]{2,1,0:T(8,128)(2,1)S(1)} collective-permute-done((bf16[2,160,768]{2,1,0:T(8,128)(2,1)S(1)}, bf16[2,160,768]{2,1,0:T(8,128)(2,1)S(1)}, u32[]{:S(2)}, u32[]{:S(2)}) %collective-permute-start.3) | collective-permute-done | bytes 491552 | tf_op jit(solution)/shard_map/ppermute | solution.py:198
  53.6 14.6 %all-gather.3.cloned.1.call-done = bf16[2432,768]{1,0:T(8,128)(2,1)} async-done(((bf16[304,768]{1,0:T(8,128)(2,1)}), bf16[2432,768]{1,0:T(8,128)(2,1)}) %all-gather.3.cloned.1.call-update) | async-done | bytes 3735568 | tf_op jit(solution)/shard_map/all_gather | solution.py:208
  69.0 2.1 %copy-done.2 = bf16[2432,768]{1,0:T(8,128)(2,1)S(1)} copy-done((bf16[2432,768]{1,0:T(8,128)(2,1)S(1)}, bf16[2432,768]{1,0:T(8,128)(2,1)}, u32[]{:S(2)}) %copy-start.2) | copy-done | bytes 3735576
  71.1 19.8 %attend.1 = (f32[16,72,1536]{2,1,0:T(8,128)S(1)}, f32[8,1152]{1,0:T(8,128)S(1)}) custom-call(s32[16]{0:T(128)S(1)} %reshape.50.r_0_, s32[16]{0:T(128)S(1)} %reshape.51.r_1_, bf16[2,160,768]{2,1,0:T(8,128)(2,1)S(1)} %pad_maximum_fusion.r_2_, bf16[2,160,768]{2,1,0:T(8,128)(2,1)S(1)} %collective-permute-done.1.r_3_, ...), custom_call_target="tpu_custom_call" | custom-call | tf_op jit(solution)/shard_map/attend/pallas_call | solution.py:126
  90.9 2.9 %copy-done = f32[16,72,1536]{2,1,0:T(8,128)} copy-done((f32[16,72,1536]{2,1,0:T(8,128)}, f32[16,72,1536]{2,1,0:T(8,128)S(1)}, u32[]{:S(2)}) %copy-start) | copy-done | bytes 7077912
  93.8 2.6 %collective-permute-start.4 = (f32[8,1152]{1,0:T(8,128)S(1)}, f32[8,1152]{1,0:T(8,128)S(1)}, u32[]{:S(2)}, u32[]{:S(2)}) collective-permute-start(f32[8,1152]{1,0:T(8,128)S(1)} %get-tuple-element.7.r_2_), channel_id=1, source_target_pairs={{0,16},{16,0},{1,17},{17,1},{2,18},{18,2},{3,19},{19,3},{4,20},{20... | collective-permute-start | bytes 110600 | tf_op jit(solution)/shard_map/ppermute | solution.py:198
  98.5 2.8 %collective-permute-done.5 = f32[8,1152]{1,0:T(8,128)S(1)} collective-permute-done((f32[8,1152]{1,0:T(8,128)S(1)}, f32[8,1152]{1,0:T(8,128)S(1)}, u32[]{:S(2)}, u32[]{:S(2)}) %collective-permute-start.5) | collective-permute-done | bytes 36896 | tf_op jit(solution)/shard_map/ppermute | solution.py:198
  101.5 2.3 %collective-permute-start.6 = (f32[8,1152]{1,0:T(8,128)S(1)}, f32[8,1152]{1,0:T(8,128)S(1)}, u32[]{:S(2)}, u32[]{:S(2)}) collective-permute-start(f32[8,1152]{1,0:T(8,128)S(1)} %multiply_add_fusion.1), channel_id=1, source_target_pairs={{0,12},{4,8},{8,4},{12,0},{1,13},{5,9},{9,5},{13,1},{2,14},{6,10},... | collective-permute-start | bytes 110600 | tf_op jit(solution)/shard_map/ppermute | solution.py:198
  103.8 2.0 %collective-permute-done.6 = f32[8,1152]{1,0:T(8,128)S(1)} collective-permute-done((f32[8,1152]{1,0:T(8,128)S(1)}, f32[8,1152]{1,0:T(8,128)S(1)}, u32[]{:S(2)}, u32[]{:S(2)}) %collective-permute-start.6) | collective-permute-done | bytes 36896 | tf_op jit(solution)/shard_map/ppermute | solution.py:198
  106.0 3.0 %copy-done.1 = f32[16,72,1536]{2,1,0:T(8,128)S(1)} copy-done((f32[16,72,1536]{2,1,0:T(8,128)S(1)}, f32[16,72,1536]{2,1,0:T(8,128)}, u32[]{:S(2)}) %copy-start.1) | copy-done | bytes 7077912
  109.0 2.4 %weigh.1 = bf16[8,144,768]{2,1,0:T(8,128)(2,1)S(1)} custom-call(s32[8]{0:T(128)S(1)} %xor_add_fusion.r_0_, f32[3]{0:T(128)S(1)} %subtract_add_fusion.r_1_, f32[8,1152]{1,0:T(8,128)S(1)} %get-tuple-element.7.r_2_, f32[8,1152]{1,0:T(8,128)S(1)} %multiply_add_fusion.r_3_, f32[16,72,1536]{2,1,0:T(8,128)S(1)} %copy-done.1), custom_call_target="tpu_custom_call" | custom-call | tf_op jit(solution)/shard_map/weigh/pallas_call | solution.py:171
  111.4 25.5 %all_to_all.5 = bf16[8,144,768]{2,1,0:T(8,128)(2,1)S(1)} all-to-all(bf16[8,144,768]{2,1,0:T(8,128)(2,1)S(1)} %weigh.1), channel_id=1, replica_groups=mesh['z'=8,'h'=2,'y'=4,'l'=2,'c'=2] {'h','y'}, dimensions={0} | all-to-all | bytes 3538944 | tf_op jit(solution)/shard_map/all_to_all | solution.py:239
  138.1 6.2 %collective-permute-start.7 = (bf16[144,768]{1,0:T(8,128)(2,1)S(1)}, bf16[144,768]{1,0:T(8,128)(2,1)S(1)}, u32[]{:S(2)}, u32[]{:S(2)}) collective-permute-start(bf16[144,768]{1,0:T(8,128)(2,1)S(1)} %multiply_convert_fusion), channel_id=1, source_target_pairs={{0,1},{1,0},{2,3},{3,2},{4,5},{5,4},{6,7},{7,6},{8,9},{9,8},{10,11... | collective-permute-start | bytes 663560 | tf_op jit(solution)/shard_map/ppermute | solution.py:198
  144.4 6.4 %copy.19 = bf16[768,2,1,1280]{3,0,2,1:T(8,128)(2,1)} copy(bf16[768,2,1,1280]{0,3,2,1:T(8,128)(2,1)} %get-tuple-element.12) | data formatting | bytes 7864320 | tf_op jit(solution)/shard_map/jit(dynamic_index_in_dim)/dynamic_slice | solution.py:218
  150.8 2.9 %fusion.17 = bf16[144,1280]{1,0:T(8,128)(2,1)S(1)} fusion(s32[]{:T(128)S(6)} %select_n.33, bf16[768,2,1280]{2,0,1:T(8,128)(2,1)} %bitcast.43, bf16[768,2,1280]{2,0,1:T(8,128)(2,1)} %collective-permute-done.8, bf16[144,768]{1,0:T(8,128)(2,1)S(1)} %collective-permute-done.7, bf16[144,768]{1,0:T(8,128)(2,1)S(1)} %multiply_convert_fusion), kind=kOutput, calls=%fused_computation.14 | convolution fusion | flops 575164416 | bytes 8675332 | tf_op jit(solution)/shard_map/dot_general | solution.py:246
  154.1 9.9 %collective-permute-done.9 = bf16[144,1280]{1,0:T(8,128)(2,1)S(1)} collective-permute-done((bf16[144,1280]{1,0:T(8,128)(2,1)S(1)}, bf16[144,1280]{1,0:T(8,128)(2,1)S(1)}, u32[]{:S(2)}, u32[]{:S(2)}) %collective-permute-start.9) | collective-permute-done | bytes 368672 | tf_op jit(solution)/shard_map/ppermute | solution.py:198
  164.0 3.7 %fusion.14 = bf16[144,1280]{1,0:T(8,128)(2,1)} fusion(s32[]{:T(128)S(6)} %select_n.32, bf16[768,2,1280]{2,0,1:T(8,128)(2,1)} %bitcast.44, bf16[768,2,1280]{2,0,1:T(8,128)(2,1)} %collective-permute-done.8, bf16[144,1280]{1,0:T(8,128)(2,1)S(1)} %copy-done.5, bf16[144,1280]{1,0:T(8,128)(2,1)S(1)} %collective-permute-done.9, ...), kind=kOutput, calls=%fused_computation.13 | convolution fusion | flops 575901696 | bytes 9412612 | tf_op jit(solution)/shard_map/dot_general | solution.py:248
  (58 shorter events, 8.6 us)
Async XLA Ops:
  6.5 61.6 %all-gather.3.cloned.1.call-start = ((), (), s32[]{:S(2)}) async-start(), calls=%async_computation.1 | async-start | bytes 4202496 | tf_op jit(solution)/shard_map/all_gather | solution.py:208
  14.7 14.3 %collective-permute-start = (bf16[160,768]{1,0:T(8,128)(2,1)S(1)}, bf16[160,768]{1,0:T(8,128)(2,1)S(1)}, u32[]{:S(2)}, u32[]{:S(2)}) collective-permute-start(bf16[160,768]{1,0:T(8,128)(2,1)S(1)} %get-tuple-element.14), channel_id=1, source_target_pairs={{0,16},{16,0},{1,17},{17,1},{2,18},{18,2},{3,19},{19,3},{4,20},{20... | collective-permute-start | bytes 737288 | tf_op jit(solution)/shard_map/ppermute | solution.py:198
  29.1 23.8 %collective-permute-start.3 = (bf16[2,160,768]{2,1,0:T(8,128)(2,1)S(1)}, bf16[2,160,768]{2,1,0:T(8,128)(2,1)S(1)}, u32[]{:S(2)}, u32[]{:S(2)}) collective-permute-start(bf16[2,160,768]{2,1,0:T(8,128)(2,1)S(1)} %pad_maximum_fusion.r_2_), channel_id=1, source_target_pairs={{0,12},{4,8},{8,4},{12,0},{1,13},{5,9},{9,5},{13,1},{2,14},{6,10},... | collective-permute-start | bytes 1474568 | tf_op jit(solution)/shard_map/ppermute | solution.py:198
  31.9 21.0 %collective-permute-start.2 = (bf16[2,160,768]{2,1,0:T(8,128)(2,1)S(1)}, bf16[2,160,768]{2,1,0:T(8,128)(2,1)S(1)}, u32[]{:S(2)}, u32[]{:S(2)}) collective-permute-start(bf16[2,160,768]{2,1,0:T(8,128)(2,1)S(1)} %pad_maximum_fusion.r_2_), channel_id=1, source_target_pairs={{0,8},{4,12},{8,0},{12,4},{1,9},{5,13},{9,1},{13,5},{2,10},{6,14},... | collective-permute-start | bytes 1474568 | tf_op jit(solution)/shard_map/ppermute | solution.py:198
  32.2 21.2 %collective-permute-start.1 = (bf16[2,160,768]{2,1,0:T(8,128)(2,1)S(1)}, bf16[2,160,768]{2,1,0:T(8,128)(2,1)S(1)}, u32[]{:S(2)}, u32[]{:S(2)}) collective-permute-start(bf16[2,160,768]{2,1,0:T(8,128)(2,1)S(1)} %pad_maximum_fusion.r_2_), channel_id=1, source_target_pairs={{0,4},{4,0},{8,12},{12,8},{1,5},{5,1},{9,13},{13,9},{2,6},{6,2},{1... | collective-permute-start | bytes 1474568 | tf_op jit(solution)/shard_map/ppermute | solution.py:198
  45.8 50.5 %copy-start.3 = (f32[4,3,128]{2,0,1:T(4,128)S(1)}, f32[4,3,128]{2,0,1:T(4,128)}, u32[]{:S(2)}) copy-start(f32[4,3,128]{2,0,1:T(4,128)} %param.12) | copy-start | bytes 18436
  45.8 104.9 %collective-permute-start.8 = (bf16[768,2,1280]{2,0,1:T(8,128)(2,1)}, bf16[768,2,1280]{2,0,1:T(8,128)(2,1)}, u32[]{:S(2)}, u32[]{:S(2)}) collective-permute-start(bf16[768,2,1280]{2,0,1:T(8,128)(2,1)} %bitcast.42), channel_id=1, source_target_pairs={{0,1},{1,0},{2,3},{3,2},{4,5},{5,4},{6,7},{7,6},{8,9},{9,8},{10,11... | collective-permute-start | bytes 11796488 | tf_op jit(solution)/shard_map/ppermute | solution.py:198
  69.0 2.1 %copy-start.2 = (bf16[2432,768]{1,0:T(8,128)(2,1)S(1)}, bf16[2432,768]{1,0:T(8,128)(2,1)}, u32[]{:S(2)}) copy-start(bf16[2432,768]{1,0:T(8,128)(2,1)} %all-gather.3.cloned.1.call-done) | copy-start | bytes 11206660
  90.9 2.9 %copy-start = (f32[16,72,1536]{2,1,0:T(8,128)}, f32[16,72,1536]{2,1,0:T(8,128)S(1)}, u32[]{:S(2)}) copy-start(f32[16,72,1536]{2,1,0:T(8,128)S(1)} %get-tuple-element.8.r_4_) | copy-start | bytes 21233668
  93.8 4.3 %collective-permute-start.4 = (f32[8,1152]{1,0:T(8,128)S(1)}, f32[8,1152]{1,0:T(8,128)S(1)}, u32[]{:S(2)}, u32[]{:S(2)}) collective-permute-start(f32[8,1152]{1,0:T(8,128)S(1)} %get-tuple-element.7.r_2_), channel_id=1, source_target_pairs={{0,16},{16,0},{1,17},{17,1},{2,18},{18,2},{3,19},{19,3},{4,20},{20... | collective-permute-start | bytes 110600 | tf_op jit(solution)/shard_map/ppermute | solution.py:198
  98.3 2.9 %collective-permute-start.5 = (f32[8,1152]{1,0:T(8,128)S(1)}, f32[8,1152]{1,0:T(8,128)S(1)}, u32[]{:S(2)}, u32[]{:S(2)}) collective-permute-start(f32[8,1152]{1,0:T(8,128)S(1)} %multiply_add_fusion.2), channel_id=1, source_target_pairs={{0,4},{4,0},{8,12},{12,8},{1,5},{5,1},{9,13},{13,9},{2,6},{6,2},{1... | collective-permute-start | bytes 110600 | tf_op jit(solution)/shard_map/ppermute | solution.py:198
  101.5 4.3 %collective-permute-start.6 = (f32[8,1152]{1,0:T(8,128)S(1)}, f32[8,1152]{1,0:T(8,128)S(1)}, u32[]{:S(2)}, u32[]{:S(2)}) collective-permute-start(f32[8,1152]{1,0:T(8,128)S(1)} %multiply_add_fusion.1), channel_id=1, source_target_pairs={{0,12},{4,8},{8,4},{12,0},{1,13},{5,9},{9,5},{13,1},{2,14},{6,10},... | collective-permute-start | bytes 110600 | tf_op jit(solution)/shard_map/ppermute | solution.py:198
  105.9 3.0 %copy-start.1 = (f32[16,72,1536]{2,1,0:T(8,128)S(1)}, f32[16,72,1536]{2,1,0:T(8,128)}, u32[]{:S(2)}) copy-start(f32[16,72,1536]{2,1,0:T(8,128)} %copy-done) | copy-start | bytes 21233668
  136.9 1.1 copy-start.4
  138.1 12.6 %collective-permute-start.7 = (bf16[144,768]{1,0:T(8,128)(2,1)S(1)}, bf16[144,768]{1,0:T(8,128)(2,1)S(1)}, u32[]{:S(2)}, u32[]{:S(2)}) collective-permute-start(bf16[144,768]{1,0:T(8,128)(2,1)S(1)} %multiply_convert_fusion), channel_id=1, source_target_pairs={{0,1},{1,0},{2,3},{3,2},{4,5},{5,4},{6,7},{7,6},{8,9},{9,8},{10,11... | collective-permute-start | bytes 663560 | tf_op jit(solution)/shard_map/ppermute | solution.py:198
  150.8 13.2 %copy-start.5 = (bf16[144,1280]{1,0:T(8,128)(2,1)S(1)}, bf16[144,1280]{1,0:T(8,128)(2,1)}, u32[]{:S(2)}) copy-start(bf16[144,1280]{1,0:T(8,128)(2,1)} %param.15) | copy-start | bytes 1105924
  153.7 10.3 %collective-permute-start.9 = (bf16[144,1280]{1,0:T(8,128)(2,1)S(1)}, bf16[144,1280]{1,0:T(8,128)(2,1)S(1)}, u32[]{:S(2)}, u32[]{:S(2)}) collective-permute-start(bf16[144,1280]{1,0:T(8,128)(2,1)S(1)} %fusion.17), channel_id=1, source_target_pairs={{0,2},{2,0},{1,3},{3,1},{4,6},{6,4},{5,7},{7,5},{8,10},{10,8},{9,1... | collective-permute-start | bytes 1105928 | tf_op jit(solution)/shard_map/ppermute | solution.py:198
Sparse Core Ops, SparseCore 0:
  13.8 54.3 all-gather.2

commit v3 on v2

--- a/solution.py
+++ b/solution.py
@@ -21,7 +21,8 @@
 
 
 def attend_kernel(rows, qb, kb, *refs):
-    q_refs, (kv_ref, o_ref, lse_ref) = refs[:-11], refs[-11:-8]
+    slots = (len(refs) - 11) // 2
+    q_refs, kv_refs, (o_ref, lse_ref) = refs[:slots], refs[slots:-10], refs[-10:-8]
     q3, k3, v3, q_s, k_s, v_s, lse_s, order = refs[-8:]
     head = pl.program_id(0)
     blocks = q3.shape[0]
@@ -54,10 +55,10 @@
     for i in range(blocks):
         z, d = i // per, i % per
         r = order[0, i]
-        k3[r] = kv_ref[z, d * RUN : (d + 1) * RUN, :]
-        v3[r] = kv_ref[z, rows + d * RUN : rows + (d + 1) * RUN, :]
-        p, e = z // 2, z % 2
-        q3[order[2, i]] = q_refs[p][e, d * RUN : (d + 1) * RUN, :]
+        v_off = rows if z < slots - 1 else 0
+        k3[r] = kv_refs[z][d * RUN : (d + 1) * RUN, :]
+        v3[r] = kv_refs[min(z, slots - 1) + (z == slots - 1)][v_off + d * RUN : v_off + (d + 1) * RUN, :]
+        q3[order[2, i]] = q_refs[z][d * RUN : (d + 1) * RUN, :]
     for i in range(blocks):
         q_s[i * RUN : (i + 1) * RUN, :] = q3[i]
         k_s[i * RUN : (i + 1) * RUN, :] = k3[i]
@@ -80,7 +81,7 @@
         def put(a, num, lse):
             for i in range(TILE):
                 g = order[3, t * TILE + i]
-                o_ref[g, :, a * 2 * HD : (a + 1) * 2 * HD] = num[i * RUN : (i + 1) * RUN]
+                o_ref[g, :, a * 2 * HD : (a + 1) * 2 * HD] = num[i * RUN : (i + 1) * RUN].astype(bf16)
                 lse_s[g] = jnp.where(lane == head * 2 + a, lse[i * RUN : (i + 1) * RUN], lse_s[g])
 
         for n in range(1, tiles + 1):
@@ -118,22 +119,18 @@
         lse_ref[...] = jnp.transpose(lse_s[...].reshape(blocks * RUN, HD))[: lse_ref.shape[0], :]
 
 
-def attend(q_parts, kv, qb, kb, rows, heads):
-    nq = len(q_parts)
-    blocks = 2 * nq * rows // RUN
-    zs = kv.shape[0]
-    pad = q_parts[0].shape[1]
+def attend(q_parts, kv_parts, qb, kb, rows, heads):
+    blocks = len(q_parts) * rows // RUN
     return pl.pallas_call(
         lambda *r: attend_kernel(rows, *r),
         out_shape=[
-            jax.ShapeDtypeStruct((blocks, RUN, heads * 4 * HD), f32),
+            jax.ShapeDtypeStruct((blocks, RUN, heads * 4 * HD), bf16),
             jax.ShapeDtypeStruct((8, blocks * RUN), f32),
         ],
         grid_spec=pltpu.PrefetchScalarGridSpec(
             num_scalar_prefetch=2,
             grid=(heads,),
-            in_specs=[pl.BlockSpec((2, pad, 2 * HD), lambda h, *_: (0, 0, h))] * nq
-            + [pl.BlockSpec((zs, kv.shape[1], 2 * HD), lambda h, *_: (0, 0, h))],
+            in_specs=[pl.BlockSpec((x.shape[0], 2 * HD), lambda h, *_: (0, h)) for x in q_parts + kv_parts],
             out_specs=[
                 pl.BlockSpec((blocks, RUN, 4 * HD), lambda h, *_: (0, 0, h)),
                 pl.BlockSpec((8, blocks * RUN), lambda h, *_: (0, 0)),
@@ -142,9 +139,9 @@
             + [pltpu.VMEM((blocks * RUN, 2 * HD), bf16)] * 3
             + [pltpu.VMEM((blocks, RUN, HD), f32), pltpu.SMEM((6, 128), jnp.int32)],
         ),
-        compiler_params=pltpu.CompilerParams(vmem_limit_bytes=40 << 20),
+        compiler_params=pltpu.CompilerParams(vmem_limit_bytes=32 << 20),
         name="attend",
-    )(qb, kb, *q_parts, kv)
+    )(qb, kb, *[pltpu.with_memory_space_constraint(x, pltpu.HBM) for x in q_parts + kv_parts])
 
 
 def weigh_kernel(heads, place, lam, lse_ref, all_ref, o_ref, out_ref, w_s):
@@ -161,8 +158,8 @@
     for h in range(heads):
         w1 = w[:, 2 * h : 2 * h + 1]
         w2 = w[:, 2 * h + 1 : 2 * h + 2] * lam[h]
-        o1 = o_ref[:, :, h * 4 * HD : h * 4 * HD + 2 * HD].reshape(rows, 2 * HD)
-        o2 = o_ref[:, :, h * 4 * HD + 2 * HD : (h + 1) * 4 * HD].reshape(rows, 2 * HD)
+        o1 = o_ref[:, :, h * 4 * HD : h * 4 * HD + 2 * HD].reshape(rows, 2 * HD).astype(f32)
+        o2 = o_ref[:, :, h * 4 * HD + 2 * HD : (h + 1) * 4 * HD].reshape(rows, 2 * HD).astype(f32)
         out_ref[0, :, h * 2 * HD : (h + 1) * 2 * HD] = (w1 * o1 - w2 * o2).astype(bf16)
 
 
@@ -184,6 +181,48 @@
     )(place, lam, lse, lse_all, o)
 
 
+def project_kernel(heads, cols, got_ref, gain_ref, w_ref, send_ref, keep_ref, n_s):
+    total = got_ref[0].astype(f32)
+    for i in range(1, got_ref.shape[0]):
+        total = total + got_ref[i].astype(f32)
+    for h in range(heads):
+        d = total[:, h * 2 * HD : (h + 1) * 2 * HD]
+        mean_square = jnp.mean(d * d, -1, keepdims=True)
+        g = gain_ref[0:1, h * 2 * HD : (h + 1) * 2 * HD]
+        n_s[:, h * 2 * HD : (h + 1) * 2 * HD] = (out_factor * d / jnp.sqrt(mean_square + norm_eps) * g).astype(bf16)
+    n = n_s[...]
+    width = keep_ref.shape[2]
+    for i in range(4):
+        w = w_ref[:, pl.ds(pl.multiple_of(cols[i] * width, HD), width)]
+        share = jnp.dot(n, w, preferred_element_type=f32)
+        if i < 2:
+            send_ref[i] = share.astype(bf16)
+        else:
+            keep_ref[i - 2] = share
+
+
+def project(cols, got, gain, weight, heads):
+    rows = got.shape[1]
+    width = weight.shape[1] // 4
+    vm = pl.BlockSpec(memory_space=pltpu.VMEM)
+    return pl.pallas_call(
+        lambda *r: project_kernel(heads, *r),
+        out_shape=[
+            jax.ShapeDtypeStruct((2, rows, width), bf16),
+            jax.ShapeDtypeStruct((2, rows, width), f32),
+        ],
+        in_specs=[pl.BlockSpec(memory_space=pltpu.SMEM), vm, vm, vm],
+        out_specs=[vm, vm],
+        scratch_shapes=[pltpu.VMEM((rows, got.shape[2]), bf16)],
+        compiler_params=pltpu.CompilerParams(vmem_limit_bytes=16 << 20),
+        name="project",
+    )(cols, got, gain, weight)
+
+
+def shift(x, axis, size, step):
+    return lax.ppermute(x, axis, [(i, (i + step) % size) for i in range(size)])
+
+
 def logsum(a, b):
     top = jnp.maximum(a, b)
     return top + jnp.log2(jnp.exp2(a - top) + jnp.exp2(b - top))
@@ -202,26 +241,36 @@
     nz, nh, ny, nl, nc = sizes
     rows, width = queries.shape
     heads = lambda_vecs.shape[1]
-    lane = lax.broadcasted_iota(jnp.int32, (16, width), 1)
-    ids = jnp.where(lane == 0, positions[0] // RUN, positions[RUN] // RUN).astype(bf16)
-
-    kv = lax.all_gather(jnp.concatenate([keys, values, ids], 0), "z", axis=0, tiled=False)
-    kb = kv[:, 2 * rows, : rows // RUN].astype(jnp.int32).reshape(-1)
+    block = ((positions[::RUN].astype(f32) + 0.5) * (1.0 / RUN)).astype(jnp.int32).astype(bf16)
+    ids = jnp.broadcast_to(jnp.pad(block, (0, width - block.shape[0]))[None, :], (16, width))
 
     q_mine = jnp.concatenate([queries, ids], 0)
-    q_pair = jnp.stack([q_mine, swap(q_mine, "h", nh, 1)], 0)
-    q_parts = [q_pair] + [swap(q_pair, "y", ny, d) for d in range(1, ny)]
-    qb = jnp.stack([q[:, rows, : rows // RUN] for q in q_parts], 0).astype(jnp.int32).reshape(-1)
-
-    l, c = lax.axis_index("l"), lax.axis_index("c")
-    w4 = out_weight.reshape(width, nl, nc, -1)
-    w_keep = lax.dynamic_index_in_dim(w4, c, 2, False)
-    w_away = swap(lax.dynamic_index_in_dim(w4, 1 - c, 2, False), "c", nc, 1)
-    w_both = jnp.concatenate([w_keep, w_away], 0)
-    w_mine = lax.dynamic_index_in_dim(w_both, l, 1, False)
-    w_other = lax.dynamic_index_in_dim(w_both, 1 - l, 1, False)
-
-    o, lse = attend(q_parts, kv, qb, kb, rows, heads)
+    kv_mine = jnp.concatenate([keys, values, ids], 0)
+    q_pair = swap(q_mine, "h", nh, 1)
+    up, down = shift(kv_mine, "z", nz, 1), shift(kv_mine, "z", nz, -1)
+    q_near = [swap(q_mine, "y", ny, d) for d in range(1, ny)]
+    kv_parts = [kv_mine, up, down]
+    up, down, q_pair = lax.optimization_barrier((up, down, q_pair))
+    up, down = shift(up, "z", nz, 1), shift(down, "z", nz, -1)
+    q_far = [swap(q_pair, "y", ny, d) for d in range(1, ny)]
+    kv_parts += [up, down]
+    up, down, q_near = lax.optimization_barrier((up, down, q_near))
+    up, down = shift(up, "z", nz, 1), shift(down, "z", nz, -1)
+    kv_parts += [up, down]
+    up, down, q_far = lax.optimization_barrier((up, down, q_far))
+    kv_parts += [shift(up[:rows], "z", nz, 1), shift(down[rows:], "z", nz, -1)]
+    q_parts = [q_mine, q_pair]
+    for d in range(ny - 1):
+        q_parts += [q_near[d], q_far[d]]
+
+    def numbers(parts):
+        spots = [p[p.shape[0] - 16 : p.shape[0] - 15, : rows // RUN] for p in parts]
+        return jnp.concatenate(spots, 0).astype(jnp.int32).reshape(-1)
+
+    qb = numbers(q_parts)
+    kb = numbers(kv_parts[: nz - 1] + kv_parts[nz:])
+
+    o, lse = attend(q_parts, kv_parts, qb, kb, rows, heads)
 
     whole = lse
     for axis, size, mask, slot in (("h", nh, 1, 1), ("y", ny, 1, 2), ("y", ny, 3, 6)):
@@ -237,16 +286,12 @@
     parts = weigh(place, lam, lse, whole, o, rows, heads)
 
     got = lax.all_to_all(parts, ("h", "y"), 0, 0, tiled=False)
-    diff = jnp.sum(got.astype(f32), 0).reshape(rows, heads, 2 * HD)
-    mean_square = jnp.mean(diff * diff, -1, keepdims=True)
-    normed = out_factor * diff / jnp.sqrt(mean_square + norm_eps) * head_gain.reshape(1, heads, 2 * HD)
-    normed = normed.reshape(rows, width).astype(bf16)
-
-    normed = jnp.concatenate([normed, swap(normed, "c", nc, 1)], 1)
-    send = jnp.dot(normed, w_other, preferred_element_type=f32).astype(bf16)
-    away = swap(send, "l", nl, 1)
-    keep = jnp.dot(normed, w_mine, preferred_element_type=f32)
-    return (keep + away.astype(f32) + residual.astype(f32)).astype(bf16)
+    l, c = lax.axis_index("l"), lax.axis_index("c")
+    cols = jnp.stack([l * nc + 1 - c, (1 - l) * nc + 1 - c, l * nc + c, (1 - l) * nc + c]).astype(jnp.int32)
+    send, keep = project(cols, got, head_gain.reshape(1, width), out_weight, heads)
+    near = swap(send, "c", nc, 1)
+    far = swap((keep[1] + near[1].astype(f32)).astype(bf16), "l", nl, 1)
+    return (keep[0] + near[0].astype(f32) + far.astype(f32) + residual.astype(f32)).astype(bf16)
 
 
 def solution(mesh):

time: 175 us -> 182 us (1.040)
  blocking collectives: 25.5 us -> 0 us
  waiting for transfers between devices: 36.8 us -> 61.9 us
  starting transfers between devices: 20.4 us -> 44.2 us
  between operations: 17.5 us -> 0.26 us
  matrix products: 6.6 us -> 0 us
  Pallas kernels: 22.3 us -> 26.7 us
  other arithmetic: 4.51 us -> 8.75 us
    all_to_all x1 -> x0, blocking collectives: 25.5 us -> none  [per_device(): got = lax.all_to_all(parts, ('h', 'y'), 0, 0, tiled=False)]
    ppermute x10 -> x12, waiting for transfers between devices: 22.2 us -> 44.8 us  [swap(): return lax.ppermute(x, axis, [(i, i ^ mask) for i in range(size)])]
    slice x4 -> x33, local copies, waits for them, and re-layouts: 1.37 us -> 22.9 us  [the longest x30 20.7 us: numbers(): spots = [p[p.shape[0] - 16:p.shape[0] - 15, :rows // RUN] for p in parts]]
    dynamic_slice x3 -> x0, local copies, waits for them, and re-layouts: 19.7 us -> none  [the longest x2 13.3 us: per_device(): w_away = swap(lax.dynamic_index_in_dim(w4, 1 - c, 2, False), 'c', nc, 1)]
    all_to_all x0 -> x1, waiting for transfers between devices: none -> 16.4 us  [per_device(): got = lax.all_to_all(parts, ('h', 'y'), 0, 0, tiled=False)]
    all_gather x1 -> x0, waiting for transfers between devices: 14.6 us -> none  [per_device(): lax.all_gather(jnp.concatenate([keys, values, ids], 0), 'z', axis=0, tile...]
    ppermute x0 -> x8, starting transfers between devices: none -> 14.4 us  [shift(): return lax.ppermute(x, axis, [(i, (i + step) % size) for i in range(size)])]
    unnamed x18 -> x44, local copies, waits for them, and re-layouts: 18.7 us -> 5.97 us
  transfers between devices with their start and end apart: 11 -> 21, of which waited for: 7 -> 14; matrix products, arithmetic and copies ran while one was open for 20% -> 15% of each run, Pallas kernels for 13% -> 0%
where the time goes in v3:
time: 182 us; the launch traced here: 181 us
  waiting for transfers between devices  61.9 us (34%)
  starting transfers between devices  44.2 us (24%)
  local copies, waits for them, and re-layouts  39.1 us (21%)
  Pallas kernels  26.7 us (15%)
  other arithmetic  8.75 us (5%)
    ppermute x12, waiting for transfers between devices, swap(): return lax.ppermute(x, axis, [(i, i ^ mask) for i in range(size)])  44.8 us
    ppermute x12, starting transfers between devices, swap(): return lax.ppermute(x, axis, [(i, i ^ mask) for i in range(size)])  24.1 us
    slice x30, local copies, waits for them, and re-layouts, numbers(): spots = [p[p.shape[0] - 16:p.shape[0] - 15, :rows // RUN] for p in parts]  20.7 us
    pallas_call x1, Pallas kernels, attend(): pl.pallas_call(lambda *r: attend_kernel(rows, *r), out_shape=[jax.ShapeDt...  19.9 us
    all_to_all x1, waiting for transfers between devices, per_device(): got = lax.all_to_all(parts, ('h', 'y'), 0, 0, tiled=False)  16.4 us
    ppermute x8, starting transfers between devices, shift(): return lax.ppermute(x, axis, [(i, (i + step) % size) for i in range(size)])  14.4 us
    unnamed x44, local copies, waits for them, and re-layouts  5.97 us
    all_to_all x1, starting transfers between devices, per_device(): got = lax.all_to_all(parts, ('h', 'y'), 0, 0, tiled=False)  5.63 us
  transfers between devices with their start and end apart: 21, of which 14 were waited for; matrix products, arithmetic and copies ran while one was open for 15% of the time, Pallas kernels for 0%

profile of v3, /device:TPU:1, one launch (start us, length us, event | category | flops | bytes accessed | tf_op | source)
XLA Modules:
  0.0 180.8 jit_solution(12306606456738184445)
XLA Ops:
  1.9 2.5 %collective-permute-start = (bf16[304,768]{1,0:T(8,128)(2,1)S(1)}, bf16[304,768]{1,0:T(8,128)(2,1)S(1)}, u32[]{:S(2)}, u32[]{:S(2)}) collective-permute-start(bf16[304,768]{1,0:T(8,128)(2,1)S(1)} %pad_maximum_fusion.r_10_), channel_id=1, source_target_pairs={{0,32},{32,64},{64,96},{96,128},{128,160},{160,192},{192,224},{224... | collective-permute-start | bytes 1400840 | tf_op jit(solution)/shard_map/ppermute | solution.py:223
  4.4 4.6 %collective-permute-start.1 = (bf16[304,768]{1,0:T(8,128)(2,1)S(1)}, bf16[304,768]{1,0:T(8,128)(2,1)S(1)}, u32[]{:S(2)}, u32[]{:S(2)}) collective-permute-start(bf16[304,768]{1,0:T(8,128)(2,1)S(1)} %pad_maximum_fusion.r_10_), channel_id=1, source_target_pairs={{0,224},{32,0},{64,32},{96,64},{128,96},{160,128},{192,160},{224,1... | collective-permute-start | bytes 1400840 | tf_op jit(solution)/shard_map/ppermute | solution.py:223
  10.0 2.8 %collective-permute-start.2 = (bf16[160,768]{1,0:T(8,128)(2,1)S(1)}, bf16[160,768]{1,0:T(8,128)(2,1)S(1)}, u32[]{:S(2)}, u32[]{:S(2)}) collective-permute-start(bf16[160,768]{1,0:T(8,128)(2,1)S(1)} %pad_maximum_fusion.1.r_2_), channel_id=1, source_target_pairs={{0,16},{16,0},{1,17},{17,1},{2,18},{18,2},{3,19},{19,3},{4,20},{20... | collective-permute-start | bytes 737288 | tf_op jit(solution)/shard_map/ppermute | solution.py:237
  12.8 5.3 %collective-permute-done.2.r_3_ = bf16[160,768]{1,0:T(8,128)(2,1)S(1)} collective-permute-done((bf16[160,768]{1,0:T(8,128)(2,1)S(1)}, bf16[160,768]{1,0:T(8,128)(2,1)S(1)}, u32[]{:S(2)}, u32[]{:S(2)}) %collective-permute-start.2) | collective-permute-done | bytes 245792 | tf_op jit(solution)/shard_map/ppermute | solution.py:237
  18.9 2.9 %collective-permute-start.4 = (bf16[304,768]{1,0:T(8,128)(2,1)S(1)}, bf16[304,768]{1,0:T(8,128)(2,1)S(1)}, u32[]{:S(2)}, u32[]{:S(2)}) collective-permute-start(bf16[304,768]{1,0:T(8,128)(2,1)S(1)} %collective-permute-done.1.r_12_), channel_id=1, source_target_pairs={{0,224},{32,0},{64,32},{96,64},{128,96},{160,128},{192,160},{224,1... | collective-permute-start | bytes 1400840 | tf_op jit(solution)/shard_map/ppermute | solution.py:223
  23.1 2.6 %collective-permute-start.6 = (bf16[160,768]{1,0:T(8,128)(2,1)S(1)}, bf16[160,768]{1,0:T(8,128)(2,1)S(1)}, u32[]{:S(2)}, u32[]{:S(2)}) collective-permute-start(bf16[160,768]{1,0:T(8,128)(2,1)S(1)} %pad_maximum_fusion.1.r_2_), channel_id=1, source_target_pairs={{0,8},{4,12},{8,0},{12,4},{1,9},{5,13},{9,1},{13,5},{2,10},{6,14},... | collective-permute-start | bytes 737288 | tf_op jit(solution)/shard_map/ppermute | solution.py:237
  27.4 7.7 %collective-permute-done.6.r_6_ = bf16[160,768]{1,0:T(8,128)(2,1)S(1)} collective-permute-done((bf16[160,768]{1,0:T(8,128)(2,1)S(1)}, bf16[160,768]{1,0:T(8,128)(2,1)S(1)}, u32[]{:S(2)}, u32[]{:S(2)}) %collective-permute-start.6) | collective-permute-done | bytes 245792 | tf_op jit(solution)/shard_map/ppermute | solution.py:237
  35.2 3.4 %collective-permute-done.7.r_8_ = bf16[160,768]{1,0:T(8,128)(2,1)S(1)} collective-permute-done((bf16[160,768]{1,0:T(8,128)(2,1)S(1)}, bf16[160,768]{1,0:T(8,128)(2,1)S(1)}, u32[]{:S(2)}, u32[]{:S(2)}) %collective-permute-start.7) | collective-permute-done | bytes 245792 | tf_op jit(solution)/shard_map/ppermute | solution.py:237
  38.7 2.7 %collective-permute-start.9 = (bf16[304,768]{1,0:T(8,128)(2,1)S(1)}, bf16[304,768]{1,0:T(8,128)(2,1)S(1)}, u32[]{:S(2)}, u32[]{:S(2)}) collective-permute-start(bf16[304,768]{1,0:T(8,128)(2,1)S(1)} %collective-permute-done.4.r_14_), channel_id=1, source_target_pairs={{0,224},{32,0},{64,32},{96,64},{128,96},{160,128},{192,160},{224,1... | collective-permute-start | bytes 1400840 | tf_op jit(solution)/shard_map/ppermute | solution.py:223
  42.6 2.6 %collective-permute-start.12 = (bf16[160,768]{1,0:T(8,128)(2,1)S(1)}, bf16[160,768]{1,0:T(8,128)(2,1)S(1)}, u32[]{:S(2)}, u32[]{:S(2)}) collective-permute-start(bf16[160,768]{1,0:T(8,128)(2,1)S(1)} %collective-permute-done.2.r_3_), channel_id=1, source_target_pairs={{0,12},{4,8},{8,4},{12,0},{1,13},{5,9},{9,5},{13,1},{2,14},{6,10},... | collective-permute-start | bytes 737288 | tf_op jit(solution)/shard_map/ppermute | solution.py:237
  46.7 4.4 %collective-permute-done.11.r_7_ = bf16[160,768]{1,0:T(8,128)(2,1)S(1)} collective-permute-done((bf16[160,768]{1,0:T(8,128)(2,1)S(1)}, bf16[160,768]{1,0:T(8,128)(2,1)S(1)}, u32[]{:S(2)}, u32[]{:S(2)}) %collective-permute-start.11) | collective-permute-done | bytes 245792 | tf_op jit(solution)/shard_map/ppermute | solution.py:237
  51.1 4.3 %collective-permute-done.12.r_9_ = bf16[160,768]{1,0:T(8,128)(2,1)S(1)} collective-permute-done((bf16[160,768]{1,0:T(8,128)(2,1)S(1)}, bf16[160,768]{1,0:T(8,128)(2,1)S(1)}, u32[]{:S(2)}, u32[]{:S(2)}) %collective-permute-start.12) | collective-permute-done | bytes 245792 | tf_op jit(solution)/shard_map/ppermute | solution.py:237
  84.0 19.9 %attend.1 = (bf16[16,72,1536]{2,1,0:T(8,128)(2,1)S(1)}, f32[8,1152]{1,0:T(8,128)S(1)}) custom-call(s32[16]{0:T(128)S(1)} %reshape.23.r_0_, s32[16]{0:T(128)S(1)} %reshape.24.r_1_, bf16[160,768]{1,0:T(8,128)(2,1)} %copy-done.6, bf16[160,768]{1,0:T(8,128)(2,1)} %copy-done.12, bf16[160,768]{1,0:T(8,128)(2,1)} %copy-done.13, bf16[160,768]{1,0:T(8,128)(2,1)} %copy-done.16, ...), custom_call_target="tpu_custom_call" | custom-call | tf_op jit(solution)/shard_map/attend/pallas_call | solution.py:124
  104.6 2.0 %collective-permute-start.15 = (f32[8,1152]{1,0:T(8,128)S(1)}, f32[8,1152]{1,0:T(8,128)S(1)}, u32[]{:S(2)}, u32[]{:S(2)}) collective-permute-start(f32[8,1152]{1,0:T(8,128)S(1)} %get-tuple-element.35.r_2_), channel_id=1, source_target_pairs={{0,16},{16,0},{1,17},{17,1},{2,18},{18,2},{3,19},{19,3},{4,20},{20... | collective-permute-start | bytes 110600 | tf_op jit(solution)/shard_map/ppermute | solution.py:237
  113.2 2.5 %collective-permute-done.16 = f32[8,1152]{1,0:T(8,128)} collective-permute-done((f32[8,1152]{1,0:T(8,128)}, f32[8,1152]{1,0:T(8,128)}, u32[]{:S(2)}, u32[]{:S(2)}) %collective-permute-start.16) | collective-permute-done | bytes 36896 | tf_op jit(solution)/shard_map/ppermute | solution.py:237
  119.9 3.5 %collective-permute-start.17 = (f32[8,1152]{1,0:T(8,128)S(1)}, f32[8,1152]{1,0:T(8,128)S(1)}, u32[]{:S(2)}, u32[]{:S(2)}) collective-permute-start(f32[8,1152]{1,0:T(8,128)S(1)} %multiply_add_fusion.1), channel_id=1, source_target_pairs={{0,12},{4,8},{8,4},{12,0},{1,13},{5,9},{9,5},{13,1},{2,14},{6,10},... | collective-permute-start | bytes 110600 | tf_op jit(solution)/shard_map/ppermute | solution.py:237
  128.5 4.6 %weigh.1 = bf16[8,144,768]{2,1,0:T(8,128)(2,1)} custom-call(s32[8]{0:T(128)S(1)} %xor_add_fusion.r_0_, f32[3]{0:T(128)S(1)} %subtract_add_fusion.r_1_, f32[8,1152]{1,0:T(8,128)S(1)} %copy-done.2, f32[8,1152]{1,0:T(8,128)S(1)} %multiply_add_fusion.r_3_, bf16[16,72,1536]{2,1,0:T(8,128)(2,1)S(1)} %get-tuple-element.36.r_4_), custom_call_target="tpu_custom_call" | custom-call | tf_op jit(solution)/shard_map/weigh/pallas_call | solution.py:168
  133.1 5.6 %all-to-all-start = ((bf16[8,144,768]{2,1,0:T(8,128)(2,1)}), bf16[8,144,768]{2,1,0:T(8,128)(2,1)S(1)}, u32[]{:S(2)}, u32[]{:S(2)}) async-start(bf16[8,144,768]{2,1,0:T(8,128)(2,1)} %weigh.1), calls=%async_computation | async-start | bytes 3538944 | tf_op jit(solution)/shard_map/all_to_all | solution.py:288
  138.8 16.4 %all-to-all-done.r_1_ = bf16[8,144,768]{2,1,0:T(8,128)(2,1)S(1)} async-done(((bf16[8,144,768]{2,1,0:T(8,128)(2,1)}), bf16[8,144,768]{2,1,0:T(8,128)(2,1)S(1)}, u32[]{:S(2)}, u32[]{:S(2)}) %all-to-all-start) | async-done | bytes 1769504 | tf_op jit(solution)/shard_map/all_to_all | solution.py:288
  155.3 3.2 %copy-done = bf16[768,5120]{1,0:T(8,128)(2,1)S(1)} copy-done((bf16[768,5120]{1,0:T(8,128)(2,1)S(1)}, bf16[768,5120]{1,0:T(8,128)(2,1)}, u32[]{:S(2)}) %copy-start) | copy-done | bytes 7864344
  158.5 2.1 %project.1 = (bf16[2,144,1280]{2,1,0:T(8,128)(2,1)S(1)}, f32[2,144,1280]{2,1,0:T(8,128)S(1)}) custom-call(s32[4]{0:T(128)S(1)} %pad_add_fusion.r_0_, bf16[8,144,768]{2,1,0:T(8,128)(2,1)S(1)} %all-to-all-done.r_1_, f32[1,768]{1,0:T(1,128)S(1)} %reshape.22.r_2_, bf16[768,5120]{1,0:T(8,128)(2,1)S(1)} %copy-done), custom_call_target="tpu_custom_call" | custom-call | tf_op jit(solution)/shard_map/project/pallas_call | solution.py:208
  160.6 7.4 %collective-permute-start.18 = (bf16[2,144,1280]{2,1,0:T(8,128)(2,1)S(1)}, bf16[2,144,1280]{2,1,0:T(8,128)(2,1)S(1)}, u32[]{:S(2)}, u32[]{:S(2)}) collective-permute-start(bf16[2,144,1280]{2,1,0:T(8,128)(2,1)S(1)} %get-tuple-element.38), channel_id=1, source_target_pairs={{0,1},{1,0},{2,3},{3,2},{4,5},{5,4},{6,7},{7,6},{8,9},{9,8},{10,11... | collective-permute-start | bytes 2211848 | tf_op jit(solution)/shard_map/ppermute | solution.py:237
  168.1 1.8 %collective-permute-done.18 = bf16[2,144,1280]{2,1,0:T(8,128)(2,1)S(1)} collective-permute-done((bf16[2,144,1280]{2,1,0:T(8,128)(2,1)S(1)}, bf16[2,144,1280]{2,1,0:T(8,128)(2,1)S(1)}, u32[]{:S(2)}, u32[]{:S(2)}) %collective-permute-start.18) | collective-permute-done | bytes 737312 | tf_op jit(solution)/shard_map/ppermute | solution.py:237
  170.6 9.3 %collective-permute-done.19 = bf16[144,1280]{1,0:T(8,128)(2,1)S(1)} collective-permute-done((bf16[144,1280]{1,0:T(8,128)(2,1)S(1)}, bf16[144,1280]{1,0:T(8,128)(2,1)S(1)}, u32[]{:S(2)}, u32[]{:S(2)}) %collective-permute-start.19) | collective-permute-done | bytes 368672 | tf_op jit(solution)/shard_map/ppermute | solution.py:237
  (128 shorter events, 56.2 us)
Async XLA Ops:
  1.9 16.9 %collective-permute-start = (bf16[304,768]{1,0:T(8,128)(2,1)S(1)}, bf16[304,768]{1,0:T(8,128)(2,1)S(1)}, u32[]{:S(2)}, u32[]{:S(2)}) collective-permute-start(bf16[304,768]{1,0:T(8,128)(2,1)S(1)} %pad_maximum_fusion.r_10_), channel_id=1, source_target_pairs={{0,32},{32,64},{64,96},{96,128},{128,160},{160,192},{192,224},{224... | collective-permute-start | bytes 1400840 | tf_op jit(solution)/shard_map/ppermute | solution.py:223
  4.4 14.4 %collective-permute-start.1 = (bf16[304,768]{1,0:T(8,128)(2,1)S(1)}, bf16[304,768]{1,0:T(8,128)(2,1)S(1)}, u32[]{:S(2)}, u32[]{:S(2)}) collective-permute-start(bf16[304,768]{1,0:T(8,128)(2,1)S(1)} %pad_maximum_fusion.r_10_), channel_id=1, source_target_pairs={{0,224},{32,0},{64,32},{96,64},{128,96},{160,128},{192,160},{224,1... | collective-permute-start | bytes 1400840 | tf_op jit(solution)/shard_map/ppermute | solution.py:223
  10.0 8.1 %collective-permute-start.2 = (bf16[160,768]{1,0:T(8,128)(2,1)S(1)}, bf16[160,768]{1,0:T(8,128)(2,1)S(1)}, u32[]{:S(2)}, u32[]{:S(2)}) collective-permute-start(bf16[160,768]{1,0:T(8,128)(2,1)S(1)} %pad_maximum_fusion.1.r_2_), channel_id=1, source_target_pairs={{0,16},{16,0},{1,17},{17,1},{2,18},{18,2},{3,19},{19,3},{4,20},{20... | collective-permute-start | bytes 737288 | tf_op jit(solution)/shard_map/ppermute | solution.py:237
  18.1 65.8 %copy-start.12 = (bf16[160,768]{1,0:T(8,128)(2,1)}, bf16[160,768]{1,0:T(8,128)(2,1)S(1)}, u32[]{:S(2)}) copy-start(bf16[160,768]{1,0:T(8,128)(2,1)S(1)} %collective-permute-done.2.r_3_) | copy-start | bytes 737284
  18.8 65.1 %copy-start.7 = (bf16[304,768]{1,0:T(8,128)(2,1)}, bf16[304,768]{1,0:T(8,128)(2,1)S(1)}, u32[]{:S(2)}) copy-start(bf16[304,768]{1,0:T(8,128)(2,1)S(1)} %collective-permute-done.r_11_) | copy-start | bytes 1400836
  18.8 65.1 %copy-start.8 = (bf16[304,768]{1,0:T(8,128)(2,1)}, bf16[304,768]{1,0:T(8,128)(2,1)S(1)}, u32[]{:S(2)}) copy-start(bf16[304,768]{1,0:T(8,128)(2,1)S(1)} %collective-permute-done.1.r_12_) | copy-start | bytes 1400836
  18.8 19.8 %collective-permute-start.3 = (bf16[304,768]{1,0:T(8,128)(2,1)S(1)}, bf16[304,768]{1,0:T(8,128)(2,1)S(1)}, u32[]{:S(2)}, u32[]{:S(2)}) collective-permute-start(bf16[304,768]{1,0:T(8,128)(2,1)S(1)} %collective-permute-done.r_11_), channel_id=1, source_target_pairs={{0,32},{32,64},{64,96},{96,128},{128,160},{160,192},{192,224},{224... | collective-permute-start | bytes 1400840 | tf_op jit(solution)/shard_map/ppermute | solution.py:223
  18.9 19.7 %collective-permute-start.4 = (bf16[304,768]{1,0:T(8,128)(2,1)S(1)}, bf16[304,768]{1,0:T(8,128)(2,1)S(1)}, u32[]{:S(2)}, u32[]{:S(2)}) collective-permute-start(bf16[304,768]{1,0:T(8,128)(2,1)S(1)} %collective-permute-done.1.r_12_), channel_id=1, source_target_pairs={{0,224},{32,0},{64,32},{96,64},{128,96},{160,128},{192,160},{224,1... | collective-permute-start | bytes 1400840 | tf_op jit(solution)/shard_map/ppermute | solution.py:223
  21.8 5.6 %collective-permute-start.5 = (bf16[160,768]{1,0:T(8,128)(2,1)S(1)}, bf16[160,768]{1,0:T(8,128)(2,1)S(1)}, u32[]{:S(2)}, u32[]{:S(2)}) collective-permute-start(bf16[160,768]{1,0:T(8,128)(2,1)S(1)} %pad_maximum_fusion.1.r_2_), channel_id=1, source_target_pairs={{0,4},{4,0},{8,12},{12,8},{1,5},{5,1},{9,13},{13,9},{2,6},{6,2},{1... | collective-permute-start | bytes 737288 | tf_op jit(solution)/shard_map/ppermute | solution.py:237
  23.1 12.0 %collective-permute-start.6 = (bf16[160,768]{1,0:T(8,128)(2,1)S(1)}, bf16[160,768]{1,0:T(8,128)(2,1)S(1)}, u32[]{:S(2)}, u32[]{:S(2)}) collective-permute-start(bf16[160,768]{1,0:T(8,128)(2,1)S(1)} %pad_maximum_fusion.1.r_2_), channel_id=1, source_target_pairs={{0,8},{4,12},{8,0},{12,4},{1,9},{5,13},{9,1},{13,5},{2,10},{6,14},... | collective-permute-start | bytes 737288 | tf_op jit(solution)/shard_map/ppermute | solution.py:237
  25.7 12.8 %collective-permute-start.7 = (bf16[160,768]{1,0:T(8,128)(2,1)S(1)}, bf16[160,768]{1,0:T(8,128)(2,1)S(1)}, u32[]{:S(2)}, u32[]{:S(2)}) collective-permute-start(bf16[160,768]{1,0:T(8,128)(2,1)S(1)} %pad_maximum_fusion.1.r_2_), channel_id=1, source_target_pairs={{0,12},{4,8},{8,4},{12,0},{1,13},{5,9},{9,5},{13,1},{2,14},{6,10},... | collective-permute-start | bytes 737288 | tf_op jit(solution)/shard_map/ppermute | solution.py:237
  38.6 16.8 %collective-permute-start.8 = (bf16[304,768]{1,0:T(8,128)(2,1)S(1)}, bf16[304,768]{1,0:T(8,128)(2,1)S(1)}, u32[]{:S(2)}, u32[]{:S(2)}) collective-permute-start(bf16[304,768]{1,0:T(8,128)(2,1)S(1)} %collective-permute-done.3.r_13_), channel_id=1, source_target_pairs={{0,32},{32,64},{64,96},{96,128},{128,160},{160,192},{192,224},{224... | collective-permute-start | bytes 1400840 | tf_op jit(solution)/shard_map/ppermute | solution.py:223
  38.7 17.4 %collective-permute-start.9 = (bf16[304,768]{1,0:T(8,128)(2,1)S(1)}, bf16[304,768]{1,0:T(8,128)(2,1)S(1)}, u32[]{:S(2)}, u32[]{:S(2)}) collective-permute-start(bf16[304,768]{1,0:T(8,128)(2,1)S(1)} %collective-permute-done.4.r_14_), channel_id=1, source_target_pairs={{0,224},{32,0},{64,32},{96,64},{128,96},{160,128},{192,160},{224,1... | collective-permute-start | bytes 1400840 | tf_op jit(solution)/shard_map/ppermute | solution.py:223
  41.4 5.3 %collective-permute-start.10 = (bf16[160,768]{1,0:T(8,128)(2,1)S(1)}, bf16[160,768]{1,0:T(8,128)(2,1)S(1)}, u32[]{:S(2)}, u32[]{:S(2)}) collective-permute-start(bf16[160,768]{1,0:T(8,128)(2,1)S(1)} %collective-permute-done.2.r_3_), channel_id=1, source_target_pairs={{0,4},{4,0},{8,12},{12,8},{1,5},{5,1},{9,13},{13,9},{2,6},{6,2},{1... | collective-permute-start | bytes 737288 | tf_op jit(solution)/shard_map/ppermute | solution.py:237
  41.4 9.7 %collective-permute-start.11 = (bf16[160,768]{1,0:T(8,128)(2,1)S(1)}, bf16[160,768]{1,0:T(8,128)(2,1)S(1)}, u32[]{:S(2)}, u32[]{:S(2)}) collective-permute-start(bf16[160,768]{1,0:T(8,128)(2,1)S(1)} %collective-permute-done.2.r_3_), channel_id=1, source_target_pairs={{0,8},{4,12},{8,0},{12,4},{1,9},{5,13},{9,1},{13,5},{2,10},{6,14},... | collective-permute-start | bytes 737288 | tf_op jit(solution)/shard_map/ppermute | solution.py:237
  42.6 12.8 %collective-permute-start.12 = (bf16[160,768]{1,0:T(8,128)(2,1)S(1)}, bf16[160,768]{1,0:T(8,128)(2,1)S(1)}, u32[]{:S(2)}, u32[]{:S(2)}) collective-permute-start(bf16[160,768]{1,0:T(8,128)(2,1)S(1)} %collective-permute-done.2.r_3_), channel_id=1, source_target_pairs={{0,12},{4,8},{8,4},{12,0},{1,13},{5,9},{9,5},{13,1},{2,14},{6,10},... | collective-permute-start | bytes 737288 | tf_op jit(solution)/shard_map/ppermute | solution.py:237
  56.9 23.1 %collective-permute-start.13 = (bf16[160,768]{1,0:T(8,128)(2,1)}, bf16[160,768]{1,0:T(8,128)(2,1)}, u32[]{:S(2)}, u32[]{:S(2)}) collective-permute-start(bf16[160,768]{1,0:T(8,128)(2,1)} %slice.164), channel_id=1, source_target_pairs={{0,224},{32,0},{64,32},{96,64},{128,96},{160,128},{192,160},{224,1... | collective-permute-start | bytes 737288 | tf_op jit(solution)/shard_map/ppermute | solution.py:223
  57.7 26.3 %collective-permute-start.14 = (bf16[144,768]{1,0:T(8,128)(2,1)}, bf16[144,768]{1,0:T(8,128)(2,1)}, u32[]{:S(2)}, u32[]{:S(2)}) collective-permute-start(bf16[144,768]{1,0:T(8,128)(2,1)} %slice.166), channel_id=1, source_target_pairs={{0,32},{32,64},{64,96},{96,128},{128,160},{160,192},{192,224},{224... | collective-permute-start | bytes 663560 | tf_op jit(solution)/shard_map/ppermute | solution.py:223
  104.6 4.3 %collective-permute-start.15 = (f32[8,1152]{1,0:T(8,128)S(1)}, f32[8,1152]{1,0:T(8,128)S(1)}, u32[]{:S(2)}, u32[]{:S(2)}) collective-permute-start(f32[8,1152]{1,0:T(8,128)S(1)} %get-tuple-element.35.r_2_), channel_id=1, source_target_pairs={{0,16},{16,0},{1,17},{17,1},{2,18},{18,2},{3,19},{19,3},{4,20},{20... | collective-permute-start | bytes 110600 | tf_op jit(solution)/shard_map/ppermute | solution.py:237
  112.5 3.1 %collective-permute-start.16 = (f32[8,1152]{1,0:T(8,128)}, f32[8,1152]{1,0:T(8,128)}, u32[]{:S(2)}, u32[]{:S(2)}) collective-permute-start(f32[8,1152]{1,0:T(8,128)} %multiply_add_fusion.2), channel_id=1, source_target_pairs={{0,4},{4,0},{8,12},{12,8},{1,5},{5,1},{9,13},{13,9},{2,6},{6,2},{1... | collective-permute-start | bytes 110600 | tf_op jit(solution)/shard_map/ppermute | solution.py:237
  119.9 4.9 %collective-permute-start.17 = (f32[8,1152]{1,0:T(8,128)S(1)}, f32[8,1152]{1,0:T(8,128)S(1)}, u32[]{:S(2)}, u32[]{:S(2)}) collective-permute-start(f32[8,1152]{1,0:T(8,128)S(1)} %multiply_add_fusion.1), channel_id=1, source_target_pairs={{0,12},{4,8},{8,4},{12,0},{1,13},{5,9},{9,5},{13,1},{2,14},{6,10},... | collective-permute-start | bytes 110600 | tf_op jit(solution)/shard_map/ppermute | solution.py:237
  133.1 22.2 %all-to-all-start = ((bf16[8,144,768]{2,1,0:T(8,128)(2,1)}), bf16[8,144,768]{2,1,0:T(8,128)(2,1)S(1)}, u32[]{:S(2)}, u32[]{:S(2)}) async-start(bf16[8,144,768]{2,1,0:T(8,128)(2,1)} %weigh.1), calls=%async_computation | async-start | bytes 3538944 | tf_op jit(solution)/shard_map/all_to_all | solution.py:288
  160.6 9.3 %collective-permute-start.18 = (bf16[2,144,1280]{2,1,0:T(8,128)(2,1)S(1)}, bf16[2,144,1280]{2,1,0:T(8,128)(2,1)S(1)}, u32[]{:S(2)}, u32[]{:S(2)}) collective-permute-start(bf16[2,144,1280]{2,1,0:T(8,128)(2,1)S(1)} %get-tuple-element.38), channel_id=1, source_target_pairs={{0,1},{1,0},{2,3},{3,2},{4,5},{5,4},{6,7},{7,6},{8,9},{9,8},{10,11... | collective-permute-start | bytes 2211848 | tf_op jit(solution)/shard_map/ppermute | solution.py:237
  170.0 9.9 %collective-permute-start.19 = (bf16[144,1280]{1,0:T(8,128)(2,1)S(1)}, bf16[144,1280]{1,0:T(8,128)(2,1)S(1)}, u32[]{:S(2)}, u32[]{:S(2)}) collective-permute-start(bf16[144,1280]{1,0:T(8,128)(2,1)S(1)} %fusion.2), channel_id=1, source_target_pairs={{0,2},{2,0},{1,3},{3,1},{4,6},{6,4},{5,7},{7,5},{8,10},{10,8},{9,1... | collective-permute-start | bytes 1105928 | tf_op jit(solution)/shard_map/ppermute | solution.py:237
  (19 other events, 385.7 us)

commit v4 on v3

--- a/solution.py
+++ b/solution.py
@@ -20,7 +20,7 @@
 bf16 = jnp.bfloat16
 
 
-def attend_kernel(rows, qb, kb, *refs):
+def attend_kernel(rows, *refs):
     slots = (len(refs) - 11) // 2
     q_refs, kv_refs, (o_ref, lse_ref) = refs[:slots], refs[slots:-10], refs[-10:-8]
     q3, k3, v3, q_s, k_s, v_s, lse_s, order = refs[-8:]
@@ -34,6 +34,15 @@
     @pl.when(head == 0)
     def _():
         lse_s[...] = jnp.zeros_like(lse_s)
+        first = lax.broadcasted_iota(jnp.int32, (16, HD), 0) == 0
+        lanes = lax.broadcasted_iota(jnp.int32, (16, HD), 1)
+
+        def numbers(part):
+            tail = part[part.shape[0] - 16 :, :HD].astype(f32)
+            return [jnp.sum(jnp.where(first & (lanes == d), tail, 0.0)).astype(jnp.int32) for d in range(per)]
+
+        kb = [v for p in [*kv_refs[: slots - 1], kv_refs[slots]] for v in numbers(p)]
+        qb = [v for p in q_refs for v in numbers(p)]
         for i in range(blocks):
             rk = jnp.int32(0)
             rq = jnp.int32(0)
@@ -49,7 +58,7 @@
             last = order[4, t * TILE + TILE - 1]
             need = jnp.int32(0)
             for j in range(blocks):
-                need = need + (kb[j] <= last).astype(jnp.int32)
+                need = need + (order[1, j] <= last).astype(jnp.int32)
             order[5, t] = lax.div(need + (TILE - 1), TILE)
 
     for i in range(blocks):
@@ -119,7 +128,7 @@
         lse_ref[...] = jnp.transpose(lse_s[...].reshape(blocks * RUN, HD))[: lse_ref.shape[0], :]
 
 
-def attend(q_parts, kv_parts, qb, kb, rows, heads):
+def attend(q_parts, kv_parts, rows, heads):
     blocks = len(q_parts) * rows // RUN
     return pl.pallas_call(
         lambda *r: attend_kernel(rows, *r),
@@ -128,7 +137,7 @@
             jax.ShapeDtypeStruct((8, blocks * RUN), f32),
         ],
         grid_spec=pltpu.PrefetchScalarGridSpec(
-            num_scalar_prefetch=2,
+            num_scalar_prefetch=0,
             grid=(heads,),
             in_specs=[pl.BlockSpec((x.shape[0], 2 * HD), lambda h, *_: (0, h)) for x in q_parts + kv_parts],
             out_specs=[
@@ -141,16 +150,49 @@
         ),
         compiler_params=pltpu.CompilerParams(vmem_limit_bytes=32 << 20),
         name="attend",
-    )(qb, kb, *[pltpu.with_memory_space_constraint(x, pltpu.HBM) for x in q_parts + kv_parts])
-
-
-def weigh_kernel(heads, place, lam, lse_ref, all_ref, o_ref, out_ref, w_s):
+    )(*[pltpu.with_memory_space_constraint(x, pltpu.HBM) for x in q_parts + kv_parts])
+
+
+def logsum(parts):
+    top = parts[0]
+    for p in parts[1:]:
+        top = jnp.maximum(top, p)
+    total = jnp.exp2(parts[0] - top)
+    for p in parts[1:]:
+        total = total + jnp.exp2(p - top)
+    return top + jnp.log2(total)
+
+
+def reorder(x, rows, mask):
+    slots = x.shape[1] // rows
+    return jnp.concatenate([x[:, (s ^ mask) * rows : ((s ^ mask) + 1) * rows] for s in range(slots)], 1)
+
+
+def merge_kernel(rows, a_ref, b_ref, o_ref):
+    o_ref[...] = logsum([a_ref[...], reorder(b_ref[...], rows, 1)])
+
+
+def merge(a, b, rows):
+    vm = pl.BlockSpec(memory_space=pltpu.VMEM)
+    return pl.pallas_call(
+        lambda *r: merge_kernel(rows, *r),
+        out_shape=jax.ShapeDtypeStruct(a.shape, a.dtype),
+        in_specs=[vm, vm],
+        out_specs=vm,
+        compiler_params=pltpu.CompilerParams(vmem_limit_bytes=4 << 20),
+        name="merge",
+    )(a, b)
+
+
+def weigh_kernel(heads, place, lam, lse_ref, *refs):
+    all_refs, o_ref, out_ref, w_s = refs[:-3], refs[-3], refs[-2], refs[-1]
     s = pl.program_id(0)
     rows = out_ref.shape[1]
 
     @pl.when(s == 0)
     def _():
-        w = jnp.exp2(lse_ref[...] - all_ref[...])
+        whole = logsum([reorder(r[...], rows, 2 * i) for i, r in enumerate(all_refs)])
+        w = jnp.exp2(lse_ref[...] - whole)
         w = jnp.concatenate([w, jnp.zeros((HD - w.shape[0], w.shape[1]), f32)], 0)
         w_s[...] = jnp.transpose(w)
 
@@ -163,7 +205,7 @@
         out_ref[0, :, h * 2 * HD : (h + 1) * 2 * HD] = (w1 * o1 - w2 * o2).astype(bf16)
 
 
-def weigh(place, lam, lse, lse_all, o, rows, heads):
+def weigh(place, lam, lse, lses, o, rows, heads):
     slots = lse.shape[1] // rows
     return pl.pallas_call(
         lambda *r: weigh_kernel(heads, *r),
@@ -171,66 +213,71 @@
         grid_spec=pltpu.PrefetchScalarGridSpec(
             num_scalar_prefetch=2,
             grid=(slots,),
-            in_specs=[pl.BlockSpec(lse.shape, lambda s, *_: (0, 0))] * 2
+            in_specs=[pl.BlockSpec(lse.shape, lambda s, *_: (0, 0))] * (1 + len(lses))
             + [pl.BlockSpec((rows // RUN, RUN, heads * 4 * HD), lambda s, *_: (s, 0, 0))],
             out_specs=pl.BlockSpec((1, rows, heads * 2 * HD), lambda s, place, lam: (place[s], 0, 0)),
             scratch_shapes=[pltpu.VMEM((slots * rows, HD), f32)],
         ),
         compiler_params=pltpu.CompilerParams(vmem_limit_bytes=16 << 20),
         name="weigh",
-    )(place, lam, lse, lse_all, o)
+    )(place, lam, lse, *lses, o)
 
 
 def project_kernel(heads, cols, got_ref, gain_ref, w_ref, send_ref, keep_ref, n_s):
-    total = got_ref[0].astype(f32)
-    for i in range(1, got_ref.shape[0]):
-        total = total + got_ref[i].astype(f32)
-    for h in range(heads):
-        d = total[:, h * 2 * HD : (h + 1) * 2 * HD]
-        mean_square = jnp.mean(d * d, -1, keepdims=True)
-        g = gain_ref[0:1, h * 2 * HD : (h + 1) * 2 * HD]
-        n_s[:, h * 2 * HD : (h + 1) * 2 * HD] = (out_factor * d / jnp.sqrt(mean_square + norm_eps) * g).astype(bf16)
-    n = n_s[...]
-    width = keep_ref.shape[2]
-    for i in range(4):
-        w = w_ref[:, pl.ds(pl.multiple_of(cols[i] * width, HD), width)]
-        share = jnp.dot(n, w, preferred_element_type=f32)
-        if i < 2:
-            send_ref[i] = share.astype(bf16)
-        else:
-            keep_ref[i - 2] = share
+    i = pl.program_id(0)
+
+    @pl.when(i == 0)
+    def _():
+        total = got_ref[0].astype(f32)
+        for j in range(1, got_ref.shape[0]):
+            total = total + got_ref[j].astype(f32)
+        for h in range(heads):
+            d = total[:, h * 2 * HD : (h + 1) * 2 * HD]
+            mean_square = jnp.mean(d * d, -1, keepdims=True)
+            g = gain_ref[0:1, h * 2 * HD : (h + 1) * 2 * HD]
+            n_s[:, h * 2 * HD : (h + 1) * 2 * HD] = (out_factor * d / jnp.sqrt(mean_square + norm_eps) * g).astype(bf16)
+
+    share = jnp.dot(n_s[...], w_ref[...], preferred_element_type=f32)
+
+    @pl.when(i < 2)
+    def _():
+        send_ref[0] = share.astype(bf16)
+
+    @pl.when(i >= 2)
+    def _():
+        keep_ref[0] = share
 
 
 def project(cols, got, gain, weight, heads):
     rows = got.shape[1]
     width = weight.shape[1] // 4
-    vm = pl.BlockSpec(memory_space=pltpu.VMEM)
     return pl.pallas_call(
         lambda *r: project_kernel(heads, *r),
         out_shape=[
             jax.ShapeDtypeStruct((2, rows, width), bf16),
             jax.ShapeDtypeStruct((2, rows, width), f32),
         ],
-        in_specs=[pl.BlockSpec(memory_space=pltpu.SMEM), vm, vm, vm],
-        out_specs=[vm, vm],
-        scratch_shapes=[pltpu.VMEM((rows, got.shape[2]), bf16)],
-        compiler_params=pltpu.CompilerParams(vmem_limit_bytes=16 << 20),
+        grid_spec=pltpu.PrefetchScalarGridSpec(
+            num_scalar_prefetch=1,
+            grid=(4,),
+            in_specs=[
+                pl.BlockSpec(got.shape, lambda i, cols: (0, 0, 0)),
+                pl.BlockSpec(gain.shape, lambda i, cols: (0, 0)),
+                pl.BlockSpec((weight.shape[0], width), lambda i, cols: (0, cols[i])),
+            ],
+            out_specs=[
+                pl.BlockSpec((1, rows, width), lambda i, cols: (jnp.minimum(i, 1), 0, 0)),
+                pl.BlockSpec((1, rows, width), lambda i, cols: (jnp.maximum(i, 2) - 2, 0, 0)),
+            ],
+            scratch_shapes=[pltpu.VMEM((rows, got.shape[2]), bf16)],
+        ),
+        compiler_params=pltpu.CompilerParams(vmem_limit_bytes=24 << 20),
         name="project",
-    )(cols, got, gain, weight)
+    )(cols, got, gain, pltpu.with_memory_space_constraint(weight, pltpu.HBM))
 
 
 def shift(x, axis, size, step):
     return lax.ppermute(x, axis, [(i, (i + step) % size) for i in range(size)])
-
-
-def logsum(a, b):
-    top = jnp.maximum(a, b)
-    return top + jnp.log2(jnp.exp2(a - top) + jnp.exp2(b - top))
-
-
-def reorder(x, rows, mask):
-    slots = x.shape[1] // rows
-    return jnp.concatenate([x[:, (s ^ mask) * rows : ((s ^ mask) + 1) * rows] for s in range(slots)], 1)
 
 
 def swap(x, axis, size, mask):
@@ -243,47 +290,38 @@
     heads = lambda_vecs.shape[1]
     block = ((positions[::RUN].astype(f32) + 0.5) * (1.0 / RUN)).astype(jnp.int32).astype(bf16)
     ids = jnp.broadcast_to(jnp.pad(block, (0, width - block.shape[0]))[None, :], (16, width))
+    slot = jnp.arange(nh * ny, dtype=jnp.int32)
+    place = (lax.axis_index("h") ^ (slot & 1)) * ny + (lax.axis_index("y") ^ (slot >> 1))
 
     q_mine = jnp.concatenate([queries, ids], 0)
     kv_mine = jnp.concatenate([keys, values, ids], 0)
+    up, down = shift(kv_mine, "z", nz, 1), shift(kv_mine, "z", nz, -1)
     q_pair = swap(q_mine, "h", nh, 1)
-    up, down = shift(kv_mine, "z", nz, 1), shift(kv_mine, "z", nz, -1)
     q_near = [swap(q_mine, "y", ny, d) for d in range(1, ny)]
     kv_parts = [kv_mine, up, down]
-    up, down, q_pair = lax.optimization_barrier((up, down, q_pair))
+    up, down, q_pair, q_near = lax.optimization_barrier((up, down, q_pair, q_near))
     up, down = shift(up, "z", nz, 1), shift(down, "z", nz, -1)
     q_far = [swap(q_pair, "y", ny, d) for d in range(1, ny)]
     kv_parts += [up, down]
-    up, down, q_near = lax.optimization_barrier((up, down, q_near))
+    up, down, q_far = lax.optimization_barrier((up, down, q_far))
     up, down = shift(up, "z", nz, 1), shift(down, "z", nz, -1)
     kv_parts += [up, down]
-    up, down, q_far = lax.optimization_barrier((up, down, q_far))
     kv_parts += [shift(up[:rows], "z", nz, 1), shift(down[rows:], "z", nz, -1)]
     q_parts = [q_mine, q_pair]
     for d in range(ny - 1):
         q_parts += [q_near[d], q_far[d]]
 
-    def numbers(parts):
-        spots = [p[p.shape[0] - 16 : p.shape[0] - 15, : rows // RUN] for p in parts]
-        return jnp.concatenate(spots, 0).astype(jnp.int32).reshape(-1)
-
-    qb = numbers(q_parts)
-    kb = numbers(kv_parts[: nz - 1] + kv_parts[nz:])
-
-    o, lse = attend(q_parts, kv_parts, qb, kb, rows, heads)
-
-    whole = lse
-    for axis, size, mask, slot in (("h", nh, 1, 1), ("y", ny, 1, 2), ("y", ny, 3, 6)):
-        whole = logsum(whole, reorder(swap(whole, axis, size, mask), rows, slot))
+    o, lse = attend(q_parts, kv_parts, rows, heads)
+
+    pair = merge(lse, swap(lse, "h", nh, 1), rows)
+    others = [swap(pair, "y", ny, d) for d in range(1, ny)]
 
     lam = (
         jnp.exp(jnp.sum(lambda_vecs[0] * lambda_vecs[1], -1))
         - jnp.exp(jnp.sum(lambda_vecs[2] * lambda_vecs[3], -1))
         + lambda_init
     )
-    slot = jnp.arange(nh * ny, dtype=jnp.int32)
-    place = (lax.axis_index("h") ^ (slot & 1)) * ny + (lax.axis_index("y") ^ (slot >> 1))
-    parts = weigh(place, lam, lse, whole, o, rows, heads)
+    parts = weigh(place, lam, lse, [pair] + others, o, rows, heads)
 
     got = lax.all_to_all(parts, ("h", "y"), 0, 0, tiled=False)
     l, c = lax.axis_index("l"), lax.axis_index("c")

time: 182 us -> 151 us (0.83)
  local copies, waits for them, and re-layouts: 39.1 us -> 2.15 us
  Pallas kernels: 26.7 us -> 33 us
  other arithmetic: 8.75 us -> 3.25 us
  waiting for transfers between devices: 61.9 us -> 66.8 us
    slice x33 -> x0, local copies, waits for them, and re-layouts: 23.6 us -> none  [the longest x30 20.7 us: numbers(): spots = [p[p.shape[0] - 16:p.shape[0] - 15, :rows // RUN] for p in parts]]
    ppermute x8, waiting for transfers between devices: 0.7 us -> 12.7 us  [shift(): return lax.ppermute(x, axis, [(i, (i + step) % size) for i in range(size)])]
    concatenate x5 -> x0, local copies, waits for them, and re-layouts: 6.92 us -> none  [the longest x3 4.33 us: reorder(): jnp.concatenate([x[:, (s ^ mask) * rows:((s ^ mask) + 1) * rows] for s in...]
    ppermute x12 -> x13, waiting for transfers between devices: 44.8 us -> 39.2 us  [swap(): return lax.ppermute(x, axis, [(i, i ^ mask) for i in range(size)])]
    unnamed x44 -> x40, local copies, waits for them, and re-layouts: 5.97 us -> 1.32 us
    pallas_call x1, Pallas kernels: 2.14 us -> 5.76 us  [project(): pl.pallas_call(lambda *r: project_kernel(heads, *r), out_shape=[jax.Shape...]
    add x3 -> x0, other arithmetic: 3.07 us -> none  [logsum(): return top + jnp.log2(jnp.exp2(a - top) + jnp.exp2(b - top))]
    ppermute x12 -> x13, starting transfers between devices: 24.1 us -> 27 us  [swap(): return lax.ppermute(x, axis, [(i, i ^ mask) for i in range(size)])]
  transfers between devices with their start and end apart: 21 -> 22, of which waited for: 14 -> 13; matrix products, arithmetic and copies ran while one was open for 15% -> 1% of each run, Pallas kernels for 0% -> 0%
where the time goes in v4:
time: 151 us; the launch traced here: 149 us
  waiting for transfers between devices  66.8 us (44%)
  starting transfers between devices  43.2 us (29%)
  Pallas kernels  33 us (22%)
  other arithmetic  3.25 us (2%)
  local copies, waits for them, and re-layouts  2.15 us (1%)
    ppermute x13, waiting for transfers between devices, swap(): return lax.ppermute(x, axis, [(i, i ^ mask) for i in range(size)])  39.2 us
    ppermute x13, starting transfers between devices, swap(): return lax.ppermute(x, axis, [(i, i ^ mask) for i in range(size)])  27 us
    pallas_call x1, Pallas kernels, attend(): pl.pallas_call(lambda *r: attend_kernel(rows, *r), out_shape=[jax.ShapeDt...  20.9 us
    all_to_all x1, waiting for transfers between devices, per_device(): got = lax.all_to_all(parts, ('h', 'y'), 0, 0, tiled=False)  14.9 us
    ppermute x8, waiting for transfers between devices, shift(): return lax.ppermute(x, axis, [(i, (i + step) % size) for i in range(size)])  12.7 us
    ppermute x8, starting transfers between devices, shift(): return lax.ppermute(x, axis, [(i, (i + step) % size) for i in range(size)])  11.8 us
    pallas_call x1, Pallas kernels, project(): pl.pallas_call(lambda *r: project_kernel(heads, *r), out_shape=[jax.Shape...  5.76 us
    pallas_call x1, Pallas kernels, weigh(): pl.pallas_call(lambda *r: weigh_kernel(heads, *r), out_shape=jax.ShapeDty...  5.43 us
  transfers between devices with their start and end apart: 22, of which 13 were waited for; matrix products, arithmetic and copies ran while one was open for 1% of the time, Pallas kernels for 0%

profile of v4, /device:TPU:1, one launch (start us, length us, event | category | flops | bytes accessed | tf_op | source)
XLA Modules:
  0.0 148.7 jit_solution(16447990407242522156)
XLA Ops:
  1.8 3.7 %collective-permute-start.2 = (bf16[160,768]{1,0:T(8,128)(2,1)S(1)}, bf16[160,768]{1,0:T(8,128)(2,1)S(1)}, u32[]{:S(2)}, u32[]{:S(2)}) collective-permute-start(bf16[160,768]{1,0:T(8,128)(2,1)S(1)} %pad_maximum_fusion.1.r_0_), channel_id=1, source_target_pairs={{0,16},{16,0},{1,17},{17,1},{2,18},{18,2},{3,19},{19,3},{4,20},{20... | collective-permute-start | bytes 737288 | tf_op jit(solution)/shard_map/ppermute | solution.py:284
  8.2 4.0 %collective-permute-start.1 = (bf16[304,768]{1,0:T(8,128)(2,1)S(1)}, bf16[304,768]{1,0:T(8,128)(2,1)S(1)}, u32[]{:S(2)}, u32[]{:S(2)}) collective-permute-start(bf16[304,768]{1,0:T(8,128)(2,1)S(1)} %pad_maximum_fusion.r_8_), channel_id=1, source_target_pairs={{0,224},{32,0},{64,32},{96,64},{128,96},{160,128},{192,160},{224,1... | collective-permute-start | bytes 1400840 | tf_op jit(solution)/shard_map/ppermute | solution.py:280
  13.6 2.6 %collective-permute-start.4 = (bf16[160,768]{1,0:T(8,128)(2,1)S(1)}, bf16[160,768]{1,0:T(8,128)(2,1)S(1)}, u32[]{:S(2)}, u32[]{:S(2)}) collective-permute-start(bf16[160,768]{1,0:T(8,128)(2,1)S(1)} %pad_maximum_fusion.1.r_0_), channel_id=1, source_target_pairs={{0,8},{4,12},{8,0},{12,4},{1,9},{5,13},{9,1},{13,5},{2,10},{6,14},... | collective-permute-start | bytes 737288 | tf_op jit(solution)/shard_map/ppermute | solution.py:284
  16.2 2.3 %collective-permute-done.3.r_2_ = bf16[160,768]{1,0:T(8,128)(2,1)S(1)} collective-permute-done((bf16[160,768]{1,0:T(8,128)(2,1)S(1)}, bf16[160,768]{1,0:T(8,128)(2,1)S(1)}, u32[]{:S(2)}, u32[]{:S(2)}) %collective-permute-start.3) | collective-permute-done | bytes 245792 | tf_op jit(solution)/shard_map/ppermute | solution.py:284
  18.5 7.8 %collective-permute-done.4.r_4_ = bf16[160,768]{1,0:T(8,128)(2,1)S(1)} collective-permute-done((bf16[160,768]{1,0:T(8,128)(2,1)S(1)}, bf16[160,768]{1,0:T(8,128)(2,1)S(1)}, u32[]{:S(2)}, u32[]{:S(2)}) %collective-permute-start.4) | collective-permute-done | bytes 245792 | tf_op jit(solution)/shard_map/ppermute | solution.py:284
  26.2 2.8 %collective-permute-done.5.r_6_ = bf16[160,768]{1,0:T(8,128)(2,1)S(1)} collective-permute-done((bf16[160,768]{1,0:T(8,128)(2,1)S(1)}, bf16[160,768]{1,0:T(8,128)(2,1)S(1)}, u32[]{:S(2)}, u32[]{:S(2)}) %collective-permute-start.5) | collective-permute-done | bytes 245792 | tf_op jit(solution)/shard_map/ppermute | solution.py:284
  29.2 2.7 %collective-permute-start.7 = (bf16[304,768]{1,0:T(8,128)(2,1)S(1)}, bf16[304,768]{1,0:T(8,128)(2,1)S(1)}, u32[]{:S(2)}, u32[]{:S(2)}) collective-permute-start(bf16[304,768]{1,0:T(8,128)(2,1)S(1)} %collective-permute-done.1.r_10_), channel_id=1, source_target_pairs={{0,224},{32,0},{64,32},{96,64},{128,96},{160,128},{192,160},{224,1... | collective-permute-start | bytes 1400840 | tf_op jit(solution)/shard_map/ppermute | solution.py:280
  32.3 3.4 %collective-permute-start.9 = (bf16[160,768]{1,0:T(8,128)(2,1)S(1)}, bf16[160,768]{1,0:T(8,128)(2,1)S(1)}, u32[]{:S(2)}, u32[]{:S(2)}) collective-permute-start(bf16[160,768]{1,0:T(8,128)(2,1)S(1)} %collective-permute-done.2.r_1_), channel_id=1, source_target_pairs={{0,8},{4,12},{8,0},{12,4},{1,9},{5,13},{9,1},{13,5},{2,10},{6,14},... | collective-permute-start | bytes 737288 | tf_op jit(solution)/shard_map/ppermute | solution.py:284
  35.7 2.7 %collective-permute-done.10.r_7_ = bf16[160,768]{1,0:T(8,128)(2,1)S(1)} collective-permute-done((bf16[160,768]{1,0:T(8,128)(2,1)S(1)}, bf16[160,768]{1,0:T(8,128)(2,1)S(1)}, u32[]{:S(2)}, u32[]{:S(2)}) %collective-permute-start.10) | collective-permute-done | bytes 245792 | tf_op jit(solution)/shard_map/ppermute | solution.py:284
  38.4 5.4 %collective-permute-done.9.r_5_ = bf16[160,768]{1,0:T(8,128)(2,1)S(1)} collective-permute-done((bf16[160,768]{1,0:T(8,128)(2,1)S(1)}, bf16[160,768]{1,0:T(8,128)(2,1)S(1)}, u32[]{:S(2)}, u32[]{:S(2)}) %collective-permute-start.9) | collective-permute-done | bytes 245792 | tf_op jit(solution)/shard_map/ppermute | solution.py:284
  45.4 6.7 %collective-permute-done.12.r_14_ = bf16[304,768]{1,0:T(8,128)(2,1)S(1)} collective-permute-done((bf16[304,768]{1,0:T(8,128)(2,1)S(1)}, bf16[304,768]{1,0:T(8,128)(2,1)S(1)}, u32[]{:S(2)}, u32[]{:S(2)}) %collective-permute-start.12) | collective-permute-done | bytes 466976 | tf_op jit(solution)/shard_map/ppermute | solution.py:280
  54.0 6.1 %collective-permute-done.13.r_15_ = bf16[144,768]{1,0:T(8,128)(2,1)S(1)} collective-permute-done((bf16[144,768]{1,0:T(8,128)(2,1)S(1)}, bf16[144,768]{1,0:T(8,128)(2,1)S(1)}, u32[]{:S(2)}, u32[]{:S(2)}) %collective-permute-start.13) | collective-permute-done | bytes 221216 | tf_op jit(solution)/shard_map/ppermute | solution.py:280
  61.5 20.9 %attend.1 = (bf16[16,72,1536]{2,1,0:T(8,128)(2,1)S(1)}, f32[8,1152]{1,0:T(8,128)}) custom-call(bf16[160,768]{1,0:T(8,128)(2,1)} %copy-done.3, bf16[160,768]{1,0:T(8,128)(2,1)} %copy-done.9, bf16[160,768]{1,0:T(8,128)(2,1)} %copy-done.10, bf16[160,768]{1,0:T(8,128)(2,1)} %copy-done.14, bf16[160,768]{1,0:T(8,128)(2,1)} %copy-done.11, ...), custom_call_target="tpu_custom_call" | custom-call | tf_op jit(solution)/shard_map/attend/pallas_call | solution.py:133
  82.3 2.1 %collective-permute-start.15 = (f32[8,1152]{1,0:T(8,128)}, f32[8,1152]{1,0:T(8,128)}, u32[]{:S(2)}, u32[]{:S(2)}) collective-permute-start(f32[8,1152]{1,0:T(8,128)} %get-tuple-element.31.r_0_.r_2_), channel_id=1, source_target_pairs={{0,16},{16,0},{1,17},{17,1},{2,18},{18,2},{3,19},{19,3},{4,20},{20... | collective-permute-start | bytes 110600 | tf_op jit(solution)/shard_map/ppermute | solution.py:284
  84.4 2.7 %collective-permute-done.15.r_1_ = f32[8,1152]{1,0:T(8,128)} collective-permute-done((f32[8,1152]{1,0:T(8,128)}, f32[8,1152]{1,0:T(8,128)}, u32[]{:S(2)}, u32[]{:S(2)}) %collective-permute-start.15) | collective-permute-done | bytes 36896 | tf_op jit(solution)/shard_map/ppermute | solution.py:284
  88.7 3.6 %collective-permute-start.17 = (f32[8,1152]{1,0:T(8,128)S(1)}, f32[8,1152]{1,0:T(8,128)S(1)}, u32[]{:S(2)}, u32[]{:S(2)}) collective-permute-start(f32[8,1152]{1,0:T(8,128)S(1)} %merge.1.r_3_), channel_id=1, source_target_pairs={{0,8},{4,12},{8,0},{12,4},{1,9},{5,13},{9,1},{13,5},{2,10},{6,14},... | collective-permute-start | bytes 110600 | tf_op jit(solution)/shard_map/ppermute | solution.py:284
  92.4 2.0 %collective-permute-done.17.r_5_ = f32[8,1152]{1,0:T(8,128)S(1)} collective-permute-done((f32[8,1152]{1,0:T(8,128)S(1)}, f32[8,1152]{1,0:T(8,128)S(1)}, u32[]{:S(2)}, u32[]{:S(2)}) %collective-permute-start.17) | collective-permute-done | bytes 36896 | tf_op jit(solution)/shard_map/ppermute | solution.py:284
  94.4 2.0 %collective-permute-done.18.r_6_ = f32[8,1152]{1,0:T(8,128)S(1)} collective-permute-done((f32[8,1152]{1,0:T(8,128)S(1)}, f32[8,1152]{1,0:T(8,128)S(1)}, u32[]{:S(2)}, u32[]{:S(2)}) %collective-permute-start.18) | collective-permute-done | bytes 36896 | tf_op jit(solution)/shard_map/ppermute | solution.py:284
  96.4 5.4 %weigh.1 = bf16[8,144,768]{2,1,0:T(8,128)(2,1)} custom-call(s32[8]{0:T(128)S(1)} %xor_add_fusion.r_0_, f32[3]{0:T(128)S(1)} %subtract_add_fusion.r_1_, f32[8,1152]{1,0:T(8,128)} %get-tuple-element.31.r_0_.r_2_, f32[8,1152]{1,0:T(8,128)S(1)} %merge.1.r_3_, f32[8,1152]{1,0:T(8,128)S(1)} %collective-permute-done.16.r_4_, ...), custom_call_target="tpu_custom_call" | custom-call | tf_op jit(solution)/shard_map/weigh/pallas_call | solution.py:210
  101.9 4.4 %all-to-all-start = ((bf16[8,144,768]{2,1,0:T(8,128)(2,1)}), bf16[8,144,768]{2,1,0:T(8,128)(2,1)S(1)}, u32[]{:S(2)}, u32[]{:S(2)}) async-start(bf16[8,144,768]{2,1,0:T(8,128)(2,1)} %weigh.1), calls=%async_computation | async-start | bytes 3538944 | tf_op jit(solution)/shard_map/all_to_all | solution.py:326
  106.4 14.9 %all-to-all-done.r_1_ = bf16[8,144,768]{2,1,0:T(8,128)(2,1)S(1)} async-done(((bf16[8,144,768]{2,1,0:T(8,128)(2,1)}), bf16[8,144,768]{2,1,0:T(8,128)(2,1)S(1)}, u32[]{:S(2)}, u32[]{:S(2)}) %all-to-all-start) | async-done | bytes 1769504 | tf_op jit(solution)/shard_map/all_to_all | solution.py:326
  121.2 5.8 %project.1 = (bf16[2,144,1280]{2,1,0:T(8,128)(2,1)S(1)}, f32[2,144,1280]{2,1,0:T(8,128)S(1)}) custom-call(s32[4]{0:T(128)S(1)} %pad_add_fusion.r_0_, bf16[8,144,768]{2,1,0:T(8,128)(2,1)S(1)} %all-to-all-done.r_1_, f32[1,768]{1,0:T(1,128)S(1)} %reshape.11.r_2_, bf16[768,5120]{1,0:T(8,128)(2,1)} %r_3_.1), custom_call_target="tpu_custom_call" | custom-call | tf_op jit(solution)/shard_map/project/pallas_call | solution.py:254
  127.0 9.0 %collective-permute-start.19 = (bf16[2,144,1280]{2,1,0:T(8,128)(2,1)S(1)}, bf16[2,144,1280]{2,1,0:T(8,128)(2,1)S(1)}, u32[]{:S(2)}, u32[]{:S(2)}) collective-permute-start(bf16[2,144,1280]{2,1,0:T(8,128)(2,1)S(1)} %get-tuple-element.34), channel_id=1, source_target_pairs={{0,1},{1,0},{2,3},{3,2},{4,5},{5,4},{6,7},{7,6},{8,9},{9,8},{10,11... | collective-permute-start | bytes 2211848 | tf_op jit(solution)/shard_map/ppermute | solution.py:284
  138.0 9.8 %collective-permute-done.20 = bf16[144,1280]{1,0:T(8,128)(2,1)S(1)} collective-permute-done((bf16[144,1280]{1,0:T(8,128)(2,1)S(1)}, bf16[144,1280]{1,0:T(8,128)(2,1)S(1)}, u32[]{:S(2)}, u32[]{:S(2)}) %collective-permute-start.20) | collective-permute-done | bytes 368672 | tf_op jit(solution)/shard_map/ppermute | solution.py:284
  (79 shorter events, 15.9 us)
Async XLA Ops:
  0.0 53.9 %copy-start.18 = (f32[4,3,128]{2,0,1:T(4,128)S(1)}, f32[4,3,128]{2,0,1:T(4,128)}, u32[]{:S(2)}) copy-start(f32[4,3,128]{2,0,1:T(4,128)} %param.12) | copy-start | bytes 18436
  1.8 58.3 %copy-start.3 = (bf16[160,768]{1,0:T(8,128)(2,1)}, bf16[160,768]{1,0:T(8,128)(2,1)S(1)}, u32[]{:S(2)}) copy-start(bf16[160,768]{1,0:T(8,128)(2,1)S(1)} %pad_maximum_fusion.1.r_0_) | copy-start | bytes 737284
  1.8 14.4 %collective-permute-start.2 = (bf16[160,768]{1,0:T(8,128)(2,1)S(1)}, bf16[160,768]{1,0:T(8,128)(2,1)S(1)}, u32[]{:S(2)}, u32[]{:S(2)}) collective-permute-start(bf16[160,768]{1,0:T(8,128)(2,1)S(1)} %pad_maximum_fusion.1.r_0_), channel_id=1, source_target_pairs={{0,16},{16,0},{1,17},{17,1},{2,18},{18,2},{3,19},{19,3},{4,20},{20... | collective-permute-start | bytes 737288 | tf_op jit(solution)/shard_map/ppermute | solution.py:284
  6.5 22.5 %collective-permute-start = (bf16[304,768]{1,0:T(8,128)(2,1)S(1)}, bf16[304,768]{1,0:T(8,128)(2,1)S(1)}, u32[]{:S(2)}, u32[]{:S(2)}) collective-permute-start(bf16[304,768]{1,0:T(8,128)(2,1)S(1)} %pad_maximum_fusion.r_8_), channel_id=1, source_target_pairs={{0,32},{32,64},{64,96},{96,128},{128,160},{160,192},{192,224},{224... | collective-permute-start | bytes 1400840 | tf_op jit(solution)/shard_map/ppermute | solution.py:280
  8.2 20.8 %collective-permute-start.1 = (bf16[304,768]{1,0:T(8,128)(2,1)S(1)}, bf16[304,768]{1,0:T(8,128)(2,1)S(1)}, u32[]{:S(2)}, u32[]{:S(2)}) collective-permute-start(bf16[304,768]{1,0:T(8,128)(2,1)S(1)} %pad_maximum_fusion.r_8_), channel_id=1, source_target_pairs={{0,224},{32,0},{64,32},{96,64},{128,96},{160,128},{192,160},{224,1... | collective-permute-start | bytes 1400840 | tf_op jit(solution)/shard_map/ppermute | solution.py:280
  12.3 6.2 %collective-permute-start.3 = (bf16[160,768]{1,0:T(8,128)(2,1)S(1)}, bf16[160,768]{1,0:T(8,128)(2,1)S(1)}, u32[]{:S(2)}, u32[]{:S(2)}) collective-permute-start(bf16[160,768]{1,0:T(8,128)(2,1)S(1)} %pad_maximum_fusion.1.r_0_), channel_id=1, source_target_pairs={{0,4},{4,0},{8,12},{12,8},{1,5},{5,1},{9,13},{13,9},{2,6},{6,2},{1... | collective-permute-start | bytes 737288 | tf_op jit(solution)/shard_map/ppermute | solution.py:284
  13.6 12.7 %collective-permute-start.4 = (bf16[160,768]{1,0:T(8,128)(2,1)S(1)}, bf16[160,768]{1,0:T(8,128)(2,1)S(1)}, u32[]{:S(2)}, u32[]{:S(2)}) collective-permute-start(bf16[160,768]{1,0:T(8,128)(2,1)S(1)} %pad_maximum_fusion.1.r_0_), channel_id=1, source_target_pairs={{0,8},{4,12},{8,0},{12,4},{1,9},{5,13},{9,1},{13,5},{2,10},{6,14},... | collective-permute-start | bytes 737288 | tf_op jit(solution)/shard_map/ppermute | solution.py:284
  16.2 12.8 %collective-permute-start.5 = (bf16[160,768]{1,0:T(8,128)(2,1)S(1)}, bf16[160,768]{1,0:T(8,128)(2,1)S(1)}, u32[]{:S(2)}, u32[]{:S(2)}) collective-permute-start(bf16[160,768]{1,0:T(8,128)(2,1)S(1)} %pad_maximum_fusion.1.r_0_), channel_id=1, source_target_pairs={{0,12},{4,8},{8,4},{12,0},{1,13},{5,9},{9,5},{13,1},{2,14},{6,10},... | collective-permute-start | bytes 737288 | tf_op jit(solution)/shard_map/ppermute | solution.py:284
  29.1 14.7 %collective-permute-start.6 = (bf16[304,768]{1,0:T(8,128)(2,1)S(1)}, bf16[304,768]{1,0:T(8,128)(2,1)S(1)}, u32[]{:S(2)}, u32[]{:S(2)}) collective-permute-start(bf16[304,768]{1,0:T(8,128)(2,1)S(1)} %collective-permute-done.r_9_), channel_id=1, source_target_pairs={{0,32},{32,64},{64,96},{96,128},{128,160},{160,192},{192,224},{224... | collective-permute-start | bytes 1400840 | tf_op jit(solution)/shard_map/ppermute | solution.py:280
  29.2 14.6 %collective-permute-start.7 = (bf16[304,768]{1,0:T(8,128)(2,1)S(1)}, bf16[304,768]{1,0:T(8,128)(2,1)S(1)}, u32[]{:S(2)}, u32[]{:S(2)}) collective-permute-start(bf16[304,768]{1,0:T(8,128)(2,1)S(1)} %collective-permute-done.1.r_10_), channel_id=1, source_target_pairs={{0,224},{32,0},{64,32},{96,64},{128,96},{160,128},{192,160},{224,1... | collective-permute-start | bytes 1400840 | tf_op jit(solution)/shard_map/ppermute | solution.py:280
  31.8 6.6 %collective-permute-start.10 = (bf16[160,768]{1,0:T(8,128)(2,1)S(1)}, bf16[160,768]{1,0:T(8,128)(2,1)S(1)}, u32[]{:S(2)}, u32[]{:S(2)}) collective-permute-start(bf16[160,768]{1,0:T(8,128)(2,1)S(1)} %collective-permute-done.2.r_1_), channel_id=1, source_target_pairs={{0,12},{4,8},{8,4},{12,0},{1,13},{5,9},{9,5},{13,1},{2,14},{6,10},... | collective-permute-start | bytes 737288 | tf_op jit(solution)/shard_map/ppermute | solution.py:284
  32.3 6.1 %collective-permute-start.8 = (bf16[160,768]{1,0:T(8,128)(2,1)S(1)}, bf16[160,768]{1,0:T(8,128)(2,1)S(1)}, u32[]{:S(2)}, u32[]{:S(2)}) collective-permute-start(bf16[160,768]{1,0:T(8,128)(2,1)S(1)} %collective-permute-done.2.r_1_), channel_id=1, source_target_pairs={{0,4},{4,0},{8,12},{12,8},{1,5},{5,1},{9,13},{13,9},{2,6},{6,2},{1... | collective-permute-start | bytes 737288 | tf_op jit(solution)/shard_map/ppermute | solution.py:284
  32.3 11.5 %collective-permute-start.9 = (bf16[160,768]{1,0:T(8,128)(2,1)S(1)}, bf16[160,768]{1,0:T(8,128)(2,1)S(1)}, u32[]{:S(2)}, u32[]{:S(2)}) collective-permute-start(bf16[160,768]{1,0:T(8,128)(2,1)S(1)} %collective-permute-done.2.r_1_), channel_id=1, source_target_pairs={{0,8},{4,12},{8,0},{12,4},{1,9},{5,13},{9,1},{13,5},{2,10},{6,14},... | collective-permute-start | bytes 737288 | tf_op jit(solution)/shard_map/ppermute | solution.py:284
  43.8 8.2 %collective-permute-start.12 = (bf16[304,768]{1,0:T(8,128)(2,1)S(1)}, bf16[304,768]{1,0:T(8,128)(2,1)S(1)}, u32[]{:S(2)}, u32[]{:S(2)}) collective-permute-start(bf16[304,768]{1,0:T(8,128)(2,1)S(1)} %collective-permute-done.7.r_12_), channel_id=1, source_target_pairs={{0,224},{32,0},{64,32},{96,64},{128,96},{160,128},{192,160},{224,1... | collective-permute-start | bytes 1400840 | tf_op jit(solution)/shard_map/ppermute | solution.py:280
  44.0 9.4 %collective-permute-start.11 = (bf16[304,768]{1,0:T(8,128)(2,1)S(1)}, bf16[304,768]{1,0:T(8,128)(2,1)S(1)}, u32[]{:S(2)}, u32[]{:S(2)}) collective-permute-start(bf16[304,768]{1,0:T(8,128)(2,1)S(1)} %collective-permute-done.6.r_11_), channel_id=1, source_target_pairs={{0,32},{32,64},{64,96},{96,128},{128,160},{160,192},{192,224},{224... | collective-permute-start | bytes 1400840 | tf_op jit(solution)/shard_map/ppermute | solution.py:280
  52.0 8.0 %collective-permute-start.14 = (bf16[160,768]{1,0:T(8,128)(2,1)S(1)}, bf16[160,768]{1,0:T(8,128)(2,1)S(1)}, u32[]{:S(2)}, u32[]{:S(2)}) collective-permute-start(bf16[160,768]{1,0:T(8,128)(2,1)S(1)} %slice.45), channel_id=1, source_target_pairs={{0,224},{32,0},{64,32},{96,64},{128,96},{160,128},{192,160},{224,1... | collective-permute-start | bytes 737288 | tf_op jit(solution)/shard_map/ppermute | solution.py:280
  53.5 6.5 %collective-permute-start.13 = (bf16[144,768]{1,0:T(8,128)(2,1)S(1)}, bf16[144,768]{1,0:T(8,128)(2,1)S(1)}, u32[]{:S(2)}, u32[]{:S(2)}) collective-permute-start(bf16[144,768]{1,0:T(8,128)(2,1)S(1)} %slice.44), channel_id=1, source_target_pairs={{0,32},{32,64},{64,96},{96,128},{128,160},{160,192},{192,224},{224... | collective-permute-start | bytes 663560 | tf_op jit(solution)/shard_map/ppermute | solution.py:280
  82.3 4.7 %collective-permute-start.15 = (f32[8,1152]{1,0:T(8,128)}, f32[8,1152]{1,0:T(8,128)}, u32[]{:S(2)}, u32[]{:S(2)}) collective-permute-start(f32[8,1152]{1,0:T(8,128)} %get-tuple-element.31.r_0_.r_2_), channel_id=1, source_target_pairs={{0,16},{16,0},{1,17},{17,1},{2,18},{18,2},{3,19},{19,3},{4,20},{20... | collective-permute-start | bytes 110600 | tf_op jit(solution)/shard_map/ppermute | solution.py:284
  87.9 4.5 %collective-permute-start.16 = (f32[8,1152]{1,0:T(8,128)S(1)}, f32[8,1152]{1,0:T(8,128)S(1)}, u32[]{:S(2)}, u32[]{:S(2)}) collective-permute-start(f32[8,1152]{1,0:T(8,128)S(1)} %merge.1.r_3_), channel_id=1, source_target_pairs={{0,4},{4,0},{8,12},{12,8},{1,5},{5,1},{9,13},{13,9},{2,6},{6,2},{1... | collective-permute-start | bytes 110600 | tf_op jit(solution)/shard_map/ppermute | solution.py:284
  88.7 5.7 %collective-permute-start.17 = (f32[8,1152]{1,0:T(8,128)S(1)}, f32[8,1152]{1,0:T(8,128)S(1)}, u32[]{:S(2)}, u32[]{:S(2)}) collective-permute-start(f32[8,1152]{1,0:T(8,128)S(1)} %merge.1.r_3_), channel_id=1, source_target_pairs={{0,8},{4,12},{8,0},{12,4},{1,9},{5,13},{9,1},{13,5},{2,10},{6,14},... | collective-permute-start | bytes 110600 | tf_op jit(solution)/shard_map/ppermute | solution.py:284
  92.4 4.0 %collective-permute-start.18 = (f32[8,1152]{1,0:T(8,128)S(1)}, f32[8,1152]{1,0:T(8,128)S(1)}, u32[]{:S(2)}, u32[]{:S(2)}) collective-permute-start(f32[8,1152]{1,0:T(8,128)S(1)} %merge.1.r_3_), channel_id=1, source_target_pairs={{0,12},{4,8},{8,4},{12,0},{1,13},{5,9},{9,5},{13,1},{2,14},{6,10},... | collective-permute-start | bytes 110600 | tf_op jit(solution)/shard_map/ppermute | solution.py:284
  101.9 19.4 %all-to-all-start = ((bf16[8,144,768]{2,1,0:T(8,128)(2,1)}), bf16[8,144,768]{2,1,0:T(8,128)(2,1)S(1)}, u32[]{:S(2)}, u32[]{:S(2)}) async-start(bf16[8,144,768]{2,1,0:T(8,128)(2,1)} %weigh.1), calls=%async_computation | async-start | bytes 3538944 | tf_op jit(solution)/shard_map/all_to_all | solution.py:326
  127.0 10.8 %collective-permute-start.19 = (bf16[2,144,1280]{2,1,0:T(8,128)(2,1)S(1)}, bf16[2,144,1280]{2,1,0:T(8,128)(2,1)S(1)}, u32[]{:S(2)}, u32[]{:S(2)}) collective-permute-start(bf16[2,144,1280]{2,1,0:T(8,128)(2,1)S(1)} %get-tuple-element.34), channel_id=1, source_target_pairs={{0,1},{1,0},{2,3},{3,2},{4,5},{5,4},{6,7},{7,6},{8,9},{9,8},{10,11... | collective-permute-start | bytes 2211848 | tf_op jit(solution)/shard_map/ppermute | solution.py:284
  137.9 9.9 %collective-permute-start.20 = (bf16[144,1280]{1,0:T(8,128)(2,1)S(1)}, bf16[144,1280]{1,0:T(8,128)(2,1)S(1)}, u32[]{:S(2)}, u32[]{:S(2)}) collective-permute-start(bf16[144,1280]{1,0:T(8,128)(2,1)S(1)} %fusion.2), channel_id=1, source_target_pairs={{0,2},{2,0},{1,3},{3,1},{4,6},{6,4},{5,7},{7,5},{8,10},{10,8},{9,1... | collective-permute-start | bytes 1105928 | tf_op jit(solution)/shard_map/ppermute | solution.py:284
  (18 other events, 420.9 us)

commit v5 on v4

--- a/solution.py
+++ b/solution.py
@@ -20,13 +20,18 @@
 bf16 = jnp.bfloat16
 
 
-def attend_kernel(rows, *refs):
-    slots = (len(refs) - 11) // 2
-    q_refs, kv_refs, (o_ref, lse_ref) = refs[:slots], refs[slots:-10], refs[-10:-8]
-    q3, k3, v3, q_s, k_s, v_s, lse_s, order = refs[-8:]
+def attend_kernel(rows, spans, slots, spots, prev, *refs):
+    q_refs, refs = refs[:slots], refs[slots:]
+    count = len(refs) - 10 - 2 * prev
+    kv_refs, refs = refs[:count], refs[count:]
+    if prev:
+        prev_o, prev_lse = refs[:2]
+        refs = refs[2:]
+    o_ref, lse_ref, q3, k3, v3, q_s, k_s, v_s, lse_s, order = refs
     head = pl.program_id(0)
-    blocks = q3.shape[0]
     per = rows // RUN
+    blocks = slots * per
+    keys = len(spots) * per
     tile = TILE * RUN
     tiles = blocks // TILE
     scale = math.log2(math.e) / math.sqrt(HD)
@@ -41,41 +46,44 @@
             tail = part[part.shape[0] - 16 :, :HD].astype(f32)
             return [jnp.sum(jnp.where(first & (lanes == d), tail, 0.0)).astype(jnp.int32) for d in range(per)]
 
-        kb = [v for p in [*kv_refs[: slots - 1], kv_refs[slots]] for v in numbers(p)]
+        kb = [v for k, kr, v, vr in spots for v in numbers(kv_refs[v])]
         qb = [v for p in q_refs for v in numbers(p)]
-        for i in range(blocks):
-            rk = jnp.int32(0)
-            rq = jnp.int32(0)
-            for j in range(blocks):
-                rk = rk + (kb[j] < kb[i]).astype(jnp.int32)
-                rq = rq + (qb[j] < qb[i]).astype(jnp.int32)
-            order[0, i] = rk
-            order[1, rk] = kb[i]
-            order[2, i] = rq
-            order[3, rq] = i
-            order[4, rq] = qb[i]
+        for numbered, row in ((kb, 0), (qb, 2)):
+            for i in range(len(numbered)):
+                rank = jnp.int32(0)
+                for j in range(len(numbered)):
+                    rank = rank + (numbered[j] < numbered[i]).astype(jnp.int32)
+                order[row, i] = rank
+                if row == 0:
+                    order[1, rank] = numbered[i]
+                else:
+                    order[3, rank] = i
+                    order[4, rank] = numbered[i]
         for t in range(tiles):
             last = order[4, t * TILE + TILE - 1]
             need = jnp.int32(0)
-            for j in range(blocks):
-                need = need + (order[1, j] <= last).astype(jnp.int32)
-            order[5, t] = lax.div(need + (TILE - 1), TILE)
-
+            for j in range(keys):
+                need = need + (kb[j] <= last).astype(jnp.int32)
+            order[5, t] = need
+
+    for i in range(keys):
+        k, kr, v, vr = spots[i // per]
+        d = i % per * RUN
+        r = order[0, i]
+        k3[r] = kv_refs[k][kr + d : kr + d + RUN, :]
+        v3[r] = kv_refs[v][vr + d : vr + d + RUN, :]
     for i in range(blocks):
-        z, d = i // per, i % per
-        r = order[0, i]
-        v_off = rows if z < slots - 1 else 0
-        k3[r] = kv_refs[z][d * RUN : (d + 1) * RUN, :]
-        v3[r] = kv_refs[min(z, slots - 1) + (z == slots - 1)][v_off + d * RUN : v_off + (d + 1) * RUN, :]
-        q3[order[2, i]] = q_refs[z][d * RUN : (d + 1) * RUN, :]
+        d = i % per * RUN
+        q3[order[2, i]] = q_refs[i // per][d : d + RUN, :]
+    for i in range(keys):
+        k_s[i * RUN : (i + 1) * RUN, :] = k3[i]
+        v_s[i * RUN : (i + 1) * RUN, :] = v3[i]
     for i in range(blocks):
         q_s[i * RUN : (i + 1) * RUN, :] = q3[i]
-        k_s[i * RUN : (i + 1) * RUN, :] = k3[i]
-        v_s[i * RUN : (i + 1) * RUN, :] = v3[i]
-
-    col = lax.broadcasted_iota(jnp.int32, (1, blocks * RUN), 1)
+
+    col = lax.broadcasted_iota(jnp.int32, (1, keys * RUN), 1)
     kpos = lax.rem(col, RUN)
-    for i in range(blocks):
+    for i in range(keys):
         kpos = kpos + jnp.where(lax.div(col, RUN) == i, order[1, i] * RUN, 0)
     row = lax.broadcasted_iota(jnp.int32, (tile, 1), 0)
     lane = lax.broadcasted_iota(jnp.int32, (RUN, HD), 1)
@@ -90,26 +98,40 @@
         def put(a, num, lse):
             for i in range(TILE):
                 g = order[3, t * TILE + i]
-                o_ref[g, :, a * 2 * HD : (a + 1) * 2 * HD] = num[i * RUN : (i + 1) * RUN].astype(bf16)
-                lse_s[g] = jnp.where(lane == head * 2 + a, lse[i * RUN : (i + 1) * RUN], lse_s[g])
-
-        for n in range(1, tiles + 1):
-
-            @pl.when(need == n)
-            def _(n=n):
-                allowed = kpos[:, : n * tile] <= qpos
-                for a in range(2):
-                    s = lax.dot_general(
+                o = num[i * RUN : (i + 1) * RUN]
+                e = lse[i * RUN : (i + 1) * RUN]
+                if prev:
+                    pick = lane == head * 2 + a
+                    before = jnp.max(jnp.where(pick, prev_lse[g], -3e38), -1, keepdims=True)
+                    both = logsum([before, e])
+                    o = o * jnp.exp2(e - both) + prev_o[g, :, a * 2 * HD : (a + 1) * 2 * HD].astype(f32) * jnp.exp2(before - both)
+                    e = both
+                o_ref[g, :, a * 2 * HD : (a + 1) * 2 * HD] = o.astype(bf16)
+                lse_s[g] = jnp.where(lane == head * 2 + a, e, lse_s[g])
+
+        for low, high in zip((0,) + spans[:-1], spans):
+
+            @pl.when((need > low) & (need <= high))
+            def _(span=high * RUN):
+                allowed = kpos[:, :span] <= qpos
+                ss = [
+                    lax.dot_general(
                         q_s[pl.ds(start, tile), a * HD : (a + 1) * HD],
-                        k_s[: n * tile, a * HD : (a + 1) * HD],
+                        k_s[:span, a * HD : (a + 1) * HD],
                         (((1,), (1,)), ((), ())),
                         preferred_element_type=f32,
                     )
-                    s = jnp.where(allowed, s, NEG)
+                    for a in range(2)
+                ]
+                ps = []
+                for a in range(2):
+                    s = jnp.where(allowed, ss[a], NEG)
                     m = jnp.maximum(jnp.max(s, -1, keepdims=True), FLOOR) * scale
                     p = jnp.exp2(s * scale - m)
-                    total = jnp.sum(p, -1, keepdims=True)
-                    num = jnp.dot(p.astype(bf16), v_s[: n * tile, :], preferred_element_type=f32)
+                    ps.append((p.astype(bf16), m, jnp.sum(p, -1, keepdims=True)))
+                for a in range(2):
+                    p, m, total = ps[a]
+                    num = jnp.dot(p, v_s[:span, :], preferred_element_type=f32)
                     some = total > 0.0
                     safe = jnp.where(some, total, 1.0)
                     put(a, num * (1.0 / safe), jnp.where(some, m + jnp.log2(safe), NEG))
@@ -125,32 +147,49 @@
 
     @pl.when(head == pl.num_programs(0) - 1)
     def _():
-        lse_ref[...] = jnp.transpose(lse_s[...].reshape(blocks * RUN, HD))[: lse_ref.shape[0], :]
-
-
-def attend(q_parts, kv_parts, rows, heads):
-    blocks = len(q_parts) * rows // RUN
+        if prev:
+            lse_ref[...] = jnp.transpose(lse_s[...].reshape(blocks * RUN, HD))[: lse_ref.shape[0], :]
+        else:
+            lse_ref[...] = lse_s[...]
+
+
+def attend(q_parts, kv_parts, spots, spans, rows, heads, before=()):
+    slots = len(q_parts)
+    blocks = slots * rows // RUN
+    keys = len(spots) * rows // RUN
+    wide = jax.ShapeDtypeStruct((blocks, RUN, HD), f32)
+    flat = jax.ShapeDtypeStruct((8, blocks * RUN), f32)
+    lse = flat if before else wide
+    out_block = pl.BlockSpec((blocks, RUN, 4 * HD), lambda h: (0, 0, h))
+    ins = [pltpu.with_memory_space_constraint(x, pltpu.HBM) for x in [*q_parts, *kv_parts, *before]]
     return pl.pallas_call(
-        lambda *r: attend_kernel(rows, *r),
-        out_shape=[
-            jax.ShapeDtypeStruct((blocks, RUN, heads * 4 * HD), bf16),
-            jax.ShapeDtypeStruct((8, blocks * RUN), f32),
-        ],
+        lambda *r: attend_kernel(rows, spans, slots, spots, bool(before), *r),
+        out_shape=[jax.ShapeDtypeStruct((blocks, RUN, heads * 4 * HD), bf16), lse],
         grid_spec=pltpu.PrefetchScalarGridSpec(
             num_scalar_prefetch=0,
             grid=(heads,),
-            in_specs=[pl.BlockSpec((x.shape[0], 2 * HD), lambda h, *_: (0, h)) for x in q_parts + kv_parts],
-            out_specs=[
-                pl.BlockSpec((blocks, RUN, 4 * HD), lambda h, *_: (0, 0, h)),
-                pl.BlockSpec((8, blocks * RUN), lambda h, *_: (0, 0)),
+            in_specs=[pl.BlockSpec((x.shape[0], 2 * HD), lambda h: (0, h)) for x in [*q_parts, *kv_parts]]
+            + ([out_block, pl.BlockSpec(wide.shape, lambda h: (0, 0, 0))] if before else []),
+            out_specs=[out_block, pl.BlockSpec(lse.shape, lambda h: (0,) * len(lse.shape))],
+            scratch_shapes=[
+                pltpu.VMEM((blocks, RUN, 2 * HD), bf16),
+                pltpu.VMEM((keys, RUN, 2 * HD), bf16),
+                pltpu.VMEM((keys, RUN, 2 * HD), bf16),
+                pltpu.VMEM((blocks * RUN, 2 * HD), bf16),
+                pltpu.VMEM((keys * RUN, 2 * HD), bf16),
+                pltpu.VMEM((keys * RUN, 2 * HD), bf16),
+                pltpu.VMEM((blocks, RUN, HD), f32),
+                pltpu.SMEM((6, 128), jnp.int32),
             ],
-            scratch_shapes=[pltpu.VMEM((blocks, RUN, 2 * HD), bf16)] * 3
-            + [pltpu.VMEM((blocks * RUN, 2 * HD), bf16)] * 3
-            + [pltpu.VMEM((blocks, RUN, HD), f32), pltpu.SMEM((6, 128), jnp.int32)],
         ),
-        compiler_params=pltpu.CompilerParams(vmem_limit_bytes=32 << 20),
+        compiler_params=pltpu.CompilerParams(vmem_limit_bytes=36 << 20),
+        cost_estimate=pl.CostEstimate(
+            flops=heads * 2 * blocks * keys * RUN * RUN * 6 * HD * 8,
+            bytes_accessed=(slots * 2 + len(spots) * 2) * rows * heads * 4 * HD,
+            transcendentals=heads * 2 * blocks * keys * RUN * RUN,
+        ),
         name="attend",
-    )(*[pltpu.with_memory_space_constraint(x, pltpu.HBM) for x in q_parts + kv_parts])
+    )(*ins)
 
 
 def logsum(parts):
@@ -184,43 +223,48 @@
     )(a, b)
 
 
-def weigh_kernel(heads, place, lam, lse_ref, *refs):
+def weigh_kernel(heads, where, lam, lse_ref, *refs):
     all_refs, o_ref, out_ref, w_s = refs[:-3], refs[-3], refs[-2], refs[-1]
-    s = pl.program_id(0)
-    rows = out_ref.shape[1]
-
-    @pl.when(s == 0)
+    j = pl.program_id(0)
+    rows = out_ref.shape[2]
+
+    @pl.when(j == 0)
     def _():
         whole = logsum([reorder(r[...], rows, 2 * i) for i, r in enumerate(all_refs)])
         w = jnp.exp2(lse_ref[...] - whole)
         w = jnp.concatenate([w, jnp.zeros((HD - w.shape[0], w.shape[1]), f32)], 0)
         w_s[...] = jnp.transpose(w)
 
-    w = w_s[pl.ds(pl.multiple_of(s * rows, rows), rows), :]
-    for h in range(heads):
-        w1 = w[:, 2 * h : 2 * h + 1]
-        w2 = w[:, 2 * h + 1 : 2 * h + 2] * lam[h]
-        o1 = o_ref[:, :, h * 4 * HD : h * 4 * HD + 2 * HD].reshape(rows, 2 * HD).astype(f32)
-        o2 = o_ref[:, :, h * 4 * HD + 2 * HD : (h + 1) * 4 * HD].reshape(rows, 2 * HD).astype(f32)
-        out_ref[0, :, h * 2 * HD : (h + 1) * 2 * HD] = (w1 * o1 - w2 * o2).astype(bf16)
-
-
-def weigh(place, lam, lse, lses, o, rows, heads):
-    slots = lse.shape[1] // rows
+    for d in range(2):
+        w = w_s[pl.ds(pl.multiple_of((2 * j + d) * rows, rows), rows), :]
+        o = o_ref[d * (rows // RUN) : (d + 1) * (rows // RUN)]
+        place = where[0] ^ d
+        for h in range(heads):
+            w1 = w[:, 2 * h : 2 * h + 1]
+            w2 = w[:, 2 * h + 1 : 2 * h + 2] * lam[h]
+            o1 = o[:, :, h * 4 * HD : h * 4 * HD + 2 * HD].reshape(rows, 2 * HD).astype(f32)
+            o2 = o[:, :, h * 4 * HD + 2 * HD : (h + 1) * 4 * HD].reshape(rows, 2 * HD).astype(f32)
+            out_ref[place, 0, :, h * 2 * HD : (h + 1) * 2 * HD] = (w1 * o1 - w2 * o2).astype(bf16)
+
+
+def weigh(where, lam, lse, lses, o, rows, heads):
+    pairs = lse.shape[1] // rows // 2
     return pl.pallas_call(
         lambda *r: weigh_kernel(heads, *r),
-        out_shape=jax.ShapeDtypeStruct((slots, rows, heads * 2 * HD), bf16),
+        out_shape=jax.ShapeDtypeStruct((2, pairs, rows, heads * 2 * HD), bf16),
         grid_spec=pltpu.PrefetchScalarGridSpec(
             num_scalar_prefetch=2,
-            grid=(slots,),
-            in_specs=[pl.BlockSpec(lse.shape, lambda s, *_: (0, 0))] * (1 + len(lses))
-            + [pl.BlockSpec((rows // RUN, RUN, heads * 4 * HD), lambda s, *_: (s, 0, 0))],
-            out_specs=pl.BlockSpec((1, rows, heads * 2 * HD), lambda s, place, lam: (place[s], 0, 0)),
-            scratch_shapes=[pltpu.VMEM((slots * rows, HD), f32)],
+            grid=(pairs,),
+            in_specs=[pl.BlockSpec(lse.shape, lambda j, *_: (0, 0))] * (1 + len(lses))
+            + [pl.BlockSpec((2 * rows // RUN, RUN, heads * 4 * HD), lambda j, *_: (j, 0, 0))],
+            out_specs=pl.BlockSpec(
+                (2, 1, rows, heads * 2 * HD), lambda j, where, lam: (0, where[1] ^ j, 0, 0)
+            ),
+            scratch_shapes=[pltpu.VMEM((2 * pairs * rows, HD), f32)],
         ),
-        compiler_params=pltpu.CompilerParams(vmem_limit_bytes=16 << 20),
+        compiler_params=pltpu.CompilerParams(vmem_limit_bytes=20 << 20),
         name="weigh",
-    )(place, lam, lse, *lses, o)
+    )(where, lam, lse, *lses, o)
 
 
 def project_kernel(heads, cols, got_ref, gain_ref, w_ref, send_ref, keep_ref, n_s):
@@ -290,8 +334,7 @@
     heads = lambda_vecs.shape[1]
     block = ((positions[::RUN].astype(f32) + 0.5) * (1.0 / RUN)).astype(jnp.int32).astype(bf16)
     ids = jnp.broadcast_to(jnp.pad(block, (0, width - block.shape[0]))[None, :], (16, width))
-    slot = jnp.arange(nh * ny, dtype=jnp.int32)
-    place = (lax.axis_index("h") ^ (slot & 1)) * ny + (lax.axis_index("y") ^ (slot >> 1))
+    where = jnp.stack([lax.axis_index("h"), lax.axis_index("y")]).astype(jnp.int32)
 
     q_mine = jnp.concatenate([queries, ids], 0)
     kv_mine = jnp.concatenate([keys, values, ids], 0)
@@ -303,15 +346,18 @@
     up, down = shift(up, "z", nz, 1), shift(down, "z", nz, -1)
     q_far = [swap(q_pair, "y", ny, d) for d in range(1, ny)]
     kv_parts += [up, down]
-    up, down, q_far = lax.optimization_barrier((up, down, q_far))
+    up, down, q_far, q_near = lax.optimization_barrier((up, down, q_far, q_near))
     up, down = shift(up, "z", nz, 1), shift(down, "z", nz, -1)
     kv_parts += [up, down]
-    kv_parts += [shift(up[:rows], "z", nz, 1), shift(down[rows:], "z", nz, -1)]
     q_parts = [q_mine, q_pair]
     for d in range(ny - 1):
         q_parts += [q_near[d], q_far[d]]
-
-    o, lse = attend(q_parts, kv_parts, rows, heads)
+    near = [(i, 0, i, rows) for i in range(5)]
+    far = [(0, 0, 0, rows), (1, 0, 1, rows), (2, 0, 3, 0)]
+    before = attend(q_parts, kv_parts[:5], near, (3, 6, 8, 10), rows, heads)
+    up, down, before = lax.optimization_barrier((up, down, before))
+    last = [up, down, shift(up[:rows], "z", nz, 1), shift(down[rows:], "z", nz, -1)]
+    o, lse = attend(q_parts, last, far, (2, 4, 6), rows, heads, before)
 
     pair = merge(lse, swap(lse, "h", nh, 1), rows)
     others = [swap(pair, "y", ny, d) for d in range(1, ny)]
@@ -321,8 +367,9 @@
         - jnp.exp(jnp.sum(lambda_vecs[2] * lambda_vecs[3], -1))
         + lambda_init
     )
-    parts = weigh(place, lam, lse, [pair] + others, o, rows, heads)
-
+    parts = weigh(where, lam, lse, [pair] + others, o, rows, heads)
+
+    parts = parts.reshape(nh * ny, rows, width)
     got = lax.all_to_all(parts, ("h", "y"), 0, 0, tiled=False)
     l, c = lax.axis_index("l"), lax.axis_index("c")
     cols = jnp.stack([l * nc + 1 - c, (1 - l) * nc + 1 - c, l * nc + c, (1 - l) * nc + c]).astype(jnp.int32)

time: 151 us -> 149 us (0.987); the launches traced: 149 us -> 148 us
  waiting for transfers between devices: 66.8 us -> 57.3 us
  Pallas kernels: 33 us -> 38.2 us
  starting transfers between devices: 43.2 us -> 45.1 us
  local copies, waits for them, and re-layouts: 2.15 us -> 3.97 us
    ppermute x8, waiting for transfers between devices: 12.7 us -> 5.88 us  [shift(): return lax.ppermute(x, axis, [(i, (i + step) % size) for i in range(size)])]
    pallas_call x1 -> x2, Pallas kernels: 20.9 us -> 27.3 us  [attend(): pl.pallas_call(lambda *r: attend_kernel(rows, spans, slots, spots, bool(b...]
    ppermute x8, starting transfers between devices: 11.8 us -> 14.7 us  [shift(): return lax.ppermute(x, axis, [(i, (i + step) % size) for i in range(size)])]
    unnamed x40 -> x44, local copies, waits for them, and re-layouts: 1.32 us -> 3.15 us
    ppermute x13, waiting for transfers between devices: 39.2 us -> 37.6 us  [swap(): return lax.ppermute(x, axis, [(i, i ^ mask) for i in range(size)])]
  transfers between devices with their start and end apart: 22 -> 22, of which waited for: 13 -> 12; matrix products, arithmetic and copies ran while one was open for 1% -> 1% of each run, Pallas kernels for 0% -> 8%
where the time goes in v5:
time: 149 us; the launch traced here: 148 us
  waiting for transfers between devices  57.3 us (38%)
  starting transfers between devices  45.1 us (30%)
  Pallas kernels  38.2 us (26%)
  local copies, waits for them, and re-layouts  3.97 us (3%)
  other arithmetic  3.32 us (2%)
    ppermute x13, waiting for transfers between devices, swap(): return lax.ppermute(x, axis, [(i, i ^ mask) for i in range(size)])  37.6 us
    pallas_call x2, Pallas kernels, attend(): pl.pallas_call(lambda *r: attend_kernel(rows, spans, slots, spots, bool(b...  27.3 us
    ppermute x13, starting transfers between devices, swap(): return lax.ppermute(x, axis, [(i, i ^ mask) for i in range(size)])  26.7 us
    ppermute x8, starting transfers between devices, shift(): return lax.ppermute(x, axis, [(i, (i + step) % size) for i in range(size)])  14.7 us
    all_to_all x1, waiting for transfers between devices, per_device(): got = lax.all_to_all(parts, ('h', 'y'), 0, 0, tiled=False)  13.8 us
    ppermute x8, waiting for transfers between devices, shift(): return lax.ppermute(x, axis, [(i, (i + step) % size) for i in range(size)])  5.88 us
    pallas_call x1, Pallas kernels, project(): pl.pallas_call(lambda *r: project_kernel(heads, *r), out_shape=[jax.Shape...  5.76 us
    pallas_call x1, Pallas kernels, weigh(): pl.pallas_call(lambda *r: weigh_kernel(heads, *r), out_shape=jax.ShapeDty...  4.28 us
  transfers between devices with their start and end apart: 22, of which 12 were waited for; matrix products, arithmetic and copies ran while one was open for 1% of the time, Pallas kernels for 8%

profile of v5, /device:TPU:1, one launch (start us, length us, event | category | flops | bytes accessed | tf_op | source)
XLA Modules:
  0.0 148.3 jit_solution(7173708436478995570)
XLA Ops:
  1.8 3.7 %collective-permute-start.2 = (bf16[160,768]{1,0:T(8,128)(2,1)S(1)}, bf16[160,768]{1,0:T(8,128)(2,1)S(1)}, u32[]{:S(2)}, u32[]{:S(2)}) collective-permute-start(bf16[160,768]{1,0:T(8,128)(2,1)S(1)} %pad_maximum_fusion.1.r_0_), channel_id=1, source_target_pairs={{0,16},{16,0},{1,17},{17,1},{2,18},{18,2},{3,19},{19,3},{4,20},{20... | collective-permute-start | bytes 737288 | tf_op jit(solution)/shard_map/ppermute | solution.py:328
  8.2 4.0 %collective-permute-start.1 = (bf16[304,768]{1,0:T(8,128)(2,1)S(1)}, bf16[304,768]{1,0:T(8,128)(2,1)S(1)}, u32[]{:S(2)}, u32[]{:S(2)}) collective-permute-start(bf16[304,768]{1,0:T(8,128)(2,1)S(1)} %pad_maximum_fusion.r_8_), channel_id=1, source_target_pairs={{0,224},{32,0},{64,32},{96,64},{128,96},{160,128},{192,160},{224,1... | collective-permute-start | bytes 1400840 | tf_op jit(solution)/shard_map/ppermute | solution.py:324
  13.6 2.6 %collective-permute-start.4 = (bf16[160,768]{1,0:T(8,128)(2,1)S(1)}, bf16[160,768]{1,0:T(8,128)(2,1)S(1)}, u32[]{:S(2)}, u32[]{:S(2)}) collective-permute-start(bf16[160,768]{1,0:T(8,128)(2,1)S(1)} %pad_maximum_fusion.1.r_0_), channel_id=1, source_target_pairs={{0,8},{4,12},{8,0},{12,4},{1,9},{5,13},{9,1},{13,5},{2,10},{6,14},... | collective-permute-start | bytes 737288 | tf_op jit(solution)/shard_map/ppermute | solution.py:328
  16.2 2.3 %collective-permute-done.3.r_2_ = bf16[160,768]{1,0:T(8,128)(2,1)S(1)} collective-permute-done((bf16[160,768]{1,0:T(8,128)(2,1)S(1)}, bf16[160,768]{1,0:T(8,128)(2,1)S(1)}, u32[]{:S(2)}, u32[]{:S(2)}) %collective-permute-start.3) | collective-permute-done | bytes 245792 | tf_op jit(solution)/shard_map/ppermute | solution.py:328
  18.5 7.8 %collective-permute-done.4.r_4_ = bf16[160,768]{1,0:T(8,128)(2,1)S(1)} collective-permute-done((bf16[160,768]{1,0:T(8,128)(2,1)S(1)}, bf16[160,768]{1,0:T(8,128)(2,1)S(1)}, u32[]{:S(2)}, u32[]{:S(2)}) %collective-permute-start.4) | collective-permute-done | bytes 245792 | tf_op jit(solution)/shard_map/ppermute | solution.py:328
  26.2 2.8 %collective-permute-done.5.r_6_ = bf16[160,768]{1,0:T(8,128)(2,1)S(1)} collective-permute-done((bf16[160,768]{1,0:T(8,128)(2,1)S(1)}, bf16[160,768]{1,0:T(8,128)(2,1)S(1)}, u32[]{:S(2)}, u32[]{:S(2)}) %collective-permute-start.5) | collective-permute-done | bytes 245792 | tf_op jit(solution)/shard_map/ppermute | solution.py:328
  29.1 2.7 %collective-permute-start.7 = (bf16[304,768]{1,0:T(8,128)(2,1)S(1)}, bf16[304,768]{1,0:T(8,128)(2,1)S(1)}, u32[]{:S(2)}, u32[]{:S(2)}) collective-permute-start(bf16[304,768]{1,0:T(8,128)(2,1)S(1)} %collective-permute-done.1.r_10_), channel_id=1, source_target_pairs={{0,224},{32,0},{64,32},{96,64},{128,96},{160,128},{192,160},{224,1... | collective-permute-start | bytes 1400840 | tf_op jit(solution)/shard_map/ppermute | solution.py:324
  32.3 3.4 %collective-permute-start.9 = (bf16[160,768]{1,0:T(8,128)(2,1)S(1)}, bf16[160,768]{1,0:T(8,128)(2,1)S(1)}, u32[]{:S(2)}, u32[]{:S(2)}) collective-permute-start(bf16[160,768]{1,0:T(8,128)(2,1)S(1)} %collective-permute-done.2.r_1_), channel_id=1, source_target_pairs={{0,8},{4,12},{8,0},{12,4},{1,9},{5,13},{9,1},{13,5},{2,10},{6,14},... | collective-permute-start | bytes 737288 | tf_op jit(solution)/shard_map/ppermute | solution.py:328
  35.7 2.7 %collective-permute-done.10.r_7_ = bf16[160,768]{1,0:T(8,128)(2,1)S(1)} collective-permute-done((bf16[160,768]{1,0:T(8,128)(2,1)S(1)}, bf16[160,768]{1,0:T(8,128)(2,1)S(1)}, u32[]{:S(2)}, u32[]{:S(2)}) %collective-permute-start.10) | collective-permute-done | bytes 245792 | tf_op jit(solution)/shard_map/ppermute | solution.py:328
  38.4 5.4 %collective-permute-done.9.r_5_ = bf16[160,768]{1,0:T(8,128)(2,1)S(1)} collective-permute-done((bf16[160,768]{1,0:T(8,128)(2,1)S(1)}, bf16[160,768]{1,0:T(8,128)(2,1)S(1)}, u32[]{:S(2)}, u32[]{:S(2)}) %collective-permute-start.9) | collective-permute-done | bytes 245792 | tf_op jit(solution)/shard_map/ppermute | solution.py:328
  43.9 2.7 %collective-permute-start.12 = (bf16[304,768]{1,0:T(8,128)(2,1)S(1)}, bf16[304,768]{1,0:T(8,128)(2,1)S(1)}, u32[]{:S(2)}, u32[]{:S(2)}) collective-permute-start(bf16[304,768]{1,0:T(8,128)(2,1)S(1)} %collective-permute-done.7.r_12_), channel_id=1, source_target_pairs={{0,224},{32,0},{64,32},{96,64},{128,96},{160,128},{192,160},{224,1... | collective-permute-start | bytes 1400840 | tf_op jit(solution)/shard_map/ppermute | solution.py:324
  46.7 11.7 %attend.2 = (bf16[16,72,1536]{2,1,0:T(8,128)(2,1)S(1)}, f32[16,72,128]{2,1,0:T(8,128)S(1)}) custom-call(bf16[160,768]{1,0:T(8,128)(2,1)} %copy-done.4, bf16[160,768]{1,0:T(8,128)(2,1)} %copy-done.13, bf16[160,768]{1,0:T(8,128)(2,1)} %copy-done.14, bf16[160,768]{1,0:T(8,128)(2,1)} %copy-done.18, bf16[160,768]{1,0:T(8,128)(2,1)} %copy-done.15, ...), custom_call_target="tpu_custom_call" | custom-call | flops 30576476160 | bytes 5750784 | tf_op jit(solution)/shard_map/attend/pallas_call | solution.py:165
  60.2 3.3 %collective-permute-start.14 = (bf16[160,768]{1,0:T(8,128)(2,1)S(1)}, bf16[160,768]{1,0:T(8,128)(2,1)S(1)}, u32[]{:S(2)}, u32[]{:S(2)}) collective-permute-start(bf16[160,768]{1,0:T(8,128)(2,1)S(1)} %slice.39), channel_id=1, source_target_pairs={{0,224},{32,0},{64,32},{96,64},{128,96},{160,128},{192,160},{224,1... | collective-permute-start | bytes 737288 | tf_op jit(solution)/shard_map/ppermute | solution.py:324
  63.8 5.9 %collective-permute-done.13.r_10_ = bf16[144,768]{1,0:T(8,128)(2,1)S(1)} collective-permute-done((bf16[144,768]{1,0:T(8,128)(2,1)S(1)}, bf16[144,768]{1,0:T(8,128)(2,1)S(1)}, u32[]{:S(2)}, u32[]{:S(2)}) %collective-permute-start.13) | collective-permute-done | bytes 221216 | tf_op jit(solution)/shard_map/ppermute | solution.py:324
  71.0 15.6 %attend.3 = (bf16[16,72,1536]{2,1,0:T(8,128)(2,1)S(1)}, f32[8,1152]{1,0:T(8,128)}) custom-call(bf16[160,768]{1,0:T(8,128)(2,1)} %copy-done.4, bf16[160,768]{1,0:T(8,128)(2,1)} %copy-done.13, bf16[160,768]{1,0:T(8,128)(2,1)} %copy-done.14, bf16[160,768]{1,0:T(8,128)(2,1)} %copy-done.18, bf16[160,768]{1,0:T(8,128)(2,1)} %copy-done.15, ...), custom_call_target="tpu_custom_call" | custom-call | flops 18345885696 | bytes 4866048 | tf_op jit(solution)/shard_map/attend/pallas_call | solution.py:165
  86.8 4.5 %collective-permute-done.15.r_1_ = f32[8,1152]{1,0:T(8,128)} collective-permute-done((f32[8,1152]{1,0:T(8,128)}, f32[8,1152]{1,0:T(8,128)}, u32[]{:S(2)}, u32[]{:S(2)}) %collective-permute-start.15) | collective-permute-done | bytes 36896 | tf_op jit(solution)/shard_map/ppermute | solution.py:328
  92.5 3.6 %collective-permute-start.18 = (f32[8,1152]{1,0:T(8,128)S(1)}, f32[8,1152]{1,0:T(8,128)S(1)}, u32[]{:S(2)}, u32[]{:S(2)}) collective-permute-start(f32[8,1152]{1,0:T(8,128)S(1)} %merge.1.r_3_), channel_id=1, source_target_pairs={{0,12},{4,8},{8,4},{12,0},{1,13},{5,9},{9,5},{13,1},{2,14},{6,10},... | collective-permute-start | bytes 110600 | tf_op jit(solution)/shard_map/ppermute | solution.py:328
  97.8 4.3 %weigh.1 = bf16[2,4,144,768]{3,2,1,0:T(8,128)(2,1)} custom-call(s32[2]{0:T(128)S(1)} %pad_add_fusion.1.r_0_, f32[3]{0:T(128)S(1)} %subtract_add_fusion.r_1_, f32[8,1152]{1,0:T(8,128)} %get-tuple-element.49.r_0_.r_2_, f32[8,1152]{1,0:T(8,128)S(1)} %merge.1.r_3_, f32[8,1152]{1,0:T(8,128)S(1)} %collective-permute-done.16.r_4_, ...), custom_call_target="tpu_custom_call" | custom-call | tf_op jit(solution)/shard_map/weigh/pallas_call | solution.py:252
  102.1 3.7 %all-to-all-start = ((bf16[8,144,768]{2,1,0:T(8,128)(2,1)}), bf16[8,144,768]{2,1,0:T(8,128)(2,1)S(1)}, u32[]{:S(2)}, u32[]{:S(2)}) async-start(bf16[8,144,768]{2,1,0:T(8,128)(2,1)} %bitcast.6), calls=%async_computation | async-start | bytes 3538944 | tf_op jit(solution)/shard_map/all_to_all | solution.py:373
  106.0 13.8 %all-to-all-done.r_1_ = bf16[8,144,768]{2,1,0:T(8,128)(2,1)S(1)} async-done(((bf16[8,144,768]{2,1,0:T(8,128)(2,1)}), bf16[8,144,768]{2,1,0:T(8,128)(2,1)S(1)}, u32[]{:S(2)}, u32[]{:S(2)}) %all-to-all-start) | async-done | bytes 1769504 | tf_op jit(solution)/shard_map/all_to_all | solution.py:373
  119.8 5.8 %project.1 = (bf16[2,144,1280]{2,1,0:T(8,128)(2,1)S(1)}, f32[2,144,1280]{2,1,0:T(8,128)S(1)}) custom-call(s32[4]{0:T(128)S(1)} %pad_add_fusion.r_0_, bf16[8,144,768]{2,1,0:T(8,128)(2,1)S(1)} %all-to-all-done.r_1_, f32[1,768]{1,0:T(1,128)S(1)} %reshape.15.r_2_, bf16[768,5120]{1,0:T(8,128)(2,1)} %r_3_.1), custom_call_target="tpu_custom_call" | custom-call | tf_op jit(solution)/shard_map/project/pallas_call | solution.py:298
  125.5 10.0 %collective-permute-start.19 = (bf16[2,144,1280]{2,1,0:T(8,128)(2,1)S(1)}, bf16[2,144,1280]{2,1,0:T(8,128)(2,1)S(1)}, u32[]{:S(2)}, u32[]{:S(2)}) collective-permute-start(bf16[2,144,1280]{2,1,0:T(8,128)(2,1)S(1)} %get-tuple-element.52), channel_id=1, source_target_pairs={{0,1},{1,0},{2,3},{3,2},{4,5},{5,4},{6,7},{7,6},{8,9},{9,8},{10,11... | collective-permute-start | bytes 2211848 | tf_op jit(solution)/shard_map/ppermute | solution.py:328
  135.5 1.8 %collective-permute-done.19 = bf16[2,144,1280]{2,1,0:T(8,128)(2,1)S(1)} collective-permute-done((bf16[2,144,1280]{2,1,0:T(8,128)(2,1)S(1)}, bf16[2,144,1280]{2,1,0:T(8,128)(2,1)S(1)}, u32[]{:S(2)}, u32[]{:S(2)}) %collective-permute-start.19) | collective-permute-done | bytes 737312 | tf_op jit(solution)/shard_map/ppermute | solution.py:328
  138.6 8.8 %collective-permute-done.20 = bf16[144,1280]{1,0:T(8,128)(2,1)S(1)} collective-permute-done((bf16[144,1280]{1,0:T(8,128)(2,1)S(1)}, bf16[144,1280]{1,0:T(8,128)(2,1)S(1)}, u32[]{:S(2)}, u32[]{:S(2)}) %collective-permute-start.20) | collective-permute-done | bytes 368672 | tf_op jit(solution)/shard_map/ppermute | solution.py:328
  (84 shorter events, 15.2 us)
Async XLA Ops:
  1.8 44.8 %copy-start.4 = (bf16[160,768]{1,0:T(8,128)(2,1)}, bf16[160,768]{1,0:T(8,128)(2,1)S(1)}, u32[]{:S(2)}) copy-start(bf16[160,768]{1,0:T(8,128)(2,1)S(1)} %pad_maximum_fusion.1.r_0_) | copy-start | bytes 737284
  1.8 14.4 %collective-permute-start.2 = (bf16[160,768]{1,0:T(8,128)(2,1)S(1)}, bf16[160,768]{1,0:T(8,128)(2,1)S(1)}, u32[]{:S(2)}, u32[]{:S(2)}) collective-permute-start(bf16[160,768]{1,0:T(8,128)(2,1)S(1)} %pad_maximum_fusion.1.r_0_), channel_id=1, source_target_pairs={{0,16},{16,0},{1,17},{17,1},{2,18},{18,2},{3,19},{19,3},{4,20},{20... | collective-permute-start | bytes 737288 | tf_op jit(solution)/shard_map/ppermute | solution.py:328
  6.5 57.2 %copy-start.7 = (f32[4,3,128]{2,0,1:T(4,128)S(1)}, f32[4,3,128]{2,0,1:T(4,128)}, u32[]{:S(2)}) copy-start(f32[4,3,128]{2,0,1:T(4,128)} %param.12) | copy-start | bytes 18436
  6.5 22.5 %collective-permute-start = (bf16[304,768]{1,0:T(8,128)(2,1)S(1)}, bf16[304,768]{1,0:T(8,128)(2,1)S(1)}, u32[]{:S(2)}, u32[]{:S(2)}) collective-permute-start(bf16[304,768]{1,0:T(8,128)(2,1)S(1)} %pad_maximum_fusion.r_8_), channel_id=1, source_target_pairs={{0,32},{32,64},{64,96},{96,128},{128,160},{160,192},{192,224},{224... | collective-permute-start | bytes 1400840 | tf_op jit(solution)/shard_map/ppermute | solution.py:324
  8.2 20.8 %collective-permute-start.1 = (bf16[304,768]{1,0:T(8,128)(2,1)S(1)}, bf16[304,768]{1,0:T(8,128)(2,1)S(1)}, u32[]{:S(2)}, u32[]{:S(2)}) collective-permute-start(bf16[304,768]{1,0:T(8,128)(2,1)S(1)} %pad_maximum_fusion.r_8_), channel_id=1, source_target_pairs={{0,224},{32,0},{64,32},{96,64},{128,96},{160,128},{192,160},{224,1... | collective-permute-start | bytes 1400840 | tf_op jit(solution)/shard_map/ppermute | solution.py:324
  12.3 6.2 %collective-permute-start.3 = (bf16[160,768]{1,0:T(8,128)(2,1)S(1)}, bf16[160,768]{1,0:T(8,128)(2,1)S(1)}, u32[]{:S(2)}, u32[]{:S(2)}) collective-permute-start(bf16[160,768]{1,0:T(8,128)(2,1)S(1)} %pad_maximum_fusion.1.r_0_), channel_id=1, source_target_pairs={{0,4},{4,0},{8,12},{12,8},{1,5},{5,1},{9,13},{13,9},{2,6},{6,2},{1... | collective-permute-start | bytes 737288 | tf_op jit(solution)/shard_map/ppermute | solution.py:328
  13.6 12.7 %collective-permute-start.4 = (bf16[160,768]{1,0:T(8,128)(2,1)S(1)}, bf16[160,768]{1,0:T(8,128)(2,1)S(1)}, u32[]{:S(2)}, u32[]{:S(2)}) collective-permute-start(bf16[160,768]{1,0:T(8,128)(2,1)S(1)} %pad_maximum_fusion.1.r_0_), channel_id=1, source_target_pairs={{0,8},{4,12},{8,0},{12,4},{1,9},{5,13},{9,1},{13,5},{2,10},{6,14},... | collective-permute-start | bytes 737288 | tf_op jit(solution)/shard_map/ppermute | solution.py:328
  16.2 12.8 %collective-permute-start.5 = (bf16[160,768]{1,0:T(8,128)(2,1)S(1)}, bf16[160,768]{1,0:T(8,128)(2,1)S(1)}, u32[]{:S(2)}, u32[]{:S(2)}) collective-permute-start(bf16[160,768]{1,0:T(8,128)(2,1)S(1)} %pad_maximum_fusion.1.r_0_), channel_id=1, source_target_pairs={{0,12},{4,8},{8,4},{12,0},{1,13},{5,9},{9,5},{13,1},{2,14},{6,10},... | collective-permute-start | bytes 737288 | tf_op jit(solution)/shard_map/ppermute | solution.py:328
  29.1 14.7 %collective-permute-start.6 = (bf16[304,768]{1,0:T(8,128)(2,1)S(1)}, bf16[304,768]{1,0:T(8,128)(2,1)S(1)}, u32[]{:S(2)}, u32[]{:S(2)}) collective-permute-start(bf16[304,768]{1,0:T(8,128)(2,1)S(1)} %collective-permute-done.r_9_), channel_id=1, source_target_pairs={{0,32},{32,64},{64,96},{96,128},{128,160},{160,192},{192,224},{224... | collective-permute-start | bytes 1400840 | tf_op jit(solution)/shard_map/ppermute | solution.py:324
  29.1 14.6 %collective-permute-start.7 = (bf16[304,768]{1,0:T(8,128)(2,1)S(1)}, bf16[304,768]{1,0:T(8,128)(2,1)S(1)}, u32[]{:S(2)}, u32[]{:S(2)}) collective-permute-start(bf16[304,768]{1,0:T(8,128)(2,1)S(1)} %collective-permute-done.1.r_10_), channel_id=1, source_target_pairs={{0,224},{32,0},{64,32},{96,64},{128,96},{160,128},{192,160},{224,1... | collective-permute-start | bytes 1400840 | tf_op jit(solution)/shard_map/ppermute | solution.py:324
  31.8 6.6 %collective-permute-start.10 = (bf16[160,768]{1,0:T(8,128)(2,1)S(1)}, bf16[160,768]{1,0:T(8,128)(2,1)S(1)}, u32[]{:S(2)}, u32[]{:S(2)}) collective-permute-start(bf16[160,768]{1,0:T(8,128)(2,1)S(1)} %collective-permute-done.2.r_1_), channel_id=1, source_target_pairs={{0,12},{4,8},{8,4},{12,0},{1,13},{5,9},{9,5},{13,1},{2,14},{6,10},... | collective-permute-start | bytes 737288 | tf_op jit(solution)/shard_map/ppermute | solution.py:328
  32.3 6.1 %collective-permute-start.8 = (bf16[160,768]{1,0:T(8,128)(2,1)S(1)}, bf16[160,768]{1,0:T(8,128)(2,1)S(1)}, u32[]{:S(2)}, u32[]{:S(2)}) collective-permute-start(bf16[160,768]{1,0:T(8,128)(2,1)S(1)} %collective-permute-done.2.r_1_), channel_id=1, source_target_pairs={{0,4},{4,0},{8,12},{12,8},{1,5},{5,1},{9,13},{13,9},{2,6},{6,2},{1... | collective-permute-start | bytes 737288 | tf_op jit(solution)/shard_map/ppermute | solution.py:328
  32.3 11.5 %collective-permute-start.9 = (bf16[160,768]{1,0:T(8,128)(2,1)S(1)}, bf16[160,768]{1,0:T(8,128)(2,1)S(1)}, u32[]{:S(2)}, u32[]{:S(2)}) collective-permute-start(bf16[160,768]{1,0:T(8,128)(2,1)S(1)} %collective-permute-done.2.r_1_), channel_id=1, source_target_pairs={{0,8},{4,12},{8,0},{12,4},{1,9},{5,13},{9,1},{13,5},{2,10},{6,14},... | collective-permute-start | bytes 737288 | tf_op jit(solution)/shard_map/ppermute | solution.py:328
  43.8 16.4 %collective-permute-start.11 = (bf16[304,768]{1,0:T(8,128)(2,1)S(1)}, bf16[304,768]{1,0:T(8,128)(2,1)S(1)}, u32[]{:S(2)}, u32[]{:S(2)}) collective-permute-start(bf16[304,768]{1,0:T(8,128)(2,1)S(1)} %collective-permute-done.6.r_11_), channel_id=1, source_target_pairs={{0,32},{32,64},{64,96},{96,128},{128,160},{160,192},{192,224},{224... | collective-permute-start | bytes 1400840 | tf_op jit(solution)/shard_map/ppermute | solution.py:324
  43.9 16.3 %collective-permute-start.12 = (bf16[304,768]{1,0:T(8,128)(2,1)S(1)}, bf16[304,768]{1,0:T(8,128)(2,1)S(1)}, u32[]{:S(2)}, u32[]{:S(2)}) collective-permute-start(bf16[304,768]{1,0:T(8,128)(2,1)S(1)} %collective-permute-done.7.r_12_), channel_id=1, source_target_pairs={{0,224},{32,0},{64,32},{96,64},{128,96},{160,128},{192,160},{224,1... | collective-permute-start | bytes 1400840 | tf_op jit(solution)/shard_map/ppermute | solution.py:324
  60.2 9.4 %collective-permute-start.14 = (bf16[160,768]{1,0:T(8,128)(2,1)S(1)}, bf16[160,768]{1,0:T(8,128)(2,1)S(1)}, u32[]{:S(2)}, u32[]{:S(2)}) collective-permute-start(bf16[160,768]{1,0:T(8,128)(2,1)S(1)} %slice.39), channel_id=1, source_target_pairs={{0,224},{32,0},{64,32},{96,64},{128,96},{160,128},{192,160},{224,1... | collective-permute-start | bytes 737288 | tf_op jit(solution)/shard_map/ppermute | solution.py:324
  63.6 6.1 %collective-permute-start.13 = (bf16[144,768]{1,0:T(8,128)(2,1)S(1)}, bf16[144,768]{1,0:T(8,128)(2,1)S(1)}, u32[]{:S(2)}, u32[]{:S(2)}) collective-permute-start(bf16[144,768]{1,0:T(8,128)(2,1)S(1)} %slice.38), channel_id=1, source_target_pairs={{0,32},{32,64},{64,96},{96,128},{128,160},{160,192},{192,224},{224... | collective-permute-start | bytes 663560 | tf_op jit(solution)/shard_map/ppermute | solution.py:324
  86.6 4.7 %collective-permute-start.15 = (f32[8,1152]{1,0:T(8,128)}, f32[8,1152]{1,0:T(8,128)}, u32[]{:S(2)}, u32[]{:S(2)}) collective-permute-start(f32[8,1152]{1,0:T(8,128)} %get-tuple-element.49.r_0_.r_2_), channel_id=1, source_target_pairs={{0,16},{16,0},{1,17},{17,1},{2,18},{18,2},{3,19},{19,3},{4,20},{20... | collective-permute-start | bytes 110600 | tf_op jit(solution)/shard_map/ppermute | solution.py:328
  92.2 4.0 %collective-permute-start.16 = (f32[8,1152]{1,0:T(8,128)S(1)}, f32[8,1152]{1,0:T(8,128)S(1)}, u32[]{:S(2)}, u32[]{:S(2)}) collective-permute-start(f32[8,1152]{1,0:T(8,128)S(1)} %merge.1.r_3_), channel_id=1, source_target_pairs={{0,4},{4,0},{8,12},{12,8},{1,5},{5,1},{9,13},{13,9},{2,6},{6,2},{1... | collective-permute-start | bytes 110600 | tf_op jit(solution)/shard_map/ppermute | solution.py:328
  92.3 4.4 %collective-permute-start.17 = (f32[8,1152]{1,0:T(8,128)S(1)}, f32[8,1152]{1,0:T(8,128)S(1)}, u32[]{:S(2)}, u32[]{:S(2)}) collective-permute-start(f32[8,1152]{1,0:T(8,128)S(1)} %merge.1.r_3_), channel_id=1, source_target_pairs={{0,8},{4,12},{8,0},{12,4},{1,9},{5,13},{9,1},{13,5},{2,10},{6,14},... | collective-permute-start | bytes 110600 | tf_op jit(solution)/shard_map/ppermute | solution.py:328
  92.5 5.3 %collective-permute-start.18 = (f32[8,1152]{1,0:T(8,128)S(1)}, f32[8,1152]{1,0:T(8,128)S(1)}, u32[]{:S(2)}, u32[]{:S(2)}) collective-permute-start(f32[8,1152]{1,0:T(8,128)S(1)} %merge.1.r_3_), channel_id=1, source_target_pairs={{0,12},{4,8},{8,4},{12,0},{1,13},{5,9},{9,5},{13,1},{2,14},{6,10},... | collective-permute-start | bytes 110600 | tf_op jit(solution)/shard_map/ppermute | solution.py:328
  102.1 17.6 %all-to-all-start = ((bf16[8,144,768]{2,1,0:T(8,128)(2,1)}), bf16[8,144,768]{2,1,0:T(8,128)(2,1)S(1)}, u32[]{:S(2)}, u32[]{:S(2)}) async-start(bf16[8,144,768]{2,1,0:T(8,128)(2,1)} %bitcast.6), calls=%async_computation | async-start | bytes 3538944 | tf_op jit(solution)/shard_map/all_to_all | solution.py:373
  125.5 11.9 %collective-permute-start.19 = (bf16[2,144,1280]{2,1,0:T(8,128)(2,1)S(1)}, bf16[2,144,1280]{2,1,0:T(8,128)(2,1)S(1)}, u32[]{:S(2)}, u32[]{:S(2)}) collective-permute-start(bf16[2,144,1280]{2,1,0:T(8,128)(2,1)S(1)} %get-tuple-element.52), channel_id=1, source_target_pairs={{0,1},{1,0},{2,3},{3,2},{4,5},{5,4},{6,7},{7,6},{8,9},{9,8},{10,11... | collective-permute-start | bytes 2211848 | tf_op jit(solution)/shard_map/ppermute | solution.py:328
  137.5 9.9 %collective-permute-start.20 = (bf16[144,1280]{1,0:T(8,128)(2,1)S(1)}, bf16[144,1280]{1,0:T(8,128)(2,1)S(1)}, u32[]{:S(2)}, u32[]{:S(2)}) collective-permute-start(bf16[144,1280]{1,0:T(8,128)(2,1)S(1)} %fusion.2), channel_id=1, source_target_pairs={{0,2},{2,0},{1,3},{3,1},{4,6},{6,4},{5,7},{7,5},{8,10},{10,8},{9,1... | collective-permute-start | bytes 1105928 | tf_op jit(solution)/shard_map/ppermute | solution.py:328
  (20 other events, 273.3 us)

commit v6 on v5

--- a/solution.py
+++ b/solution.py
@@ -20,13 +20,9 @@
 bf16 = jnp.bfloat16
 
 
-def attend_kernel(rows, spans, slots, spots, prev, *refs):
-    q_refs, refs = refs[:slots], refs[slots:]
-    count = len(refs) - 10 - 2 * prev
-    kv_refs, refs = refs[:count], refs[count:]
-    if prev:
-        prev_o, prev_lse = refs[:2]
-        refs = refs[2:]
+def attend_kernel(rows, spans, slots, spots, *refs):
+    q_refs = [refs[0].at[i // 2, i % 2] for i in range(slots)]
+    kv_refs, refs = refs[1:-10], refs[-10:]
     o_ref, lse_ref, q3, k3, v3, q_s, k_s, v_s, lse_s, order = refs
     head = pl.program_id(0)
     per = rows // RUN
@@ -44,7 +40,9 @@
 
         def numbers(part):
             tail = part[part.shape[0] - 16 :, :HD].astype(f32)
-            return [jnp.sum(jnp.where(first & (lanes == d), tail, 0.0)).astype(jnp.int32) for d in range(per)]
+            weight = jnp.where(first & (lanes < per), jnp.where(lanes == 0, float(HD), 1.0), 0.0)
+            both = jnp.sum(tail * weight).astype(jnp.int32)
+            return [lax.div(both, HD), lax.rem(both, HD)]
 
         kb = [v for k, kr, v, vr in spots for v in numbers(kv_refs[v])]
         qb = [v for p in q_refs for v in numbers(p)]
@@ -100,12 +98,6 @@
                 g = order[3, t * TILE + i]
                 o = num[i * RUN : (i + 1) * RUN]
                 e = lse[i * RUN : (i + 1) * RUN]
-                if prev:
-                    pick = lane == head * 2 + a
-                    before = jnp.max(jnp.where(pick, prev_lse[g], -3e38), -1, keepdims=True)
-                    both = logsum([before, e])
-                    o = o * jnp.exp2(e - both) + prev_o[g, :, a * 2 * HD : (a + 1) * 2 * HD].astype(f32) * jnp.exp2(before - both)
-                    e = both
                 o_ref[g, :, a * 2 * HD : (a + 1) * 2 * HD] = o.astype(bf16)
                 lse_s[g] = jnp.where(lane == head * 2 + a, e, lse_s[g])
 
@@ -147,30 +139,30 @@
 
     @pl.when(head == pl.num_programs(0) - 1)
     def _():
-        if prev:
-            lse_ref[...] = jnp.transpose(lse_s[...].reshape(blocks * RUN, HD))[: lse_ref.shape[0], :]
-        else:
-            lse_ref[...] = lse_s[...]
-
-
-def attend(q_parts, kv_parts, spots, spans, rows, heads, before=()):
-    slots = len(q_parts)
+        lse_ref[...] = jnp.transpose(lse_s[...].reshape(blocks * RUN, HD))[: lse_ref.shape[0], :]
+
+
+def attend(q_pair, kv_parts, spots, spans, rows, heads):
+    ny, _, pad, width = q_pair.shape
+    slots = 2 * ny
     blocks = slots * rows // RUN
     keys = len(spots) * rows // RUN
-    wide = jax.ShapeDtypeStruct((blocks, RUN, HD), f32)
-    flat = jax.ShapeDtypeStruct((8, blocks * RUN), f32)
-    lse = flat if before else wide
-    out_block = pl.BlockSpec((blocks, RUN, 4 * HD), lambda h: (0, 0, h))
-    ins = [pltpu.with_memory_space_constraint(x, pltpu.HBM) for x in [*q_parts, *kv_parts, *before]]
+    ins = [pltpu.with_memory_space_constraint(x, pltpu.HBM) for x in [q_pair, *kv_parts]]
     return pl.pallas_call(
-        lambda *r: attend_kernel(rows, spans, slots, spots, bool(before), *r),
-        out_shape=[jax.ShapeDtypeStruct((blocks, RUN, heads * 4 * HD), bf16), lse],
+        lambda *r: attend_kernel(rows, spans, slots, spots, *r),
+        out_shape=[
+            jax.ShapeDtypeStruct((blocks, RUN, heads * 4 * HD), bf16),
+            jax.ShapeDtypeStruct((8, blocks * RUN), f32),
+        ],
         grid_spec=pltpu.PrefetchScalarGridSpec(
             num_scalar_prefetch=0,
             grid=(heads,),
-            in_specs=[pl.BlockSpec((x.shape[0], 2 * HD), lambda h: (0, h)) for x in [*q_parts, *kv_parts]]
-            + ([out_block, pl.BlockSpec(wide.shape, lambda h: (0, 0, 0))] if before else []),
-            out_specs=[out_block, pl.BlockSpec(lse.shape, lambda h: (0,) * len(lse.shape))],
+            in_specs=[pl.BlockSpec((ny, 2, pad, 2 * HD), lambda h: (0, 0, 0, h))]
+            + [pl.BlockSpec((x.shape[0], 2 * HD), lambda h: (0, h)) for x in kv_parts],
+            out_specs=[
+                pl.BlockSpec((blocks, RUN, 4 * HD), lambda h: (0, 0, h)),
+                pl.BlockSpec((8, blocks * RUN), lambda h: (0, 0)),
+            ],
             scratch_shapes=[
                 pltpu.VMEM((blocks, RUN, 2 * HD), bf16),
                 pltpu.VMEM((keys, RUN, 2 * HD), bf16),
@@ -230,7 +222,7 @@
 
     @pl.when(j == 0)
     def _():
-        whole = logsum([reorder(r[...], rows, 2 * i) for i, r in enumerate(all_refs)])
+        whole = logsum([r[...] for r in all_refs])
         w = jnp.exp2(lse_ref[...] - whole)
         w = jnp.concatenate([w, jnp.zeros((HD - w.shape[0], w.shape[1]), f32)], 0)
         w_s[...] = jnp.transpose(w)
@@ -258,7 +250,7 @@
             in_specs=[pl.BlockSpec(lse.shape, lambda j, *_: (0, 0))] * (1 + len(lses))
             + [pl.BlockSpec((2 * rows // RUN, RUN, heads * 4 * HD), lambda j, *_: (j, 0, 0))],
             out_specs=pl.BlockSpec(
-                (2, 1, rows, heads * 2 * HD), lambda j, where, lam: (0, where[1] ^ j, 0, 0)
+                (2, 1, rows, heads * 2 * HD), lambda j, where, lam: (0, j, 0, 0)
             ),
             scratch_shapes=[pltpu.VMEM((2 * pairs * rows, HD), f32)],
         ),
@@ -267,57 +259,60 @@
     )(where, lam, lse, *lses, o)
 
 
-def project_kernel(heads, cols, got_ref, gain_ref, w_ref, send_ref, keep_ref, n_s):
+def norm(got_ref, gain_ref, n_s, heads):
+    total = got_ref[0].astype(f32)
+    for j in range(1, got_ref.shape[0]):
+        total = total + got_ref[j].astype(f32)
+    for h in range(heads):
+        d = total[:, h * 2 * HD : (h + 1) * 2 * HD]
+        mean_square = jnp.mean(d * d, -1, keepdims=True)
+        g = gain_ref[0:1, h * 2 * HD : (h + 1) * 2 * HD]
+        n_s[:, h * 2 * HD : (h + 1) * 2 * HD] = (out_factor * d / jnp.sqrt(mean_square + norm_eps) * g).astype(bf16)
+
+
+def project_kernel(heads, cols, *refs):
     i = pl.program_id(0)
+    if heads:
+        got_ref, gain_ref, w_ref, send_ref, keep_ref, n_ref = refs
+
+        @pl.when(i == 0)
+        def _():
+            norm(got_ref, gain_ref, n_ref, heads)
+
+    else:
+        n_ref, w_ref, send_ref, keep_ref = refs
+    share = jnp.dot(n_ref[...], w_ref[...], preferred_element_type=f32)
 
     @pl.when(i == 0)
     def _():
-        total = got_ref[0].astype(f32)
-        for j in range(1, got_ref.shape[0]):
-            total = total + got_ref[j].astype(f32)
-        for h in range(heads):
-            d = total[:, h * 2 * HD : (h + 1) * 2 * HD]
-            mean_square = jnp.mean(d * d, -1, keepdims=True)
-            g = gain_ref[0:1, h * 2 * HD : (h + 1) * 2 * HD]
-            n_s[:, h * 2 * HD : (h + 1) * 2 * HD] = (out_factor * d / jnp.sqrt(mean_square + norm_eps) * g).astype(bf16)
-
-    share = jnp.dot(n_s[...], w_ref[...], preferred_element_type=f32)
-
-    @pl.when(i < 2)
-    def _():
-        send_ref[0] = share.astype(bf16)
-
-    @pl.when(i >= 2)
-    def _():
-        keep_ref[0] = share
-
-
-def project(cols, got, gain, weight, heads):
-    rows = got.shape[1]
+        send_ref[...] = share.astype(bf16)
+
+    @pl.when(i == 1)
+    def _():
+        keep_ref[...] = share
+
+
+def project(cols, ins, weight, rows, heads=0):
+    depth = weight.shape[0]
     width = weight.shape[1] // 4
+    zeros = lambda x: pl.BlockSpec(x.shape, lambda i, cols: (0,) * len(x.shape))
+    outs = [
+        jax.ShapeDtypeStruct((rows, width), bf16),
+        jax.ShapeDtypeStruct((rows, width), f32),
+    ] + [jax.ShapeDtypeStruct((rows, depth), bf16)] * bool(heads)
     return pl.pallas_call(
         lambda *r: project_kernel(heads, *r),
-        out_shape=[
-            jax.ShapeDtypeStruct((2, rows, width), bf16),
-            jax.ShapeDtypeStruct((2, rows, width), f32),
-        ],
+        out_shape=outs,
         grid_spec=pltpu.PrefetchScalarGridSpec(
             num_scalar_prefetch=1,
-            grid=(4,),
-            in_specs=[
-                pl.BlockSpec(got.shape, lambda i, cols: (0, 0, 0)),
-                pl.BlockSpec(gain.shape, lambda i, cols: (0, 0)),
-                pl.BlockSpec((weight.shape[0], width), lambda i, cols: (0, cols[i])),
-            ],
-            out_specs=[
-                pl.BlockSpec((1, rows, width), lambda i, cols: (jnp.minimum(i, 1), 0, 0)),
-                pl.BlockSpec((1, rows, width), lambda i, cols: (jnp.maximum(i, 2) - 2, 0, 0)),
-            ],
-            scratch_shapes=[pltpu.VMEM((rows, got.shape[2]), bf16)],
+            grid=(2,),
+            in_specs=[zeros(x) for x in ins] + [pl.BlockSpec((depth, width), lambda i, cols: (0, cols[i]))],
+            out_specs=[zeros(x) for x in outs],
         ),
         compiler_params=pltpu.CompilerParams(vmem_limit_bytes=24 << 20),
+        cost_estimate=pl.CostEstimate(flops=rows * depth * width * 32, bytes_accessed=depth * width * 4, transcendentals=0),
         name="project",
-    )(cols, got, gain, pltpu.with_memory_space_constraint(weight, pltpu.HBM))
+    )(cols, *ins, pltpu.with_memory_space_constraint(weight, pltpu.HBM))
 
 
 def shift(x, axis, size, step):
@@ -334,30 +329,21 @@
     heads = lambda_vecs.shape[1]
     block = ((positions[::RUN].astype(f32) + 0.5) * (1.0 / RUN)).astype(jnp.int32).astype(bf16)
     ids = jnp.broadcast_to(jnp.pad(block, (0, width - block.shape[0]))[None, :], (16, width))
-    where = jnp.stack([lax.axis_index("h"), lax.axis_index("y")]).astype(jnp.int32)
+    where = lax.axis_index("h").astype(jnp.int32).reshape(1)
 
     q_mine = jnp.concatenate([queries, ids], 0)
     kv_mine = jnp.concatenate([keys, values, ids], 0)
+    q_far = swap(q_mine, "h", nh, 1)
     up, down = shift(kv_mine, "z", nz, 1), shift(kv_mine, "z", nz, -1)
-    q_pair = swap(q_mine, "h", nh, 1)
-    q_near = [swap(q_mine, "y", ny, d) for d in range(1, ny)]
     kv_parts = [kv_mine, up, down]
-    up, down, q_pair, q_near = lax.optimization_barrier((up, down, q_pair, q_near))
-    up, down = shift(up, "z", nz, 1), shift(down, "z", nz, -1)
-    q_far = [swap(q_pair, "y", ny, d) for d in range(1, ny)]
-    kv_parts += [up, down]
-    up, down, q_far, q_near = lax.optimization_barrier((up, down, q_far, q_near))
-    up, down = shift(up, "z", nz, 1), shift(down, "z", nz, -1)
-    kv_parts += [up, down]
-    q_parts = [q_mine, q_pair]
-    for d in range(ny - 1):
-        q_parts += [q_near[d], q_far[d]]
-    near = [(i, 0, i, rows) for i in range(5)]
-    far = [(0, 0, 0, rows), (1, 0, 1, rows), (2, 0, 3, 0)]
-    before = attend(q_parts, kv_parts[:5], near, (3, 6, 8, 10), rows, heads)
-    up, down, before = lax.optimization_barrier((up, down, before))
-    last = [up, down, shift(up[:rows], "z", nz, 1), shift(down[rows:], "z", nz, -1)]
-    o, lse = attend(q_parts, last, far, (2, 4, 6), rows, heads, before)
+    up, down, q_far = lax.optimization_barrier((up, down, q_far))
+    q_pair = lax.all_gather(jnp.stack([q_mine, q_far]), "y", axis=0)
+    for _ in range(2):
+        up, down = shift(up, "z", nz, 1), shift(down, "z", nz, -1)
+        kv_parts += [up, down]
+    kv_parts += [shift(up[:rows], "z", nz, 1), shift(down[rows:], "z", nz, -1)]
+    spots = [(i, 0, i, rows) for i in range(nz - 1)] + [(nz - 1, 0, nz, 0)]
+    o, lse = attend(q_pair, kv_parts, spots, (4, 8, 12, 16), rows, heads)
 
     pair = merge(lse, swap(lse, "h", nh, 1), rows)
     others = [swap(pair, "y", ny, d) for d in range(1, ny)]
@@ -372,11 +358,14 @@
     parts = parts.reshape(nh * ny, rows, width)
     got = lax.all_to_all(parts, ("h", "y"), 0, 0, tiled=False)
     l, c = lax.axis_index("l"), lax.axis_index("c")
-    cols = jnp.stack([l * nc + 1 - c, (1 - l) * nc + 1 - c, l * nc + c, (1 - l) * nc + c]).astype(jnp.int32)
-    send, keep = project(cols, got, head_gain.reshape(1, width), out_weight, heads)
-    near = swap(send, "c", nc, 1)
-    far = swap((keep[1] + near[1].astype(f32)).astype(bf16), "l", nl, 1)
-    return (keep[0] + near[0].astype(f32) + far.astype(f32) + residual.astype(f32)).astype(bf16)
+    cols = [jnp.stack([r * nc + 1 - c, r * nc + c]).astype(jnp.int32) for r in (1 - l, l)]
+    send, keep, normed = project(cols[0], [got, head_gain.reshape(1, width)], out_weight, rows, heads)
+    away = (keep + swap(send, "c", nc, 1).astype(f32)).astype(bf16)
+    away, normed = lax.optimization_barrier((away, normed))
+    far = swap(away, "l", nl, 1)
+    send, keep = project(cols[1], [normed], out_weight, rows)
+    rest = lax.optimization_barrier(far.astype(f32) + residual.astype(f32))
+    return (rest + keep + swap(send, "c", nc, 1).astype(f32)).astype(bf16)
 
 
 def solution(mesh):

time: 149 us -> 149 us (level)
  between operations: 0.32 us -> 13.5 us
  Pallas kernels: 38.2 us -> 31.9 us
  starting transfers between devices: 45.1 us -> 39.9 us
  waiting for transfers between devices: 57.3 us -> 55.2 us
    ppermute x13 -> x8, waiting for transfers between devices: 37.6 us -> 16.9 us  [swap(): return lax.ppermute(x, axis, [(i, i ^ mask) for i in range(size)])]
    ppermute x8, waiting for transfers between devices: 5.88 us -> 23 us  [shift(): return lax.ppermute(x, axis, [(i, (i + step) % size) for i in range(size)])]
    ppermute x13 -> x8, starting transfers between devices: 26.7 us -> 18.2 us  [swap(): return lax.ppermute(x, axis, [(i, i ^ mask) for i in range(size)])]
    pallas_call x3, Pallas kernels: 33.1 us -> 26.9 us  [the longest x1 20.2 us: attend(): pl.pallas_call(lambda *r: attend_kernel(rows, spans, slots, spots, *r), o...]
    ppermute x8, starting transfers between devices: 14.7 us -> 17.6 us  [shift(): return lax.ppermute(x, axis, [(i, (i + step) % size) for i in range(size)])]
    another operation x2 -> x4, other arithmetic: 0.16 us -> 1.99 us  [the longest x2 1.84 us: per_device(): q_pair = lax.all_gather(jnp.stack([q_mine, q_far]), 'y', axis=0)]
    all_to_all x1, waiting for transfers between devices: 13.8 us -> 15.3 us  [per_device(): got = lax.all_to_all(parts, ('h', 'y'), 0, 0, tiled=False)]
    unnamed x44 -> x26, local copies, waits for them, and re-layouts: 3.15 us -> 2.11 us
  transfers between devices with their start and end apart: 22 -> 18, of which waited for: 12 -> 11; matrix products, arithmetic and copies ran while one was open for 1% -> 1% of each run, Pallas kernels for 8% -> 2%
where the time goes in v6:
time: 149 us; the launch traced here: 148 us
  waiting for transfers between devices  55.2 us (37%)
  starting transfers between devices  39.9 us (27%)
  Pallas kernels  31.9 us (21%)
  between operations  13.5 us (9%)
  other arithmetic  4.19 us (3%)
  local copies, waits for them, and re-layouts  2.93 us (2%)
    ppermute x8, waiting for transfers between devices, shift(): return lax.ppermute(x, axis, [(i, (i + step) % size) for i in range(size)])  23 us
    pallas_call x1, Pallas kernels, attend(): pl.pallas_call(lambda *r: attend_kernel(rows, spans, slots, spots, *r), o...  20.2 us
    ppermute x8, starting transfers between devices, swap(): return lax.ppermute(x, axis, [(i, i ^ mask) for i in range(size)])  18.2 us
    ppermute x8, starting transfers between devices, shift(): return lax.ppermute(x, axis, [(i, (i + step) % size) for i in range(size)])  17.6 us
    ppermute x8, waiting for transfers between devices, swap(): return lax.ppermute(x, axis, [(i, i ^ mask) for i in range(size)])  16.9 us
    all_to_all x1, waiting for transfers between devices, per_device(): got = lax.all_to_all(parts, ('h', 'y'), 0, 0, tiled=False)  15.3 us
    pallas_call x2, Pallas kernels, project(): pl.pallas_call(lambda *r: project_kernel(heads, *r), out_shape=outs, grid...  6.73 us
    pallas_call x1, Pallas kernels, weigh(): pl.pallas_call(lambda *r: weigh_kernel(heads, *r), out_shape=jax.ShapeDty...  4.23 us
  transfers between devices with their start and end apart: 18, of which 11 were waited for; matrix products, arithmetic and copies ran while one was open for 1% of the time, Pallas kernels for 2%

profile of v6, /device:TPU:1, one launch (start us, length us, event | category | flops | bytes accessed | tf_op | source)
XLA Modules:
  0.0 147.7 jit_solution(13356683492039676900)
XLA Ops:
  8.4 2.5 %collective-permute-start = (bf16[304,768]{1,0:T(8,128)(2,1)S(1)}, bf16[304,768]{1,0:T(8,128)(2,1)S(1)}, u32[]{:S(2)}, u32[]{:S(2)}) collective-permute-start(bf16[304,768]{1,0:T(8,128)(2,1)S(1)} %pad_maximum_fusion.1.r_1_), channel_id=1, source_target_pairs={{0,32},{32,64},{64,96},{96,128},{128,160},{160,192},{192,224},{224... | collective-permute-start | bytes 1400840 | tf_op jit(solution)/shard_map/ppermute | solution.py:319
  11.0 4.6 %collective-permute-start.1 = (bf16[304,768]{1,0:T(8,128)(2,1)S(1)}, bf16[304,768]{1,0:T(8,128)(2,1)S(1)}, u32[]{:S(2)}, u32[]{:S(2)}) collective-permute-start(bf16[304,768]{1,0:T(8,128)(2,1)S(1)} %pad_maximum_fusion.1.r_1_), channel_id=1, source_target_pairs={{0,224},{32,0},{64,32},{96,64},{128,96},{160,128},{192,160},{224,1... | collective-permute-start | bytes 1400840 | tf_op jit(solution)/shard_map/ppermute | solution.py:319
  16.6 2.8 %collective-permute-start.2 = (bf16[160,768]{1,0:T(8,128)(2,1)S(1)}, bf16[160,768]{1,0:T(8,128)(2,1)S(1)}, u32[]{:S(2)}, u32[]{:S(2)}) collective-permute-start(bf16[160,768]{1,0:T(8,128)(2,1)S(1)} %get-tuple-element.32), channel_id=1, source_target_pairs={{0,16},{16,0},{1,17},{17,1},{2,18},{18,2},{3,19},{19,3},{4,20},{20... | collective-permute-start | bytes 737288 | tf_op jit(solution)/shard_map/ppermute | solution.py:323
  19.4 5.3 %collective-permute-done.2 = bf16[160,768]{1,0:T(8,128)(2,1)S(1)} collective-permute-done((bf16[160,768]{1,0:T(8,128)(2,1)S(1)}, bf16[160,768]{1,0:T(8,128)(2,1)S(1)}, u32[]{:S(2)}, u32[]{:S(2)}) %collective-permute-start.2) | collective-permute-done | bytes 245792 | tf_op jit(solution)/shard_map/ppermute | solution.py:323
  26.2 3.1 %collective-permute-start.4 = (bf16[304,768]{1,0:T(8,128)(2,1)S(1)}, bf16[304,768]{1,0:T(8,128)(2,1)S(1)}, u32[]{:S(2)}, u32[]{:S(2)}) collective-permute-start(bf16[304,768]{1,0:T(8,128)(2,1)S(1)} %collective-permute-done.1.r_3_), channel_id=1, source_target_pairs={{0,224},{32,0},{64,32},{96,64},{128,96},{160,128},{192,160},{224,1... | collective-permute-start | bytes 1400840 | tf_op jit(solution)/shard_map/ppermute | solution.py:319
  29.3 8.4 %collective-permute-done.4.r_5_ = bf16[304,768]{1,0:T(8,128)(2,1)S(1)} collective-permute-done((bf16[304,768]{1,0:T(8,128)(2,1)S(1)}, bf16[304,768]{1,0:T(8,128)(2,1)S(1)}, u32[]{:S(2)}, u32[]{:S(2)}) %collective-permute-start.4) | collective-permute-done | bytes 466976 | tf_op jit(solution)/shard_map/ppermute | solution.py:319
  37.8 3.4 %collective-permute-start.6 = (bf16[304,768]{1,0:T(8,128)(2,1)S(1)}, bf16[304,768]{1,0:T(8,128)(2,1)S(1)}, u32[]{:S(2)}, u32[]{:S(2)}) collective-permute-start(bf16[304,768]{1,0:T(8,128)(2,1)S(1)} %collective-permute-done.4.r_5_), channel_id=1, source_target_pairs={{0,224},{32,0},{64,32},{96,64},{128,96},{160,128},{192,160},{224,1... | collective-permute-start | bytes 1400840 | tf_op jit(solution)/shard_map/ppermute | solution.py:319
  41.2 7.5 %collective-permute-done.6.r_7_ = bf16[304,768]{1,0:T(8,128)(2,1)S(1)} collective-permute-done((bf16[304,768]{1,0:T(8,128)(2,1)S(1)}, bf16[304,768]{1,0:T(8,128)(2,1)S(1)}, u32[]{:S(2)}, u32[]{:S(2)}) %collective-permute-start.6) | collective-permute-done | bytes 466976 | tf_op jit(solution)/shard_map/ppermute | solution.py:319
  48.7 3.6 %collective-permute-start.8 = (bf16[160,768]{1,0:T(8,128)(2,1)S(1)}, bf16[160,768]{1,0:T(8,128)(2,1)}, u32[]{:S(2)}, u32[]{:S(2)}) collective-permute-start(bf16[160,768]{1,0:T(8,128)(2,1)S(1)} %slice.29), channel_id=1, source_target_pairs={{0,224},{32,0},{64,32},{96,64},{128,96},{160,128},{192,160},{224,1... | collective-permute-start | bytes 737288 | tf_op jit(solution)/shard_map/ppermute | solution.py:319
  52.6 6.4 %collective-permute-done.7.r_8_ = bf16[144,768]{1,0:T(8,128)(2,1)S(1)} collective-permute-done((bf16[144,768]{1,0:T(8,128)(2,1)S(1)}, bf16[144,768]{1,0:T(8,128)(2,1)S(1)}, u32[]{:S(2)}, u32[]{:S(2)}) %collective-permute-start.7) | collective-permute-done | bytes 221216 | tf_op jit(solution)/shard_map/ppermute | solution.py:319
  59.7 20.2 %attend.1 = (bf16[16,72,1536]{2,1,0:T(8,128)(2,1)S(1)}, f32[8,1152]{1,0:T(8,128)S(1)}) custom-call(bf16[4,2,160,768]{3,2,1,0:T(8,128)(2,1)} %bitcast.11, bf16[304,768]{1,0:T(8,128)(2,1)} %copy-done.2, bf16[304,768]{1,0:T(8,128)(2,1)} %copy-done.8, bf16[304,768]{1,0:T(8,128)(2,1)} %copy-done.9, bf16[304,768]{1,0:T(8,128)(2,1)} %copy-done.11, ...), custom_call_target="tpu_custom_call" | custom-call | flops 48922361856 | bytes 7077888 | tf_op jit(solution)/shard_map/attend/pallas_call | solution.py:151
  79.9 1.3 collective-permute-start.9
  81.3 3.0 %collective-permute-done.9.r_1_ = f32[8,1152]{1,0:T(8,128)S(1)} collective-permute-done((f32[8,1152]{1,0:T(8,128)S(1)}, f32[8,1152]{1,0:T(8,128)S(1)}, u32[]{:S(2)}, u32[]{:S(2)}) %collective-permute-start.9) | collective-permute-done | bytes 36896 | tf_op jit(solution)/shard_map/ppermute | solution.py:323
  85.7 1.9 %collective-permute-start.11 = (f32[8,1152]{1,0:T(8,128)}, f32[8,1152]{1,0:T(8,128)}, u32[]{:S(2)}, u32[]{:S(2)}) collective-permute-start(f32[8,1152]{1,0:T(8,128)} %merge.1.r_3_), channel_id=1, source_target_pairs={{0,8},{4,12},{8,0},{12,4},{1,9},{5,13},{9,1},{13,5},{2,10},{6,14},... | collective-permute-start | bytes 110600 | tf_op jit(solution)/shard_map/ppermute | solution.py:323
  87.6 1.9 %collective-permute-start.12 = (f32[8,1152]{1,0:T(8,128)}, f32[8,1152]{1,0:T(8,128)}, u32[]{:S(2)}, u32[]{:S(2)}) collective-permute-start(f32[8,1152]{1,0:T(8,128)} %merge.1.r_3_), channel_id=1, source_target_pairs={{0,12},{4,8},{8,4},{12,0},{1,13},{5,9},{9,5},{13,1},{2,14},{6,10},... | collective-permute-start | bytes 110600 | tf_op jit(solution)/shard_map/ppermute | solution.py:323
  90.3 1.6 %collective-permute-done.12.r_6_ = f32[8,1152]{1,0:T(8,128)} collective-permute-done((f32[8,1152]{1,0:T(8,128)}, f32[8,1152]{1,0:T(8,128)}, u32[]{:S(2)}, u32[]{:S(2)}) %collective-permute-start.12) | collective-permute-done | bytes 36896 | tf_op jit(solution)/shard_map/ppermute | solution.py:323
  92.7 4.2 %weigh.1 = bf16[2,4,144,768]{3,2,1,0:T(8,128)(2,1)} custom-call(s32[1]{0:T(128)} %bitcast.2.r_0_, f32[3]{0:T(128)S(1)} %subtract_add_fusion.r_1_, f32[8,1152]{1,0:T(8,128)S(1)} %copy-done.1, f32[8,1152]{1,0:T(8,128)} %merge.1.r_3_, f32[8,1152]{1,0:T(8,128)} %collective-permute-done.10.r_4_, f32[8,1152]{1,0:T(8,128)} %collective-permute-done.11.r_5_, ...), custom_call_target="tpu_custom_call" | custom-call | tf_op jit(solution)/shard_map/weigh/pallas_call | solution.py:244
  96.9 4.2 %all-to-all-start = ((bf16[8,144,768]{2,1,0:T(8,128)(2,1)}), bf16[8,144,768]{2,1,0:T(8,128)(2,1)S(1)}, u32[]{:S(2)}, u32[]{:S(2)}) async-start(bf16[8,144,768]{2,1,0:T(8,128)(2,1)} %bitcast.6), calls=%async_computation | async-start | bytes 3538944 | tf_op jit(solution)/shard_map/all_to_all | solution.py:359
  101.2 15.3 %all-to-all-done.r_1_ = bf16[8,144,768]{2,1,0:T(8,128)(2,1)S(1)} async-done(((bf16[8,144,768]{2,1,0:T(8,128)(2,1)}), bf16[8,144,768]{2,1,0:T(8,128)(2,1)S(1)}, u32[]{:S(2)}, u32[]{:S(2)}) %all-to-all-start) | async-done | bytes 1769504 | tf_op jit(solution)/shard_map/all_to_all | solution.py:359
  116.5 3.5 %project.2 = (bf16[144,1280]{1,0:T(8,128)(2,1)S(1)}, f32[144,1280]{1,0:T(8,128)S(1)}, bf16[144,768]{1,0:T(8,128)(2,1)S(1)}) custom-call(s32[2]{0:T(128)S(1)} %pad_add_fusion.r_0_, bf16[8,144,768]{2,1,0:T(8,128)(2,1)S(1)} %all-to-all-done.r_1_, f32[1,768]{1,0:T(1,128)S(1)} %reshape.14.r_2_, bf16[768,5120]{1,0:T(8,128)(2,1)} %r_2_.1), custom_call_target="tpu_custom_call" | custom-call | flops 4529848320 | bytes 3932160 | tf_op jit(solution)/shard_map/project/pallas_call | solution.py:303
  120.1 8.6 %collective-permute-start.13 = (bf16[144,1280]{1,0:T(8,128)(2,1)S(1)}, bf16[144,1280]{1,0:T(8,128)(2,1)S(1)}, u32[]{:S(2)}, u32[]{:S(2)}) collective-permute-start(bf16[144,1280]{1,0:T(8,128)(2,1)S(1)} %get-tuple-element.23), channel_id=1, source_target_pairs={{0,1},{1,0},{2,3},{3,2},{4,5},{5,4},{6,7},{7,6},{8,9},{9,8},{10,11... | collective-permute-start | bytes 1105928 | tf_op jit(solution)/shard_map/ppermute | solution.py:323
  128.7 1.2 collective-permute-done.13
  130.9 3.2 %project.3 = (bf16[144,1280]{1,0:T(8,128)(2,1)S(1)}, f32[144,1280]{1,0:T(8,128)S(1)}) custom-call(s32[2]{0:T(128)S(1)} %pad_add_fusion.1.r_0_, bf16[144,768]{1,0:T(8,128)(2,1)S(1)} %get-tuple-element.26.r_1_, bf16[768,5120]{1,0:T(8,128)(2,1)} %r_2_.1), custom_call_target="tpu_custom_call" | custom-call | flops 4529848320 | bytes 3932160 | tf_op jit(solution)/shard_map/project/pallas_call | solution.py:303
  134.9 5.0 %collective-permute-done.14 = bf16[144,1280]{1,0:T(8,128)(2,1)S(1)} collective-permute-done((bf16[144,1280]{1,0:T(8,128)(2,1)S(1)}, bf16[144,1280]{1,0:T(8,128)(2,1)S(1)}, u32[]{:S(2)}, u32[]{:S(2)}) %collective-permute-start.14) | collective-permute-done | bytes 368672 | tf_op jit(solution)/shard_map/ppermute | solution.py:323
  (61 shorter events, 11.3 us)
Async XLA Ops:
  6.5 53.2 %all-gather.3.cloned.1.call-start = ((), (), s32[]{:S(2)}) async-start(), calls=%async_computation.1 | async-start | bytes 2457600 | tf_op jit(solution)/shard_map/all_gather | solution.py:340
  8.4 16.9 %collective-permute-start = (bf16[304,768]{1,0:T(8,128)(2,1)S(1)}, bf16[304,768]{1,0:T(8,128)(2,1)S(1)}, u32[]{:S(2)}, u32[]{:S(2)}) collective-permute-start(bf16[304,768]{1,0:T(8,128)(2,1)S(1)} %pad_maximum_fusion.1.r_1_), channel_id=1, source_target_pairs={{0,32},{32,64},{64,96},{96,128},{128,160},{160,192},{192,224},{224... | collective-permute-start | bytes 1400840 | tf_op jit(solution)/shard_map/ppermute | solution.py:319
  11.0 14.4 %collective-permute-start.1 = (bf16[304,768]{1,0:T(8,128)(2,1)S(1)}, bf16[304,768]{1,0:T(8,128)(2,1)S(1)}, u32[]{:S(2)}, u32[]{:S(2)}) collective-permute-start(bf16[304,768]{1,0:T(8,128)(2,1)S(1)} %pad_maximum_fusion.1.r_1_), channel_id=1, source_target_pairs={{0,224},{32,0},{64,32},{96,64},{128,96},{160,128},{192,160},{224,1... | collective-permute-start | bytes 1400840 | tf_op jit(solution)/shard_map/ppermute | solution.py:319
  16.6 8.1 %collective-permute-start.2 = (bf16[160,768]{1,0:T(8,128)(2,1)S(1)}, bf16[160,768]{1,0:T(8,128)(2,1)S(1)}, u32[]{:S(2)}, u32[]{:S(2)}) collective-permute-start(bf16[160,768]{1,0:T(8,128)(2,1)S(1)} %get-tuple-element.32), channel_id=1, source_target_pairs={{0,16},{16,0},{1,17},{17,1},{2,18},{18,2},{3,19},{19,3},{4,20},{20... | collective-permute-start | bytes 737288 | tf_op jit(solution)/shard_map/ppermute | solution.py:323
  25.3 34.4 %copy-start.8 = (bf16[304,768]{1,0:T(8,128)(2,1)}, bf16[304,768]{1,0:T(8,128)(2,1)S(1)}, u32[]{:S(2)}) copy-start(bf16[304,768]{1,0:T(8,128)(2,1)S(1)} %collective-permute-done.r_2_) | copy-start | bytes 1400836
  25.3 34.4 %copy-start.9 = (bf16[304,768]{1,0:T(8,128)(2,1)}, bf16[304,768]{1,0:T(8,128)(2,1)S(1)}, u32[]{:S(2)}) copy-start(bf16[304,768]{1,0:T(8,128)(2,1)S(1)} %collective-permute-done.1.r_3_) | copy-start | bytes 1400836
  26.2 11.6 %collective-permute-start.4 = (bf16[304,768]{1,0:T(8,128)(2,1)S(1)}, bf16[304,768]{1,0:T(8,128)(2,1)S(1)}, u32[]{:S(2)}, u32[]{:S(2)}) collective-permute-start(bf16[304,768]{1,0:T(8,128)(2,1)S(1)} %collective-permute-done.1.r_3_), channel_id=1, source_target_pairs={{0,224},{32,0},{64,32},{96,64},{128,96},{160,128},{192,160},{224,1... | collective-permute-start | bytes 1400840 | tf_op jit(solution)/shard_map/ppermute | solution.py:319
  29.3 11.9 %collective-permute-start.3 = (bf16[304,768]{1,0:T(8,128)(2,1)S(1)}, bf16[304,768]{1,0:T(8,128)(2,1)S(1)}, u32[]{:S(2)}, u32[]{:S(2)}) collective-permute-start(bf16[304,768]{1,0:T(8,128)(2,1)S(1)} %collective-permute-done.r_2_), channel_id=1, source_target_pairs={{0,32},{32,64},{64,96},{96,128},{128,160},{160,192},{192,224},{224... | collective-permute-start | bytes 1400840 | tf_op jit(solution)/shard_map/ppermute | solution.py:319
  37.8 10.9 %collective-permute-start.6 = (bf16[304,768]{1,0:T(8,128)(2,1)S(1)}, bf16[304,768]{1,0:T(8,128)(2,1)S(1)}, u32[]{:S(2)}, u32[]{:S(2)}) collective-permute-start(bf16[304,768]{1,0:T(8,128)(2,1)S(1)} %collective-permute-done.4.r_5_), channel_id=1, source_target_pairs={{0,224},{32,0},{64,32},{96,64},{128,96},{160,128},{192,160},{224,1... | collective-permute-start | bytes 1400840 | tf_op jit(solution)/shard_map/ppermute | solution.py:319
  41.2 17.8 %copy-start.11 = (bf16[304,768]{1,0:T(8,128)(2,1)}, bf16[304,768]{1,0:T(8,128)(2,1)S(1)}, u32[]{:S(2)}) copy-start(bf16[304,768]{1,0:T(8,128)(2,1)S(1)} %collective-permute-done.3.r_4_) | copy-start | bytes 1400836
  41.2 11.1 %collective-permute-start.5 = (bf16[304,768]{1,0:T(8,128)(2,1)S(1)}, bf16[304,768]{1,0:T(8,128)(2,1)S(1)}, u32[]{:S(2)}, u32[]{:S(2)}) collective-permute-start(bf16[304,768]{1,0:T(8,128)(2,1)S(1)} %collective-permute-done.3.r_4_), channel_id=1, source_target_pairs={{0,32},{32,64},{64,96},{96,128},{128,160},{160,192},{192,224},{224... | collective-permute-start | bytes 1400840 | tf_op jit(solution)/shard_map/ppermute | solution.py:319
  48.7 11.0 %collective-permute-start.8 = (bf16[160,768]{1,0:T(8,128)(2,1)S(1)}, bf16[160,768]{1,0:T(8,128)(2,1)}, u32[]{:S(2)}, u32[]{:S(2)}) collective-permute-start(bf16[160,768]{1,0:T(8,128)(2,1)S(1)} %slice.29), channel_id=1, source_target_pairs={{0,224},{32,0},{64,32},{96,64},{128,96},{160,128},{192,160},{224,1... | collective-permute-start | bytes 737288 | tf_op jit(solution)/shard_map/ppermute | solution.py:319
  52.3 6.7 %copy-start.5 = (bf16[304,768]{1,0:T(8,128)(2,1)}, bf16[304,768]{1,0:T(8,128)(2,1)S(1)}, u32[]{:S(2)}) copy-start(bf16[304,768]{1,0:T(8,128)(2,1)S(1)} %collective-permute-done.5.r_6_) | copy-start | bytes 1400836
  52.4 6.7 %collective-permute-start.7 = (bf16[144,768]{1,0:T(8,128)(2,1)S(1)}, bf16[144,768]{1,0:T(8,128)(2,1)S(1)}, u32[]{:S(2)}, u32[]{:S(2)}) collective-permute-start(bf16[144,768]{1,0:T(8,128)(2,1)S(1)} %slice.28), channel_id=1, source_target_pairs={{0,32},{32,64},{64,96},{96,128},{128,160},{160,192},{192,224},{224... | collective-permute-start | bytes 663560 | tf_op jit(solution)/shard_map/ppermute | solution.py:319
  59.7 21.5 %copy-start.6 = (f32[4,3,128]{2,0,1:T(4,128)S(1)}, f32[4,3,128]{2,0,1:T(4,128)}, u32[]{:S(2)}) copy-start(f32[4,3,128]{2,0,1:T(4,128)} %param.12) | copy-start | bytes 18436
  79.9 4.4 %collective-permute-start.9 = (f32[8,1152]{1,0:T(8,128)S(1)}, f32[8,1152]{1,0:T(8,128)S(1)}, u32[]{:S(2)}, u32[]{:S(2)}) collective-permute-start(f32[8,1152]{1,0:T(8,128)S(1)} %get-tuple-element.20.r_0_.r_2_), channel_id=1, source_target_pairs={{0,16},{16,0},{1,17},{17,1},{2,18},{18,2},{3,19},{19,3},{4,20},{20... | collective-permute-start | bytes 110600 | tf_op jit(solution)/shard_map/ppermute | solution.py:323
  85.7 3.9 %collective-permute-start.10 = (f32[8,1152]{1,0:T(8,128)}, f32[8,1152]{1,0:T(8,128)}, u32[]{:S(2)}, u32[]{:S(2)}) collective-permute-start(f32[8,1152]{1,0:T(8,128)} %merge.1.r_3_), channel_id=1, source_target_pairs={{0,4},{4,0},{8,12},{12,8},{1,5},{5,1},{9,13},{13,9},{2,6},{6,2},{1... | collective-permute-start | bytes 110600 | tf_op jit(solution)/shard_map/ppermute | solution.py:323
  85.7 4.6 %collective-permute-start.11 = (f32[8,1152]{1,0:T(8,128)}, f32[8,1152]{1,0:T(8,128)}, u32[]{:S(2)}, u32[]{:S(2)}) collective-permute-start(f32[8,1152]{1,0:T(8,128)} %merge.1.r_3_), channel_id=1, source_target_pairs={{0,8},{4,12},{8,0},{12,4},{1,9},{5,13},{9,1},{13,5},{2,10},{6,14},... | collective-permute-start | bytes 110600 | tf_op jit(solution)/shard_map/ppermute | solution.py:323
  87.6 4.3 %collective-permute-start.12 = (f32[8,1152]{1,0:T(8,128)}, f32[8,1152]{1,0:T(8,128)}, u32[]{:S(2)}, u32[]{:S(2)}) collective-permute-start(f32[8,1152]{1,0:T(8,128)} %merge.1.r_3_), channel_id=1, source_target_pairs={{0,12},{4,8},{8,4},{12,0},{1,13},{5,9},{9,5},{13,1},{2,14},{6,10},... | collective-permute-start | bytes 110600 | tf_op jit(solution)/shard_map/ppermute | solution.py:323
  96.9 19.6 %all-to-all-start = ((bf16[8,144,768]{2,1,0:T(8,128)(2,1)}), bf16[8,144,768]{2,1,0:T(8,128)(2,1)S(1)}, u32[]{:S(2)}, u32[]{:S(2)}) async-start(bf16[8,144,768]{2,1,0:T(8,128)(2,1)} %bitcast.6), calls=%async_computation | async-start | bytes 3538944 | tf_op jit(solution)/shard_map/all_to_all | solution.py:359
  120.1 9.9 %collective-permute-start.13 = (bf16[144,1280]{1,0:T(8,128)(2,1)S(1)}, bf16[144,1280]{1,0:T(8,128)(2,1)S(1)}, u32[]{:S(2)}, u32[]{:S(2)}) collective-permute-start(bf16[144,1280]{1,0:T(8,128)(2,1)S(1)} %get-tuple-element.23), channel_id=1, source_target_pairs={{0,1},{1,0},{2,3},{3,2},{4,5},{5,4},{6,7},{7,6},{8,9},{9,8},{10,11... | collective-permute-start | bytes 1105928 | tf_op jit(solution)/shard_map/ppermute | solution.py:323
  130.0 9.9 %copy-start.3 = (bf16[144,1280]{1,0:T(8,128)(2,1)S(1)}, bf16[144,1280]{1,0:T(8,128)(2,1)}, u32[]{:S(2)}) copy-start(bf16[144,1280]{1,0:T(8,128)(2,1)} %param.15) | copy-start | bytes 1105924
  130.0 9.9 %collective-permute-start.14 = (bf16[144,1280]{1,0:T(8,128)(2,1)S(1)}, bf16[144,1280]{1,0:T(8,128)(2,1)S(1)}, u32[]{:S(2)}, u32[]{:S(2)}) collective-permute-start(bf16[144,1280]{1,0:T(8,128)(2,1)S(1)} %add_convert_fusion.1), channel_id=1, source_target_pairs={{0,2},{2,0},{1,3},{3,1},{4,6},{6,4},{5,7},{7,5},{8,10},{10,8},{9,1... | collective-permute-start | bytes 1105928 | tf_op jit(solution)/shard_map/ppermute | solution.py:323
  134.2 5.8 %collective-permute-start.15 = (bf16[144,1280]{1,0:T(8,128)(2,1)S(1)}, bf16[144,1280]{1,0:T(8,128)(2,1)S(1)}, u32[]{:S(2)}, u32[]{:S(2)}) collective-permute-start(bf16[144,1280]{1,0:T(8,128)(2,1)S(1)} %get-tuple-element.28), channel_id=1, source_target_pairs={{0,1},{1,0},{2,3},{3,2},{4,5},{5,4},{6,7},{7,6},{8,9},{9,8},{10,11... | collective-permute-start | bytes 1105928 | tf_op jit(solution)/shard_map/ppermute | solution.py:323
  (7 other events, 15.9 us)
Sparse Core Ops, SparseCore 0:
  26.3 33.2 all-gather.2

commit v7 on v6

--- a/solution.py
+++ b/solution.py
@@ -21,7 +21,7 @@
 
 
 def attend_kernel(rows, spans, slots, spots, *refs):
-    q_refs = [refs[0].at[i // 2, i % 2] for i in range(slots)]
+    q_refs = [refs[0].at[i] for i in range(slots)]
     kv_refs, refs = refs[1:-10], refs[-10:]
     o_ref, lse_ref, q3, k3, v3, q_s, k_s, v_s, lse_s, order = refs
     head = pl.program_id(0)
@@ -142,12 +142,11 @@
         lse_ref[...] = jnp.transpose(lse_s[...].reshape(blocks * RUN, HD))[: lse_ref.shape[0], :]
 
 
-def attend(q_pair, kv_parts, spots, spans, rows, heads):
-    ny, _, pad, width = q_pair.shape
-    slots = 2 * ny
+def attend(q_all, kv_parts, spots, spans, rows, heads):
+    slots, pad, width = q_all.shape
     blocks = slots * rows // RUN
     keys = len(spots) * rows // RUN
-    ins = [pltpu.with_memory_space_constraint(x, pltpu.HBM) for x in [q_pair, *kv_parts]]
+    ins = [pltpu.with_memory_space_constraint(x, pltpu.HBM) for x in [q_all, *kv_parts]]
     return pl.pallas_call(
         lambda *r: attend_kernel(rows, spans, slots, spots, *r),
         out_shape=[
@@ -157,7 +156,7 @@
         grid_spec=pltpu.PrefetchScalarGridSpec(
             num_scalar_prefetch=0,
             grid=(heads,),
-            in_specs=[pl.BlockSpec((ny, 2, pad, 2 * HD), lambda h: (0, 0, 0, h))]
+            in_specs=[pl.BlockSpec((slots, pad, 2 * HD), lambda h: (0, 0, h))]
             + [pl.BlockSpec((x.shape[0], 2 * HD), lambda h: (0, h)) for x in kv_parts],
             out_specs=[
                 pl.BlockSpec((blocks, RUN, 4 * HD), lambda h: (0, 0, h)),
@@ -194,19 +193,14 @@
     return top + jnp.log2(total)
 
 
-def reorder(x, rows, mask):
-    slots = x.shape[1] // rows
-    return jnp.concatenate([x[:, (s ^ mask) * rows : ((s ^ mask) + 1) * rows] for s in range(slots)], 1)
-
-
-def merge_kernel(rows, a_ref, b_ref, o_ref):
-    o_ref[...] = logsum([a_ref[...], reorder(b_ref[...], rows, 1)])
-
-
-def merge(a, b, rows):
+def merge_kernel(a_ref, b_ref, o_ref):
+    o_ref[...] = logsum([a_ref[...], b_ref[...]])
+
+
+def merge(a, b):
     vm = pl.BlockSpec(memory_space=pltpu.VMEM)
     return pl.pallas_call(
-        lambda *r: merge_kernel(rows, *r),
+        merge_kernel,
         out_shape=jax.ShapeDtypeStruct(a.shape, a.dtype),
         in_specs=[vm, vm],
         out_specs=vm,
@@ -215,10 +209,10 @@
     )(a, b)
 
 
-def weigh_kernel(heads, where, lam, lse_ref, *refs):
+def weigh_kernel(heads, lam, lse_ref, *refs):
     all_refs, o_ref, out_ref, w_s = refs[:-3], refs[-3], refs[-2], refs[-1]
     j = pl.program_id(0)
-    rows = out_ref.shape[2]
+    slots, rows = out_ref.shape[:2]
 
     @pl.when(j == 0)
     def _():
@@ -227,36 +221,33 @@
         w = jnp.concatenate([w, jnp.zeros((HD - w.shape[0], w.shape[1]), f32)], 0)
         w_s[...] = jnp.transpose(w)
 
-    for d in range(2):
-        w = w_s[pl.ds(pl.multiple_of((2 * j + d) * rows, rows), rows), :]
+    for d in range(slots):
+        w = w_s[pl.ds(pl.multiple_of((slots * j + d) * rows, rows), rows), :]
         o = o_ref[d * (rows // RUN) : (d + 1) * (rows // RUN)]
-        place = where[0] ^ d
         for h in range(heads):
             w1 = w[:, 2 * h : 2 * h + 1]
             w2 = w[:, 2 * h + 1 : 2 * h + 2] * lam[h]
             o1 = o[:, :, h * 4 * HD : h * 4 * HD + 2 * HD].reshape(rows, 2 * HD).astype(f32)
             o2 = o[:, :, h * 4 * HD + 2 * HD : (h + 1) * 4 * HD].reshape(rows, 2 * HD).astype(f32)
-            out_ref[place, 0, :, h * 2 * HD : (h + 1) * 2 * HD] = (w1 * o1 - w2 * o2).astype(bf16)
-
-
-def weigh(where, lam, lse, lses, o, rows, heads):
-    pairs = lse.shape[1] // rows // 2
+            out_ref[d, :, h * 2 * HD : (h + 1) * 2 * HD] = (w1 * o1 - w2 * o2).astype(bf16)
+
+
+def weigh(lam, lse, lses, o, rows, heads):
+    slots = lse.shape[1] // rows
     return pl.pallas_call(
         lambda *r: weigh_kernel(heads, *r),
-        out_shape=jax.ShapeDtypeStruct((2, pairs, rows, heads * 2 * HD), bf16),
+        out_shape=jax.ShapeDtypeStruct((slots, rows, heads * 2 * HD), bf16),
         grid_spec=pltpu.PrefetchScalarGridSpec(
-            num_scalar_prefetch=2,
-            grid=(pairs,),
-            in_specs=[pl.BlockSpec(lse.shape, lambda j, *_: (0, 0))] * (1 + len(lses))
-            + [pl.BlockSpec((2 * rows // RUN, RUN, heads * 4 * HD), lambda j, *_: (j, 0, 0))],
-            out_specs=pl.BlockSpec(
-                (2, 1, rows, heads * 2 * HD), lambda j, where, lam: (0, j, 0, 0)
-            ),
-            scratch_shapes=[pltpu.VMEM((2 * pairs * rows, HD), f32)],
+            num_scalar_prefetch=1,
+            grid=(slots // 2,),
+            in_specs=[pl.BlockSpec(lse.shape, lambda j, lam: (0, 0))] * (1 + len(lses))
+            + [pl.BlockSpec((2 * rows // RUN, RUN, heads * 4 * HD), lambda j, lam: (j, 0, 0))],
+            out_specs=pl.BlockSpec((2, rows, heads * 2 * HD), lambda j, lam: (j, 0, 0)),
+            scratch_shapes=[pltpu.VMEM((slots * rows, HD), f32)],
         ),
         compiler_params=pltpu.CompilerParams(vmem_limit_bytes=20 << 20),
         name="weigh",
-    )(where, lam, lse, *lses, o)
+    )(lam, lse, *lses, o)
 
 
 def norm(got_ref, gain_ref, n_s, heads):
@@ -329,23 +320,19 @@
     heads = lambda_vecs.shape[1]
     block = ((positions[::RUN].astype(f32) + 0.5) * (1.0 / RUN)).astype(jnp.int32).astype(bf16)
     ids = jnp.broadcast_to(jnp.pad(block, (0, width - block.shape[0]))[None, :], (16, width))
-    where = lax.axis_index("h").astype(jnp.int32).reshape(1)
-
     q_mine = jnp.concatenate([queries, ids], 0)
+    q_all = lax.all_to_all(jnp.broadcast_to(q_mine[None], (nh * ny, *q_mine.shape)), ("h", "y"), 0, 0)
     kv_mine = jnp.concatenate([keys, values, ids], 0)
-    q_far = swap(q_mine, "h", nh, 1)
     up, down = shift(kv_mine, "z", nz, 1), shift(kv_mine, "z", nz, -1)
     kv_parts = [kv_mine, up, down]
-    up, down, q_far = lax.optimization_barrier((up, down, q_far))
-    q_pair = lax.all_gather(jnp.stack([q_mine, q_far]), "y", axis=0)
     for _ in range(2):
         up, down = shift(up, "z", nz, 1), shift(down, "z", nz, -1)
         kv_parts += [up, down]
     kv_parts += [shift(up[:rows], "z", nz, 1), shift(down[rows:], "z", nz, -1)]
     spots = [(i, 0, i, rows) for i in range(nz - 1)] + [(nz - 1, 0, nz, 0)]
-    o, lse = attend(q_pair, kv_parts, spots, (4, 8, 12, 16), rows, heads)
-
-    pair = merge(lse, swap(lse, "h", nh, 1), rows)
+    o, lse = attend(q_all, kv_parts, spots, (4, 8, 12, 16), rows, heads)
+
+    pair = merge(lse, swap(lse, "h", nh, 1))
     others = [swap(pair, "y", ny, d) for d in range(1, ny)]
 
     lam = (
@@ -353,9 +340,8 @@
         - jnp.exp(jnp.sum(lambda_vecs[2] * lambda_vecs[3], -1))
         + lambda_init
     )
-    parts = weigh(where, lam, lse, [pair] + others, o, rows, heads)
-
-    parts = parts.reshape(nh * ny, rows, width)
+    parts = weigh(lam, lse, [pair] + others, o, rows, heads)
+
     got = lax.all_to_all(parts, ("h", "y"), 0, 0, tiled=False)
     l, c = lax.axis_index("l"), lax.axis_index("c")
     cols = [jnp.stack([r * nc + 1 - c, r * nc + c]).astype(jnp.int32) for r in (1 - l, l)]

time: 149 us -> 139 us (0.933)
  between operations: 13.5 us -> 0.2 us
  starting transfers between devices: 39.9 us -> 46.4 us
  other arithmetic: 4.19 us -> 2.26 us
  Pallas kernels: 31.9 us -> 30.3 us
    all_to_all x0 -> x1, starting transfers between devices: none -> 7.61 us  [per_device(): lax.all_to_all(jnp.broadcast_to(q_mine[None], (nh * ny, *q_mine.shape)),...]
    ppermute x8, waiting for transfers between devices: 23 us -> 30.3 us  [shift(): return lax.ppermute(x, axis, [(i, (i + step) % size) for i in range(size)])]
    ppermute x8 -> x7, waiting for transfers between devices: 16.9 us -> 10.8 us  [swap(): return lax.ppermute(x, axis, [(i, i ^ mask) for i in range(size)])]
    another operation x2 -> x0, other arithmetic: 1.84 us -> none  [per_device(): q_pair = lax.all_gather(jnp.stack([q_mine, q_far]), 'y', axis=0)]
    ppermute x8 -> x7, starting transfers between devices: 18.2 us -> 17.3 us  [swap(): return lax.ppermute(x, axis, [(i, i ^ mask) for i in range(size)])]
  transfers between devices with their start and end apart: 18 -> 17, of which waited for: 11 -> 10; matrix products, arithmetic and copies ran while one was open for 1% -> 0% of each run, Pallas kernels for 2% -> 2%
where the time goes in v7:
time: 139 us
  waiting for transfers between devices  55.5 us (40%)
  starting transfers between devices  46.4 us (33%)
  Pallas kernels  30.3 us (22%)
  local copies, waits for them, and re-layouts  4.25 us (3%)
  other arithmetic  2.26 us (2%)
    ppermute x8, waiting for transfers between devices, shift(): return lax.ppermute(x, axis, [(i, (i + step) % size) for i in range(size)])  30.3 us
    pallas_call x1, Pallas kernels, attend(): pl.pallas_call(lambda *r: attend_kernel(rows, spans, slots, spots, *r), o...  20.2 us
    ppermute x7, starting transfers between devices, swap(): return lax.ppermute(x, axis, [(i, i ^ mask) for i in range(size)])  17.3 us
    ppermute x8, starting transfers between devices, shift(): return lax.ppermute(x, axis, [(i, (i + step) % size) for i in range(size)])  16.2 us
    all_to_all x1, waiting for transfers between devices, per_device(): got = lax.all_to_all(parts, ('h', 'y'), 0, 0, tiled=False)  14.5 us
    ppermute x7, waiting for transfers between devices, swap(): return lax.ppermute(x, axis, [(i, i ^ mask) for i in range(size)])  10.8 us
    all_to_all x1, starting transfers between devices, per_device(): lax.all_to_all(jnp.broadcast_to(q_mine[None], (nh * ny, *q_mine.shape)),...  7.61 us
    pallas_call x2, Pallas kernels, project(): pl.pallas_call(lambda *r: project_kernel(heads, *r), out_shape=outs, grid...  6.73 us
  transfers between devices with their start and end apart: 17, of which 10 were waited for; matrix products, arithmetic and copies ran while one was open for 0% of the time, Pallas kernels for 2%

profile of v7, /device:TPU:1, one launch (start us, length us, event | category | flops | bytes accessed | tf_op | source)
XLA Modules:
  0.0 138.9 jit_solution(3643176180757028681)
XLA Ops:
  1.8 1.4 %broadcast_in_dim.5 = bf16[8,160,768]{2,1,0:T(8,128)(2,1)} broadcast(bf16[160,768]{1,0:T(8,128)(2,1)S(1)} %pad_maximum_fusion.1), dimensions={1,2} | broadcast | bytes 2211840 | tf_op jit(solution)/shard_map/broadcast_in_dim | solution.py:324
  3.2 7.6 %all-to-all-start = ((bf16[8,160,768]{2,1,0:T(8,128)(2,1)}), bf16[8,160,768]{2,1,0:T(8,128)(2,1)S(1)}, u32[]{:S(2)}, u32[]{:S(2)}) async-start(bf16[8,160,768]{2,1,0:T(8,128)(2,1)} %broadcast_in_dim.5), calls=%async_computation | async-start | bytes 3932160 | tf_op jit(solution)/shard_map/all_to_all | solution.py:324
  10.9 5.7 %collective-permute-start.1 = (bf16[304,768]{1,0:T(8,128)(2,1)S(1)}, bf16[304,768]{1,0:T(8,128)(2,1)S(1)}, u32[]{:S(2)}, u32[]{:S(2)}) collective-permute-start(bf16[304,768]{1,0:T(8,128)(2,1)S(1)} %pad_maximum_fusion.r_1_), channel_id=1, source_target_pairs={{0,224},{32,0},{64,32},{96,64},{128,96},{160,128},{192,160},{224,1... | collective-permute-start | bytes 1400840 | tf_op jit(solution)/shard_map/ppermute | solution.py:310
  16.5 9.0 %collective-permute-done.1.r_3_ = bf16[304,768]{1,0:T(8,128)(2,1)S(1)} collective-permute-done((bf16[304,768]{1,0:T(8,128)(2,1)S(1)}, bf16[304,768]{1,0:T(8,128)(2,1)S(1)}, u32[]{:S(2)}, u32[]{:S(2)}) %collective-permute-start.1) | collective-permute-done | bytes 466976 | tf_op jit(solution)/shard_map/ppermute | solution.py:310
  25.6 3.4 %collective-permute-start.3 = (bf16[304,768]{1,0:T(8,128)(2,1)S(1)}, bf16[304,768]{1,0:T(8,128)(2,1)S(1)}, u32[]{:S(2)}, u32[]{:S(2)}) collective-permute-start(bf16[304,768]{1,0:T(8,128)(2,1)S(1)} %collective-permute-done.1.r_3_), channel_id=1, source_target_pairs={{0,224},{32,0},{64,32},{96,64},{128,96},{160,128},{192,160},{224,1... | collective-permute-start | bytes 1400840 | tf_op jit(solution)/shard_map/ppermute | solution.py:310
  29.0 8.1 %collective-permute-done.3.r_5_ = bf16[304,768]{1,0:T(8,128)(2,1)S(1)} collective-permute-done((bf16[304,768]{1,0:T(8,128)(2,1)S(1)}, bf16[304,768]{1,0:T(8,128)(2,1)S(1)}, u32[]{:S(2)}, u32[]{:S(2)}) %collective-permute-start.3) | collective-permute-done | bytes 466976 | tf_op jit(solution)/shard_map/ppermute | solution.py:310
  37.1 3.4 %collective-permute-start.5 = (bf16[304,768]{1,0:T(8,128)(2,1)S(1)}, bf16[304,768]{1,0:T(8,128)(2,1)S(1)}, u32[]{:S(2)}, u32[]{:S(2)}) collective-permute-start(bf16[304,768]{1,0:T(8,128)(2,1)S(1)} %collective-permute-done.3.r_5_), channel_id=1, source_target_pairs={{0,224},{32,0},{64,32},{96,64},{128,96},{160,128},{192,160},{224,1... | collective-permute-start | bytes 1400840 | tf_op jit(solution)/shard_map/ppermute | solution.py:310
  40.5 7.2 %collective-permute-done.5.r_7_ = bf16[304,768]{1,0:T(8,128)(2,1)S(1)} collective-permute-done((bf16[304,768]{1,0:T(8,128)(2,1)S(1)}, bf16[304,768]{1,0:T(8,128)(2,1)S(1)}, u32[]{:S(2)}, u32[]{:S(2)}) %collective-permute-start.5) | collective-permute-done | bytes 466976 | tf_op jit(solution)/shard_map/ppermute | solution.py:310
  47.7 3.5 %collective-permute-start.7 = (bf16[160,768]{1,0:T(8,128)(2,1)S(1)}, bf16[160,768]{1,0:T(8,128)(2,1)}, u32[]{:S(2)}, u32[]{:S(2)}) collective-permute-start(bf16[160,768]{1,0:T(8,128)(2,1)S(1)} %slice.29), channel_id=1, source_target_pairs={{0,224},{32,0},{64,32},{96,64},{128,96},{160,128},{192,160},{224,1... | collective-permute-start | bytes 737288 | tf_op jit(solution)/shard_map/ppermute | solution.py:310
  51.5 6.0 %collective-permute-done.6.r_8_ = bf16[144,768]{1,0:T(8,128)(2,1)S(1)} collective-permute-done((bf16[144,768]{1,0:T(8,128)(2,1)S(1)}, bf16[144,768]{1,0:T(8,128)(2,1)S(1)}, u32[]{:S(2)}, u32[]{:S(2)}) %collective-permute-start.6) | collective-permute-done | bytes 221216 | tf_op jit(solution)/shard_map/ppermute | solution.py:310
  58.2 1.3 copy-done
  59.5 20.2 %attend.1 = (bf16[16,72,1536]{2,1,0:T(8,128)(2,1)S(1)}, f32[8,1152]{1,0:T(8,128)S(1)}) custom-call(bf16[8,160,768]{2,1,0:T(8,128)(2,1)} %copy-done, bf16[304,768]{1,0:T(8,128)(2,1)} %copy-done.1, bf16[304,768]{1,0:T(8,128)(2,1)} %copy-done.10, bf16[304,768]{1,0:T(8,128)(2,1)} %copy-done.9, bf16[304,768]{1,0:T(8,128)(2,1)} %copy-done.12, ...), custom_call_target="tpu_custom_call" | custom-call | flops 48922361856 | bytes 7077888 | tf_op jit(solution)/shard_map/attend/pallas_call | solution.py:150
  79.7 3.8 %collective-permute-start.8 = (f32[8,1152]{1,0:T(8,128)S(1)}, f32[8,1152]{1,0:T(8,128)S(1)}, u32[]{:S(2)}, u32[]{:S(2)}) collective-permute-start(f32[8,1152]{1,0:T(8,128)S(1)} %get-tuple-element.14.a_ref.r_1_), channel_id=1, source_target_pairs={{0,16},{16,0},{1,17},{17,1},{2,18},{18,2},{3,19},{19,3},{4,20},{20... | collective-permute-start | bytes 110600 | tf_op jit(solution)/shard_map/ppermute | solution.py:314
  84.9 1.4 %collective-permute-start.10 = (f32[8,1152]{1,0:T(8,128)S(1)}, f32[8,1152]{1,0:T(8,128)S(1)}, u32[]{:S(2)}, u32[]{:S(2)}) collective-permute-start(f32[8,1152]{1,0:T(8,128)S(1)} %merge.1.r_2_), channel_id=1, source_target_pairs={{0,8},{4,12},{8,0},{12,4},{1,9},{5,13},{9,1},{13,5},{2,10},{6,14},... | collective-permute-start | bytes 110600 | tf_op jit(solution)/shard_map/ppermute | solution.py:314
  86.4 1.2 collective-permute-start.9
  87.6 1.7 %collective-permute-done.10.r_4_ = f32[8,1152]{1,0:T(8,128)S(1)} collective-permute-done((f32[8,1152]{1,0:T(8,128)S(1)}, f32[8,1152]{1,0:T(8,128)S(1)}, u32[]{:S(2)}, u32[]{:S(2)}) %collective-permute-start.10) | collective-permute-done | bytes 36896 | tf_op jit(solution)/shard_map/ppermute | solution.py:314
  89.3 1.3 collective-permute-done.11.r_5_
  90.6 3.3 %weigh.1 = bf16[8,144,768]{2,1,0:T(8,128)(2,1)} custom-call(f32[3]{0:T(128)S(1)} %subtract_add_fusion.r_0_, f32[8,1152]{1,0:T(8,128)S(1)} %get-tuple-element.14.a_ref.r_1_, f32[8,1152]{1,0:T(8,128)S(1)} %merge.1.r_2_, f32[8,1152]{1,0:T(8,128)S(1)} %collective-permute-done.9.r_3_, f32[8,1152]{1,0:T(8,128)S(1)} %collective-permute-done.10.r_4_, ...), custom_call_target="tpu_custom_call" | custom-call | tf_op jit(solution)/shard_map/weigh/pallas_call | solution.py:237
  93.9 5.3 %all-to-all-start.1 = ((bf16[8,144,768]{2,1,0:T(8,128)(2,1)}), bf16[8,144,768]{2,1,0:T(8,128)(2,1)S(1)}, u32[]{:S(2)}, u32[]{:S(2)}) async-start(bf16[8,144,768]{2,1,0:T(8,128)(2,1)} %weigh.1), calls=%async_computation.1 | async-start | bytes 3538944 | tf_op jit(solution)/shard_map/all_to_all | solution.py:345
  99.3 14.5 %all-to-all-done.1.r_1_ = bf16[8,144,768]{2,1,0:T(8,128)(2,1)S(1)} async-done(((bf16[8,144,768]{2,1,0:T(8,128)(2,1)}), bf16[8,144,768]{2,1,0:T(8,128)(2,1)S(1)}, u32[]{:S(2)}, u32[]{:S(2)}) %all-to-all-start.1) | async-done | bytes 1769504 | tf_op jit(solution)/shard_map/all_to_all | solution.py:345
  113.8 3.5 %project.2 = (bf16[144,1280]{1,0:T(8,128)(2,1)S(1)}, f32[144,1280]{1,0:T(8,128)S(1)}, bf16[144,768]{1,0:T(8,128)(2,1)S(1)}) custom-call(s32[2]{0:T(128)S(1)} %pad_add_fusion.r_0_, bf16[8,144,768]{2,1,0:T(8,128)(2,1)S(1)} %all-to-all-done.1.r_1_, f32[1,768]{1,0:T(1,128)S(1)} %reshape.7.r_2_, bf16[768,5120]{1,0:T(8,128)(2,1)} %r_2_.1), custom_call_target="tpu_custom_call" | custom-call | flops 4529848320 | bytes 3932160 | tf_op jit(solution)/shard_map/project/pallas_call | solution.py:294
  117.3 9.4 %collective-permute-start.12 = (bf16[144,1280]{1,0:T(8,128)(2,1)S(1)}, bf16[144,1280]{1,0:T(8,128)(2,1)S(1)}, u32[]{:S(2)}, u32[]{:S(2)}) collective-permute-start(bf16[144,1280]{1,0:T(8,128)(2,1)S(1)} %get-tuple-element.17), channel_id=1, source_target_pairs={{0,1},{1,0},{2,3},{3,2},{4,5},{5,4},{6,7},{7,6},{8,9},{9,8},{10,11... | collective-permute-start | bytes 1105928 | tf_op jit(solution)/shard_map/ppermute | solution.py:314
  128.7 3.2 %project.3 = (bf16[144,1280]{1,0:T(8,128)(2,1)S(1)}, f32[144,1280]{1,0:T(8,128)S(1)}) custom-call(s32[2]{0:T(128)S(1)} %pad_add_fusion.1.r_0_, bf16[144,768]{1,0:T(8,128)(2,1)S(1)} %get-tuple-element.20.r_1_, bf16[768,5120]{1,0:T(8,128)(2,1)} %r_2_.1), custom_call_target="tpu_custom_call" | custom-call | flops 4529848320 | bytes 3932160 | tf_op jit(solution)/shard_map/project/pallas_call | solution.py:294
  132.7 5.3 %collective-permute-done.13 = bf16[144,1280]{1,0:T(8,128)(2,1)S(1)} collective-permute-done((bf16[144,1280]{1,0:T(8,128)(2,1)S(1)}, bf16[144,1280]{1,0:T(8,128)(2,1)S(1)}, u32[]{:S(2)}, u32[]{:S(2)}) %collective-permute-start.13) | collective-permute-done | bytes 368672 | tf_op jit(solution)/shard_map/ppermute | solution.py:314
  (60 shorter events, 8.0 us)
Async XLA Ops:
  3.2 55.0 %all-to-all-start = ((bf16[8,160,768]{2,1,0:T(8,128)(2,1)}), bf16[8,160,768]{2,1,0:T(8,128)(2,1)S(1)}, u32[]{:S(2)}, u32[]{:S(2)}) async-start(bf16[8,160,768]{2,1,0:T(8,128)(2,1)} %broadcast_in_dim.5), calls=%async_computation | async-start | bytes 3932160 | tf_op jit(solution)/shard_map/all_to_all | solution.py:324
  10.8 47.4 %copy-start.1 = (bf16[304,768]{1,0:T(8,128)(2,1)}, bf16[304,768]{1,0:T(8,128)(2,1)S(1)}, u32[]{:S(2)}) copy-start(bf16[304,768]{1,0:T(8,128)(2,1)S(1)} %pad_maximum_fusion.r_1_) | copy-start | bytes 1400836
  10.9 14.7 %collective-permute-start.1 = (bf16[304,768]{1,0:T(8,128)(2,1)S(1)}, bf16[304,768]{1,0:T(8,128)(2,1)S(1)}, u32[]{:S(2)}, u32[]{:S(2)}) collective-permute-start(bf16[304,768]{1,0:T(8,128)(2,1)S(1)} %pad_maximum_fusion.r_1_), channel_id=1, source_target_pairs={{0,224},{32,0},{64,32},{96,64},{128,96},{160,128},{192,160},{224,1... | collective-permute-start | bytes 1400840 | tf_op jit(solution)/shard_map/ppermute | solution.py:310
  16.5 12.5 %collective-permute-start = (bf16[304,768]{1,0:T(8,128)(2,1)S(1)}, bf16[304,768]{1,0:T(8,128)(2,1)S(1)}, u32[]{:S(2)}, u32[]{:S(2)}) collective-permute-start(bf16[304,768]{1,0:T(8,128)(2,1)S(1)} %pad_maximum_fusion.r_1_), channel_id=1, source_target_pairs={{0,32},{32,64},{64,96},{96,128},{128,160},{160,192},{192,224},{224... | collective-permute-start | bytes 1400840 | tf_op jit(solution)/shard_map/ppermute | solution.py:310
  25.6 15.0 %copy-start.9 = (bf16[304,768]{1,0:T(8,128)(2,1)}, bf16[304,768]{1,0:T(8,128)(2,1)S(1)}, u32[]{:S(2)}) copy-start(bf16[304,768]{1,0:T(8,128)(2,1)S(1)} %collective-permute-done.1.r_3_) | copy-start | bytes 1400836
  25.6 11.5 %collective-permute-start.3 = (bf16[304,768]{1,0:T(8,128)(2,1)S(1)}, bf16[304,768]{1,0:T(8,128)(2,1)S(1)}, u32[]{:S(2)}, u32[]{:S(2)}) collective-permute-start(bf16[304,768]{1,0:T(8,128)(2,1)S(1)} %collective-permute-done.1.r_3_), channel_id=1, source_target_pairs={{0,224},{32,0},{64,32},{96,64},{128,96},{160,128},{192,160},{224,1... | collective-permute-start | bytes 1400840 | tf_op jit(solution)/shard_map/ppermute | solution.py:310
  29.0 11.6 %copy-start.10 = (bf16[304,768]{1,0:T(8,128)(2,1)}, bf16[304,768]{1,0:T(8,128)(2,1)S(1)}, u32[]{:S(2)}) copy-start(bf16[304,768]{1,0:T(8,128)(2,1)S(1)} %collective-permute-done.r_2_) | copy-start | bytes 1400836
  29.0 11.5 %collective-permute-start.2 = (bf16[304,768]{1,0:T(8,128)(2,1)S(1)}, bf16[304,768]{1,0:T(8,128)(2,1)S(1)}, u32[]{:S(2)}, u32[]{:S(2)}) collective-permute-start(bf16[304,768]{1,0:T(8,128)(2,1)S(1)} %collective-permute-done.r_2_), channel_id=1, source_target_pairs={{0,32},{32,64},{64,96},{96,128},{128,160},{160,192},{192,224},{224... | collective-permute-start | bytes 1400840 | tf_op jit(solution)/shard_map/ppermute | solution.py:310
  37.1 10.6 %collective-permute-start.5 = (bf16[304,768]{1,0:T(8,128)(2,1)S(1)}, bf16[304,768]{1,0:T(8,128)(2,1)S(1)}, u32[]{:S(2)}, u32[]{:S(2)}) collective-permute-start(bf16[304,768]{1,0:T(8,128)(2,1)S(1)} %collective-permute-done.3.r_5_), channel_id=1, source_target_pairs={{0,224},{32,0},{64,32},{96,64},{128,96},{160,128},{192,160},{224,1... | collective-permute-start | bytes 1400840 | tf_op jit(solution)/shard_map/ppermute | solution.py:310
  40.5 10.7 %copy-start.12 = (bf16[304,768]{1,0:T(8,128)(2,1)}, bf16[304,768]{1,0:T(8,128)(2,1)S(1)}, u32[]{:S(2)}) copy-start(bf16[304,768]{1,0:T(8,128)(2,1)S(1)} %collective-permute-done.2.r_4_) | copy-start | bytes 1400836
  40.5 10.7 %collective-permute-start.4 = (bf16[304,768]{1,0:T(8,128)(2,1)S(1)}, bf16[304,768]{1,0:T(8,128)(2,1)S(1)}, u32[]{:S(2)}, u32[]{:S(2)}) collective-permute-start(bf16[304,768]{1,0:T(8,128)(2,1)S(1)} %collective-permute-done.2.r_4_), channel_id=1, source_target_pairs={{0,32},{32,64},{64,96},{96,128},{128,160},{160,192},{192,224},{224... | collective-permute-start | bytes 1400840 | tf_op jit(solution)/shard_map/ppermute | solution.py:310
  47.7 10.5 %copy-start.5 = (bf16[304,768]{1,0:T(8,128)(2,1)}, bf16[304,768]{1,0:T(8,128)(2,1)S(1)}, u32[]{:S(2)}) copy-start(bf16[304,768]{1,0:T(8,128)(2,1)S(1)} %collective-permute-done.5.r_7_) | copy-start | bytes 1400836
  47.7 10.5 %collective-permute-start.7 = (bf16[160,768]{1,0:T(8,128)(2,1)S(1)}, bf16[160,768]{1,0:T(8,128)(2,1)}, u32[]{:S(2)}, u32[]{:S(2)}) collective-permute-start(bf16[160,768]{1,0:T(8,128)(2,1)S(1)} %slice.29), channel_id=1, source_target_pairs={{0,224},{32,0},{64,32},{96,64},{128,96},{160,128},{192,160},{224,1... | collective-permute-start | bytes 737288 | tf_op jit(solution)/shard_map/ppermute | solution.py:310
  51.2 32.2 %copy-start.7 = (f32[4,3,128]{2,0,1:T(4,128)S(1)}, f32[4,3,128]{2,0,1:T(4,128)}, u32[]{:S(2)}) copy-start(f32[4,3,128]{2,0,1:T(4,128)} %param.12) | copy-start | bytes 18436
  51.3 6.3 %collective-permute-start.6 = (bf16[144,768]{1,0:T(8,128)(2,1)S(1)}, bf16[144,768]{1,0:T(8,128)(2,1)S(1)}, u32[]{:S(2)}, u32[]{:S(2)}) collective-permute-start(bf16[144,768]{1,0:T(8,128)(2,1)S(1)} %slice.28), channel_id=1, source_target_pairs={{0,32},{32,64},{64,96},{96,128},{128,160},{160,192},{192,224},{224... | collective-permute-start | bytes 663560 | tf_op jit(solution)/shard_map/ppermute | solution.py:310
  79.7 5.1 %collective-permute-start.8 = (f32[8,1152]{1,0:T(8,128)S(1)}, f32[8,1152]{1,0:T(8,128)S(1)}, u32[]{:S(2)}, u32[]{:S(2)}) collective-permute-start(f32[8,1152]{1,0:T(8,128)S(1)} %get-tuple-element.14.a_ref.r_1_), channel_id=1, source_target_pairs={{0,16},{16,0},{1,17},{17,1},{2,18},{18,2},{3,19},{19,3},{4,20},{20... | collective-permute-start | bytes 110600 | tf_op jit(solution)/shard_map/ppermute | solution.py:314
  84.9 4.4 %collective-permute-start.10 = (f32[8,1152]{1,0:T(8,128)S(1)}, f32[8,1152]{1,0:T(8,128)S(1)}, u32[]{:S(2)}, u32[]{:S(2)}) collective-permute-start(f32[8,1152]{1,0:T(8,128)S(1)} %merge.1.r_2_), channel_id=1, source_target_pairs={{0,8},{4,12},{8,0},{12,4},{1,9},{5,13},{9,1},{13,5},{2,10},{6,14},... | collective-permute-start | bytes 110600 | tf_op jit(solution)/shard_map/ppermute | solution.py:314
  86.3 4.3 %collective-permute-start.11 = (f32[8,1152]{1,0:T(8,128)S(1)}, f32[8,1152]{1,0:T(8,128)S(1)}, u32[]{:S(2)}, u32[]{:S(2)}) collective-permute-start(f32[8,1152]{1,0:T(8,128)S(1)} %merge.1.r_2_), channel_id=1, source_target_pairs={{0,12},{4,8},{8,4},{12,0},{1,13},{5,9},{9,5},{13,1},{2,14},{6,10},... | collective-permute-start | bytes 110600 | tf_op jit(solution)/shard_map/ppermute | solution.py:314
  86.4 4.3 %collective-permute-start.9 = (f32[8,1152]{1,0:T(8,128)S(1)}, f32[8,1152]{1,0:T(8,128)S(1)}, u32[]{:S(2)}, u32[]{:S(2)}) collective-permute-start(f32[8,1152]{1,0:T(8,128)S(1)} %merge.1.r_2_), channel_id=1, source_target_pairs={{0,4},{4,0},{8,12},{12,8},{1,5},{5,1},{9,13},{13,9},{2,6},{6,2},{1... | collective-permute-start | bytes 110600 | tf_op jit(solution)/shard_map/ppermute | solution.py:314
  93.9 19.8 %all-to-all-start.1 = ((bf16[8,144,768]{2,1,0:T(8,128)(2,1)}), bf16[8,144,768]{2,1,0:T(8,128)(2,1)S(1)}, u32[]{:S(2)}, u32[]{:S(2)}) async-start(bf16[8,144,768]{2,1,0:T(8,128)(2,1)} %weigh.1), calls=%async_computation.1 | async-start | bytes 3538944 | tf_op jit(solution)/shard_map/all_to_all | solution.py:345
  117.3 10.7 %collective-permute-start.12 = (bf16[144,1280]{1,0:T(8,128)(2,1)S(1)}, bf16[144,1280]{1,0:T(8,128)(2,1)S(1)}, u32[]{:S(2)}, u32[]{:S(2)}) collective-permute-start(bf16[144,1280]{1,0:T(8,128)(2,1)S(1)} %get-tuple-element.17), channel_id=1, source_target_pairs={{0,1},{1,0},{2,3},{3,2},{4,5},{5,4},{6,7},{7,6},{8,9},{9,8},{10,11... | collective-permute-start | bytes 1105928 | tf_op jit(solution)/shard_map/ppermute | solution.py:314
  128.0 9.9 %copy-start.2 = (bf16[144,1280]{1,0:T(8,128)(2,1)S(1)}, bf16[144,1280]{1,0:T(8,128)(2,1)}, u32[]{:S(2)}) copy-start(bf16[144,1280]{1,0:T(8,128)(2,1)} %param.15) | copy-start | bytes 1105924
  128.1 9.9 %collective-permute-start.13 = (bf16[144,1280]{1,0:T(8,128)(2,1)S(1)}, bf16[144,1280]{1,0:T(8,128)(2,1)S(1)}, u32[]{:S(2)}, u32[]{:S(2)}) collective-permute-start(bf16[144,1280]{1,0:T(8,128)(2,1)S(1)} %add_convert_fusion.1), channel_id=1, source_target_pairs={{0,2},{2,0},{1,3},{3,1},{4,6},{6,4},{5,7},{7,5},{8,10},{10,8},{9,1... | collective-permute-start | bytes 1105928 | tf_op jit(solution)/shard_map/ppermute | solution.py:314
  131.9 6.1 %collective-permute-start.14 = (bf16[144,1280]{1,0:T(8,128)(2,1)S(1)}, bf16[144,1280]{1,0:T(8,128)(2,1)S(1)}, u32[]{:S(2)}, u32[]{:S(2)}) collective-permute-start(bf16[144,1280]{1,0:T(8,128)(2,1)S(1)} %get-tuple-element.22), channel_id=1, source_target_pairs={{0,1},{1,0},{2,3},{3,2},{4,5},{5,4},{6,7},{7,6},{8,9},{9,8},{10,11... | collective-permute-start | bytes 1105928 | tf_op jit(solution)/shard_map/ppermute | solution.py:314
  (7 other events, 32.9 us)

commit v8 on v7

--- a/solution.py
+++ b/solution.py
@@ -146,7 +146,7 @@
     slots, pad, width = q_all.shape
     blocks = slots * rows // RUN
     keys = len(spots) * rows // RUN
-    ins = [pltpu.with_memory_space_constraint(x, pltpu.HBM) for x in [q_all, *kv_parts]]
+    ins = [pltpu.with_memory_space_constraint(x, pltpu.HBM) for x in kv_parts]
     return pl.pallas_call(
         lambda *r: attend_kernel(rows, spans, slots, spots, *r),
         out_shape=[
@@ -180,7 +180,7 @@
             transcendentals=heads * 2 * blocks * keys * RUN * RUN,
         ),
         name="attend",
-    )(*ins)
+    )(q_all, *ins)
 
 
 def logsum(parts):
@@ -306,6 +306,43 @@
     )(cols, *ins, pltpu.with_memory_space_constraint(weight, pltpu.HBM))
 
 
+def repeat_kernel(x_ref, ids_ref, o_ref):
+    rows = x_ref.shape[0]
+    for i in range(o_ref.shape[0]):
+        o_ref[i, :rows] = x_ref[...]
+        o_ref[i, rows:] = ids_ref[...]
+
+
+def repeat(x, ids, count):
+    rows, width = x.shape
+    vm = pl.BlockSpec(memory_space=pltpu.VMEM)
+    return pl.pallas_call(
+        repeat_kernel,
+        out_shape=jax.ShapeDtypeStruct((count, rows + ids.shape[0], width), x.dtype),
+        in_specs=[vm, vm],
+        out_specs=vm,
+        name="repeat",
+    )(x, ids)
+
+
+def lambda_kernel(x_ref, o_ref):
+    first = jnp.sum(x_ref[0] * x_ref[1], -1, keepdims=True)
+    second = jnp.sum(x_ref[2] * x_ref[3], -1, keepdims=True)
+    o_ref[...] = jnp.broadcast_to(jnp.exp(first) - jnp.exp(second) + lambda_init, o_ref.shape)
+
+
+def lambdas(x):
+    vm = pl.BlockSpec(memory_space=pltpu.VMEM)
+    return pl.pallas_call(
+        lambda_kernel,
+        out_shape=jax.ShapeDtypeStruct(x.shape[1:], f32),
+        in_specs=[vm],
+        out_specs=vm,
+        cost_estimate=pl.CostEstimate(flops=10**11, bytes_accessed=4 * 10**4, transcendentals=0),
+        name="lambdas",
+    )(x)
+
+
 def shift(x, axis, size, step):
     return lax.ppermute(x, axis, [(i, (i + step) % size) for i in range(size)])
 
@@ -320,27 +357,23 @@
     heads = lambda_vecs.shape[1]
     block = ((positions[::RUN].astype(f32) + 0.5) * (1.0 / RUN)).astype(jnp.int32).astype(bf16)
     ids = jnp.broadcast_to(jnp.pad(block, (0, width - block.shape[0]))[None, :], (16, width))
-    q_mine = jnp.concatenate([queries, ids], 0)
-    q_all = lax.all_to_all(jnp.broadcast_to(q_mine[None], (nh * ny, *q_mine.shape)), ("h", "y"), 0, 0)
     kv_mine = jnp.concatenate([keys, values, ids], 0)
+    kv_mine, queries = lax.optimization_barrier((kv_mine, queries))
+    q_all = lax.all_to_all(repeat(queries, ids, nh * ny), ("h", "y"), 0, 0)
     up, down = shift(kv_mine, "z", nz, 1), shift(kv_mine, "z", nz, -1)
     kv_parts = [kv_mine, up, down]
+    up, down, lam = lax.optimization_barrier((up, down, lambdas(lambda_vecs)))
     for _ in range(2):
         up, down = shift(up, "z", nz, 1), shift(down, "z", nz, -1)
         kv_parts += [up, down]
     kv_parts += [shift(up[:rows], "z", nz, 1), shift(down[rows:], "z", nz, -1)]
     spots = [(i, 0, i, rows) for i in range(nz - 1)] + [(nz - 1, 0, nz, 0)]
-    o, lse = attend(q_all, kv_parts, spots, (4, 8, 12, 16), rows, heads)
+    o, lse = attend(q_all, kv_parts, spots, (3, 6, 9, 12, 16), rows, heads)
 
     pair = merge(lse, swap(lse, "h", nh, 1))
     others = [swap(pair, "y", ny, d) for d in range(1, ny)]
 
-    lam = (
-        jnp.exp(jnp.sum(lambda_vecs[0] * lambda_vecs[1], -1))
-        - jnp.exp(jnp.sum(lambda_vecs[2] * lambda_vecs[3], -1))
-        + lambda_init
-    )
-    parts = weigh(lam, lse, [pair] + others, o, rows, heads)
+    parts = weigh(lam[:, 0], lse, [pair] + others, o, rows, heads)
 
     got = lax.all_to_all(parts, ("h", "y"), 0, 0, tiled=False)
     l, c = lax.axis_index("l"), lax.axis_index("c")

time: 139 us -> 130 us (0.935)
  waiting for transfers between devices: 55.5 us -> 49.2 us
  local copies, waits for them, and re-layouts: 4.25 us -> 2.26 us
    ppermute x8, waiting for transfers between devices: 30.3 us -> 23 us  [shift(): return lax.ppermute(x, axis, [(i, (i + step) % size) for i in range(size)])]
    pallas_call x0 -> x2, Pallas kernels: none -> 3.72 us  [the longest x1 2.35 us: repeat(): pl.pallas_call(repeat_kernel, out_shape=jax.ShapeDtypeStruct((count, rows...]
    pallas_call x1, Pallas kernels: 20.2 us -> 16.8 us  [attend(): pl.pallas_call(lambda *r: attend_kernel(rows, spans, slots, spots, *r), o...]
    ppermute x7, starting transfers between devices: 17.3 us -> 19.8 us  [swap(): return lax.ppermute(x, axis, [(i, i ^ mask) for i in range(size)])]
    ppermute x8, starting transfers between devices: 16.2 us -> 14.6 us  [shift(): return lax.ppermute(x, axis, [(i, (i + step) % size) for i in range(size)])]
    broadcast_in_dim x1 -> x0, local copies, waits for them, and re-layouts: 1.42 us -> none  [per_device(): jnp.broadcast_to(q_mine[None], (nh * ny, *q_mine.shape))]
  transfers between devices with their start and end apart: 17 -> 17, of which waited for: 10 -> 9; matrix products, arithmetic and copies ran while one was open for 0% -> 1% of each run, Pallas kernels for 2% -> 5%
where the time goes in v8:
time: 130 us
  waiting for transfers between devices  49.2 us (38%)
  starting transfers between devices  45.4 us (35%)
  Pallas kernels  30.6 us (24%)
  local copies, waits for them, and re-layouts  2.26 us (2%)
  other arithmetic  2.23 us (2%)
    ppermute x8, waiting for transfers between devices, shift(): return lax.ppermute(x, axis, [(i, (i + step) % size) for i in range(size)])  23 us
    ppermute x7, starting transfers between devices, swap(): return lax.ppermute(x, axis, [(i, i ^ mask) for i in range(size)])  19.8 us
    pallas_call x1, Pallas kernels, attend(): pl.pallas_call(lambda *r: attend_kernel(rows, spans, slots, spots, *r), o...  16.8 us
    all_to_all x1, waiting for transfers between devices, per_device(): got = lax.all_to_all(parts, ('h', 'y'), 0, 0, tiled=False)  14.8 us
    ppermute x8, starting transfers between devices, shift(): return lax.ppermute(x, axis, [(i, (i + step) % size) for i in range(size)])  14.6 us
    ppermute x7, waiting for transfers between devices, swap(): return lax.ppermute(x, axis, [(i, i ^ mask) for i in range(size)])  11.4 us
    all_to_all x1, starting transfers between devices, per_device(): q_all = lax.all_to_all(repeat(queries, ids, nh * ny), ('h', 'y'), 0, 0)  6.78 us
    pallas_call x2, Pallas kernels, project(): pl.pallas_call(lambda *r: project_kernel(heads, *r), out_shape=outs, grid...  6.73 us
  transfers between devices with their start and end apart: 17, of which 9 were waited for; matrix products, arithmetic and copies ran while one was open for 1% of the time, Pallas kernels for 5%

profile of v8, /device:TPU:1, one launch (start us, length us, event | category | flops | bytes accessed | tf_op | source)
XLA Modules:
  0.0 129.9 jit_solution(15421826908944189432)
XLA Ops:
  1.9 2.5 %collective-permute-start = (bf16[304,768]{1,0:T(8,128)(2,1)S(1)}, bf16[304,768]{1,0:T(8,128)(2,1)S(1)}, u32[]{:S(2)}, u32[]{:S(2)}) collective-permute-start(bf16[304,768]{1,0:T(8,128)(2,1)S(1)} %pad_maximum_fusion.r_1_), channel_id=1, source_target_pairs={{0,32},{32,64},{64,96},{96,128},{128,160},{160,192},{192,224},{224... | collective-permute-start | bytes 1400840 | tf_op jit(solution)/shard_map/ppermute | solution.py:347
  4.4 4.0 %collective-permute-start.1 = (bf16[304,768]{1,0:T(8,128)(2,1)S(1)}, bf16[304,768]{1,0:T(8,128)(2,1)}, u32[]{:S(2)}, u32[]{:S(2)}) collective-permute-start(bf16[304,768]{1,0:T(8,128)(2,1)S(1)} %pad_maximum_fusion.r_1_), channel_id=1, source_target_pairs={{0,224},{32,0},{64,32},{96,64},{128,96},{160,128},{192,160},{224,1... | collective-permute-start | bytes 1400840 | tf_op jit(solution)/shard_map/ppermute | solution.py:347
  8.5 2.4 %repeat.1 = bf16[8,160,768]{2,1,0:T(8,128)(2,1)} custom-call(bf16[144,768]{1,0:T(8,128)(2,1)} %x_ref.1, bf16[16,768]{1,0:T(8,128)(2,1)} %copy-done.2), custom_call_target="tpu_custom_call" | custom-call | tf_op jit(solution)/shard_map/repeat/pallas_call | solution.py:319
  10.8 6.8 %all-to-all-start = ((bf16[8,160,768]{2,1,0:T(8,128)(2,1)}), bf16[8,160,768]{2,1,0:T(8,128)(2,1)S(1)}, u32[]{:S(2)}, u32[]{:S(2)}) async-start(bf16[8,160,768]{2,1,0:T(8,128)(2,1)} %repeat.1), calls=%async_computation | async-start | bytes 3932160 | tf_op jit(solution)/shard_map/all_to_all | solution.py:362
  18.2 1.4 %lambdas.1 = f32[3,128]{1,0:T(4,128)} custom-call(f32[4,3,128]{2,1,0:T(4,128)} %copy.10.x_ref), custom_call_target="tpu_custom_call" | custom-call | flops 99999997952 | bytes 40000 | tf_op jit(solution)/shard_map/lambdas/pallas_call | solution.py:336
  19.6 1.7 %collective-permute-start.3 = (bf16[304,768]{1,0:T(8,128)(2,1)}, bf16[304,768]{1,0:T(8,128)(2,1)S(1)}, u32[]{:S(2)}, u32[]{:S(2)}) collective-permute-start(bf16[304,768]{1,0:T(8,128)(2,1)} %collective-permute-done.1.r_3_), channel_id=1, source_target_pairs={{0,224},{32,0},{64,32},{96,64},{128,96},{160,128},{192,160},{224,1... | collective-permute-start | bytes 1400840 | tf_op jit(solution)/shard_map/ppermute | solution.py:347
  21.4 9.5 %collective-permute-done.3.r_5_ = bf16[304,768]{1,0:T(8,128)(2,1)S(1)} collective-permute-done((bf16[304,768]{1,0:T(8,128)(2,1)}, bf16[304,768]{1,0:T(8,128)(2,1)S(1)}, u32[]{:S(2)}, u32[]{:S(2)}) %collective-permute-start.3) | collective-permute-done | bytes 466976 | tf_op jit(solution)/shard_map/ppermute | solution.py:347
  30.8 2.6 %collective-permute-start.5 = (bf16[304,768]{1,0:T(8,128)(2,1)S(1)}, bf16[304,768]{1,0:T(8,128)(2,1)S(1)}, u32[]{:S(2)}, u32[]{:S(2)}) collective-permute-start(bf16[304,768]{1,0:T(8,128)(2,1)S(1)} %collective-permute-done.3.r_5_), channel_id=1, source_target_pairs={{0,224},{32,0},{64,32},{96,64},{128,96},{160,128},{192,160},{224,1... | collective-permute-start | bytes 1400840 | tf_op jit(solution)/shard_map/ppermute | solution.py:347
  33.4 7.5 %collective-permute-done.5.r_7_ = bf16[304,768]{1,0:T(8,128)(2,1)S(1)} collective-permute-done((bf16[304,768]{1,0:T(8,128)(2,1)S(1)}, bf16[304,768]{1,0:T(8,128)(2,1)S(1)}, u32[]{:S(2)}, u32[]{:S(2)}) %collective-permute-start.5) | collective-permute-done | bytes 466976 | tf_op jit(solution)/shard_map/ppermute | solution.py:347
  41.0 3.5 %collective-permute-start.7 = (bf16[160,768]{1,0:T(8,128)(2,1)S(1)}, bf16[160,768]{1,0:T(8,128)(2,1)}, u32[]{:S(2)}, u32[]{:S(2)}) collective-permute-start(bf16[160,768]{1,0:T(8,128)(2,1)S(1)} %slice.17), channel_id=1, source_target_pairs={{0,224},{32,0},{64,32},{96,64},{128,96},{160,128},{192,160},{224,1... | collective-permute-start | bytes 737288 | tf_op jit(solution)/shard_map/ppermute | solution.py:347
  44.8 6.0 %collective-permute-done.6.r_8_ = bf16[144,768]{1,0:T(8,128)(2,1)S(1)} collective-permute-done((bf16[144,768]{1,0:T(8,128)(2,1)S(1)}, bf16[144,768]{1,0:T(8,128)(2,1)S(1)}, u32[]{:S(2)}, u32[]{:S(2)}) %collective-permute-start.6) | collective-permute-done | bytes 221216 | tf_op jit(solution)/shard_map/ppermute | solution.py:347
  51.5 16.8 %attend.1 = (bf16[16,72,1536]{2,1,0:T(8,128)(2,1)S(1)}, f32[8,1152]{1,0:T(8,128)S(1)}) custom-call(bf16[8,160,768]{2,1,0:T(8,128)(2,1)S(1)} %all-to-all-done.r_0_, bf16[304,768]{1,0:T(8,128)(2,1)} %copy-done, bf16[304,768]{1,0:T(8,128)(2,1)} %copy-done.8, bf16[304,768]{1,0:T(8,128)(2,1)} %collective-permute-done.1.r_3_, bf16[304,768]{1,0:T(8,128)(2,1)} %copy-done.10, ...), custom_call_target="tpu_custom_call" | custom-call | flops 48922361856 | bytes 7077888 | tf_op jit(solution)/shard_map/attend/pallas_call | solution.py:150
  68.3 3.7 %collective-permute-start.8 = (f32[8,1152]{1,0:T(8,128)S(1)}, f32[8,1152]{1,0:T(8,128)S(1)}, u32[]{:S(2)}, u32[]{:S(2)}) collective-permute-start(f32[8,1152]{1,0:T(8,128)S(1)} %get-tuple-element.24.a_ref.r_1_), channel_id=1, source_target_pairs={{0,16},{16,0},{1,17},{17,1},{2,18},{18,2},{3,19},{19,3},{4,20},{20... | collective-permute-start | bytes 110600 | tf_op jit(solution)/shard_map/ppermute | solution.py:351
  73.3 2.1 %collective-permute-start.9 = (f32[8,1152]{1,0:T(8,128)S(1)}, f32[8,1152]{1,0:T(8,128)S(1)}, u32[]{:S(2)}, u32[]{:S(2)}) collective-permute-start(f32[8,1152]{1,0:T(8,128)S(1)} %merge.1.r_2_), channel_id=1, source_target_pairs={{0,4},{4,0},{8,12},{12,8},{1,5},{5,1},{9,13},{13,9},{2,6},{6,2},{1... | collective-permute-start | bytes 110600 | tf_op jit(solution)/shard_map/ppermute | solution.py:351
  75.5 3.3 %collective-permute-start.10 = (f32[8,1152]{1,0:T(8,128)S(1)}, f32[8,1152]{1,0:T(8,128)S(1)}, u32[]{:S(2)}, u32[]{:S(2)}) collective-permute-start(f32[8,1152]{1,0:T(8,128)S(1)} %merge.1.r_2_), channel_id=1, source_target_pairs={{0,8},{4,12},{8,0},{12,4},{1,9},{5,13},{9,1},{13,5},{2,10},{6,14},... | collective-permute-start | bytes 110600 | tf_op jit(solution)/shard_map/ppermute | solution.py:351
  78.9 1.6 %collective-permute-done.10.r_4_ = f32[8,1152]{1,0:T(8,128)S(1)} collective-permute-done((f32[8,1152]{1,0:T(8,128)S(1)}, f32[8,1152]{1,0:T(8,128)S(1)}, u32[]{:S(2)}, u32[]{:S(2)}) %collective-permute-start.10) | collective-permute-done | bytes 36896 | tf_op jit(solution)/shard_map/ppermute | solution.py:351
  80.5 2.3 %collective-permute-done.11.r_5_ = f32[8,1152]{1,0:T(8,128)S(1)} collective-permute-done((f32[8,1152]{1,0:T(8,128)S(1)}, f32[8,1152]{1,0:T(8,128)S(1)}, u32[]{:S(2)}, u32[]{:S(2)}) %collective-permute-start.11) | collective-permute-done | bytes 36896 | tf_op jit(solution)/shard_map/ppermute | solution.py:351
  82.8 3.3 %weigh.1 = bf16[8,144,768]{2,1,0:T(8,128)(2,1)} custom-call(f32[3]{0:T(128)S(1)} %slice_reduce_fusion.r_0_, f32[8,1152]{1,0:T(8,128)S(1)} %get-tuple-element.24.a_ref.r_1_, f32[8,1152]{1,0:T(8,128)S(1)} %merge.1.r_2_, f32[8,1152]{1,0:T(8,128)S(1)} %collective-permute-done.9.r_3_, f32[8,1152]{1,0:T(8,128)S(1)} %collective-permute-done.10.r_4_, ...), custom_call_target="tpu_custom_call" | custom-call | tf_op jit(solution)/shard_map/weigh/pallas_call | solution.py:237
  86.1 4.2 %all-to-all-start.1 = ((bf16[8,144,768]{2,1,0:T(8,128)(2,1)}), bf16[8,144,768]{2,1,0:T(8,128)(2,1)S(1)}, u32[]{:S(2)}, u32[]{:S(2)}) async-start(bf16[8,144,768]{2,1,0:T(8,128)(2,1)} %weigh.1), calls=%async_computation.1 | async-start | bytes 3538944 | tf_op jit(solution)/shard_map/all_to_all | solution.py:378
  90.4 14.8 %all-to-all-done.1.r_1_ = bf16[8,144,768]{2,1,0:T(8,128)(2,1)S(1)} async-done(((bf16[8,144,768]{2,1,0:T(8,128)(2,1)}), bf16[8,144,768]{2,1,0:T(8,128)(2,1)S(1)}, u32[]{:S(2)}, u32[]{:S(2)}) %all-to-all-start.1) | async-done | bytes 1769504 | tf_op jit(solution)/shard_map/all_to_all | solution.py:378
  105.2 3.5 %project.2 = (bf16[144,1280]{1,0:T(8,128)(2,1)S(1)}, f32[144,1280]{1,0:T(8,128)S(1)}, bf16[144,768]{1,0:T(8,128)(2,1)S(1)}) custom-call(s32[2]{0:T(128)S(1)} %pad_add_fusion.r_0_, bf16[8,144,768]{2,1,0:T(8,128)(2,1)S(1)} %all-to-all-done.1.r_1_, f32[1,768]{1,0:T(1,128)S(1)} %reshape.4.r_2_, bf16[768,5120]{1,0:T(8,128)(2,1)} %r_2_.1), custom_call_target="tpu_custom_call" | custom-call | flops 4529848320 | bytes 3932160 | tf_op jit(solution)/shard_map/project/pallas_call | solution.py:294
  108.7 9.0 %collective-permute-start.12 = (bf16[144,1280]{1,0:T(8,128)(2,1)S(1)}, bf16[144,1280]{1,0:T(8,128)(2,1)S(1)}, u32[]{:S(2)}, u32[]{:S(2)}) collective-permute-start(bf16[144,1280]{1,0:T(8,128)(2,1)S(1)} %get-tuple-element.27), channel_id=1, source_target_pairs={{0,1},{1,0},{2,3},{3,2},{4,5},{5,4},{6,7},{7,6},{8,9},{9,8},{10,11... | collective-permute-start | bytes 1105928 | tf_op jit(solution)/shard_map/ppermute | solution.py:351
  120.1 3.2 %project.3 = (bf16[144,1280]{1,0:T(8,128)(2,1)S(1)}, f32[144,1280]{1,0:T(8,128)S(1)}) custom-call(s32[2]{0:T(128)S(1)} %pad_add_fusion.1.r_0_, bf16[144,768]{1,0:T(8,128)(2,1)S(1)} %get-tuple-element.30.r_1_, bf16[768,5120]{1,0:T(8,128)(2,1)} %r_2_.1), custom_call_target="tpu_custom_call" | custom-call | flops 4529848320 | bytes 3932160 | tf_op jit(solution)/shard_map/project/pallas_call | solution.py:294
  124.1 5.0 %collective-permute-done.13 = bf16[144,1280]{1,0:T(8,128)(2,1)S(1)} collective-permute-done((bf16[144,1280]{1,0:T(8,128)(2,1)S(1)}, bf16[144,1280]{1,0:T(8,128)(2,1)S(1)}, u32[]{:S(2)}, u32[]{:S(2)}) %collective-permute-start.13) | collective-permute-done | bytes 368672 | tf_op jit(solution)/shard_map/ppermute | solution.py:351
  (56 shorter events, 9.1 us)
Async XLA Ops:
  0.8 7.7 %copy-start.2 = (bf16[16,768]{1,0:T(8,128)(2,1)}, bf16[16,768]{1,0:T(8,128)(2,1)S(1)}, u32[]{:S(2)}) copy-start(bf16[16,768]{1,0:T(8,128)(2,1)S(1)} %broadcast_in_dim.2.ids_ref) | copy-start | bytes 73732
  1.9 8.9 %copy-start = (bf16[304,768]{1,0:T(8,128)(2,1)}, bf16[304,768]{1,0:T(8,128)(2,1)S(1)}, u32[]{:S(2)}) copy-start(bf16[304,768]{1,0:T(8,128)(2,1)S(1)} %pad_maximum_fusion.r_1_) | copy-start | bytes 1400836
  1.9 17.7 %collective-permute-start = (bf16[304,768]{1,0:T(8,128)(2,1)S(1)}, bf16[304,768]{1,0:T(8,128)(2,1)S(1)}, u32[]{:S(2)}, u32[]{:S(2)}) collective-permute-start(bf16[304,768]{1,0:T(8,128)(2,1)S(1)} %pad_maximum_fusion.r_1_), channel_id=1, source_target_pairs={{0,32},{32,64},{64,96},{96,128},{128,160},{160,192},{192,224},{224... | collective-permute-start | bytes 1400840 | tf_op jit(solution)/shard_map/ppermute | solution.py:347
  4.4 15.2 %collective-permute-start.1 = (bf16[304,768]{1,0:T(8,128)(2,1)S(1)}, bf16[304,768]{1,0:T(8,128)(2,1)}, u32[]{:S(2)}, u32[]{:S(2)}) collective-permute-start(bf16[304,768]{1,0:T(8,128)(2,1)S(1)} %pad_maximum_fusion.r_1_), channel_id=1, source_target_pairs={{0,224},{32,0},{64,32},{96,64},{128,96},{160,128},{192,160},{224,1... | collective-permute-start | bytes 1400840 | tf_op jit(solution)/shard_map/ppermute | solution.py:347
  10.8 40.6 %all-to-all-start = ((bf16[8,160,768]{2,1,0:T(8,128)(2,1)}), bf16[8,160,768]{2,1,0:T(8,128)(2,1)S(1)}, u32[]{:S(2)}, u32[]{:S(2)}) async-start(bf16[8,160,768]{2,1,0:T(8,128)(2,1)} %repeat.1), calls=%async_computation | async-start | bytes 3932160 | tf_op jit(solution)/shard_map/all_to_all | solution.py:362
  19.6 31.8 %copy-start.8 = (bf16[304,768]{1,0:T(8,128)(2,1)}, bf16[304,768]{1,0:T(8,128)(2,1)S(1)}, u32[]{:S(2)}) copy-start(bf16[304,768]{1,0:T(8,128)(2,1)S(1)} %collective-permute-done.r_2_) | copy-start | bytes 1400836
  19.6 11.2 %collective-permute-start.3 = (bf16[304,768]{1,0:T(8,128)(2,1)}, bf16[304,768]{1,0:T(8,128)(2,1)S(1)}, u32[]{:S(2)}, u32[]{:S(2)}) collective-permute-start(bf16[304,768]{1,0:T(8,128)(2,1)} %collective-permute-done.1.r_3_), channel_id=1, source_target_pairs={{0,224},{32,0},{64,32},{96,64},{128,96},{160,128},{192,160},{224,1... | collective-permute-start | bytes 1400840 | tf_op jit(solution)/shard_map/ppermute | solution.py:347
  21.3 12.1 %collective-permute-start.2 = (bf16[304,768]{1,0:T(8,128)(2,1)S(1)}, bf16[304,768]{1,0:T(8,128)(2,1)S(1)}, u32[]{:S(2)}, u32[]{:S(2)}) collective-permute-start(bf16[304,768]{1,0:T(8,128)(2,1)S(1)} %collective-permute-done.r_2_), channel_id=1, source_target_pairs={{0,32},{32,64},{64,96},{96,128},{128,160},{160,192},{192,224},{224... | collective-permute-start | bytes 1400840 | tf_op jit(solution)/shard_map/ppermute | solution.py:347
  30.8 10.1 %collective-permute-start.5 = (bf16[304,768]{1,0:T(8,128)(2,1)S(1)}, bf16[304,768]{1,0:T(8,128)(2,1)S(1)}, u32[]{:S(2)}, u32[]{:S(2)}) collective-permute-start(bf16[304,768]{1,0:T(8,128)(2,1)S(1)} %collective-permute-done.3.r_5_), channel_id=1, source_target_pairs={{0,224},{32,0},{64,32},{96,64},{128,96},{160,128},{192,160},{224,1... | collective-permute-start | bytes 1400840 | tf_op jit(solution)/shard_map/ppermute | solution.py:347
  33.4 11.0 %copy-start.10 = (bf16[304,768]{1,0:T(8,128)(2,1)}, bf16[304,768]{1,0:T(8,128)(2,1)S(1)}, u32[]{:S(2)}) copy-start(bf16[304,768]{1,0:T(8,128)(2,1)S(1)} %collective-permute-done.2.r_4_) | copy-start | bytes 1400836
  33.4 11.0 %collective-permute-start.4 = (bf16[304,768]{1,0:T(8,128)(2,1)S(1)}, bf16[304,768]{1,0:T(8,128)(2,1)S(1)}, u32[]{:S(2)}, u32[]{:S(2)}) collective-permute-start(bf16[304,768]{1,0:T(8,128)(2,1)S(1)} %collective-permute-done.2.r_4_), channel_id=1, source_target_pairs={{0,32},{32,64},{64,96},{96,128},{128,160},{160,192},{192,224},{224... | collective-permute-start | bytes 1400840 | tf_op jit(solution)/shard_map/ppermute | solution.py:347
  40.9 10.5 %copy-start.3 = (bf16[304,768]{1,0:T(8,128)(2,1)}, bf16[304,768]{1,0:T(8,128)(2,1)S(1)}, u32[]{:S(2)}) copy-start(bf16[304,768]{1,0:T(8,128)(2,1)S(1)} %collective-permute-done.5.r_7_) | copy-start | bytes 1400836
  41.0 10.5 %collective-permute-start.7 = (bf16[160,768]{1,0:T(8,128)(2,1)S(1)}, bf16[160,768]{1,0:T(8,128)(2,1)}, u32[]{:S(2)}, u32[]{:S(2)}) collective-permute-start(bf16[160,768]{1,0:T(8,128)(2,1)S(1)} %slice.17), channel_id=1, source_target_pairs={{0,224},{32,0},{64,32},{96,64},{128,96},{160,128},{192,160},{224,1... | collective-permute-start | bytes 737288 | tf_op jit(solution)/shard_map/ppermute | solution.py:347
  44.5 34.3 %copy-start.7 = (f32[3,128]{1,0:T(4,128)S(1)}, f32[3,128]{1,0:T(4,128)}, u32[]{:S(2)}) copy-start(f32[3,128]{1,0:T(4,128)} %lambdas.1) | copy-start | bytes 4612
  44.5 6.3 %collective-permute-start.6 = (bf16[144,768]{1,0:T(8,128)(2,1)S(1)}, bf16[144,768]{1,0:T(8,128)(2,1)S(1)}, u32[]{:S(2)}, u32[]{:S(2)}) collective-permute-start(bf16[144,768]{1,0:T(8,128)(2,1)S(1)} %slice.16), channel_id=1, source_target_pairs={{0,32},{32,64},{64,96},{96,128},{128,160},{160,192},{192,224},{224... | collective-permute-start | bytes 663560 | tf_op jit(solution)/shard_map/ppermute | solution.py:347
  68.3 5.0 %collective-permute-start.8 = (f32[8,1152]{1,0:T(8,128)S(1)}, f32[8,1152]{1,0:T(8,128)S(1)}, u32[]{:S(2)}, u32[]{:S(2)}) collective-permute-start(f32[8,1152]{1,0:T(8,128)S(1)} %get-tuple-element.24.a_ref.r_1_), channel_id=1, source_target_pairs={{0,16},{16,0},{1,17},{17,1},{2,18},{18,2},{3,19},{19,3},{4,20},{20... | collective-permute-start | bytes 110600 | tf_op jit(solution)/shard_map/ppermute | solution.py:351
  73.3 5.5 %collective-permute-start.9 = (f32[8,1152]{1,0:T(8,128)S(1)}, f32[8,1152]{1,0:T(8,128)S(1)}, u32[]{:S(2)}, u32[]{:S(2)}) collective-permute-start(f32[8,1152]{1,0:T(8,128)S(1)} %merge.1.r_2_), channel_id=1, source_target_pairs={{0,4},{4,0},{8,12},{12,8},{1,5},{5,1},{9,13},{13,9},{2,6},{6,2},{1... | collective-permute-start | bytes 110600 | tf_op jit(solution)/shard_map/ppermute | solution.py:351
  75.5 5.0 %collective-permute-start.10 = (f32[8,1152]{1,0:T(8,128)S(1)}, f32[8,1152]{1,0:T(8,128)S(1)}, u32[]{:S(2)}, u32[]{:S(2)}) collective-permute-start(f32[8,1152]{1,0:T(8,128)S(1)} %merge.1.r_2_), channel_id=1, source_target_pairs={{0,8},{4,12},{8,0},{12,4},{1,9},{5,13},{9,1},{13,5},{2,10},{6,14},... | collective-permute-start | bytes 110600 | tf_op jit(solution)/shard_map/ppermute | solution.py:351
  78.7 4.0 %collective-permute-start.11 = (f32[8,1152]{1,0:T(8,128)S(1)}, f32[8,1152]{1,0:T(8,128)S(1)}, u32[]{:S(2)}, u32[]{:S(2)}) collective-permute-start(f32[8,1152]{1,0:T(8,128)S(1)} %merge.1.r_2_), channel_id=1, source_target_pairs={{0,12},{4,8},{8,4},{12,0},{1,13},{5,9},{9,5},{13,1},{2,14},{6,10},... | collective-permute-start | bytes 110600 | tf_op jit(solution)/shard_map/ppermute | solution.py:351
  86.1 19.1 %all-to-all-start.1 = ((bf16[8,144,768]{2,1,0:T(8,128)(2,1)}), bf16[8,144,768]{2,1,0:T(8,128)(2,1)S(1)}, u32[]{:S(2)}, u32[]{:S(2)}) async-start(bf16[8,144,768]{2,1,0:T(8,128)(2,1)} %weigh.1), calls=%async_computation.1 | async-start | bytes 3538944 | tf_op jit(solution)/shard_map/all_to_all | solution.py:378
  108.7 10.4 %collective-permute-start.12 = (bf16[144,1280]{1,0:T(8,128)(2,1)S(1)}, bf16[144,1280]{1,0:T(8,128)(2,1)S(1)}, u32[]{:S(2)}, u32[]{:S(2)}) collective-permute-start(bf16[144,1280]{1,0:T(8,128)(2,1)S(1)} %get-tuple-element.27), channel_id=1, source_target_pairs={{0,1},{1,0},{2,3},{3,2},{4,5},{5,4},{6,7},{7,6},{8,9},{9,8},{10,11... | collective-permute-start | bytes 1105928 | tf_op jit(solution)/shard_map/ppermute | solution.py:351
  119.1 9.9 %copy-start.1 = (bf16[144,1280]{1,0:T(8,128)(2,1)S(1)}, bf16[144,1280]{1,0:T(8,128)(2,1)}, u32[]{:S(2)}) copy-start(bf16[144,1280]{1,0:T(8,128)(2,1)} %param.15) | copy-start | bytes 1105924
  119.1 9.9 %collective-permute-start.13 = (bf16[144,1280]{1,0:T(8,128)(2,1)S(1)}, bf16[144,1280]{1,0:T(8,128)(2,1)S(1)}, u32[]{:S(2)}, u32[]{:S(2)}) collective-permute-start(bf16[144,1280]{1,0:T(8,128)(2,1)S(1)} %add_convert_fusion.1), channel_id=1, source_target_pairs={{0,2},{2,0},{1,3},{3,1},{4,6},{6,4},{5,7},{7,5},{8,10},{10,8},{9,1... | collective-permute-start | bytes 1105928 | tf_op jit(solution)/shard_map/ppermute | solution.py:351
  123.3 5.8 %collective-permute-start.14 = (bf16[144,1280]{1,0:T(8,128)(2,1)S(1)}, bf16[144,1280]{1,0:T(8,128)(2,1)S(1)}, u32[]{:S(2)}, u32[]{:S(2)}) collective-permute-start(bf16[144,1280]{1,0:T(8,128)(2,1)S(1)} %get-tuple-element.32), channel_id=1, source_target_pairs={{0,1},{1,0},{2,3},{3,2},{4,5},{5,4},{6,7},{7,6},{8,9},{9,8},{10,11... | collective-permute-start | bytes 1105928 | tf_op jit(solution)/shard_map/ppermute | solution.py:351
  (5 other events, 21.2 us)

commit v9 on v8

--- a/solution.py
+++ b/solution.py
@@ -40,7 +40,7 @@
 
         def numbers(part):
             tail = part[part.shape[0] - 16 :, :HD].astype(f32)
-            weight = jnp.where(first & (lanes < per), jnp.where(lanes == 0, float(HD), 1.0), 0.0)
+            weight = jnp.where(first & (lanes == 0), float(HD), jnp.where(first & (lanes == RUN), 1.0, 0.0))
             both = jnp.sum(tail * weight).astype(jnp.int32)
             return [lax.div(both, HD), lax.rem(both, HD)]
 
@@ -146,7 +146,7 @@
     slots, pad, width = q_all.shape
     blocks = slots * rows // RUN
     keys = len(spots) * rows // RUN
-    ins = [pltpu.with_memory_space_constraint(x, pltpu.HBM) for x in kv_parts]
+    ins = [pltpu.with_memory_space_constraint(x, pltpu.HBM) for x in kv_parts[:-2]]
     return pl.pallas_call(
         lambda *r: attend_kernel(rows, spans, slots, spots, *r),
         out_shape=[
@@ -180,7 +180,7 @@
             transcendentals=heads * 2 * blocks * keys * RUN * RUN,
         ),
         name="attend",
-    )(q_all, *ins)
+    )(q_all, *ins, *kv_parts[-2:])
 
 
 def logsum(parts):
@@ -306,28 +306,35 @@
     )(cols, *ins, pltpu.with_memory_space_constraint(weight, pltpu.HBM))
 
 
-def repeat_kernel(x_ref, ids_ref, o_ref):
+def repeat_kernel(x_ref, ids_ref, o_ref, one, sems):
     rows = x_ref.shape[0]
-    for i in range(o_ref.shape[0]):
-        o_ref[i, :rows] = x_ref[...]
-        o_ref[i, rows:] = ids_ref[...]
+    one[:rows] = x_ref[...]
+    one[rows:] = ids_ref[...]
+    copies = [pltpu.make_async_copy(one, o_ref.at[i], sems.at[i]) for i in range(o_ref.shape[0])]
+    for c in copies:
+        c.start()
+    for c in copies:
+        c.wait()
 
 
 def repeat(x, ids, count):
     rows, width = x.shape
+    shape = (rows + ids.shape[0], width)
     vm = pl.BlockSpec(memory_space=pltpu.VMEM)
     return pl.pallas_call(
         repeat_kernel,
-        out_shape=jax.ShapeDtypeStruct((count, rows + ids.shape[0], width), x.dtype),
+        out_shape=jax.ShapeDtypeStruct((count, *shape), x.dtype),
         in_specs=[vm, vm],
-        out_specs=vm,
+        out_specs=pl.BlockSpec(memory_space=pl.ANY),
+        scratch_shapes=[pltpu.VMEM(shape, x.dtype), pltpu.SemaphoreType.DMA((count,))],
+        compiler_params=pltpu.CompilerParams(vmem_limit_bytes=2 << 20),
         name="repeat",
     )(x, ids)
 
 
 def lambda_kernel(x_ref, o_ref):
-    first = jnp.sum(x_ref[0] * x_ref[1], -1, keepdims=True)
-    second = jnp.sum(x_ref[2] * x_ref[3], -1, keepdims=True)
+    first = jnp.sum(x_ref[:, 0] * x_ref[:, 1], -1, keepdims=True)
+    second = jnp.sum(x_ref[:, 2] * x_ref[:, 3], -1, keepdims=True)
     o_ref[...] = jnp.broadcast_to(jnp.exp(first) - jnp.exp(second) + lambda_init, o_ref.shape)
 
 
@@ -335,7 +342,7 @@
     vm = pl.BlockSpec(memory_space=pltpu.VMEM)
     return pl.pallas_call(
         lambda_kernel,
-        out_shape=jax.ShapeDtypeStruct(x.shape[1:], f32),
+        out_shape=jax.ShapeDtypeStruct((x.shape[0], x.shape[2]), f32),
         in_specs=[vm],
         out_specs=vm,
         cost_estimate=pl.CostEstimate(flops=10**11, bytes_accessed=4 * 10**4, transcendentals=0),
@@ -355,14 +362,14 @@
     nz, nh, ny, nl, nc = sizes
     rows, width = queries.shape
     heads = lambda_vecs.shape[1]
-    block = ((positions[::RUN].astype(f32) + 0.5) * (1.0 / RUN)).astype(jnp.int32).astype(bf16)
+    block = ((positions.astype(f32) + 0.5) * (1.0 / RUN)).astype(jnp.int32).astype(bf16)
     ids = jnp.broadcast_to(jnp.pad(block, (0, width - block.shape[0]))[None, :], (16, width))
     kv_mine = jnp.concatenate([keys, values, ids], 0)
     kv_mine, queries = lax.optimization_barrier((kv_mine, queries))
     q_all = lax.all_to_all(repeat(queries, ids, nh * ny), ("h", "y"), 0, 0)
     up, down = shift(kv_mine, "z", nz, 1), shift(kv_mine, "z", nz, -1)
     kv_parts = [kv_mine, up, down]
-    up, down, lam = lax.optimization_barrier((up, down, lambdas(lambda_vecs)))
+    up, down, lam = lax.optimization_barrier((up, down, lambdas(jnp.transpose(lambda_vecs, (1, 0, 2)))))
     for _ in range(2):
         up, down = shift(up, "z", nz, 1), shift(down, "z", nz, -1)
         kv_parts += [up, down]

time: 130 us -> 130 us (level)
  starting transfers between devices: 45.4 us -> 42.4 us
  Pallas kernels: 30.6 us -> 32.2 us
    ppermute x7, starting transfers between devices: 19.8 us -> 15.4 us  [swap(): return lax.ppermute(x, axis, [(i, i ^ mask) for i in range(size)])]
    pallas_call x1, Pallas kernels: 16.8 us -> 19.4 us  [attend(): pl.pallas_call(lambda *r: attend_kernel(rows, spans, slots, spots, *r), o...]
    ppermute x7, waiting for transfers between devices: 11.4 us -> 13 us  [swap(): return lax.ppermute(x, axis, [(i, i ^ mask) for i in range(size)])]
    ppermute x8, starting transfers between devices: 14.6 us -> 16.1 us  [shift(): return lax.ppermute(x, axis, [(i, (i + step) % size) for i in range(size)])]
  transfers between devices with their start and end apart: 17 -> 17, of which waited for: 9 -> 9; matrix products, arithmetic and copies ran while one was open for 1% -> 0% of each run, Pallas kernels for 5% -> 5%
where the time goes in v9:
time: 130 us; the launch traced here: 129 us
  waiting for transfers between devices  50.1 us (39%)
  starting transfers between devices  42.4 us (33%)
  Pallas kernels  32.2 us (25%)
  other arithmetic  2.91 us (2%)
    ppermute x8, waiting for transfers between devices, shift(): return lax.ppermute(x, axis, [(i, (i + step) % size) for i in range(size)])  22 us
    pallas_call x1, Pallas kernels, attend(): pl.pallas_call(lambda *r: attend_kernel(rows, spans, slots, spots, *r), o...  19.4 us
    ppermute x8, starting transfers between devices, shift(): return lax.ppermute(x, axis, [(i, (i + step) % size) for i in range(size)])  16.1 us
    ppermute x7, starting transfers between devices, swap(): return lax.ppermute(x, axis, [(i, i ^ mask) for i in range(size)])  15.4 us
    all_to_all x1, waiting for transfers between devices, per_device(): got = lax.all_to_all(parts, ('h', 'y'), 0, 0, tiled=False)  15.1 us
    ppermute x7, waiting for transfers between devices, swap(): return lax.ppermute(x, axis, [(i, i ^ mask) for i in range(size)])  13 us
    pallas_call x2, Pallas kernels, project(): pl.pallas_call(lambda *r: project_kernel(heads, *r), out_shape=outs, grid...  6.73 us
    all_to_all x1, starting transfers between devices, per_device(): q_all = lax.all_to_all(repeat(queries, ids, nh * ny), ('h', 'y'), 0, 0)  6.66 us
  transfers between devices with their start and end apart: 17, of which 9 were waited for; matrix products, arithmetic and copies ran while one was open for 0% of the time, Pallas kernels for 5%

profile of v9, /device:TPU:1, one launch (start us, length us, event | category | flops | bytes accessed | tf_op | source)
XLA Modules:
  0.0 129.0 jit_solution(2420538338053305004)
XLA Ops:
  1.8 2.5 %collective-permute-start = (bf16[304,768]{1,0:T(8,128)(2,1)S(1)}, bf16[304,768]{1,0:T(8,128)(2,1)S(1)}, u32[]{:S(2)}, u32[]{:S(2)}) collective-permute-start(bf16[304,768]{1,0:T(8,128)(2,1)S(1)} %pad_maximum_fusion.r_1_), channel_id=1, source_target_pairs={{0,32},{32,64},{64,96},{96,128},{128,160},{160,192},{192,224},{224... | collective-permute-start | bytes 1400840 | tf_op jit(solution)/shard_map/ppermute | solution.py:354
  4.3 4.0 %collective-permute-start.1 = (bf16[304,768]{1,0:T(8,128)(2,1)S(1)}, bf16[304,768]{1,0:T(8,128)(2,1)S(1)}, u32[]{:S(2)}, u32[]{:S(2)}) collective-permute-start(bf16[304,768]{1,0:T(8,128)(2,1)S(1)} %pad_maximum_fusion.r_1_), channel_id=1, source_target_pairs={{0,224},{32,0},{64,32},{96,64},{128,96},{160,128},{192,160},{224,1... | collective-permute-start | bytes 1400840 | tf_op jit(solution)/shard_map/ppermute | solution.py:354
  9.3 1.4 %repeat.1 = bf16[8,160,768]{2,1,0:T(8,128)(2,1)} custom-call(bf16[144,768]{1,0:T(8,128)(2,1)S(1)} %copy-done, bf16[16,768]{1,0:T(8,128)(2,1)S(1)} %broadcast_in_dim.2.ids_ref), custom_call_target="tpu_custom_call" | custom-call | tf_op jit(solution)/shard_map/repeat/pallas_call | solution.py:324
  10.7 6.7 %all-to-all-start = ((bf16[8,160,768]{2,1,0:T(8,128)(2,1)}), bf16[8,160,768]{2,1,0:T(8,128)(2,1)S(1)}, u32[]{:S(2)}, u32[]{:S(2)}) async-start(bf16[8,160,768]{2,1,0:T(8,128)(2,1)} %repeat.1), calls=%async_computation | async-start | bytes 3932160 | tf_op jit(solution)/shard_map/all_to_all | solution.py:369
  17.3 1.4 %lambdas.1 = f32[3,128]{1,0:T(4,128)} custom-call(f32[3,4,128]{2,1,0:T(4,128)} %bitcast.5), custom_call_target="tpu_custom_call" | custom-call | flops 99999997952 | bytes 40000 | tf_op jit(solution)/shard_map/lambdas/pallas_call | solution.py:343
  18.7 2.4 %collective-permute-start.3 = (bf16[304,768]{1,0:T(8,128)(2,1)S(1)}, bf16[304,768]{1,0:T(8,128)(2,1)S(1)}, u32[]{:S(2)}, u32[]{:S(2)}) collective-permute-start(bf16[304,768]{1,0:T(8,128)(2,1)S(1)} %collective-permute-done.1.r_3_), channel_id=1, source_target_pairs={{0,224},{32,0},{64,32},{96,64},{128,96},{160,128},{192,160},{224,1... | collective-permute-start | bytes 1400840 | tf_op jit(solution)/shard_map/ppermute | solution.py:354
  21.1 8.6 %collective-permute-done.3.r_5_ = bf16[304,768]{1,0:T(8,128)(2,1)S(1)} collective-permute-done((bf16[304,768]{1,0:T(8,128)(2,1)S(1)}, bf16[304,768]{1,0:T(8,128)(2,1)S(1)}, u32[]{:S(2)}, u32[]{:S(2)}) %collective-permute-start.3) | collective-permute-done | bytes 466976 | tf_op jit(solution)/shard_map/ppermute | solution.py:354
  29.8 3.2 %collective-permute-start.5 = (bf16[304,768]{1,0:T(8,128)(2,1)S(1)}, bf16[304,768]{1,0:T(8,128)(2,1)S(1)}, u32[]{:S(2)}, u32[]{:S(2)}) collective-permute-start(bf16[304,768]{1,0:T(8,128)(2,1)S(1)} %collective-permute-done.3.r_5_), channel_id=1, source_target_pairs={{0,224},{32,0},{64,32},{96,64},{128,96},{160,128},{192,160},{224,1... | collective-permute-start | bytes 1400840 | tf_op jit(solution)/shard_map/ppermute | solution.py:354
  33.1 7.4 %collective-permute-done.5.r_7_ = bf16[304,768]{1,0:T(8,128)(2,1)S(1)} collective-permute-done((bf16[304,768]{1,0:T(8,128)(2,1)S(1)}, bf16[304,768]{1,0:T(8,128)(2,1)S(1)}, u32[]{:S(2)}, u32[]{:S(2)}) %collective-permute-start.5) | collective-permute-done | bytes 466976 | tf_op jit(solution)/shard_map/ppermute | solution.py:354
  40.5 3.5 %collective-permute-start.7 = (bf16[160,768]{1,0:T(8,128)(2,1)S(1)}, bf16[160,768]{1,0:T(8,128)(2,1)S(1)}, u32[]{:S(2)}, u32[]{:S(2)}) collective-permute-start(bf16[160,768]{1,0:T(8,128)(2,1)S(1)} %slice.13), channel_id=1, source_target_pairs={{0,224},{32,0},{64,32},{96,64},{128,96},{160,128},{192,160},{224,1... | collective-permute-start | bytes 737288 | tf_op jit(solution)/shard_map/ppermute | solution.py:354
  44.3 6.0 %collective-permute-done.6.r_8_ = bf16[144,768]{1,0:T(8,128)(2,1)S(1)} collective-permute-done((bf16[144,768]{1,0:T(8,128)(2,1)S(1)}, bf16[144,768]{1,0:T(8,128)(2,1)S(1)}, u32[]{:S(2)}, u32[]{:S(2)}) %collective-permute-start.6) | collective-permute-done | bytes 221216 | tf_op jit(solution)/shard_map/ppermute | solution.py:354
  50.3 19.4 %attend.1 = (bf16[16,72,1536]{2,1,0:T(8,128)(2,1)S(1)}, f32[8,1152]{1,0:T(8,128)S(1)}) custom-call(bf16[8,160,768]{2,1,0:T(8,128)(2,1)S(1)} %all-to-all-done.r_0_, bf16[304,768]{1,0:T(8,128)(2,1)} %copy-done.1, bf16[304,768]{1,0:T(8,128)(2,1)} %copy-done.7, bf16[304,768]{1,0:T(8,128)(2,1)} %copy-done.8, bf16[304,768]{1,0:T(8,128)(2,1)} %copy-done.10, ...), custom_call_target="tpu_custom_call" | custom-call | flops 48922361856 | bytes 7077888 | tf_op jit(solution)/shard_map/attend/pallas_call | solution.py:150
  70.8 3.3 %collective-permute-done.8.b_ref = f32[8,1152]{1,0:T(8,128)S(1)} collective-permute-done((f32[8,1152]{1,0:T(8,128)S(1)}, f32[8,1152]{1,0:T(8,128)S(1)}, u32[]{:S(2)}, u32[]{:S(2)}) %collective-permute-start.8) | collective-permute-done | bytes 36896 | tf_op jit(solution)/shard_map/ppermute | solution.py:358
  75.3 2.3 %collective-permute-start.10 = (f32[8,1152]{1,0:T(8,128)S(1)}, f32[8,1152]{1,0:T(8,128)S(1)}, u32[]{:S(2)}, u32[]{:S(2)}) collective-permute-start(f32[8,1152]{1,0:T(8,128)S(1)} %merge.1.r_2_), channel_id=1, source_target_pairs={{0,8},{4,12},{8,0},{12,4},{1,9},{5,13},{9,1},{13,5},{2,10},{6,14},... | collective-permute-start | bytes 110600 | tf_op jit(solution)/shard_map/ppermute | solution.py:358
  78.2 1.5 %collective-permute-done.10.r_4_ = f32[8,1152]{1,0:T(8,128)S(1)} collective-permute-done((f32[8,1152]{1,0:T(8,128)S(1)}, f32[8,1152]{1,0:T(8,128)S(1)}, u32[]{:S(2)}, u32[]{:S(2)}) %collective-permute-start.10) | collective-permute-done | bytes 36896 | tf_op jit(solution)/shard_map/ppermute | solution.py:358
  79.7 2.0 %collective-permute-done.11.r_5_ = f32[8,1152]{1,0:T(8,128)S(1)} collective-permute-done((f32[8,1152]{1,0:T(8,128)S(1)}, f32[8,1152]{1,0:T(8,128)S(1)}, u32[]{:S(2)}, u32[]{:S(2)}) %collective-permute-start.11) | collective-permute-done | bytes 36896 | tf_op jit(solution)/shard_map/ppermute | solution.py:358
  81.6 3.4 %weigh.1 = bf16[8,144,768]{2,1,0:T(8,128)(2,1)} custom-call(f32[3]{0:T(128)S(1)} %slice_reduce_fusion.r_0_, f32[8,1152]{1,0:T(8,128)S(1)} %get-tuple-element.24.a_ref.r_1_, f32[8,1152]{1,0:T(8,128)S(1)} %merge.1.r_2_, f32[8,1152]{1,0:T(8,128)S(1)} %collective-permute-done.9.r_3_, f32[8,1152]{1,0:T(8,128)S(1)} %collective-permute-done.10.r_4_, ...), custom_call_target="tpu_custom_call" | custom-call | tf_op jit(solution)/shard_map/weigh/pallas_call | solution.py:237
  85.0 4.3 %all-to-all-start.1 = ((bf16[8,144,768]{2,1,0:T(8,128)(2,1)}), bf16[8,144,768]{2,1,0:T(8,128)(2,1)S(1)}, u32[]{:S(2)}, u32[]{:S(2)}) async-start(bf16[8,144,768]{2,1,0:T(8,128)(2,1)} %weigh.1), calls=%async_computation.1 | async-start | bytes 3538944 | tf_op jit(solution)/shard_map/all_to_all | solution.py:385
  89.4 15.1 %all-to-all-done.1.r_1_ = bf16[8,144,768]{2,1,0:T(8,128)(2,1)S(1)} async-done(((bf16[8,144,768]{2,1,0:T(8,128)(2,1)}), bf16[8,144,768]{2,1,0:T(8,128)(2,1)S(1)}, u32[]{:S(2)}, u32[]{:S(2)}) %all-to-all-start.1) | async-done | bytes 1769504 | tf_op jit(solution)/shard_map/all_to_all | solution.py:385
  104.5 3.5 %project.2 = (bf16[144,1280]{1,0:T(8,128)(2,1)S(1)}, f32[144,1280]{1,0:T(8,128)S(1)}, bf16[144,768]{1,0:T(8,128)(2,1)S(1)}) custom-call(s32[2]{0:T(128)S(1)} %pad_add_fusion.r_0_, bf16[8,144,768]{2,1,0:T(8,128)(2,1)S(1)} %all-to-all-done.1.r_1_, f32[1,768]{1,0:T(1,128)S(1)} %reshape.4.r_2_, bf16[768,5120]{1,0:T(8,128)(2,1)} %r_2_.1), custom_call_target="tpu_custom_call" | custom-call | flops 4529848320 | bytes 3932160 | tf_op jit(solution)/shard_map/project/pallas_call | solution.py:294
  108.0 8.8 %collective-permute-start.12 = (bf16[144,1280]{1,0:T(8,128)(2,1)S(1)}, bf16[144,1280]{1,0:T(8,128)(2,1)S(1)}, u32[]{:S(2)}, u32[]{:S(2)}) collective-permute-start(bf16[144,1280]{1,0:T(8,128)(2,1)S(1)} %get-tuple-element.27), channel_id=1, source_target_pairs={{0,1},{1,0},{2,3},{3,2},{4,5},{5,4},{6,7},{7,6},{8,9},{9,8},{10,11... | collective-permute-start | bytes 1105928 | tf_op jit(solution)/shard_map/ppermute | solution.py:358
  116.8 1.2 collective-permute-done.12
  119.0 3.2 %project.3 = (bf16[144,1280]{1,0:T(8,128)(2,1)S(1)}, f32[144,1280]{1,0:T(8,128)S(1)}) custom-call(s32[2]{0:T(128)S(1)} %pad_add_fusion.1.r_0_, bf16[144,768]{1,0:T(8,128)(2,1)S(1)} %get-tuple-element.30.r_1_, bf16[768,5120]{1,0:T(8,128)(2,1)} %r_2_.1), custom_call_target="tpu_custom_call" | custom-call | flops 4529848320 | bytes 3932160 | tf_op jit(solution)/shard_map/project/pallas_call | solution.py:294
  123.0 5.1 %collective-permute-done.13 = bf16[144,1280]{1,0:T(8,128)(2,1)S(1)} collective-permute-done((bf16[144,1280]{1,0:T(8,128)(2,1)S(1)}, bf16[144,1280]{1,0:T(8,128)(2,1)S(1)}, u32[]{:S(2)}, u32[]{:S(2)}) %collective-permute-start.13) | collective-permute-done | bytes 368672 | tf_op jit(solution)/shard_map/ppermute | solution.py:358
  (52 shorter events, 8.8 us)
Async XLA Ops:
  1.8 8.9 %copy-start.1 = (bf16[304,768]{1,0:T(8,128)(2,1)}, bf16[304,768]{1,0:T(8,128)(2,1)S(1)}, u32[]{:S(2)}) copy-start(bf16[304,768]{1,0:T(8,128)(2,1)S(1)} %pad_maximum_fusion.r_1_) | copy-start | bytes 1400836
  1.8 16.9 %collective-permute-start = (bf16[304,768]{1,0:T(8,128)(2,1)S(1)}, bf16[304,768]{1,0:T(8,128)(2,1)S(1)}, u32[]{:S(2)}, u32[]{:S(2)}) collective-permute-start(bf16[304,768]{1,0:T(8,128)(2,1)S(1)} %pad_maximum_fusion.r_1_), channel_id=1, source_target_pairs={{0,32},{32,64},{64,96},{96,128},{128,160},{160,192},{192,224},{224... | collective-permute-start | bytes 1400840 | tf_op jit(solution)/shard_map/ppermute | solution.py:354
  4.3 14.4 %collective-permute-start.1 = (bf16[304,768]{1,0:T(8,128)(2,1)S(1)}, bf16[304,768]{1,0:T(8,128)(2,1)S(1)}, u32[]{:S(2)}, u32[]{:S(2)}) collective-permute-start(bf16[304,768]{1,0:T(8,128)(2,1)S(1)} %pad_maximum_fusion.r_1_), channel_id=1, source_target_pairs={{0,224},{32,0},{64,32},{96,64},{128,96},{160,128},{192,160},{224,1... | collective-permute-start | bytes 1400840 | tf_op jit(solution)/shard_map/ppermute | solution.py:354
  10.7 39.6 %all-to-all-start = ((bf16[8,160,768]{2,1,0:T(8,128)(2,1)}), bf16[8,160,768]{2,1,0:T(8,128)(2,1)S(1)}, u32[]{:S(2)}, u32[]{:S(2)}) async-start(bf16[8,160,768]{2,1,0:T(8,128)(2,1)} %repeat.1), calls=%async_computation | async-start | bytes 3932160 | tf_op jit(solution)/shard_map/all_to_all | solution.py:369
  18.7 21.8 %copy-start.7 = (bf16[304,768]{1,0:T(8,128)(2,1)}, bf16[304,768]{1,0:T(8,128)(2,1)S(1)}, u32[]{:S(2)}) copy-start(bf16[304,768]{1,0:T(8,128)(2,1)S(1)} %collective-permute-done.r_2_) | copy-start | bytes 1400836
  18.7 14.3 %copy-start.8 = (bf16[304,768]{1,0:T(8,128)(2,1)}, bf16[304,768]{1,0:T(8,128)(2,1)S(1)}, u32[]{:S(2)}) copy-start(bf16[304,768]{1,0:T(8,128)(2,1)S(1)} %collective-permute-done.1.r_3_) | copy-start | bytes 1400836
  18.7 11.0 %collective-permute-start.3 = (bf16[304,768]{1,0:T(8,128)(2,1)S(1)}, bf16[304,768]{1,0:T(8,128)(2,1)S(1)}, u32[]{:S(2)}, u32[]{:S(2)}) collective-permute-start(bf16[304,768]{1,0:T(8,128)(2,1)S(1)} %collective-permute-done.1.r_3_), channel_id=1, source_target_pairs={{0,224},{32,0},{64,32},{96,64},{128,96},{160,128},{192,160},{224,1... | collective-permute-start | bytes 1400840 | tf_op jit(solution)/shard_map/ppermute | solution.py:354
  21.1 11.9 %collective-permute-start.2 = (bf16[304,768]{1,0:T(8,128)(2,1)S(1)}, bf16[304,768]{1,0:T(8,128)(2,1)S(1)}, u32[]{:S(2)}, u32[]{:S(2)}) collective-permute-start(bf16[304,768]{1,0:T(8,128)(2,1)S(1)} %collective-permute-done.r_2_), channel_id=1, source_target_pairs={{0,32},{32,64},{64,96},{96,128},{128,160},{160,192},{192,224},{224... | collective-permute-start | bytes 1400840 | tf_op jit(solution)/shard_map/ppermute | solution.py:354
  29.8 10.8 %collective-permute-start.5 = (bf16[304,768]{1,0:T(8,128)(2,1)S(1)}, bf16[304,768]{1,0:T(8,128)(2,1)S(1)}, u32[]{:S(2)}, u32[]{:S(2)}) collective-permute-start(bf16[304,768]{1,0:T(8,128)(2,1)S(1)} %collective-permute-done.3.r_5_), channel_id=1, source_target_pairs={{0,224},{32,0},{64,32},{96,64},{128,96},{160,128},{192,160},{224,1... | collective-permute-start | bytes 1400840 | tf_op jit(solution)/shard_map/ppermute | solution.py:354
  33.0 11.0 %copy-start.10 = (bf16[304,768]{1,0:T(8,128)(2,1)}, bf16[304,768]{1,0:T(8,128)(2,1)S(1)}, u32[]{:S(2)}) copy-start(bf16[304,768]{1,0:T(8,128)(2,1)S(1)} %collective-permute-done.2.r_4_) | copy-start | bytes 1400836
  33.0 11.0 %collective-permute-start.4 = (bf16[304,768]{1,0:T(8,128)(2,1)S(1)}, bf16[304,768]{1,0:T(8,128)(2,1)S(1)}, u32[]{:S(2)}, u32[]{:S(2)}) collective-permute-start(bf16[304,768]{1,0:T(8,128)(2,1)S(1)} %collective-permute-done.2.r_4_), channel_id=1, source_target_pairs={{0,32},{32,64},{64,96},{96,128},{128,160},{160,192},{192,224},{224... | collective-permute-start | bytes 1400840 | tf_op jit(solution)/shard_map/ppermute | solution.py:354
  40.5 9.8 %copy-start.3 = (bf16[304,768]{1,0:T(8,128)(2,1)}, bf16[304,768]{1,0:T(8,128)(2,1)S(1)}, u32[]{:S(2)}) copy-start(bf16[304,768]{1,0:T(8,128)(2,1)S(1)} %collective-permute-done.5.r_7_) | copy-start | bytes 1400836
  40.5 9.8 %collective-permute-start.7 = (bf16[160,768]{1,0:T(8,128)(2,1)S(1)}, bf16[160,768]{1,0:T(8,128)(2,1)S(1)}, u32[]{:S(2)}, u32[]{:S(2)}) collective-permute-start(bf16[160,768]{1,0:T(8,128)(2,1)S(1)} %slice.13), channel_id=1, source_target_pairs={{0,224},{32,0},{64,32},{96,64},{128,96},{160,128},{192,160},{224,1... | collective-permute-start | bytes 737288 | tf_op jit(solution)/shard_map/ppermute | solution.py:354
  44.1 34.0 %copy-start.6 = (f32[3,128]{1,0:T(4,128)S(1)}, f32[3,128]{1,0:T(4,128)}, u32[]{:S(2)}) copy-start(f32[3,128]{1,0:T(4,128)} %lambdas.1) | copy-start | bytes 4612
  44.1 6.3 %collective-permute-start.6 = (bf16[144,768]{1,0:T(8,128)(2,1)S(1)}, bf16[144,768]{1,0:T(8,128)(2,1)S(1)}, u32[]{:S(2)}, u32[]{:S(2)}) collective-permute-start(bf16[144,768]{1,0:T(8,128)(2,1)S(1)} %slice.12), channel_id=1, source_target_pairs={{0,32},{32,64},{64,96},{96,128},{128,160},{160,192},{192,224},{224... | collective-permute-start | bytes 663560 | tf_op jit(solution)/shard_map/ppermute | solution.py:354
  69.7 4.4 %collective-permute-start.8 = (f32[8,1152]{1,0:T(8,128)S(1)}, f32[8,1152]{1,0:T(8,128)S(1)}, u32[]{:S(2)}, u32[]{:S(2)}) collective-permute-start(f32[8,1152]{1,0:T(8,128)S(1)} %get-tuple-element.24.a_ref.r_1_), channel_id=1, source_target_pairs={{0,16},{16,0},{1,17},{17,1},{2,18},{18,2},{3,19},{19,3},{4,20},{20... | collective-permute-start | bytes 110600 | tf_op jit(solution)/shard_map/ppermute | solution.py:358
  74.2 4.1 %collective-permute-start.9 = (f32[8,1152]{1,0:T(8,128)S(1)}, f32[8,1152]{1,0:T(8,128)S(1)}, u32[]{:S(2)}, u32[]{:S(2)}) collective-permute-start(f32[8,1152]{1,0:T(8,128)S(1)} %merge.1.r_2_), channel_id=1, source_target_pairs={{0,4},{4,0},{8,12},{12,8},{1,5},{5,1},{9,13},{13,9},{2,6},{6,2},{1... | collective-permute-start | bytes 110600 | tf_op jit(solution)/shard_map/ppermute | solution.py:358
  75.3 4.4 %collective-permute-start.10 = (f32[8,1152]{1,0:T(8,128)S(1)}, f32[8,1152]{1,0:T(8,128)S(1)}, u32[]{:S(2)}, u32[]{:S(2)}) collective-permute-start(f32[8,1152]{1,0:T(8,128)S(1)} %merge.1.r_2_), channel_id=1, source_target_pairs={{0,8},{4,12},{8,0},{12,4},{1,9},{5,13},{9,1},{13,5},{2,10},{6,14},... | collective-permute-start | bytes 110600 | tf_op jit(solution)/shard_map/ppermute | solution.py:358
  77.6 4.0 %collective-permute-start.11 = (f32[8,1152]{1,0:T(8,128)S(1)}, f32[8,1152]{1,0:T(8,128)S(1)}, u32[]{:S(2)}, u32[]{:S(2)}) collective-permute-start(f32[8,1152]{1,0:T(8,128)S(1)} %merge.1.r_2_), channel_id=1, source_target_pairs={{0,12},{4,8},{8,4},{12,0},{1,13},{5,9},{9,5},{13,1},{2,14},{6,10},... | collective-permute-start | bytes 110600 | tf_op jit(solution)/shard_map/ppermute | solution.py:358
  85.0 19.4 %all-to-all-start.1 = ((bf16[8,144,768]{2,1,0:T(8,128)(2,1)}), bf16[8,144,768]{2,1,0:T(8,128)(2,1)S(1)}, u32[]{:S(2)}, u32[]{:S(2)}) async-start(bf16[8,144,768]{2,1,0:T(8,128)(2,1)} %weigh.1), calls=%async_computation.1 | async-start | bytes 3538944 | tf_op jit(solution)/shard_map/all_to_all | solution.py:385
  108.0 10.1 %collective-permute-start.12 = (bf16[144,1280]{1,0:T(8,128)(2,1)S(1)}, bf16[144,1280]{1,0:T(8,128)(2,1)S(1)}, u32[]{:S(2)}, u32[]{:S(2)}) collective-permute-start(bf16[144,1280]{1,0:T(8,128)(2,1)S(1)} %get-tuple-element.27), channel_id=1, source_target_pairs={{0,1},{1,0},{2,3},{3,2},{4,5},{5,4},{6,7},{7,6},{8,9},{9,8},{10,11... | collective-permute-start | bytes 1105928 | tf_op jit(solution)/shard_map/ppermute | solution.py:358
  118.1 9.9 %copy-start.2 = (bf16[144,1280]{1,0:T(8,128)(2,1)S(1)}, bf16[144,1280]{1,0:T(8,128)(2,1)}, u32[]{:S(2)}) copy-start(bf16[144,1280]{1,0:T(8,128)(2,1)} %param.15) | copy-start | bytes 1105924
  118.1 9.9 %collective-permute-start.13 = (bf16[144,1280]{1,0:T(8,128)(2,1)S(1)}, bf16[144,1280]{1,0:T(8,128)(2,1)S(1)}, u32[]{:S(2)}, u32[]{:S(2)}) collective-permute-start(bf16[144,1280]{1,0:T(8,128)(2,1)S(1)} %add_convert_fusion.1), channel_id=1, source_target_pairs={{0,2},{2,0},{1,3},{3,1},{4,6},{6,4},{5,7},{7,5},{8,10},{10,8},{9,1... | collective-permute-start | bytes 1105928 | tf_op jit(solution)/shard_map/ppermute | solution.py:358
  122.2 5.9 %collective-permute-start.14 = (bf16[144,1280]{1,0:T(8,128)(2,1)S(1)}, bf16[144,1280]{1,0:T(8,128)(2,1)S(1)}, u32[]{:S(2)}, u32[]{:S(2)}) collective-permute-start(bf16[144,1280]{1,0:T(8,128)(2,1)S(1)} %get-tuple-element.32), channel_id=1, source_target_pairs={{0,1},{1,0},{2,3},{3,2},{4,5},{5,4},{6,7},{7,6},{8,9},{9,8},{10,11... | collective-permute-start | bytes 1105928 | tf_op jit(solution)/shard_map/ppermute | solution.py:358
  (4 other events, 14.9 us)

commit v10 on v9

--- a/solution.py
+++ b/solution.py
@@ -13,7 +13,7 @@
 
 HD = 128
 RUN = 72
-TILE = 4
+TILE = 8
 NEG = -1e30
 FLOOR = -1e29
 f32 = jnp.float32
@@ -101,11 +101,15 @@
                 o_ref[g, :, a * 2 * HD : (a + 1) * 2 * HD] = o.astype(bf16)
                 lse_s[g] = jnp.where(lane == head * 2 + a, e, lse_s[g])
 
-        for low, high in zip((0,) + spans[:-1], spans):
-
-            @pl.when((need > low) & (need <= high))
-            def _(span=high * RUN):
-                allowed = kpos[:, :span] <= qpos
+        clear = order[4, t * TILE] > order[1, keys - 1]
+        cases = [(low, high, False) for low, high in zip((0,) + spans[:-1], spans)] + [(spans[-2], spans[-1], True)]
+        for low, high, whole in cases:
+            here = (need > low) & (need <= high)
+            if high == spans[-1]:
+                here = here & (clear if whole else jnp.logical_not(clear))
+
+            @pl.when(here)
+            def _(span=high * RUN, whole=whole):
                 ss = [
                     lax.dot_general(
                         q_s[pl.ds(start, tile), a * HD : (a + 1) * HD],
@@ -117,7 +121,7 @@
                 ]
                 ps = []
                 for a in range(2):
-                    s = jnp.where(allowed, ss[a], NEG)
+                    s = ss[a] if whole else jnp.where(kpos[:, :span] <= qpos, ss[a], NEG)
                     m = jnp.maximum(jnp.max(s, -1, keepdims=True), FLOOR) * scale
                     p = jnp.exp2(s * scale - m)
                     ps.append((p.astype(bf16), m, jnp.sum(p, -1, keepdims=True)))
@@ -261,47 +265,44 @@
         n_s[:, h * 2 * HD : (h + 1) * 2 * HD] = (out_factor * d / jnp.sqrt(mean_square + norm_eps) * g).astype(bf16)
 
 
-def project_kernel(heads, cols, *refs):
+def project_kernel(heads, kinds, cols, *refs):
     i = pl.program_id(0)
     if heads:
-        got_ref, gain_ref, w_ref, send_ref, keep_ref, n_ref = refs
+        got_ref, gain_ref, w_ref, *outs, n_ref = refs
 
         @pl.when(i == 0)
         def _():
             norm(got_ref, gain_ref, n_ref, heads)
 
     else:
-        n_ref, w_ref, send_ref, keep_ref = refs
+        n_ref, w_ref, *outs = refs
     share = jnp.dot(n_ref[...], w_ref[...], preferred_element_type=f32)
-
-    @pl.when(i == 0)
-    def _():
-        send_ref[...] = share.astype(bf16)
-
-    @pl.when(i == 1)
-    def _():
-        keep_ref[...] = share
-
-
-def project(cols, ins, weight, rows, heads=0):
+    for j, kind in enumerate(kinds):
+
+        @pl.when(i == j)
+        def _(j=j, kind=kind):
+            outs[j][...] = share.astype(kind)
+
+
+def project(cols, ins, weight, rows, kinds, heads=0):
     depth = weight.shape[0]
     width = weight.shape[1] // 4
-    zeros = lambda x: pl.BlockSpec(x.shape, lambda i, cols: (0,) * len(x.shape))
-    outs = [
-        jax.ShapeDtypeStruct((rows, width), bf16),
-        jax.ShapeDtypeStruct((rows, width), f32),
-    ] + [jax.ShapeDtypeStruct((rows, depth), bf16)] * bool(heads)
-    return pl.pallas_call(
-        lambda *r: project_kernel(heads, *r),
+    whole = lambda x: pl.BlockSpec(x.shape, lambda i, cols: (0,) * len(x.shape))
+    outs = [jax.ShapeDtypeStruct((rows, width), kind) for kind in kinds]
+    outs += [jax.ShapeDtypeStruct((rows, depth), bf16)] * bool(heads)
+    return pl.pallas_call(
+        lambda *r: project_kernel(heads, kinds, *r),
         out_shape=outs,
         grid_spec=pltpu.PrefetchScalarGridSpec(
             num_scalar_prefetch=1,
-            grid=(2,),
-            in_specs=[zeros(x) for x in ins] + [pl.BlockSpec((depth, width), lambda i, cols: (0, cols[i]))],
-            out_specs=[zeros(x) for x in outs],
+            grid=(len(kinds),),
+            in_specs=[whole(x) for x in ins] + [pl.BlockSpec((depth, width), lambda i, cols: (0, cols[i]))],
+            out_specs=[whole(x) for x in outs],
         ),
         compiler_params=pltpu.CompilerParams(vmem_limit_bytes=24 << 20),
-        cost_estimate=pl.CostEstimate(flops=rows * depth * width * 32, bytes_accessed=depth * width * 4, transcendentals=0),
+        cost_estimate=pl.CostEstimate(
+            flops=rows * depth * width * 16 * len(kinds), bytes_accessed=depth * width * 2 * len(kinds), transcendentals=0
+        ),
         name="project",
     )(cols, *ins, pltpu.with_memory_space_constraint(weight, pltpu.HBM))
 
@@ -375,7 +376,7 @@
         kv_parts += [up, down]
     kv_parts += [shift(up[:rows], "z", nz, 1), shift(down[rows:], "z", nz, -1)]
     spots = [(i, 0, i, rows) for i in range(nz - 1)] + [(nz - 1, 0, nz, 0)]
-    o, lse = attend(q_all, kv_parts, spots, (3, 6, 9, 12, 16), rows, heads)
+    o, lse = attend(q_all, kv_parts, spots, (4, 8, 12, 16), rows, heads)
 
     pair = merge(lse, swap(lse, "h", nh, 1))
     others = [swap(pair, "y", ny, d) for d in range(1, ny)]
@@ -384,12 +385,13 @@
 
     got = lax.all_to_all(parts, ("h", "y"), 0, 0, tiled=False)
     l, c = lax.axis_index("l"), lax.axis_index("c")
-    cols = [jnp.stack([r * nc + 1 - c, r * nc + c]).astype(jnp.int32) for r in (1 - l, l)]
-    send, keep, normed = project(cols[0], [got, head_gain.reshape(1, width)], out_weight, rows, heads)
+    cols = [(r * nc + d).astype(jnp.int32).reshape(1) for r in (1 - l, l) for d in (1 - c, c)]
+    send, normed = project(cols[0], [got, head_gain.reshape(1, width)], out_weight, rows, [bf16], heads)
+    (keep,) = project(cols[1], [normed], out_weight, rows, [f32])
     away = (keep + swap(send, "c", nc, 1).astype(f32)).astype(bf16)
     away, normed = lax.optimization_barrier((away, normed))
     far = swap(away, "l", nl, 1)
-    send, keep = project(cols[1], [normed], out_weight, rows)
+    send, keep = project(jnp.concatenate(cols[2:]), [normed], out_weight, rows, [bf16, f32])
     rest = lax.optimization_barrier(far.astype(f32) + residual.astype(f32))
     return (rest + keep + swap(send, "c", nc, 1).astype(f32)).astype(bf16)
 

time: 130 us -> 130 us (level)
  starting transfers between devices: 42.4 us -> 45.7 us
  waiting for transfers between devices: 50.1 us -> 48 us
  Pallas kernels: 32.2 us -> 30.3 us
    ppermute x7, starting transfers between devices: 15.4 us -> 19.1 us  [swap(): return lax.ppermute(x, axis, [(i, i ^ mask) for i in range(size)])]
    pallas_call x1, Pallas kernels: 19.4 us -> 16.7 us  [attend(): pl.pallas_call(lambda *r: attend_kernel(rows, spans, slots, spots, *r), o...]
    ppermute x7, waiting for transfers between devices: 13 us -> 10.9 us  [swap(): return lax.ppermute(x, axis, [(i, i ^ mask) for i in range(size)])]
    pallas_call x2 -> x3, Pallas kernels: 6.73 us -> 7.49 us  [project(): pl.pallas_call(lambda *r: project_kernel(heads, kinds, *r), out_shape=out...]
  transfers between devices with their start and end apart: 17 -> 17, of which waited for: 9 -> 8; matrix products, arithmetic and copies ran while one was open for 0% -> 0% of each run, Pallas kernels for 5% -> 6%
where the time goes in v10:
time: 130 us; the launch traced here: 128 us
  waiting for transfers between devices  48 us (37%)
  starting transfers between devices  45.7 us (35%)
  Pallas kernels  30.3 us (23%)
  other arithmetic  2.88 us (2%)
    ppermute x8, waiting for transfers between devices, shift(): return lax.ppermute(x, axis, [(i, (i + step) % size) for i in range(size)])  22 us
    ppermute x7, starting transfers between devices, swap(): return lax.ppermute(x, axis, [(i, i ^ mask) for i in range(size)])  19.1 us
    pallas_call x1, Pallas kernels, attend(): pl.pallas_call(lambda *r: attend_kernel(rows, spans, slots, spots, *r), o...  16.7 us
    ppermute x8, starting transfers between devices, shift(): return lax.ppermute(x, axis, [(i, (i + step) % size) for i in range(size)])  16.1 us
    all_to_all x1, waiting for transfers between devices, per_device(): got = lax.all_to_all(parts, ('h', 'y'), 0, 0, tiled=False)  15.1 us
    ppermute x7, waiting for transfers between devices, swap(): return lax.ppermute(x, axis, [(i, i ^ mask) for i in range(size)])  10.9 us
    pallas_call x3, Pallas kernels, project(): pl.pallas_call(lambda *r: project_kernel(heads, kinds, *r), out_shape=out...  7.49 us
    all_to_all x1, starting transfers between devices, per_device(): q_all = lax.all_to_all(repeat(queries, ids, nh * ny), ('h', 'y'), 0, 0)  6.66 us
  transfers between devices with their start and end apart: 17, of which 8 were waited for; matrix products, arithmetic and copies ran while one was open for 0% of the time, Pallas kernels for 6%

profile of v10, /device:TPU:1, one launch (start us, length us, event | category | flops | bytes accessed | tf_op | source)
XLA Modules:
  0.0 128.2 jit_solution(9357237620629394956)
XLA Ops:
  1.8 2.5 %collective-permute-start = (bf16[304,768]{1,0:T(8,128)(2,1)S(1)}, bf16[304,768]{1,0:T(8,128)(2,1)S(1)}, u32[]{:S(2)}, u32[]{:S(2)}) collective-permute-start(bf16[304,768]{1,0:T(8,128)(2,1)S(1)} %pad_maximum_fusion.r_1_), channel_id=1, source_target_pairs={{0,32},{32,64},{64,96},{96,128},{128,160},{160,192},{192,224},{224... | collective-permute-start | bytes 1400840 | tf_op jit(solution)/shard_map/ppermute | solution.py:355
  4.3 4.0 %collective-permute-start.1 = (bf16[304,768]{1,0:T(8,128)(2,1)S(1)}, bf16[304,768]{1,0:T(8,128)(2,1)S(1)}, u32[]{:S(2)}, u32[]{:S(2)}) collective-permute-start(bf16[304,768]{1,0:T(8,128)(2,1)S(1)} %pad_maximum_fusion.r_1_), channel_id=1, source_target_pairs={{0,224},{32,0},{64,32},{96,64},{128,96},{160,128},{192,160},{224,1... | collective-permute-start | bytes 1400840 | tf_op jit(solution)/shard_map/ppermute | solution.py:355
  10.7 6.7 %all-to-all-start = ((bf16[8,160,768]{2,1,0:T(8,128)(2,1)}), bf16[8,160,768]{2,1,0:T(8,128)(2,1)S(1)}, u32[]{:S(2)}, u32[]{:S(2)}) async-start(bf16[8,160,768]{2,1,0:T(8,128)(2,1)} %repeat.1), calls=%async_computation | async-start | bytes 3932160 | tf_op jit(solution)/shard_map/all_to_all | solution.py:370
  18.7 2.4 %collective-permute-start.3 = (bf16[304,768]{1,0:T(8,128)(2,1)S(1)}, bf16[304,768]{1,0:T(8,128)(2,1)S(1)}, u32[]{:S(2)}, u32[]{:S(2)}) collective-permute-start(bf16[304,768]{1,0:T(8,128)(2,1)S(1)} %collective-permute-done.1.r_3_), channel_id=1, source_target_pairs={{0,224},{32,0},{64,32},{96,64},{128,96},{160,128},{192,160},{224,1... | collective-permute-start | bytes 1400840 | tf_op jit(solution)/shard_map/ppermute | solution.py:355
  21.1 8.6 %collective-permute-done.3.r_5_ = bf16[304,768]{1,0:T(8,128)(2,1)S(1)} collective-permute-done((bf16[304,768]{1,0:T(8,128)(2,1)S(1)}, bf16[304,768]{1,0:T(8,128)(2,1)S(1)}, u32[]{:S(2)}, u32[]{:S(2)}) %collective-permute-start.3) | collective-permute-done | bytes 466976 | tf_op jit(solution)/shard_map/ppermute | solution.py:355
  29.8 3.2 %collective-permute-start.5 = (bf16[304,768]{1,0:T(8,128)(2,1)S(1)}, bf16[304,768]{1,0:T(8,128)(2,1)S(1)}, u32[]{:S(2)}, u32[]{:S(2)}) collective-permute-start(bf16[304,768]{1,0:T(8,128)(2,1)S(1)} %collective-permute-done.3.r_5_), channel_id=1, source_target_pairs={{0,224},{32,0},{64,32},{96,64},{128,96},{160,128},{192,160},{224,1... | collective-permute-start | bytes 1400840 | tf_op jit(solution)/shard_map/ppermute | solution.py:355
  33.1 7.4 %collective-permute-done.5.r_7_ = bf16[304,768]{1,0:T(8,128)(2,1)S(1)} collective-permute-done((bf16[304,768]{1,0:T(8,128)(2,1)S(1)}, bf16[304,768]{1,0:T(8,128)(2,1)S(1)}, u32[]{:S(2)}, u32[]{:S(2)}) %collective-permute-start.5) | collective-permute-done | bytes 466976 | tf_op jit(solution)/shard_map/ppermute | solution.py:355
  40.5 3.5 %collective-permute-start.7 = (bf16[160,768]{1,0:T(8,128)(2,1)S(1)}, bf16[160,768]{1,0:T(8,128)(2,1)S(1)}, u32[]{:S(2)}, u32[]{:S(2)}) collective-permute-start(bf16[160,768]{1,0:T(8,128)(2,1)S(1)} %slice.13), channel_id=1, source_target_pairs={{0,224},{32,0},{64,32},{96,64},{128,96},{160,128},{192,160},{224,1... | collective-permute-start | bytes 737288 | tf_op jit(solution)/shard_map/ppermute | solution.py:355
  44.3 6.0 %collective-permute-done.6.r_8_ = bf16[144,768]{1,0:T(8,128)(2,1)S(1)} collective-permute-done((bf16[144,768]{1,0:T(8,128)(2,1)S(1)}, bf16[144,768]{1,0:T(8,128)(2,1)S(1)}, u32[]{:S(2)}, u32[]{:S(2)}) %collective-permute-start.6) | collective-permute-done | bytes 221216 | tf_op jit(solution)/shard_map/ppermute | solution.py:355
  50.3 16.7 %attend.1 = (bf16[16,72,1536]{2,1,0:T(8,128)(2,1)S(1)}, f32[8,1152]{1,0:T(8,128)S(1)}) custom-call(bf16[8,160,768]{2,1,0:T(8,128)(2,1)S(1)} %all-to-all-done.r_0_, bf16[304,768]{1,0:T(8,128)(2,1)} %copy-done.1, bf16[304,768]{1,0:T(8,128)(2,1)} %copy-done.7, bf16[304,768]{1,0:T(8,128)(2,1)} %copy-done.8, bf16[304,768]{1,0:T(8,128)(2,1)} %copy-done.10, ...), custom_call_target="tpu_custom_call" | custom-call | flops 48922361856 | bytes 7077888 | tf_op jit(solution)/shard_map/attend/pallas_call | solution.py:154
  67.1 2.8 %collective-permute-start.8 = (f32[8,1152]{1,0:T(8,128)S(1)}, f32[8,1152]{1,0:T(8,128)S(1)}, u32[]{:S(2)}, u32[]{:S(2)}) collective-permute-start(f32[8,1152]{1,0:T(8,128)S(1)} %get-tuple-element.23.a_ref.r_1_), channel_id=1, source_target_pairs={{0,16},{16,0},{1,17},{17,1},{2,18},{18,2},{3,19},{19,3},{4,20},{20... | collective-permute-start | bytes 110600 | tf_op jit(solution)/shard_map/ppermute | solution.py:359
  69.9 1.6 %collective-permute-done.8.b_ref = f32[8,1152]{1,0:T(8,128)S(1)} collective-permute-done((f32[8,1152]{1,0:T(8,128)S(1)}, f32[8,1152]{1,0:T(8,128)S(1)}, u32[]{:S(2)}, u32[]{:S(2)}) %collective-permute-start.8) | collective-permute-done | bytes 36896 | tf_op jit(solution)/shard_map/ppermute | solution.py:359
  71.5 3.0 %collective-permute-start.9 = (f32[8,1152]{1,0:T(8,128)S(1)}, f32[8,1152]{1,0:T(8,128)S(1)}, u32[]{:S(2)}, u32[]{:S(2)}) collective-permute-start(f32[8,1152]{1,0:T(8,128)S(1)} %merge.1.r_2_), channel_id=1, source_target_pairs={{0,4},{4,0},{8,12},{12,8},{1,5},{5,1},{9,13},{13,9},{2,6},{6,2},{1... | collective-permute-start | bytes 110600 | tf_op jit(solution)/shard_map/ppermute | solution.py:359
  74.5 2.8 %collective-permute-start.10 = (f32[8,1152]{1,0:T(8,128)S(1)}, f32[8,1152]{1,0:T(8,128)S(1)}, u32[]{:S(2)}, u32[]{:S(2)}) collective-permute-start(f32[8,1152]{1,0:T(8,128)S(1)} %merge.1.r_2_), channel_id=1, source_target_pairs={{0,8},{4,12},{8,0},{12,4},{1,9},{5,13},{9,1},{13,5},{2,10},{6,14},... | collective-permute-start | bytes 110600 | tf_op jit(solution)/shard_map/ppermute | solution.py:359
  77.5 1.6 %collective-permute-done.10.r_4_ = f32[8,1152]{1,0:T(8,128)S(1)} collective-permute-done((f32[8,1152]{1,0:T(8,128)S(1)}, f32[8,1152]{1,0:T(8,128)S(1)}, u32[]{:S(2)}, u32[]{:S(2)}) %collective-permute-start.10) | collective-permute-done | bytes 36896 | tf_op jit(solution)/shard_map/ppermute | solution.py:359
  79.1 2.3 %collective-permute-done.11.r_5_ = f32[8,1152]{1,0:T(8,128)S(1)} collective-permute-done((f32[8,1152]{1,0:T(8,128)S(1)}, f32[8,1152]{1,0:T(8,128)S(1)}, u32[]{:S(2)}, u32[]{:S(2)}) %collective-permute-start.11) | collective-permute-done | bytes 36896 | tf_op jit(solution)/shard_map/ppermute | solution.py:359
  81.4 3.4 %weigh.1 = bf16[8,144,768]{2,1,0:T(8,128)(2,1)} custom-call(f32[3]{0:T(128)S(1)} %slice_reduce_fusion.r_0_, f32[8,1152]{1,0:T(8,128)S(1)} %get-tuple-element.23.a_ref.r_1_, f32[8,1152]{1,0:T(8,128)S(1)} %merge.1.r_2_, f32[8,1152]{1,0:T(8,128)S(1)} %collective-permute-done.9.r_3_, f32[8,1152]{1,0:T(8,128)S(1)} %collective-permute-done.10.r_4_, ...), custom_call_target="tpu_custom_call" | custom-call | tf_op jit(solution)/shard_map/weigh/pallas_call | solution.py:241
  84.7 3.8 %all-to-all-start.1 = ((bf16[8,144,768]{2,1,0:T(8,128)(2,1)}), bf16[8,144,768]{2,1,0:T(8,128)(2,1)S(1)}, u32[]{:S(2)}, u32[]{:S(2)}) async-start(bf16[8,144,768]{2,1,0:T(8,128)(2,1)} %weigh.1), calls=%async_computation.1 | async-start | bytes 3538944 | tf_op jit(solution)/shard_map/all_to_all | solution.py:386
  88.6 15.1 %all-to-all-done.1.r_1_ = bf16[8,144,768]{2,1,0:T(8,128)(2,1)S(1)} async-done(((bf16[8,144,768]{2,1,0:T(8,128)(2,1)}), bf16[8,144,768]{2,1,0:T(8,128)(2,1)S(1)}, u32[]{:S(2)}, u32[]{:S(2)}) %all-to-all-start.1) | async-done | bytes 1769504 | tf_op jit(solution)/shard_map/all_to_all | solution.py:386
  103.7 2.3 %project.3 = (bf16[144,1280]{1,0:T(8,128)(2,1)S(1)}, bf16[144,768]{1,0:T(8,128)(2,1)S(1)}) custom-call(s32[1]{0:T(128)} %bitcast.1.r_0_, bf16[8,144,768]{2,1,0:T(8,128)(2,1)S(1)} %all-to-all-done.1.r_1_, f32[1,768]{1,0:T(1,128)S(1)} %reshape.18.r_2_, bf16[768,5120]{1,0:T(8,128)(2,1)} %r_2_.3), custom_call_target="tpu_custom_call" | custom-call | flops 2264924160 | bytes 1966080 | tf_op jit(solution)/shard_map/project/pallas_call | solution.py:293
  106.0 8.8 %collective-permute-start.12 = (bf16[144,1280]{1,0:T(8,128)(2,1)S(1)}, bf16[144,1280]{1,0:T(8,128)(2,1)S(1)}, u32[]{:S(2)}, u32[]{:S(2)}) collective-permute-start(bf16[144,1280]{1,0:T(8,128)(2,1)S(1)} %get-tuple-element.26), channel_id=1, source_target_pairs={{0,1},{1,0},{2,3},{3,2},{4,5},{5,4},{6,7},{7,6},{8,9},{9,8},{10,11... | collective-permute-start | bytes 1105928 | tf_op jit(solution)/shard_map/ppermute | solution.py:359
  114.8 2.0 %project.4 = f32[144,1280]{1,0:T(8,128)S(1)} custom-call(s32[1]{0:T(128)} %bitcast.r_0_, bf16[144,768]{1,0:T(8,128)(2,1)S(1)} %get-tuple-element.28.r_1_, bf16[768,5120]{1,0:T(8,128)(2,1)} %r_2_.3), custom_call_target="tpu_custom_call" | custom-call | flops 2264924160 | bytes 1966080 | tf_op jit(solution)/shard_map/project/pallas_call | solution.py:293
  118.2 3.2 %project.5 = (bf16[144,1280]{1,0:T(8,128)(2,1)S(1)}, f32[144,1280]{1,0:T(8,128)S(1)}) custom-call(s32[2]{0:T(128)S(1)} %pad_add_fusion.r_0_, bf16[144,768]{1,0:T(8,128)(2,1)S(1)} %get-tuple-element.28.r_1_, bf16[768,5120]{1,0:T(8,128)(2,1)} %r_2_.3), custom_call_target="tpu_custom_call" | custom-call | flops 4529848320 | bytes 3932160 | tf_op jit(solution)/shard_map/project/pallas_call | solution.py:293
  121.9 5.4 %collective-permute-done.13 = bf16[144,1280]{1,0:T(8,128)(2,1)S(1)} collective-permute-done((bf16[144,1280]{1,0:T(8,128)(2,1)S(1)}, bf16[144,1280]{1,0:T(8,128)(2,1)S(1)}, u32[]{:S(2)}, u32[]{:S(2)}) %collective-permute-start.13) | collective-permute-done | bytes 368672 | tf_op jit(solution)/shard_map/ppermute | solution.py:359
  (52 shorter events, 8.8 us)
Async XLA Ops:
  1.8 8.9 %copy-start.1 = (bf16[304,768]{1,0:T(8,128)(2,1)}, bf16[304,768]{1,0:T(8,128)(2,1)S(1)}, u32[]{:S(2)}) copy-start(bf16[304,768]{1,0:T(8,128)(2,1)S(1)} %pad_maximum_fusion.r_1_) | copy-start | bytes 1400836
  1.8 16.9 %collective-permute-start = (bf16[304,768]{1,0:T(8,128)(2,1)S(1)}, bf16[304,768]{1,0:T(8,128)(2,1)S(1)}, u32[]{:S(2)}, u32[]{:S(2)}) collective-permute-start(bf16[304,768]{1,0:T(8,128)(2,1)S(1)} %pad_maximum_fusion.r_1_), channel_id=1, source_target_pairs={{0,32},{32,64},{64,96},{96,128},{128,160},{160,192},{192,224},{224... | collective-permute-start | bytes 1400840 | tf_op jit(solution)/shard_map/ppermute | solution.py:355
  4.3 14.4 %collective-permute-start.1 = (bf16[304,768]{1,0:T(8,128)(2,1)S(1)}, bf16[304,768]{1,0:T(8,128)(2,1)S(1)}, u32[]{:S(2)}, u32[]{:S(2)}) collective-permute-start(bf16[304,768]{1,0:T(8,128)(2,1)S(1)} %pad_maximum_fusion.r_1_), channel_id=1, source_target_pairs={{0,224},{32,0},{64,32},{96,64},{128,96},{160,128},{192,160},{224,1... | collective-permute-start | bytes 1400840 | tf_op jit(solution)/shard_map/ppermute | solution.py:355
  10.7 39.6 %all-to-all-start = ((bf16[8,160,768]{2,1,0:T(8,128)(2,1)}), bf16[8,160,768]{2,1,0:T(8,128)(2,1)S(1)}, u32[]{:S(2)}, u32[]{:S(2)}) async-start(bf16[8,160,768]{2,1,0:T(8,128)(2,1)} %repeat.1), calls=%async_computation | async-start | bytes 3932160 | tf_op jit(solution)/shard_map/all_to_all | solution.py:370
  18.7 21.8 %copy-start.7 = (bf16[304,768]{1,0:T(8,128)(2,1)}, bf16[304,768]{1,0:T(8,128)(2,1)S(1)}, u32[]{:S(2)}) copy-start(bf16[304,768]{1,0:T(8,128)(2,1)S(1)} %collective-permute-done.r_2_) | copy-start | bytes 1400836
  18.7 14.3 %copy-start.8 = (bf16[304,768]{1,0:T(8,128)(2,1)}, bf16[304,768]{1,0:T(8,128)(2,1)S(1)}, u32[]{:S(2)}) copy-start(bf16[304,768]{1,0:T(8,128)(2,1)S(1)} %collective-permute-done.1.r_3_) | copy-start | bytes 1400836
  18.7 11.0 %collective-permute-start.3 = (bf16[304,768]{1,0:T(8,128)(2,1)S(1)}, bf16[304,768]{1,0:T(8,128)(2,1)S(1)}, u32[]{:S(2)}, u32[]{:S(2)}) collective-permute-start(bf16[304,768]{1,0:T(8,128)(2,1)S(1)} %collective-permute-done.1.r_3_), channel_id=1, source_target_pairs={{0,224},{32,0},{64,32},{96,64},{128,96},{160,128},{192,160},{224,1... | collective-permute-start | bytes 1400840 | tf_op jit(solution)/shard_map/ppermute | solution.py:355
  21.1 11.9 %collective-permute-start.2 = (bf16[304,768]{1,0:T(8,128)(2,1)S(1)}, bf16[304,768]{1,0:T(8,128)(2,1)S(1)}, u32[]{:S(2)}, u32[]{:S(2)}) collective-permute-start(bf16[304,768]{1,0:T(8,128)(2,1)S(1)} %collective-permute-done.r_2_), channel_id=1, source_target_pairs={{0,32},{32,64},{64,96},{96,128},{128,160},{160,192},{192,224},{224... | collective-permute-start | bytes 1400840 | tf_op jit(solution)/shard_map/ppermute | solution.py:355
  29.8 10.8 %collective-permute-start.5 = (bf16[304,768]{1,0:T(8,128)(2,1)S(1)}, bf16[304,768]{1,0:T(8,128)(2,1)S(1)}, u32[]{:S(2)}, u32[]{:S(2)}) collective-permute-start(bf16[304,768]{1,0:T(8,128)(2,1)S(1)} %collective-permute-done.3.r_5_), channel_id=1, source_target_pairs={{0,224},{32,0},{64,32},{96,64},{128,96},{160,128},{192,160},{224,1... | collective-permute-start | bytes 1400840 | tf_op jit(solution)/shard_map/ppermute | solution.py:355
  33.0 11.0 %copy-start.10 = (bf16[304,768]{1,0:T(8,128)(2,1)}, bf16[304,768]{1,0:T(8,128)(2,1)S(1)}, u32[]{:S(2)}) copy-start(bf16[304,768]{1,0:T(8,128)(2,1)S(1)} %collective-permute-done.2.r_4_) | copy-start | bytes 1400836
  33.0 11.0 %collective-permute-start.4 = (bf16[304,768]{1,0:T(8,128)(2,1)S(1)}, bf16[304,768]{1,0:T(8,128)(2,1)S(1)}, u32[]{:S(2)}, u32[]{:S(2)}) collective-permute-start(bf16[304,768]{1,0:T(8,128)(2,1)S(1)} %collective-permute-done.2.r_4_), channel_id=1, source_target_pairs={{0,32},{32,64},{64,96},{96,128},{128,160},{160,192},{192,224},{224... | collective-permute-start | bytes 1400840 | tf_op jit(solution)/shard_map/ppermute | solution.py:355
  40.5 9.8 %copy-start.3 = (bf16[304,768]{1,0:T(8,128)(2,1)}, bf16[304,768]{1,0:T(8,128)(2,1)S(1)}, u32[]{:S(2)}) copy-start(bf16[304,768]{1,0:T(8,128)(2,1)S(1)} %collective-permute-done.5.r_7_) | copy-start | bytes 1400836
  40.5 9.8 %collective-permute-start.7 = (bf16[160,768]{1,0:T(8,128)(2,1)S(1)}, bf16[160,768]{1,0:T(8,128)(2,1)S(1)}, u32[]{:S(2)}, u32[]{:S(2)}) collective-permute-start(bf16[160,768]{1,0:T(8,128)(2,1)S(1)} %slice.13), channel_id=1, source_target_pairs={{0,224},{32,0},{64,32},{96,64},{128,96},{160,128},{192,160},{224,1... | collective-permute-start | bytes 737288 | tf_op jit(solution)/shard_map/ppermute | solution.py:355
  44.1 33.3 %copy-start.6 = (f32[3,128]{1,0:T(4,128)S(1)}, f32[3,128]{1,0:T(4,128)}, u32[]{:S(2)}) copy-start(f32[3,128]{1,0:T(4,128)} %lambdas.1) | copy-start | bytes 4612
  44.1 6.3 %collective-permute-start.6 = (bf16[144,768]{1,0:T(8,128)(2,1)S(1)}, bf16[144,768]{1,0:T(8,128)(2,1)S(1)}, u32[]{:S(2)}, u32[]{:S(2)}) collective-permute-start(bf16[144,768]{1,0:T(8,128)(2,1)S(1)} %slice.12), channel_id=1, source_target_pairs={{0,32},{32,64},{64,96},{96,128},{128,160},{160,192},{192,224},{224... | collective-permute-start | bytes 663560 | tf_op jit(solution)/shard_map/ppermute | solution.py:355
  67.1 4.4 %collective-permute-start.8 = (f32[8,1152]{1,0:T(8,128)S(1)}, f32[8,1152]{1,0:T(8,128)S(1)}, u32[]{:S(2)}, u32[]{:S(2)}) collective-permute-start(f32[8,1152]{1,0:T(8,128)S(1)} %get-tuple-element.23.a_ref.r_1_), channel_id=1, source_target_pairs={{0,16},{16,0},{1,17},{17,1},{2,18},{18,2},{3,19},{19,3},{4,20},{20... | collective-permute-start | bytes 110600 | tf_op jit(solution)/shard_map/ppermute | solution.py:359
  71.5 6.0 %collective-permute-start.9 = (f32[8,1152]{1,0:T(8,128)S(1)}, f32[8,1152]{1,0:T(8,128)S(1)}, u32[]{:S(2)}, u32[]{:S(2)}) collective-permute-start(f32[8,1152]{1,0:T(8,128)S(1)} %merge.1.r_2_), channel_id=1, source_target_pairs={{0,4},{4,0},{8,12},{12,8},{1,5},{5,1},{9,13},{13,9},{2,6},{6,2},{1... | collective-permute-start | bytes 110600 | tf_op jit(solution)/shard_map/ppermute | solution.py:359
  74.5 4.6 %collective-permute-start.10 = (f32[8,1152]{1,0:T(8,128)S(1)}, f32[8,1152]{1,0:T(8,128)S(1)}, u32[]{:S(2)}, u32[]{:S(2)}) collective-permute-start(f32[8,1152]{1,0:T(8,128)S(1)} %merge.1.r_2_), channel_id=1, source_target_pairs={{0,8},{4,12},{8,0},{12,4},{1,9},{5,13},{9,1},{13,5},{2,10},{6,14},... | collective-permute-start | bytes 110600 | tf_op jit(solution)/shard_map/ppermute | solution.py:359
  77.3 4.0 %collective-permute-start.11 = (f32[8,1152]{1,0:T(8,128)S(1)}, f32[8,1152]{1,0:T(8,128)S(1)}, u32[]{:S(2)}, u32[]{:S(2)}) collective-permute-start(f32[8,1152]{1,0:T(8,128)S(1)} %merge.1.r_2_), channel_id=1, source_target_pairs={{0,12},{4,8},{8,4},{12,0},{1,13},{5,9},{9,5},{13,1},{2,14},{6,10},... | collective-permute-start | bytes 110600 | tf_op jit(solution)/shard_map/ppermute | solution.py:359
  84.7 19.0 %all-to-all-start.1 = ((bf16[8,144,768]{2,1,0:T(8,128)(2,1)}), bf16[8,144,768]{2,1,0:T(8,128)(2,1)S(1)}, u32[]{:S(2)}, u32[]{:S(2)}) async-start(bf16[8,144,768]{2,1,0:T(8,128)(2,1)} %weigh.1), calls=%async_computation.1 | async-start | bytes 3538944 | tf_op jit(solution)/shard_map/all_to_all | solution.py:386
  106.0 10.9 %collective-permute-start.12 = (bf16[144,1280]{1,0:T(8,128)(2,1)S(1)}, bf16[144,1280]{1,0:T(8,128)(2,1)S(1)}, u32[]{:S(2)}, u32[]{:S(2)}) collective-permute-start(bf16[144,1280]{1,0:T(8,128)(2,1)S(1)} %get-tuple-element.26), channel_id=1, source_target_pairs={{0,1},{1,0},{2,3},{3,2},{4,5},{5,4},{6,7},{7,6},{8,9},{9,8},{10,11... | collective-permute-start | bytes 1105928 | tf_op jit(solution)/shard_map/ppermute | solution.py:359
  117.0 10.3 %copy-start.2 = (bf16[144,1280]{1,0:T(8,128)(2,1)S(1)}, bf16[144,1280]{1,0:T(8,128)(2,1)}, u32[]{:S(2)}) copy-start(bf16[144,1280]{1,0:T(8,128)(2,1)} %param.15) | copy-start | bytes 1105924
  117.0 10.3 %collective-permute-start.13 = (bf16[144,1280]{1,0:T(8,128)(2,1)S(1)}, bf16[144,1280]{1,0:T(8,128)(2,1)S(1)}, u32[]{:S(2)}, u32[]{:S(2)}) collective-permute-start(bf16[144,1280]{1,0:T(8,128)(2,1)S(1)} %add_convert_fusion.1), channel_id=1, source_target_pairs={{0,2},{2,0},{1,3},{3,1},{4,6},{6,4},{5,7},{7,5},{8,10},{10,8},{9,1... | collective-permute-start | bytes 1105928 | tf_op jit(solution)/shard_map/ppermute | solution.py:359
  121.5 5.9 %collective-permute-start.14 = (bf16[144,1280]{1,0:T(8,128)(2,1)S(1)}, bf16[144,1280]{1,0:T(8,128)(2,1)S(1)}, u32[]{:S(2)}, u32[]{:S(2)}) collective-permute-start(bf16[144,1280]{1,0:T(8,128)(2,1)S(1)} %get-tuple-element.30), channel_id=1, source_target_pairs={{0,1},{1,0},{2,3},{3,2},{4,5},{5,4},{6,7},{7,6},{8,9},{9,8},{10,11... | collective-permute-start | bytes 1105928 | tf_op jit(solution)/shard_map/ppermute | solution.py:359
  (4 other events, 14.4 us)

commit v11 on v10

--- a/solution.py
+++ b/solution.py
@@ -13,7 +13,7 @@
 
 HD = 128
 RUN = 72
-TILE = 8
+TILE = 4
 NEG = -1e30
 FLOOR = -1e29
 f32 = jnp.float32
@@ -376,7 +376,7 @@
         kv_parts += [up, down]
     kv_parts += [shift(up[:rows], "z", nz, 1), shift(down[rows:], "z", nz, -1)]
     spots = [(i, 0, i, rows) for i in range(nz - 1)] + [(nz - 1, 0, nz, 0)]
-    o, lse = attend(q_all, kv_parts, spots, (4, 8, 12, 16), rows, heads)
+    o, lse = attend(q_all, kv_parts, spots, (3, 6, 9, 12, 16), rows, heads)
 
     pair = merge(lse, swap(lse, "h", nh, 1))
     others = [swap(pair, "y", ny, d) for d in range(1, ny)]

time: 130 us -> 130 us (level); the launches traced: 128 us -> 130 us
  Pallas kernels: 30.3 us -> 33.3 us
  starting transfers between devices: 45.7 us -> 44.1 us
    pallas_call x1, Pallas kernels: 16.7 us -> 19.7 us  [attend(): pl.pallas_call(lambda *r: attend_kernel(rows, spans, slots, spots, *r), o...]
    ppermute x7, starting transfers between devices: 19.1 us -> 17.7 us  [swap(): return lax.ppermute(x, axis, [(i, i ^ mask) for i in range(size)])]
where the time goes in v11:
time: 130 us
  waiting for transfers between devices  48.2 us (37%)
  starting transfers between devices  44.1 us (34%)
  Pallas kernels  33.3 us (26%)
  other arithmetic  2.88 us (2%)
    ppermute x8, waiting for transfers between devices, shift(): return lax.ppermute(x, axis, [(i, (i + step) % size) for i in range(size)])  22 us
    pallas_call x1, Pallas kernels, attend(): pl.pallas_call(lambda *r: attend_kernel(rows, spans, slots, spots, *r), o...  19.7 us
    ppermute x7, starting transfers between devices, swap(): return lax.ppermute(x, axis, [(i, i ^ mask) for i in range(size)])  17.7 us
    ppermute x8, starting transfers between devices, shift(): return lax.ppermute(x, axis, [(i, (i + step) % size) for i in range(size)])  16.1 us
    all_to_all x1, waiting for transfers between devices, per_device(): got = lax.all_to_all(parts, ('h', 'y'), 0, 0, tiled=False)  15.2 us
    ppermute x7, waiting for transfers between devices, swap(): return lax.ppermute(x, axis, [(i, i ^ mask) for i in range(size)])  11 us
    pallas_call x3, Pallas kernels, project(): pl.pallas_call(lambda *r: project_kernel(heads, kinds, *r), out_shape=out...  7.49 us
    all_to_all x1, starting transfers between devices, per_device(): q_all = lax.all_to_all(repeat(queries, ids, nh * ny), ('h', 'y'), 0, 0)  6.66 us
  transfers between devices with their start and end apart: 17, of which 8 were waited for; matrix products, arithmetic and copies ran while one was open for 0% of the time, Pallas kernels for 6%

profile of v11, /device:TPU:1, one launch (start us, length us, event | category | flops | bytes accessed | tf_op | source)
XLA Modules:
  0.0 129.8 jit_solution(5907884328853292652)
XLA Ops:
  1.8 2.5 %collective-permute-start = (bf16[304,768]{1,0:T(8,128)(2,1)S(1)}, bf16[304,768]{1,0:T(8,128)(2,1)S(1)}, u32[]{:S(2)}, u32[]{:S(2)}) collective-permute-start(bf16[304,768]{1,0:T(8,128)(2,1)S(1)} %pad_maximum_fusion.r_1_), channel_id=1, source_target_pairs={{0,32},{32,64},{64,96},{96,128},{128,160},{160,192},{192,224},{224... | collective-permute-start | bytes 1400840 | tf_op jit(solution)/shard_map/ppermute | solution.py:355
  4.3 4.0 %collective-permute-start.1 = (bf16[304,768]{1,0:T(8,128)(2,1)S(1)}, bf16[304,768]{1,0:T(8,128)(2,1)S(1)}, u32[]{:S(2)}, u32[]{:S(2)}) collective-permute-start(bf16[304,768]{1,0:T(8,128)(2,1)S(1)} %pad_maximum_fusion.r_1_), channel_id=1, source_target_pairs={{0,224},{32,0},{64,32},{96,64},{128,96},{160,128},{192,160},{224,1... | collective-permute-start | bytes 1400840 | tf_op jit(solution)/shard_map/ppermute | solution.py:355
  10.7 6.7 %all-to-all-start = ((bf16[8,160,768]{2,1,0:T(8,128)(2,1)}), bf16[8,160,768]{2,1,0:T(8,128)(2,1)S(1)}, u32[]{:S(2)}, u32[]{:S(2)}) async-start(bf16[8,160,768]{2,1,0:T(8,128)(2,1)} %repeat.1), calls=%async_computation | async-start | bytes 3932160 | tf_op jit(solution)/shard_map/all_to_all | solution.py:370
  18.7 2.4 %collective-permute-start.3 = (bf16[304,768]{1,0:T(8,128)(2,1)S(1)}, bf16[304,768]{1,0:T(8,128)(2,1)S(1)}, u32[]{:S(2)}, u32[]{:S(2)}) collective-permute-start(bf16[304,768]{1,0:T(8,128)(2,1)S(1)} %collective-permute-done.1.r_3_), channel_id=1, source_target_pairs={{0,224},{32,0},{64,32},{96,64},{128,96},{160,128},{192,160},{224,1... | collective-permute-start | bytes 1400840 | tf_op jit(solution)/shard_map/ppermute | solution.py:355
  21.1 8.6 %collective-permute-done.3.r_5_ = bf16[304,768]{1,0:T(8,128)(2,1)S(1)} collective-permute-done((bf16[304,768]{1,0:T(8,128)(2,1)S(1)}, bf16[304,768]{1,0:T(8,128)(2,1)S(1)}, u32[]{:S(2)}, u32[]{:S(2)}) %collective-permute-start.3) | collective-permute-done | bytes 466976 | tf_op jit(solution)/shard_map/ppermute | solution.py:355
  29.8 3.2 %collective-permute-start.5 = (bf16[304,768]{1,0:T(8,128)(2,1)S(1)}, bf16[304,768]{1,0:T(8,128)(2,1)S(1)}, u32[]{:S(2)}, u32[]{:S(2)}) collective-permute-start(bf16[304,768]{1,0:T(8,128)(2,1)S(1)} %collective-permute-done.3.r_5_), channel_id=1, source_target_pairs={{0,224},{32,0},{64,32},{96,64},{128,96},{160,128},{192,160},{224,1... | collective-permute-start | bytes 1400840 | tf_op jit(solution)/shard_map/ppermute | solution.py:355
  33.1 7.4 %collective-permute-done.5.r_7_ = bf16[304,768]{1,0:T(8,128)(2,1)S(1)} collective-permute-done((bf16[304,768]{1,0:T(8,128)(2,1)S(1)}, bf16[304,768]{1,0:T(8,128)(2,1)S(1)}, u32[]{:S(2)}, u32[]{:S(2)}) %collective-permute-start.5) | collective-permute-done | bytes 466976 | tf_op jit(solution)/shard_map/ppermute | solution.py:355
  40.5 3.5 %collective-permute-start.7 = (bf16[160,768]{1,0:T(8,128)(2,1)S(1)}, bf16[160,768]{1,0:T(8,128)(2,1)S(1)}, u32[]{:S(2)}, u32[]{:S(2)}) collective-permute-start(bf16[160,768]{1,0:T(8,128)(2,1)S(1)} %slice.13), channel_id=1, source_target_pairs={{0,224},{32,0},{64,32},{96,64},{128,96},{160,128},{192,160},{224,1... | collective-permute-start | bytes 737288 | tf_op jit(solution)/shard_map/ppermute | solution.py:355
  44.3 6.0 %collective-permute-done.6.r_8_ = bf16[144,768]{1,0:T(8,128)(2,1)S(1)} collective-permute-done((bf16[144,768]{1,0:T(8,128)(2,1)S(1)}, bf16[144,768]{1,0:T(8,128)(2,1)S(1)}, u32[]{:S(2)}, u32[]{:S(2)}) %collective-permute-start.6) | collective-permute-done | bytes 221216 | tf_op jit(solution)/shard_map/ppermute | solution.py:355
  50.3 19.7 %attend.1 = (bf16[16,72,1536]{2,1,0:T(8,128)(2,1)S(1)}, f32[8,1152]{1,0:T(8,128)S(1)}) custom-call(bf16[8,160,768]{2,1,0:T(8,128)(2,1)S(1)} %all-to-all-done.r_0_, bf16[304,768]{1,0:T(8,128)(2,1)} %copy-done.1, bf16[304,768]{1,0:T(8,128)(2,1)} %copy-done.7, bf16[304,768]{1,0:T(8,128)(2,1)} %copy-done.8, bf16[304,768]{1,0:T(8,128)(2,1)} %copy-done.10, ...), custom_call_target="tpu_custom_call" | custom-call | flops 48922361856 | bytes 7077888 | tf_op jit(solution)/shard_map/attend/pallas_call | solution.py:154
  70.0 2.6 %collective-permute-start.8 = (f32[8,1152]{1,0:T(8,128)S(1)}, f32[8,1152]{1,0:T(8,128)S(1)}, u32[]{:S(2)}, u32[]{:S(2)}) collective-permute-start(f32[8,1152]{1,0:T(8,128)S(1)} %get-tuple-element.23.a_ref.r_1_), channel_id=1, source_target_pairs={{0,16},{16,0},{1,17},{17,1},{2,18},{18,2},{3,19},{19,3},{4,20},{20... | collective-permute-start | bytes 110600 | tf_op jit(solution)/shard_map/ppermute | solution.py:359
  72.6 1.8 %collective-permute-done.8.b_ref = f32[8,1152]{1,0:T(8,128)S(1)} collective-permute-done((f32[8,1152]{1,0:T(8,128)S(1)}, f32[8,1152]{1,0:T(8,128)S(1)}, u32[]{:S(2)}, u32[]{:S(2)}) %collective-permute-start.8) | collective-permute-done | bytes 36896 | tf_op jit(solution)/shard_map/ppermute | solution.py:359
  75.6 3.4 %collective-permute-start.10 = (f32[8,1152]{1,0:T(8,128)S(1)}, f32[8,1152]{1,0:T(8,128)S(1)}, u32[]{:S(2)}, u32[]{:S(2)}) collective-permute-start(f32[8,1152]{1,0:T(8,128)S(1)} %merge.1.r_2_), channel_id=1, source_target_pairs={{0,8},{4,12},{8,0},{12,4},{1,9},{5,13},{9,1},{13,5},{2,10},{6,14},... | collective-permute-start | bytes 110600 | tf_op jit(solution)/shard_map/ppermute | solution.py:359
  79.1 1.6 %collective-permute-done.10.r_4_ = f32[8,1152]{1,0:T(8,128)S(1)} collective-permute-done((f32[8,1152]{1,0:T(8,128)S(1)}, f32[8,1152]{1,0:T(8,128)S(1)}, u32[]{:S(2)}, u32[]{:S(2)}) %collective-permute-start.10) | collective-permute-done | bytes 36896 | tf_op jit(solution)/shard_map/ppermute | solution.py:359
  80.8 2.3 %collective-permute-done.11.r_5_ = f32[8,1152]{1,0:T(8,128)S(1)} collective-permute-done((f32[8,1152]{1,0:T(8,128)S(1)}, f32[8,1152]{1,0:T(8,128)S(1)}, u32[]{:S(2)}, u32[]{:S(2)}) %collective-permute-start.11) | collective-permute-done | bytes 36896 | tf_op jit(solution)/shard_map/ppermute | solution.py:359
  83.0 3.4 %weigh.1 = bf16[8,144,768]{2,1,0:T(8,128)(2,1)} custom-call(f32[3]{0:T(128)S(1)} %slice_reduce_fusion.r_0_, f32[8,1152]{1,0:T(8,128)S(1)} %get-tuple-element.23.a_ref.r_1_, f32[8,1152]{1,0:T(8,128)S(1)} %merge.1.r_2_, f32[8,1152]{1,0:T(8,128)S(1)} %collective-permute-done.9.r_3_, f32[8,1152]{1,0:T(8,128)S(1)} %collective-permute-done.10.r_4_, ...), custom_call_target="tpu_custom_call" | custom-call | tf_op jit(solution)/shard_map/weigh/pallas_call | solution.py:241
  86.4 3.7 %all-to-all-start.1 = ((bf16[8,144,768]{2,1,0:T(8,128)(2,1)}), bf16[8,144,768]{2,1,0:T(8,128)(2,1)S(1)}, u32[]{:S(2)}, u32[]{:S(2)}) async-start(bf16[8,144,768]{2,1,0:T(8,128)(2,1)} %weigh.1), calls=%async_computation.1 | async-start | bytes 3538944 | tf_op jit(solution)/shard_map/all_to_all | solution.py:386
  90.2 15.2 %all-to-all-done.1.r_1_ = bf16[8,144,768]{2,1,0:T(8,128)(2,1)S(1)} async-done(((bf16[8,144,768]{2,1,0:T(8,128)(2,1)}), bf16[8,144,768]{2,1,0:T(8,128)(2,1)S(1)}, u32[]{:S(2)}, u32[]{:S(2)}) %all-to-all-start.1) | async-done | bytes 1769504 | tf_op jit(solution)/shard_map/all_to_all | solution.py:386
  105.3 2.3 %project.3 = (bf16[144,1280]{1,0:T(8,128)(2,1)S(1)}, bf16[144,768]{1,0:T(8,128)(2,1)S(1)}) custom-call(s32[1]{0:T(128)} %bitcast.1.r_0_, bf16[8,144,768]{2,1,0:T(8,128)(2,1)S(1)} %all-to-all-done.1.r_1_, f32[1,768]{1,0:T(1,128)S(1)} %reshape.18.r_2_, bf16[768,5120]{1,0:T(8,128)(2,1)} %r_2_.3), custom_call_target="tpu_custom_call" | custom-call | flops 2264924160 | bytes 1966080 | tf_op jit(solution)/shard_map/project/pallas_call | solution.py:293
  107.6 8.8 %collective-permute-start.12 = (bf16[144,1280]{1,0:T(8,128)(2,1)S(1)}, bf16[144,1280]{1,0:T(8,128)(2,1)S(1)}, u32[]{:S(2)}, u32[]{:S(2)}) collective-permute-start(bf16[144,1280]{1,0:T(8,128)(2,1)S(1)} %get-tuple-element.26), channel_id=1, source_target_pairs={{0,1},{1,0},{2,3},{3,2},{4,5},{5,4},{6,7},{7,6},{8,9},{9,8},{10,11... | collective-permute-start | bytes 1105928 | tf_op jit(solution)/shard_map/ppermute | solution.py:359
  116.4 2.0 %project.4 = f32[144,1280]{1,0:T(8,128)S(1)} custom-call(s32[1]{0:T(128)} %bitcast.r_0_, bf16[144,768]{1,0:T(8,128)(2,1)S(1)} %get-tuple-element.28.r_1_, bf16[768,5120]{1,0:T(8,128)(2,1)} %r_2_.3), custom_call_target="tpu_custom_call" | custom-call | flops 2264924160 | bytes 1966080 | tf_op jit(solution)/shard_map/project/pallas_call | solution.py:293
  118.5 1.4 %collective-permute-start.13 = (bf16[144,1280]{1,0:T(8,128)(2,1)S(1)}, bf16[144,1280]{1,0:T(8,128)(2,1)S(1)}, u32[]{:S(2)}, u32[]{:S(2)}) collective-permute-start(bf16[144,1280]{1,0:T(8,128)(2,1)S(1)} %add_convert_fusion.1), channel_id=1, source_target_pairs={{0,2},{2,0},{1,3},{3,1},{4,6},{6,4},{5,7},{7,5},{8,10},{10,8},{9,1... | collective-permute-start | bytes 1105928 | tf_op jit(solution)/shard_map/ppermute | solution.py:359
  119.9 3.2 %project.5 = (bf16[144,1280]{1,0:T(8,128)(2,1)S(1)}, f32[144,1280]{1,0:T(8,128)S(1)}) custom-call(s32[2]{0:T(128)S(1)} %pad_add_fusion.r_0_, bf16[144,768]{1,0:T(8,128)(2,1)S(1)} %get-tuple-element.28.r_1_, bf16[768,5120]{1,0:T(8,128)(2,1)} %r_2_.3), custom_call_target="tpu_custom_call" | custom-call | flops 4529848320 | bytes 3932160 | tf_op jit(solution)/shard_map/project/pallas_call | solution.py:293
  123.6 5.2 %collective-permute-done.13 = bf16[144,1280]{1,0:T(8,128)(2,1)S(1)} collective-permute-done((bf16[144,1280]{1,0:T(8,128)(2,1)S(1)}, bf16[144,1280]{1,0:T(8,128)(2,1)S(1)}, u32[]{:S(2)}, u32[]{:S(2)}) %collective-permute-start.13) | collective-permute-done | bytes 368672 | tf_op jit(solution)/shard_map/ppermute | solution.py:359
  (52 shorter events, 8.7 us)
Async XLA Ops:
  1.8 8.9 %copy-start.1 = (bf16[304,768]{1,0:T(8,128)(2,1)}, bf16[304,768]{1,0:T(8,128)(2,1)S(1)}, u32[]{:S(2)}) copy-start(bf16[304,768]{1,0:T(8,128)(2,1)S(1)} %pad_maximum_fusion.r_1_) | copy-start | bytes 1400836
  1.8 16.9 %collective-permute-start = (bf16[304,768]{1,0:T(8,128)(2,1)S(1)}, bf16[304,768]{1,0:T(8,128)(2,1)S(1)}, u32[]{:S(2)}, u32[]{:S(2)}) collective-permute-start(bf16[304,768]{1,0:T(8,128)(2,1)S(1)} %pad_maximum_fusion.r_1_), channel_id=1, source_target_pairs={{0,32},{32,64},{64,96},{96,128},{128,160},{160,192},{192,224},{224... | collective-permute-start | bytes 1400840 | tf_op jit(solution)/shard_map/ppermute | solution.py:355
  4.3 14.4 %collective-permute-start.1 = (bf16[304,768]{1,0:T(8,128)(2,1)S(1)}, bf16[304,768]{1,0:T(8,128)(2,1)S(1)}, u32[]{:S(2)}, u32[]{:S(2)}) collective-permute-start(bf16[304,768]{1,0:T(8,128)(2,1)S(1)} %pad_maximum_fusion.r_1_), channel_id=1, source_target_pairs={{0,224},{32,0},{64,32},{96,64},{128,96},{160,128},{192,160},{224,1... | collective-permute-start | bytes 1400840 | tf_op jit(solution)/shard_map/ppermute | solution.py:355
  10.7 39.6 %all-to-all-start = ((bf16[8,160,768]{2,1,0:T(8,128)(2,1)}), bf16[8,160,768]{2,1,0:T(8,128)(2,1)S(1)}, u32[]{:S(2)}, u32[]{:S(2)}) async-start(bf16[8,160,768]{2,1,0:T(8,128)(2,1)} %repeat.1), calls=%async_computation | async-start | bytes 3932160 | tf_op jit(solution)/shard_map/all_to_all | solution.py:370
  18.7 21.8 %copy-start.7 = (bf16[304,768]{1,0:T(8,128)(2,1)}, bf16[304,768]{1,0:T(8,128)(2,1)S(1)}, u32[]{:S(2)}) copy-start(bf16[304,768]{1,0:T(8,128)(2,1)S(1)} %collective-permute-done.r_2_) | copy-start | bytes 1400836
  18.7 14.3 %copy-start.8 = (bf16[304,768]{1,0:T(8,128)(2,1)}, bf16[304,768]{1,0:T(8,128)(2,1)S(1)}, u32[]{:S(2)}) copy-start(bf16[304,768]{1,0:T(8,128)(2,1)S(1)} %collective-permute-done.1.r_3_) | copy-start | bytes 1400836
  18.7 11.0 %collective-permute-start.3 = (bf16[304,768]{1,0:T(8,128)(2,1)S(1)}, bf16[304,768]{1,0:T(8,128)(2,1)S(1)}, u32[]{:S(2)}, u32[]{:S(2)}) collective-permute-start(bf16[304,768]{1,0:T(8,128)(2,1)S(1)} %collective-permute-done.1.r_3_), channel_id=1, source_target_pairs={{0,224},{32,0},{64,32},{96,64},{128,96},{160,128},{192,160},{224,1... | collective-permute-start | bytes 1400840 | tf_op jit(solution)/shard_map/ppermute | solution.py:355
  21.1 11.9 %collective-permute-start.2 = (bf16[304,768]{1,0:T(8,128)(2,1)S(1)}, bf16[304,768]{1,0:T(8,128)(2,1)S(1)}, u32[]{:S(2)}, u32[]{:S(2)}) collective-permute-start(bf16[304,768]{1,0:T(8,128)(2,1)S(1)} %collective-permute-done.r_2_), channel_id=1, source_target_pairs={{0,32},{32,64},{64,96},{96,128},{128,160},{160,192},{192,224},{224... | collective-permute-start | bytes 1400840 | tf_op jit(solution)/shard_map/ppermute | solution.py:355
  29.8 10.8 %collective-permute-start.5 = (bf16[304,768]{1,0:T(8,128)(2,1)S(1)}, bf16[304,768]{1,0:T(8,128)(2,1)S(1)}, u32[]{:S(2)}, u32[]{:S(2)}) collective-permute-start(bf16[304,768]{1,0:T(8,128)(2,1)S(1)} %collective-permute-done.3.r_5_), channel_id=1, source_target_pairs={{0,224},{32,0},{64,32},{96,64},{128,96},{160,128},{192,160},{224,1... | collective-permute-start | bytes 1400840 | tf_op jit(solution)/shard_map/ppermute | solution.py:355
  33.0 11.0 %copy-start.10 = (bf16[304,768]{1,0:T(8,128)(2,1)}, bf16[304,768]{1,0:T(8,128)(2,1)S(1)}, u32[]{:S(2)}) copy-start(bf16[304,768]{1,0:T(8,128)(2,1)S(1)} %collective-permute-done.2.r_4_) | copy-start | bytes 1400836
  33.0 11.0 %collective-permute-start.4 = (bf16[304,768]{1,0:T(8,128)(2,1)S(1)}, bf16[304,768]{1,0:T(8,128)(2,1)S(1)}, u32[]{:S(2)}, u32[]{:S(2)}) collective-permute-start(bf16[304,768]{1,0:T(8,128)(2,1)S(1)} %collective-permute-done.2.r_4_), channel_id=1, source_target_pairs={{0,32},{32,64},{64,96},{96,128},{128,160},{160,192},{192,224},{224... | collective-permute-start | bytes 1400840 | tf_op jit(solution)/shard_map/ppermute | solution.py:355
  40.5 9.8 %copy-start.3 = (bf16[304,768]{1,0:T(8,128)(2,1)}, bf16[304,768]{1,0:T(8,128)(2,1)S(1)}, u32[]{:S(2)}) copy-start(bf16[304,768]{1,0:T(8,128)(2,1)S(1)} %collective-permute-done.5.r_7_) | copy-start | bytes 1400836
  40.5 9.8 %collective-permute-start.7 = (bf16[160,768]{1,0:T(8,128)(2,1)S(1)}, bf16[160,768]{1,0:T(8,128)(2,1)S(1)}, u32[]{:S(2)}, u32[]{:S(2)}) collective-permute-start(bf16[160,768]{1,0:T(8,128)(2,1)S(1)} %slice.13), channel_id=1, source_target_pairs={{0,224},{32,0},{64,32},{96,64},{128,96},{160,128},{192,160},{224,1... | collective-permute-start | bytes 737288 | tf_op jit(solution)/shard_map/ppermute | solution.py:355
  44.1 35.0 %copy-start.6 = (f32[3,128]{1,0:T(4,128)S(1)}, f32[3,128]{1,0:T(4,128)}, u32[]{:S(2)}) copy-start(f32[3,128]{1,0:T(4,128)} %lambdas.1) | copy-start | bytes 4612
  44.1 6.3 %collective-permute-start.6 = (bf16[144,768]{1,0:T(8,128)(2,1)S(1)}, bf16[144,768]{1,0:T(8,128)(2,1)S(1)}, u32[]{:S(2)}, u32[]{:S(2)}) collective-permute-start(bf16[144,768]{1,0:T(8,128)(2,1)S(1)} %slice.12), channel_id=1, source_target_pairs={{0,32},{32,64},{64,96},{96,128},{128,160},{160,192},{192,224},{224... | collective-permute-start | bytes 663560 | tf_op jit(solution)/shard_map/ppermute | solution.py:355
  70.0 4.4 %collective-permute-start.8 = (f32[8,1152]{1,0:T(8,128)S(1)}, f32[8,1152]{1,0:T(8,128)S(1)}, u32[]{:S(2)}, u32[]{:S(2)}) collective-permute-start(f32[8,1152]{1,0:T(8,128)S(1)} %get-tuple-element.23.a_ref.r_1_), channel_id=1, source_target_pairs={{0,16},{16,0},{1,17},{17,1},{2,18},{18,2},{3,19},{19,3},{4,20},{20... | collective-permute-start | bytes 110600 | tf_op jit(solution)/shard_map/ppermute | solution.py:359
  74.5 4.7 %collective-permute-start.9 = (f32[8,1152]{1,0:T(8,128)S(1)}, f32[8,1152]{1,0:T(8,128)S(1)}, u32[]{:S(2)}, u32[]{:S(2)}) collective-permute-start(f32[8,1152]{1,0:T(8,128)S(1)} %merge.1.r_2_), channel_id=1, source_target_pairs={{0,4},{4,0},{8,12},{12,8},{1,5},{5,1},{9,13},{13,9},{2,6},{6,2},{1... | collective-permute-start | bytes 110600 | tf_op jit(solution)/shard_map/ppermute | solution.py:359
  75.6 5.1 %collective-permute-start.10 = (f32[8,1152]{1,0:T(8,128)S(1)}, f32[8,1152]{1,0:T(8,128)S(1)}, u32[]{:S(2)}, u32[]{:S(2)}) collective-permute-start(f32[8,1152]{1,0:T(8,128)S(1)} %merge.1.r_2_), channel_id=1, source_target_pairs={{0,8},{4,12},{8,0},{12,4},{1,9},{5,13},{9,1},{13,5},{2,10},{6,14},... | collective-permute-start | bytes 110600 | tf_op jit(solution)/shard_map/ppermute | solution.py:359
  79.0 4.0 %collective-permute-start.11 = (f32[8,1152]{1,0:T(8,128)S(1)}, f32[8,1152]{1,0:T(8,128)S(1)}, u32[]{:S(2)}, u32[]{:S(2)}) collective-permute-start(f32[8,1152]{1,0:T(8,128)S(1)} %merge.1.r_2_), channel_id=1, source_target_pairs={{0,12},{4,8},{8,4},{12,0},{1,13},{5,9},{9,5},{13,1},{2,14},{6,10},... | collective-permute-start | bytes 110600 | tf_op jit(solution)/shard_map/ppermute | solution.py:359
  86.4 18.9 %all-to-all-start.1 = ((bf16[8,144,768]{2,1,0:T(8,128)(2,1)}), bf16[8,144,768]{2,1,0:T(8,128)(2,1)S(1)}, u32[]{:S(2)}, u32[]{:S(2)}) async-start(bf16[8,144,768]{2,1,0:T(8,128)(2,1)} %weigh.1), calls=%async_computation.1 | async-start | bytes 3538944 | tf_op jit(solution)/shard_map/all_to_all | solution.py:386
  107.6 10.8 %collective-permute-start.12 = (bf16[144,1280]{1,0:T(8,128)(2,1)S(1)}, bf16[144,1280]{1,0:T(8,128)(2,1)S(1)}, u32[]{:S(2)}, u32[]{:S(2)}) collective-permute-start(bf16[144,1280]{1,0:T(8,128)(2,1)S(1)} %get-tuple-element.26), channel_id=1, source_target_pairs={{0,1},{1,0},{2,3},{3,2},{4,5},{5,4},{6,7},{7,6},{8,9},{9,8},{10,11... | collective-permute-start | bytes 1105928 | tf_op jit(solution)/shard_map/ppermute | solution.py:359
  118.5 10.3 %copy-start.2 = (bf16[144,1280]{1,0:T(8,128)(2,1)S(1)}, bf16[144,1280]{1,0:T(8,128)(2,1)}, u32[]{:S(2)}) copy-start(bf16[144,1280]{1,0:T(8,128)(2,1)} %param.15) | copy-start | bytes 1105924
  118.5 10.3 %collective-permute-start.13 = (bf16[144,1280]{1,0:T(8,128)(2,1)S(1)}, bf16[144,1280]{1,0:T(8,128)(2,1)S(1)}, u32[]{:S(2)}, u32[]{:S(2)}) collective-permute-start(bf16[144,1280]{1,0:T(8,128)(2,1)S(1)} %add_convert_fusion.1), channel_id=1, source_target_pairs={{0,2},{2,0},{1,3},{3,1},{4,6},{6,4},{5,7},{7,5},{8,10},{10,8},{9,1... | collective-permute-start | bytes 1105928 | tf_op jit(solution)/shard_map/ppermute | solution.py:359
  123.2 5.8 %collective-permute-start.14 = (bf16[144,1280]{1,0:T(8,128)(2,1)S(1)}, bf16[144,1280]{1,0:T(8,128)(2,1)S(1)}, u32[]{:S(2)}, u32[]{:S(2)}) collective-permute-start(bf16[144,1280]{1,0:T(8,128)(2,1)S(1)} %get-tuple-element.30), channel_id=1, source_target_pairs={{0,1},{1,0},{2,3},{3,2},{4,5},{5,4},{6,7},{7,6},{8,9},{9,8},{10,11... | collective-permute-start | bytes 1105928 | tf_op jit(solution)/shard_map/ppermute | solution.py:359
  (4 other events, 14.3 us)

commit v12 on v11

--- a/solution.py
+++ b/solution.py
@@ -243,10 +243,10 @@
         out_shape=jax.ShapeDtypeStruct((slots, rows, heads * 2 * HD), bf16),
         grid_spec=pltpu.PrefetchScalarGridSpec(
             num_scalar_prefetch=1,
-            grid=(slots // 2,),
+            grid=(slots // 4,),
             in_specs=[pl.BlockSpec(lse.shape, lambda j, lam: (0, 0))] * (1 + len(lses))
-            + [pl.BlockSpec((2 * rows // RUN, RUN, heads * 4 * HD), lambda j, lam: (j, 0, 0))],
-            out_specs=pl.BlockSpec((2, rows, heads * 2 * HD), lambda j, lam: (j, 0, 0)),
+            + [pl.BlockSpec((4 * rows // RUN, RUN, heads * 4 * HD), lambda j, lam: (j, 0, 0))],
+            out_specs=pl.BlockSpec((4, rows, heads * 2 * HD), lambda j, lam: (j, 0, 0)),
             scratch_shapes=[pltpu.VMEM((slots * rows, HD), f32)],
         ),
         compiler_params=pltpu.CompilerParams(vmem_limit_bytes=20 << 20),

time: 130 us -> 129 us (level)
  Pallas kernels: 33.3 us -> 29.5 us
  starting transfers between devices: 44.1 us -> 47.2 us
    pallas_call x1, Pallas kernels: 19.7 us -> 16.3 us  [attend(): pl.pallas_call(lambda *r: attend_kernel(rows, spans, slots, spots, *r), o...]
    ppermute x7, starting transfers between devices: 17.7 us -> 20.1 us  [swap(): return lax.ppermute(x, axis, [(i, i ^ mask) for i in range(size)])]
where the time goes in v12:
time: 129 us
  waiting for transfers between devices  48.3 us (37%)
  starting transfers between devices  47.2 us (37%)
  Pallas kernels  29.5 us (23%)
  other arithmetic  2.88 us (2%)
    ppermute x8, waiting for transfers between devices, shift(): return lax.ppermute(x, axis, [(i, (i + step) % size) for i in range(size)])  22 us
    ppermute x7, starting transfers between devices, swap(): return lax.ppermute(x, axis, [(i, i ^ mask) for i in range(size)])  20.1 us
    pallas_call x1, Pallas kernels, attend(): pl.pallas_call(lambda *r: attend_kernel(rows, spans, slots, spots, *r), o...  16.3 us
    ppermute x8, starting transfers between devices, shift(): return lax.ppermute(x, axis, [(i, (i + step) % size) for i in range(size)])  16.1 us
    all_to_all x1, waiting for transfers between devices, per_device(): got = lax.all_to_all(parts, ('h', 'y'), 0, 0, tiled=False)  14.9 us
    ppermute x7, waiting for transfers between devices, swap(): return lax.ppermute(x, axis, [(i, i ^ mask) for i in range(size)])  11.4 us
    pallas_call x3, Pallas kernels, project(): pl.pallas_call(lambda *r: project_kernel(heads, kinds, *r), out_shape=out...  7.49 us
    all_to_all x1, starting transfers between devices, per_device(): q_all = lax.all_to_all(repeat(queries, ids, nh * ny), ('h', 'y'), 0, 0)  6.66 us
  transfers between devices with their start and end apart: 17, of which 8 were waited for; matrix products, arithmetic and copies ran while one was open for 0% of the time, Pallas kernels for 6%

profile of v12, /device:TPU:1, one launch (start us, length us, event | category | flops | bytes accessed | tf_op | source)
XLA Modules:
  0.0 129.3 jit_solution(1707028006174991504)
XLA Ops:
  1.8 2.5 %collective-permute-start = (bf16[304,768]{1,0:T(8,128)(2,1)S(1)}, bf16[304,768]{1,0:T(8,128)(2,1)S(1)}, u32[]{:S(2)}, u32[]{:S(2)}) collective-permute-start(bf16[304,768]{1,0:T(8,128)(2,1)S(1)} %pad_maximum_fusion.r_1_), channel_id=1, source_target_pairs={{0,32},{32,64},{64,96},{96,128},{128,160},{160,192},{192,224},{224... | collective-permute-start | bytes 1400840 | tf_op jit(solution)/shard_map/ppermute | solution.py:355
  4.3 4.0 %collective-permute-start.1 = (bf16[304,768]{1,0:T(8,128)(2,1)S(1)}, bf16[304,768]{1,0:T(8,128)(2,1)S(1)}, u32[]{:S(2)}, u32[]{:S(2)}) collective-permute-start(bf16[304,768]{1,0:T(8,128)(2,1)S(1)} %pad_maximum_fusion.r_1_), channel_id=1, source_target_pairs={{0,224},{32,0},{64,32},{96,64},{128,96},{160,128},{192,160},{224,1... | collective-permute-start | bytes 1400840 | tf_op jit(solution)/shard_map/ppermute | solution.py:355
  9.3 1.4 %repeat.1 = bf16[8,160,768]{2,1,0:T(8,128)(2,1)} custom-call(bf16[144,768]{1,0:T(8,128)(2,1)S(1)} %copy-done, bf16[16,768]{1,0:T(8,128)(2,1)S(1)} %broadcast_in_dim.2.ids_ref), custom_call_target="tpu_custom_call" | custom-call | tf_op jit(solution)/shard_map/repeat/pallas_call | solution.py:325
  10.7 6.7 %all-to-all-start = ((bf16[8,160,768]{2,1,0:T(8,128)(2,1)}), bf16[8,160,768]{2,1,0:T(8,128)(2,1)S(1)}, u32[]{:S(2)}, u32[]{:S(2)}) async-start(bf16[8,160,768]{2,1,0:T(8,128)(2,1)} %repeat.1), calls=%async_computation | async-start | bytes 3932160 | tf_op jit(solution)/shard_map/all_to_all | solution.py:370
  18.7 2.4 %collective-permute-start.3 = (bf16[304,768]{1,0:T(8,128)(2,1)S(1)}, bf16[304,768]{1,0:T(8,128)(2,1)S(1)}, u32[]{:S(2)}, u32[]{:S(2)}) collective-permute-start(bf16[304,768]{1,0:T(8,128)(2,1)S(1)} %collective-permute-done.1.r_3_), channel_id=1, source_target_pairs={{0,224},{32,0},{64,32},{96,64},{128,96},{160,128},{192,160},{224,1... | collective-permute-start | bytes 1400840 | tf_op jit(solution)/shard_map/ppermute | solution.py:355
  21.1 8.6 %collective-permute-done.3.r_5_ = bf16[304,768]{1,0:T(8,128)(2,1)S(1)} collective-permute-done((bf16[304,768]{1,0:T(8,128)(2,1)S(1)}, bf16[304,768]{1,0:T(8,128)(2,1)S(1)}, u32[]{:S(2)}, u32[]{:S(2)}) %collective-permute-start.3) | collective-permute-done | bytes 466976 | tf_op jit(solution)/shard_map/ppermute | solution.py:355
  29.8 3.2 %collective-permute-start.5 = (bf16[304,768]{1,0:T(8,128)(2,1)S(1)}, bf16[304,768]{1,0:T(8,128)(2,1)S(1)}, u32[]{:S(2)}, u32[]{:S(2)}) collective-permute-start(bf16[304,768]{1,0:T(8,128)(2,1)S(1)} %collective-permute-done.3.r_5_), channel_id=1, source_target_pairs={{0,224},{32,0},{64,32},{96,64},{128,96},{160,128},{192,160},{224,1... | collective-permute-start | bytes 1400840 | tf_op jit(solution)/shard_map/ppermute | solution.py:355
  33.1 7.4 %collective-permute-done.5.r_7_ = bf16[304,768]{1,0:T(8,128)(2,1)S(1)} collective-permute-done((bf16[304,768]{1,0:T(8,128)(2,1)S(1)}, bf16[304,768]{1,0:T(8,128)(2,1)S(1)}, u32[]{:S(2)}, u32[]{:S(2)}) %collective-permute-start.5) | collective-permute-done | bytes 466976 | tf_op jit(solution)/shard_map/ppermute | solution.py:355
  40.5 3.5 %collective-permute-start.7 = (bf16[160,768]{1,0:T(8,128)(2,1)S(1)}, bf16[160,768]{1,0:T(8,128)(2,1)S(1)}, u32[]{:S(2)}, u32[]{:S(2)}) collective-permute-start(bf16[160,768]{1,0:T(8,128)(2,1)S(1)} %slice.13), channel_id=1, source_target_pairs={{0,224},{32,0},{64,32},{96,64},{128,96},{160,128},{192,160},{224,1... | collective-permute-start | bytes 737288 | tf_op jit(solution)/shard_map/ppermute | solution.py:355
  44.3 6.0 %collective-permute-done.6.r_8_ = bf16[144,768]{1,0:T(8,128)(2,1)S(1)} collective-permute-done((bf16[144,768]{1,0:T(8,128)(2,1)S(1)}, bf16[144,768]{1,0:T(8,128)(2,1)S(1)}, u32[]{:S(2)}, u32[]{:S(2)}) %collective-permute-start.6) | collective-permute-done | bytes 221216 | tf_op jit(solution)/shard_map/ppermute | solution.py:355
  50.3 16.3 %attend.1 = (bf16[16,72,1536]{2,1,0:T(8,128)(2,1)S(1)}, f32[8,1152]{1,0:T(8,128)S(1)}) custom-call(bf16[8,160,768]{2,1,0:T(8,128)(2,1)S(1)} %all-to-all-done.r_0_, bf16[304,768]{1,0:T(8,128)(2,1)} %copy-done.1, bf16[304,768]{1,0:T(8,128)(2,1)} %copy-done.7, bf16[304,768]{1,0:T(8,128)(2,1)} %copy-done.8, bf16[304,768]{1,0:T(8,128)(2,1)} %copy-done.10, ...), custom_call_target="tpu_custom_call" | custom-call | flops 48922361856 | bytes 7077888 | tf_op jit(solution)/shard_map/attend/pallas_call | solution.py:154
  66.6 3.6 %collective-permute-start.8 = (f32[8,1152]{1,0:T(8,128)S(1)}, f32[8,1152]{1,0:T(8,128)S(1)}, u32[]{:S(2)}, u32[]{:S(2)}) collective-permute-start(f32[8,1152]{1,0:T(8,128)S(1)} %get-tuple-element.23.a_ref.r_1_), channel_id=1, source_target_pairs={{0,16},{16,0},{1,17},{17,1},{2,18},{18,2},{3,19},{19,3},{4,20},{20... | collective-permute-start | bytes 110600 | tf_op jit(solution)/shard_map/ppermute | solution.py:359
  71.6 2.6 %collective-permute-start.9 = (f32[8,1152]{1,0:T(8,128)S(1)}, f32[8,1152]{1,0:T(8,128)S(1)}, u32[]{:S(2)}, u32[]{:S(2)}) collective-permute-start(f32[8,1152]{1,0:T(8,128)S(1)} %merge.1.r_2_), channel_id=1, source_target_pairs={{0,4},{4,0},{8,12},{12,8},{1,5},{5,1},{9,13},{13,9},{2,6},{6,2},{1... | collective-permute-start | bytes 110600 | tf_op jit(solution)/shard_map/ppermute | solution.py:359
  74.2 4.0 %collective-permute-start.10 = (f32[8,1152]{1,0:T(8,128)S(1)}, f32[8,1152]{1,0:T(8,128)S(1)}, u32[]{:S(2)}, u32[]{:S(2)}) collective-permute-start(f32[8,1152]{1,0:T(8,128)S(1)} %merge.1.r_2_), channel_id=1, source_target_pairs={{0,8},{4,12},{8,0},{12,4},{1,9},{5,13},{9,1},{13,5},{2,10},{6,14},... | collective-permute-start | bytes 110600 | tf_op jit(solution)/shard_map/ppermute | solution.py:359
  78.3 1.6 %collective-permute-done.10.r_4_ = f32[8,1152]{1,0:T(8,128)S(1)} collective-permute-done((f32[8,1152]{1,0:T(8,128)S(1)}, f32[8,1152]{1,0:T(8,128)S(1)}, u32[]{:S(2)}, u32[]{:S(2)}) %collective-permute-start.10) | collective-permute-done | bytes 36896 | tf_op jit(solution)/shard_map/ppermute | solution.py:359
  79.9 2.3 %collective-permute-done.11.r_5_ = f32[8,1152]{1,0:T(8,128)S(1)} collective-permute-done((f32[8,1152]{1,0:T(8,128)S(1)}, f32[8,1152]{1,0:T(8,128)S(1)}, u32[]{:S(2)}, u32[]{:S(2)}) %collective-permute-start.11) | collective-permute-done | bytes 36896 | tf_op jit(solution)/shard_map/ppermute | solution.py:359
  82.2 3.0 %weigh.1 = bf16[8,144,768]{2,1,0:T(8,128)(2,1)} custom-call(f32[3]{0:T(128)S(1)} %slice_reduce_fusion.r_0_, f32[8,1152]{1,0:T(8,128)S(1)} %get-tuple-element.23.a_ref.r_1_, f32[8,1152]{1,0:T(8,128)S(1)} %merge.1.r_2_, f32[8,1152]{1,0:T(8,128)S(1)} %collective-permute-done.9.r_3_, f32[8,1152]{1,0:T(8,128)S(1)} %collective-permute-done.10.r_4_, ...), custom_call_target="tpu_custom_call" | custom-call | tf_op jit(solution)/shard_map/weigh/pallas_call | solution.py:241
  85.2 4.4 %all-to-all-start.1 = ((bf16[8,144,768]{2,1,0:T(8,128)(2,1)}), bf16[8,144,768]{2,1,0:T(8,128)(2,1)S(1)}, u32[]{:S(2)}, u32[]{:S(2)}) async-start(bf16[8,144,768]{2,1,0:T(8,128)(2,1)} %weigh.1), calls=%async_computation.1 | async-start | bytes 3538944 | tf_op jit(solution)/shard_map/all_to_all | solution.py:386
  89.6 14.9 %all-to-all-done.1.r_1_ = bf16[8,144,768]{2,1,0:T(8,128)(2,1)S(1)} async-done(((bf16[8,144,768]{2,1,0:T(8,128)(2,1)}), bf16[8,144,768]{2,1,0:T(8,128)(2,1)S(1)}, u32[]{:S(2)}, u32[]{:S(2)}) %all-to-all-start.1) | async-done | bytes 1769504 | tf_op jit(solution)/shard_map/all_to_all | solution.py:386
  104.5 2.3 %project.3 = (bf16[144,1280]{1,0:T(8,128)(2,1)S(1)}, bf16[144,768]{1,0:T(8,128)(2,1)S(1)}) custom-call(s32[1]{0:T(128)} %bitcast.1.r_0_, bf16[8,144,768]{2,1,0:T(8,128)(2,1)S(1)} %all-to-all-done.1.r_1_, f32[1,768]{1,0:T(1,128)S(1)} %reshape.18.r_2_, bf16[768,5120]{1,0:T(8,128)(2,1)} %r_2_.3), custom_call_target="tpu_custom_call" | custom-call | flops 2264924160 | bytes 1966080 | tf_op jit(solution)/shard_map/project/pallas_call | solution.py:293
  106.8 9.1 %collective-permute-start.12 = (bf16[144,1280]{1,0:T(8,128)(2,1)S(1)}, bf16[144,1280]{1,0:T(8,128)(2,1)S(1)}, u32[]{:S(2)}, u32[]{:S(2)}) collective-permute-start(bf16[144,1280]{1,0:T(8,128)(2,1)S(1)} %get-tuple-element.26), channel_id=1, source_target_pairs={{0,1},{1,0},{2,3},{3,2},{4,5},{5,4},{6,7},{7,6},{8,9},{9,8},{10,11... | collective-permute-start | bytes 1105928 | tf_op jit(solution)/shard_map/ppermute | solution.py:359
  115.9 2.0 %project.4 = f32[144,1280]{1,0:T(8,128)S(1)} custom-call(s32[1]{0:T(128)} %bitcast.r_0_, bf16[144,768]{1,0:T(8,128)(2,1)S(1)} %get-tuple-element.28.r_1_, bf16[768,5120]{1,0:T(8,128)(2,1)} %r_2_.3), custom_call_target="tpu_custom_call" | custom-call | flops 2264924160 | bytes 1966080 | tf_op jit(solution)/shard_map/project/pallas_call | solution.py:293
  118.5 3.2 %project.5 = (bf16[144,1280]{1,0:T(8,128)(2,1)S(1)}, f32[144,1280]{1,0:T(8,128)S(1)}) custom-call(s32[2]{0:T(128)S(1)} %pad_add_fusion.r_0_, bf16[144,768]{1,0:T(8,128)(2,1)S(1)} %get-tuple-element.28.r_1_, bf16[768,5120]{1,0:T(8,128)(2,1)} %r_2_.3), custom_call_target="tpu_custom_call" | custom-call | flops 4529848320 | bytes 3932160 | tf_op jit(solution)/shard_map/project/pallas_call | solution.py:293
  122.1 6.2 %collective-permute-done.13 = bf16[144,1280]{1,0:T(8,128)(2,1)S(1)} collective-permute-done((bf16[144,1280]{1,0:T(8,128)(2,1)S(1)}, bf16[144,1280]{1,0:T(8,128)(2,1)S(1)}, u32[]{:S(2)}, u32[]{:S(2)}) %collective-permute-start.13) | collective-permute-done | bytes 368672 | tf_op jit(solution)/shard_map/ppermute | solution.py:359
  (52 shorter events, 8.0 us)
Async XLA Ops:
  1.8 8.9 %copy-start.1 = (bf16[304,768]{1,0:T(8,128)(2,1)}, bf16[304,768]{1,0:T(8,128)(2,1)S(1)}, u32[]{:S(2)}) copy-start(bf16[304,768]{1,0:T(8,128)(2,1)S(1)} %pad_maximum_fusion.r_1_) | copy-start | bytes 1400836
  1.8 16.9 %collective-permute-start = (bf16[304,768]{1,0:T(8,128)(2,1)S(1)}, bf16[304,768]{1,0:T(8,128)(2,1)S(1)}, u32[]{:S(2)}, u32[]{:S(2)}) collective-permute-start(bf16[304,768]{1,0:T(8,128)(2,1)S(1)} %pad_maximum_fusion.r_1_), channel_id=1, source_target_pairs={{0,32},{32,64},{64,96},{96,128},{128,160},{160,192},{192,224},{224... | collective-permute-start | bytes 1400840 | tf_op jit(solution)/shard_map/ppermute | solution.py:355
  4.3 14.4 %collective-permute-start.1 = (bf16[304,768]{1,0:T(8,128)(2,1)S(1)}, bf16[304,768]{1,0:T(8,128)(2,1)S(1)}, u32[]{:S(2)}, u32[]{:S(2)}) collective-permute-start(bf16[304,768]{1,0:T(8,128)(2,1)S(1)} %pad_maximum_fusion.r_1_), channel_id=1, source_target_pairs={{0,224},{32,0},{64,32},{96,64},{128,96},{160,128},{192,160},{224,1... | collective-permute-start | bytes 1400840 | tf_op jit(solution)/shard_map/ppermute | solution.py:355
  10.7 39.6 %all-to-all-start = ((bf16[8,160,768]{2,1,0:T(8,128)(2,1)}), bf16[8,160,768]{2,1,0:T(8,128)(2,1)S(1)}, u32[]{:S(2)}, u32[]{:S(2)}) async-start(bf16[8,160,768]{2,1,0:T(8,128)(2,1)} %repeat.1), calls=%async_computation | async-start | bytes 3932160 | tf_op jit(solution)/shard_map/all_to_all | solution.py:370
  18.7 21.8 %copy-start.7 = (bf16[304,768]{1,0:T(8,128)(2,1)}, bf16[304,768]{1,0:T(8,128)(2,1)S(1)}, u32[]{:S(2)}) copy-start(bf16[304,768]{1,0:T(8,128)(2,1)S(1)} %collective-permute-done.r_2_) | copy-start | bytes 1400836
  18.7 14.3 %copy-start.8 = (bf16[304,768]{1,0:T(8,128)(2,1)}, bf16[304,768]{1,0:T(8,128)(2,1)S(1)}, u32[]{:S(2)}) copy-start(bf16[304,768]{1,0:T(8,128)(2,1)S(1)} %collective-permute-done.1.r_3_) | copy-start | bytes 1400836
  18.7 11.0 %collective-permute-start.3 = (bf16[304,768]{1,0:T(8,128)(2,1)S(1)}, bf16[304,768]{1,0:T(8,128)(2,1)S(1)}, u32[]{:S(2)}, u32[]{:S(2)}) collective-permute-start(bf16[304,768]{1,0:T(8,128)(2,1)S(1)} %collective-permute-done.1.r_3_), channel_id=1, source_target_pairs={{0,224},{32,0},{64,32},{96,64},{128,96},{160,128},{192,160},{224,1... | collective-permute-start | bytes 1400840 | tf_op jit(solution)/shard_map/ppermute | solution.py:355
  21.1 11.9 %collective-permute-start.2 = (bf16[304,768]{1,0:T(8,128)(2,1)S(1)}, bf16[304,768]{1,0:T(8,128)(2,1)S(1)}, u32[]{:S(2)}, u32[]{:S(2)}) collective-permute-start(bf16[304,768]{1,0:T(8,128)(2,1)S(1)} %collective-permute-done.r_2_), channel_id=1, source_target_pairs={{0,32},{32,64},{64,96},{96,128},{128,160},{160,192},{192,224},{224... | collective-permute-start | bytes 1400840 | tf_op jit(solution)/shard_map/ppermute | solution.py:355
  29.8 10.8 %collective-permute-start.5 = (bf16[304,768]{1,0:T(8,128)(2,1)S(1)}, bf16[304,768]{1,0:T(8,128)(2,1)S(1)}, u32[]{:S(2)}, u32[]{:S(2)}) collective-permute-start(bf16[304,768]{1,0:T(8,128)(2,1)S(1)} %collective-permute-done.3.r_5_), channel_id=1, source_target_pairs={{0,224},{32,0},{64,32},{96,64},{128,96},{160,128},{192,160},{224,1... | collective-permute-start | bytes 1400840 | tf_op jit(solution)/shard_map/ppermute | solution.py:355
  33.0 11.0 %copy-start.10 = (bf16[304,768]{1,0:T(8,128)(2,1)}, bf16[304,768]{1,0:T(8,128)(2,1)S(1)}, u32[]{:S(2)}) copy-start(bf16[304,768]{1,0:T(8,128)(2,1)S(1)} %collective-permute-done.2.r_4_) | copy-start | bytes 1400836
  33.0 11.0 %collective-permute-start.4 = (bf16[304,768]{1,0:T(8,128)(2,1)S(1)}, bf16[304,768]{1,0:T(8,128)(2,1)S(1)}, u32[]{:S(2)}, u32[]{:S(2)}) collective-permute-start(bf16[304,768]{1,0:T(8,128)(2,1)S(1)} %collective-permute-done.2.r_4_), channel_id=1, source_target_pairs={{0,32},{32,64},{64,96},{96,128},{128,160},{160,192},{192,224},{224... | collective-permute-start | bytes 1400840 | tf_op jit(solution)/shard_map/ppermute | solution.py:355
  40.5 9.8 %copy-start.3 = (bf16[304,768]{1,0:T(8,128)(2,1)}, bf16[304,768]{1,0:T(8,128)(2,1)S(1)}, u32[]{:S(2)}) copy-start(bf16[304,768]{1,0:T(8,128)(2,1)S(1)} %collective-permute-done.5.r_7_) | copy-start | bytes 1400836
  40.5 9.8 %collective-permute-start.7 = (bf16[160,768]{1,0:T(8,128)(2,1)S(1)}, bf16[160,768]{1,0:T(8,128)(2,1)S(1)}, u32[]{:S(2)}, u32[]{:S(2)}) collective-permute-start(bf16[160,768]{1,0:T(8,128)(2,1)S(1)} %slice.13), channel_id=1, source_target_pairs={{0,224},{32,0},{64,32},{96,64},{128,96},{160,128},{192,160},{224,1... | collective-permute-start | bytes 737288 | tf_op jit(solution)/shard_map/ppermute | solution.py:355
  44.1 34.2 %copy-start.6 = (f32[3,128]{1,0:T(4,128)S(1)}, f32[3,128]{1,0:T(4,128)}, u32[]{:S(2)}) copy-start(f32[3,128]{1,0:T(4,128)} %lambdas.1) | copy-start | bytes 4612
  44.1 6.3 %collective-permute-start.6 = (bf16[144,768]{1,0:T(8,128)(2,1)S(1)}, bf16[144,768]{1,0:T(8,128)(2,1)S(1)}, u32[]{:S(2)}, u32[]{:S(2)}) collective-permute-start(bf16[144,768]{1,0:T(8,128)(2,1)S(1)} %slice.12), channel_id=1, source_target_pairs={{0,32},{32,64},{64,96},{96,128},{128,160},{160,192},{192,224},{224... | collective-permute-start | bytes 663560 | tf_op jit(solution)/shard_map/ppermute | solution.py:355
  66.6 5.0 %collective-permute-start.8 = (f32[8,1152]{1,0:T(8,128)S(1)}, f32[8,1152]{1,0:T(8,128)S(1)}, u32[]{:S(2)}, u32[]{:S(2)}) collective-permute-start(f32[8,1152]{1,0:T(8,128)S(1)} %get-tuple-element.23.a_ref.r_1_), channel_id=1, source_target_pairs={{0,16},{16,0},{1,17},{17,1},{2,18},{18,2},{3,19},{19,3},{4,20},{20... | collective-permute-start | bytes 110600 | tf_op jit(solution)/shard_map/ppermute | solution.py:359
  71.6 6.7 %collective-permute-start.9 = (f32[8,1152]{1,0:T(8,128)S(1)}, f32[8,1152]{1,0:T(8,128)S(1)}, u32[]{:S(2)}, u32[]{:S(2)}) collective-permute-start(f32[8,1152]{1,0:T(8,128)S(1)} %merge.1.r_2_), channel_id=1, source_target_pairs={{0,4},{4,0},{8,12},{12,8},{1,5},{5,1},{9,13},{13,9},{2,6},{6,2},{1... | collective-permute-start | bytes 110600 | tf_op jit(solution)/shard_map/ppermute | solution.py:359
  74.2 5.7 %collective-permute-start.10 = (f32[8,1152]{1,0:T(8,128)S(1)}, f32[8,1152]{1,0:T(8,128)S(1)}, u32[]{:S(2)}, u32[]{:S(2)}) collective-permute-start(f32[8,1152]{1,0:T(8,128)S(1)} %merge.1.r_2_), channel_id=1, source_target_pairs={{0,8},{4,12},{8,0},{12,4},{1,9},{5,13},{9,1},{13,5},{2,10},{6,14},... | collective-permute-start | bytes 110600 | tf_op jit(solution)/shard_map/ppermute | solution.py:359
  78.2 4.0 %collective-permute-start.11 = (f32[8,1152]{1,0:T(8,128)S(1)}, f32[8,1152]{1,0:T(8,128)S(1)}, u32[]{:S(2)}, u32[]{:S(2)}) collective-permute-start(f32[8,1152]{1,0:T(8,128)S(1)} %merge.1.r_2_), channel_id=1, source_target_pairs={{0,12},{4,8},{8,4},{12,0},{1,13},{5,9},{9,5},{13,1},{2,14},{6,10},... | collective-permute-start | bytes 110600 | tf_op jit(solution)/shard_map/ppermute | solution.py:359
  85.2 19.3 %all-to-all-start.1 = ((bf16[8,144,768]{2,1,0:T(8,128)(2,1)}), bf16[8,144,768]{2,1,0:T(8,128)(2,1)S(1)}, u32[]{:S(2)}, u32[]{:S(2)}) async-start(bf16[8,144,768]{2,1,0:T(8,128)(2,1)} %weigh.1), calls=%async_computation.1 | async-start | bytes 3538944 | tf_op jit(solution)/shard_map/all_to_all | solution.py:386
  106.8 11.1 %collective-permute-start.12 = (bf16[144,1280]{1,0:T(8,128)(2,1)S(1)}, bf16[144,1280]{1,0:T(8,128)(2,1)S(1)}, u32[]{:S(2)}, u32[]{:S(2)}) collective-permute-start(bf16[144,1280]{1,0:T(8,128)(2,1)S(1)} %get-tuple-element.26), channel_id=1, source_target_pairs={{0,1},{1,0},{2,3},{3,2},{4,5},{5,4},{6,7},{7,6},{8,9},{9,8},{10,11... | collective-permute-start | bytes 1105928 | tf_op jit(solution)/shard_map/ppermute | solution.py:359
  118.0 10.3 %copy-start.2 = (bf16[144,1280]{1,0:T(8,128)(2,1)S(1)}, bf16[144,1280]{1,0:T(8,128)(2,1)}, u32[]{:S(2)}) copy-start(bf16[144,1280]{1,0:T(8,128)(2,1)} %param.15) | copy-start | bytes 1105924
  118.0 10.3 %collective-permute-start.13 = (bf16[144,1280]{1,0:T(8,128)(2,1)S(1)}, bf16[144,1280]{1,0:T(8,128)(2,1)S(1)}, u32[]{:S(2)}, u32[]{:S(2)}) collective-permute-start(bf16[144,1280]{1,0:T(8,128)(2,1)S(1)} %add_convert_fusion.1), channel_id=1, source_target_pairs={{0,2},{2,0},{1,3},{3,1},{4,6},{6,4},{5,7},{7,5},{8,10},{10,8},{9,1... | collective-permute-start | bytes 1105928 | tf_op jit(solution)/shard_map/ppermute | solution.py:359
  121.7 6.7 %collective-permute-start.14 = (bf16[144,1280]{1,0:T(8,128)(2,1)S(1)}, bf16[144,1280]{1,0:T(8,128)(2,1)S(1)}, u32[]{:S(2)}, u32[]{:S(2)}) collective-permute-start(bf16[144,1280]{1,0:T(8,128)(2,1)S(1)} %get-tuple-element.30), channel_id=1, source_target_pairs={{0,1},{1,0},{2,3},{3,2},{4,5},{5,4},{6,7},{7,6},{8,9},{9,8},{10,11... | collective-permute-start | bytes 1105928 | tf_op jit(solution)/shard_map/ppermute | solution.py:359
  (4 other events, 15.0 us)
